TPU v7x, 256 devices: a whole 4x4x8 slice. The times are simulated.
256 devices in a mesh: dom: 16 (over x_hi, y, core), blk: 16 (over z, x_lo).
Axes of the slice: x: 4 (x_hi: 2, x_lo: 2; x = x_hi * 2 + x_lo), y: 4, z: 8, core: 2. Of those that a mesh axis runs over, the one named last changes fastest.
Arguments:
- particles: bfloat16 [32768, 4096], P(('dom', 'blk')), may hold values from -52 to 52
- references: bfloat16 [48, 12, 4096], P('blk'), may hold values from -0.09375 to 0.09375
- noise_weight: float32 [2048], replicated, may hold values from 0.5 to 2
- offsets: int32 [4, 2], replicated, may hold values from -6 to 6
- candidates: int32 [32768, 8], P(('dom', 'blk')), may hold values from 0 to 47, all different within a row
- class_owner: int32 [48], replicated, may hold values from 0 to 15, as said below
Outputs:
- class_means: float32 [128, 4096], P('dom', 'blk')
- class_mass: float32 [128], P('dom')
- log_evidence: float32 [32768], P(('dom', 'blk'))
Inputs may be any that keep to these rules, and one draw needn't show every extreme that they name: `class_owner`: each class is owned by one index; no index owns more than 8 classes and one owns exactly 8.
All inputs are finite; a program needn't handle non-finite values.
Results may differ from a plain program's by a relative error of at most 0.004.
Values may be sent and summed in bfloat16 or wider, within the bound.
No kernel may reach another device: no remote copies, remote signals or barrier semaphores. Data moves between devices by JAX's collectives and lax.ppermute only.
A program may use at most 128 MiB of HBM per device.

v0:
```python
import math

import jax
import jax.numpy as jnp
from jax import lax
from jax.sharding import PartitionSpec as P

KROW = 64
KCOL = 32
BOX = 256
SLOTS = 8


INV_TEMP = 4.0
FLOOR = -1e30


def phase_tables(offsets):
    index = jnp.arange(KROW * KCOL, dtype=jnp.int32)
    column = index % KCOL
    rowpos = index // KCOL - KROW // 2
    turns = (offsets[:, 0:1] * column[None, :] + offsets[:, 1:2] * rowpos[None, :]).astype(
        jnp.float32
    )
    angle = turns * (2.0 * math.pi / BOX)
    return (jnp.cos(angle), jnp.sin(angle))


def on_device(particles, references, noise_weight, offsets, candidates, class_owner):
    count_rows = particles.shape[0]
    width = particles.shape[1]
    half_width = width // 2
    classes = class_owner.shape[0]
    rotations = references.shape[1]
    cosine, sine = phase_tables(offsets)
    class_ids = jnp.arange(classes, dtype=jnp.int32)
    allowed = jnp.any(candidates[:, :, None] == class_ids[None, None, :], axis=1)
    piece = lax.all_gather(references, "blk", axis=0, tiled=True)
    running = jnp.full((count_rows,), FLOOR, jnp.float32)
    local_classes = piece.shape[0]
    flat = piece.reshape(local_classes * rotations, width).astype(jnp.float32)
    ref_real = flat[:, :half_width]
    ref_imag = flat[:, half_width:]
    energy = jnp.sum(noise_weight * (ref_real * ref_real + ref_imag * ref_imag), axis=1)
    energy = energy.reshape(local_classes, rotations)
    shift_start = 0
    cos_part = cosine[shift_start : shift_start + 4, None, :]
    sin_part = sine[shift_start : shift_start + 4, None, :]
    shifted_real = noise_weight * (cos_part * ref_real - sin_part * ref_imag)
    shifted_imag = noise_weight * (sin_part * ref_real + cos_part * ref_imag)
    shifted = jnp.concatenate([shifted_real, shifted_imag], axis=2).astype(jnp.bfloat16)
    shifted = shifted.reshape(4 * local_classes * rotations, width)
    scores = lax.dot_general(
        particles, shifted, (((1,), (1,)), ((), ())), preferred_element_type=jnp.float32
    )
    blocks = scores.reshape(count_rows, 4, local_classes, rotations)
    loglik = INV_TEMP * (blocks - 0.5 * energy[None, None])
    wanted = allowed[:, None, :, None]
    peak = jnp.max(jnp.where(wanted, loglik, FLOOR), axis=(1, 2, 3))
    updated = jnp.maximum(running, peak)
    terms = jnp.sum(jnp.where(wanted, jnp.exp(loglik - updated[:, None, None, None]), 0.0), axis=3)
    totals = terms
    totals, running = (totals, updated)
    evidence = jnp.sum(totals, axis=(1, 2))
    log_evidence = running + jnp.log(evidence)
    probs = totals / evidence[:, None, None]
    mass = jnp.sum(probs, axis=(0, 1))
    probs_low = probs.astype(jnp.bfloat16)
    shift_start = 0
    gathered = jnp.einsum("psc,pk->sck", probs_low, particles, preferred_element_type=jnp.float32)
    g_real = gathered[:, :, :half_width]
    g_imag = gathered[:, :, half_width:]
    cos_part = cosine[shift_start : shift_start + 4, None, :]
    sin_part = sine[shift_start : shift_start + 4, None, :]
    sum_real = jnp.sum(cos_part * g_real + sin_part * g_imag, axis=0)
    sum_imag = jnp.sum(cos_part * g_imag - sin_part * g_real, axis=0)
    class_part = jnp.concatenate([sum_real, sum_imag], axis=1)
    dom_count = lax.axis_size("dom")
    blk_count = lax.axis_size("blk")
    columns = width // blk_count
    shared_owner = class_owner[:, None] == class_owner[None, :]
    earlier = class_ids[:, None] < class_ids[None, :]
    position = jnp.sum((shared_owner & earlier).astype(jnp.int32), axis=0)
    target = class_owner * SLOTS + position
    placement = (jnp.arange(dom_count * SLOTS, dtype=jnp.int32)[:, None] == target[None, :]).astype(
        jnp.float32
    )
    highest = lax.Precision.HIGHEST
    part_three = class_part.reshape(classes, blk_count, columns)
    placement_three = placement.reshape(dom_count, SLOTS, classes)
    outgoing = jnp.einsum("dsc,cbk->dbsk", placement_three, part_three, precision=highest)
    outgoing = outgoing.reshape(dom_count * blk_count * SLOTS, columns)
    placed_mass = jnp.dot(placement, mass, precision=highest).reshape(dom_count, 1, SLOTS)
    mass_out = jnp.broadcast_to(placed_mass, (dom_count, blk_count, SLOTS)).reshape(
        dom_count * blk_count * SLOTS
    )
    owned, owned_mass = (
        lax.psum_scatter(outgoing, ("dom", "blk"), scatter_dimension=0, tiled=True),
        lax.psum_scatter(mass_out, ("dom", "blk"), scatter_dimension=0, tiled=True),
    )
    means = owned / (owned_mass[:, None] + 1.0)
    return (means, owned_mass, log_evidence)


def solution(mesh):
    return jax.shard_map(
        on_device,
        mesh=mesh,
        in_specs=(
            P(("dom", "blk"), None),
            P("blk", None, None),
            P(),
            P(),
            P(("dom", "blk"), None),
            P(),
        ),
        out_specs=(P("dom", "blk"), P("dom"), P(("dom", "blk"))),
        check_vma=False,
    )
```

profile of v0, /device:TPU:1, one launch (start us, length us, event | category | flops | bytes accessed | tf_op | source)
XLA Modules:
  0.0 1461.7 jit_solution(10733477583402181890)
XLA Ops:
  7.2 0.0 copy-start
  7.2 0.0 all-gather.2.cloned.1.call-start
  7.2 0.7 all-gather.2.cloned.1.call-update
  7.9 0.0 reduce-scatter.2.cloned.1.call-start
  8.0 0.7 fusion.12
  8.7 0.1 broadcast_in_dim.26
  8.8 0.2 broadcast_in_dim.27
  9.0 0.8 convert_reduce_fusion
  9.8 0.7 multiply_add_fusion.2
  10.5 0.8 slice_bitcast_fusion.1
  11.2 0.3 fusion.22
  11.5 0.0 copy-start.1
  11.6 142.4 %all-gather.2.cloned.1.call-done = bf16[48,12,4096]{2,1,0:T(8,128)(2,1)} async-done(((bf16[3,12,4096]{2,1,0:T(8,128)(2,1)}), bf16[48,12,4096]{2,1,0:T(8,128)(2,1)}) %all-gather.2.cloned.1.call-update) | async-done | bytes 4718608 | tf_op jit(solution)/shard_map/all_gather | solution.py:38
  153.9 8.5 reshape.231
  162.4 0.0 copy-done.1
  162.4 8.5 multiply_reduce_fusion
  171.0 0.1 mul.227
  171.1 0.1 sub.58
  171.2 11.6 multiply_subtract_fusion
  182.8 13.2 fusion.5
  196.0 0.0 copy-done
  196.0 8.5 select_reduce_fusion.2
  204.6 1.3 reshape.227
  205.9 1.7 select_reduce_fusion.1
  207.6 0.6 select_reduce_fusion
  208.2 0.6 fusion.9
  208.8 0.5 add_reduce_fusion
  209.3 0.1 pad_maximum_fusion
  209.4 0.2 copy.22
  209.6 1.4 convolution_bitcast_fusion
  211.1 2.6 copy.17
  213.6 0.0 reduce-scatter.2.cloned.1.call-update
  213.7 0.1 fusion.16
  213.8 0.4 fusion.13
  214.2 0.1 copy.19
  214.3 0.1 reshape.230
  214.4 77.8 %all-reduce = f32[2048]{0:T(1024)S(1)} all-reduce(f32[2048]{0:T(1024)S(1)} %reshape.230), channel_id=3, replica_groups=mesh['dom'=16,'blk'=16] {'dom','blk'}, use_global_device_ids=true, to_apply=%region_10.11.clone | all-reduce | flops 2048 | bytes 16384
  292.2 0.6 broadcast_add_fusion
  292.7 0.5 log_add_fusion
  293.3 1160.2 %reduce-scatter.2.cloned.1.call-done = f32[8,256]{1,0:T(8,128)} async-done(((f32[2048,256]{1,0:T(8,128)}), f32[8,256]{1,0:T(8,128)}) %reduce-scatter.2.cloned.1.call-update) | async-done | bytes 8208 | tf_op jit(solution)/shard_map/reduce_scatter | solution.py:98
  1453.5 1.4 broadcast_divide_fusion.2
  (6 shorter events, 0.1 us)
Async XLA Ops:
  7.2 188.9 %copy-start = (bf16[128,4096]{1,0:T(8,128)(2,1)S(1)}, bf16[128,4096]{1,0:T(8,128)(2,1)}, u32[]{:S(2)}) copy-start(bf16[128,4096]{1,0:T(8,128)(2,1)} %param.6) | copy-start | bytes 3145732
  7.2 146.8 %all-gather.2.cloned.1.call-start = ((), (), s32[]{:S(2)}) async-start(), calls=%async_computation.1 | async-start | bytes 6684672 | tf_op jit(solution)/shard_map/all_gather | solution.py:38
  7.9 1445.5 %reduce-scatter.2.cloned.1.call-start = ((), (), s32[]{:S(2)}) async-start(), calls=%async_computation.2 | async-start | bytes 2105344 | tf_op jit(solution)/shard_map/reduce_scatter | solution.py:98
  11.5 150.9 %copy-start.1 = (f32[2048]{0:T(1024)S(1)}, f32[2048]{0:T(1024)}, u32[]{:S(2)}) copy-start(f32[2048]{0:T(1024)} %param.8) | copy-start | bytes 24580
Sparse Core Ops, SparseCore 0:
  9.8 144.0 all-gather.1
  213.8 1239.6 reduce-scatter.1
where the time goes:
time: 1490 us; the launch traced here: 1460 us
  waiting for transfers between devices  1300 us (87%)
  blocking collectives  77.8 us (5%)
  other arithmetic  41.4 us (3%)
    reduce_scatter x1, waiting for transfers between devices, on_device(): lax.psum_scatter(outgoing, ('dom', 'blk'), scatter_dimension=0, tiled=True)  1160 us
    all_gather x1, waiting for transfers between devices, on_device(): piece = lax.all_gather(references, 'blk', axis=0, tiled=True)  142 us
    unnamed x1, blocking collectives  77.8 us
  transfers between devices with their start and end apart: 2, of which 2 were waited for; matrix products, arithmetic and copies ran while one was open for 0% of the time, Pallas kernels for 0%

commit v1 on v0

v1 whole, which is shorter than its diff:
```python
import math

import jax
import jax.numpy as jnp
import numpy as np
from jax import lax
from jax.experimental import pallas as pl
from jax.experimental.pallas import tpu as pltpu
from jax.sharding import Mesh, PartitionSpec as P

KROW = 64
KCOL = 32
BOX = 256
SLOTS = 8
INV_TEMP = 4.0
FLOOR = -1e30

FINE = (("xh", 2), ("yh", 2), ("yl", 2), ("core", 2), ("z", 8), ("xl", 2))
DOM = ("xh", "yh", "yl", "core")
BLK = ("z", "xl")
POOL = ("yl", "core")

K = 2048
CLASSES = 48
ROT = 12
NSHIFT = 4
ROWS = 128
NPOOL = 4
QROT = ROT // NPOOL
QCLS = CLASSES // NPOOL
NBLK = 16
NDOM = 16
LOCAL = 3
COLS = 256
F32 = jnp.float32
BF16 = jnp.bfloat16
VMEM = pltpu.VMEM
SMEM_SPEC = pl.BlockSpec(memory_space=pltpu.SMEM)
VMEM_SPEC = pl.BlockSpec(memory_space=pltpu.VMEM)
ANY_SPEC = pl.BlockSpec(memory_space=pl.ANY)


def params(mib):
    return pltpu.CompilerParams(vmem_limit_bytes=mib << 20)


def pack_kernel(q_ref, refs_ref, out_ref, wide, rows):
    q = q_ref[0]
    wide[...] = refs_ref[...].astype(F32)
    for c in range(LOCAL):
        for r in range(QROT):
            row = wide[c, pl.ds(QROT * q + r, 1), :]
            for a in range(32):
                at = (c * QROT + r) * 32 + a
                rows[at : at + 1, :] = row[:, a * 128 : (a + 1) * 128]
    packed = rows[...].astype(BF16)
    for d in range(NBLK):
        out_ref[d] = packed


def pool_copies(q, parts, pool, sem):
    copies = []
    for j, part in enumerate(parts):
        start = pl.multiple_of((q ^ j) * ROWS, ROWS)
        copies.append(pltpu.make_async_copy(part, pool.at[pl.ds(start, ROWS), :], sem.at[j]))
    return copies


def score_kernel(
    q_ref, refs_ref, p0, p1, p2, p3, wc_ref, ws_ref, w_ref, cand_ref, out_ref, wide, table, pool, sem
):
    q = q_ref[0]
    copies = pool_copies(q, (p0, p1, p2, p3), pool, sem)
    for copy in copies:
        copy.start()
    wide[...] = refs_ref[...].astype(F32)
    energy = [jnp.zeros((CLASSES, 128), F32) for _ in range(QROT)]
    stride = QROT * 32
    for a in range(16):
        weight = w_ref[a : a + 1, :]
        for r in range(QROT):
            real = wide[pl.ds(r * 32 + a, CLASSES, stride=stride), :]
            imag = wide[pl.ds(r * 32 + 16 + a, CLASSES, stride=stride), :]
            energy[r] = energy[r] + weight * (real * real + imag * imag)
            for s in range(NSHIFT):
                wc = wc_ref[s * 16 + a : s * 16 + a + 1, :]
                ws = ws_ref[s * 16 + a : s * 16 + a + 1, :]
                row = (s * QROT + r) * CLASSES
                table[row : row + CLASSES, a * 128 : (a + 1) * 128] = (wc * real - ws * imag).astype(BF16)
                table[row : row + CLASSES, K + a * 128 : K + (a + 1) * 128] = (ws * real + wc * imag).astype(BF16)
    half_energy = [0.5 * jnp.sum(e, axis=1, keepdims=True) for e in energy]
    for copy in copies:
        copy.wait()
    class_id = lax.broadcasted_iota(jnp.int32, (CLASSES, 256), 0)
    for n in range(2):
        lanes = slice(n * 256, (n + 1) * 256)
        scores = lax.dot_general(
            table[...], pool[lanes, :], (((1,), (1,)), ((), ())), preferred_element_type=F32
        )
        cand = jnp.concatenate([cand_ref[2 * n], cand_ref[2 * n + 1]], axis=1)
        allowed = class_id == cand[0:1, :]
        for k in range(1, 8):
            allowed = allowed | (class_id == cand[k : k + 1, :])
        loglik = []
        for s in range(NSHIFT):
            for r in range(QROT):
                row = (s * QROT + r) * CLASSES
                value = INV_TEMP * (scores[row : row + CLASSES] - half_energy[r])
                loglik.append(jnp.where(allowed, value, FLOOR))
        top = loglik[0]
        for value in loglik[1:]:
            top = jnp.maximum(top, value)
        peak = jnp.max(top, axis=0, keepdims=True)
        evidence = jnp.zeros((1, 256), F32)
        for s in range(NSHIFT):
            terms = jnp.zeros((CLASSES, 256), F32)
            for r in range(QROT):
                value = loglik[s * QROT + r]
                terms = terms + jnp.where(allowed, jnp.exp(value - peak), 0.0)
            evidence = evidence + jnp.sum(terms, axis=0, keepdims=True)
            for d in range(NPOOL):
                out_ref[d, s * QCLS : (s + 1) * QCLS, lanes] = terms[d * QCLS : (d + 1) * QCLS]
        for d in range(NPOOL):
            out_ref[d, 48:49, lanes] = peak
            out_ref[d, 49:50, lanes] = evidence
            out_ref[d, 50:56, lanes] = jnp.zeros((6, 256), F32)


def class_kernel(
    q_ref, x_ref, p0, p1, p2, p3, cos_ref, sin_ref, out_ref, log_ref, pool, slots, line, sem
):
    q = q_ref[0]
    copies = pool_copies(q, (p0, p1, p2, p3), pool, sem)
    for copy in copies:
        copy.start()
    peak = x_ref[0, 48:49, :]
    for j in range(1, NPOOL):
        peak = jnp.maximum(peak, x_ref[j, 48:49, :])
    evidence = jnp.zeros_like(peak)
    terms = jnp.zeros((NSHIFT * QCLS, NPOOL * ROWS), F32)
    for j in range(NPOOL):
        scale = jnp.exp(x_ref[j, 48:49, :] - peak)
        evidence = evidence + scale * x_ref[j, 49:50, :]
        terms = terms + scale * x_ref[j, 0:48, :]
    line[...] = peak + jnp.log(evidence)
    log_ref[...] = line[:, pl.ds(pl.multiple_of(q * ROWS, ROWS), ROWS)]
    probs = terms / evidence
    for s in range(NSHIFT):
        slots[s * 16 : s * 16 + QCLS, :] = probs[s * QCLS : (s + 1) * QCLS]
        slots[s * 16 + QCLS : (s + 1) * 16, :] = jnp.zeros((4, NPOOL * ROWS), F32)
    padded = slots[...]
    mass = jnp.sum(padded, axis=1, keepdims=True)
    mass = mass[0:16] + mass[16:32] + mass[32:48] + mass[48:64]
    low = padded.astype(BF16)
    row_id = lax.broadcasted_iota(jnp.int32, (16, COLS), 0)
    lane_id = lax.broadcasted_iota(jnp.int32, (16, COLS), 1)
    mass_row = jnp.sum(jnp.where(row_id == lane_id, mass, 0.0), axis=0, keepdims=True)
    mass_high = mass_row.astype(BF16).astype(F32)
    mass_low = mass_row - mass_high
    for copy in copies:
        copy.wait()
    for b in range(NBLK // 2):
        cols = slice(b * COLS, (b + 1) * COLS)
        cols_im = slice(K + b * COLS, K + (b + 1) * COLS)
        g_re = jnp.dot(low, pool[:, cols], preferred_element_type=F32)
        g_im = jnp.dot(low, pool[:, cols_im], preferred_element_type=F32)
        sum_re = jnp.zeros((16, COLS), F32)
        sum_im = jnp.zeros((16, COLS), F32)
        for s in range(NSHIFT):
            c = cos_ref[s : s + 1, cols]
            z = sin_ref[s : s + 1, cols]
            re = g_re[s * 16 : (s + 1) * 16]
            im = g_im[s * 16 : (s + 1) * 16]
            sum_re = sum_re + (c * re + z * im)
            sum_im = sum_im + (c * im - z * re)
        for dest, value in ((b, sum_re), (NBLK // 2 + b, sum_im)):
            value = jnp.where(row_id == QCLS, mass_high, value)
            value = jnp.where(row_id == QCLS + 1, mass_low, value)
            out_ref[dest] = value.astype(BF16)


def place_kernel(target_ref, y_ref, out_ref):
    total = y_ref[0].astype(F32)
    for b in range(1, NBLK):
        total = total + y_ref[b].astype(F32)
    mass = total[QCLS : QCLS + 1, 0:128] + total[QCLS + 1 : QCLS + 2, 0:128]
    row = lax.broadcasted_iota(jnp.int32, (NDOM * 16, 128), 0)
    slot = row % 16
    wanted = (row // 16) * SLOTS + slot % 8
    hit = target_ref[...] == wanted
    pick = jnp.where(hit & (slot < 8), 1.0, 0.0).astype(BF16)
    placed = jnp.dot(pick[:, 0:16], total.astype(BF16), preferred_element_type=F32)
    placed_mass = jnp.sum(jnp.where(hit & (slot >= 8), mass, 0.0), axis=1, keepdims=True)
    high = placed_mass.astype(BF16).astype(F32)
    lane = lax.broadcasted_iota(jnp.int32, (NDOM * 16, COLS), 1)
    extra = jnp.where(lane == 0, high, jnp.where(lane == 1, placed_mass - high, 0.0))
    out = (placed + extra).astype(BF16)
    out_ref[...] = out.reshape(NDOM, 16, COLS)


def mean_kernel(z_ref, mean_ref, mass_ref):
    total = z_ref[0].astype(F32)
    for d in range(1, NDOM):
        total = total + z_ref[d].astype(F32)
    mass = total[8:16, 0:1] + total[8:16, 1:2]
    mean_ref[...] = total[0:8] / (mass + 1.0)
    mass_ref[...] = jnp.broadcast_to(mass, (SLOTS, 128))


def phase_tables(offsets):
    index = jnp.arange(KROW * KCOL, dtype=jnp.int32)
    column = index % KCOL
    rowpos = index // KCOL - KROW // 2
    turns = (offsets[:, 0:1] * column[None, :] + offsets[:, 1:2] * rowpos[None, :]).astype(F32)
    angle = turns * (2.0 * math.pi / BOX)
    return (jnp.cos(angle), jnp.sin(angle))


def swap(x, axis):
    return lax.ppermute(x, axis, [(0, 1), (1, 0)])


def on_device(particles, references, noise_weight, offsets, candidates, class_owner):
    pool_index = (lax.axis_index("yl") * 2 + lax.axis_index("core")).astype(jnp.int32)
    q = pool_index.reshape(1)

    far = swap(particles, "yl")
    packed = pl.pallas_call(
        pack_kernel,
        out_shape=jax.ShapeDtypeStruct((NBLK, LOCAL * QROT * 32, 128), BF16),
        in_specs=[SMEM_SPEC, VMEM_SPEC],
        out_specs=VMEM_SPEC,
        scratch_shapes=[VMEM((LOCAL, ROT, 2 * K), F32), VMEM((LOCAL * QROT * 32, 128), F32)],
        compiler_params=params(16),
        name="pack",
    )(q, references)
    gathered = lax.all_to_all(packed, BLK, 0, 0, tiled=True)
    near = swap(particles, "core")
    far_near = swap(far, "core")
    pool = (particles, near, far, far_near)

    cand = lax.all_gather(candidates.T, POOL, axis=0, tiled=False)
    cosine, sine = phase_tables(offsets)
    wc = (noise_weight * cosine).reshape(NSHIFT * 16, 128)
    ws = (noise_weight * sine).reshape(NSHIFT * 16, 128)
    weight = noise_weight.reshape(16, 128)

    copies = pltpu.SemaphoreType.DMA((NPOOL,))
    pool_shape = VMEM((NPOOL * ROWS, 2 * K), BF16)
    terms = pl.pallas_call(
        score_kernel,
        out_shape=jax.ShapeDtypeStruct((NPOOL, 56, NPOOL * ROWS), F32),
        in_specs=[SMEM_SPEC, VMEM_SPEC] + [ANY_SPEC] * 4 + [VMEM_SPEC] * 4,
        out_specs=VMEM_SPEC,
        scratch_shapes=[
            VMEM((NBLK * LOCAL * QROT * 32, 128), F32),
            VMEM((NSHIFT * QROT * CLASSES, 2 * K), BF16),
            pool_shape,
            copies,
        ],
        compiler_params=params(40),
        name="score",
    )(q, gathered.reshape(NBLK * LOCAL * QROT * 32, 128), *pool, wc, ws, weight, cand)
    terms = lax.all_to_all(terms, POOL, 0, 0, tiled=True)

    sums, log_evidence = pl.pallas_call(
        class_kernel,
        out_shape=(
            jax.ShapeDtypeStruct((NBLK, 16, COLS), BF16),
            jax.ShapeDtypeStruct((1, ROWS), F32),
        ),
        in_specs=[SMEM_SPEC, VMEM_SPEC] + [ANY_SPEC] * 4 + [VMEM_SPEC] * 2,
        out_specs=(VMEM_SPEC, VMEM_SPEC),
        scratch_shapes=[
            pool_shape,
            VMEM((NSHIFT * 16, NPOOL * ROWS), F32),
            VMEM((1, NPOOL * ROWS), F32),
            copies,
        ],
        compiler_params=params(24),
        name="classes",
    )(q, terms, *pool, cosine, sine)
    sums = lax.all_to_all(sums, BLK, 0, 0, tiled=True)

    class_ids = jnp.arange(CLASSES, dtype=jnp.int32)
    shared_owner = class_owner[:, None] == class_owner[None, :]
    earlier = class_ids[:, None] < class_ids[None, :]
    position = jnp.sum((shared_owner & earlier).astype(jnp.int32), axis=0)
    target = class_owner * SLOTS + position
    mine = lax.dynamic_slice(target, (pool_index * QCLS,), (QCLS,))
    mine = jnp.pad(mine, (0, 128 - QCLS), constant_values=-1).reshape(1, 128)
    placed = pl.pallas_call(
        place_kernel,
        out_shape=jax.ShapeDtypeStruct((NDOM, 16, COLS), BF16),
        in_specs=[VMEM_SPEC, VMEM_SPEC],
        out_specs=VMEM_SPEC,
        name="place",
    )(mine, sums)
    placed = lax.all_to_all(placed, DOM, 0, 0, tiled=True)
    means, mass = pl.pallas_call(
        mean_kernel,
        out_shape=(
            jax.ShapeDtypeStruct((SLOTS, COLS), F32),
            jax.ShapeDtypeStruct((SLOTS, 128), F32),
        ),
        in_specs=[VMEM_SPEC],
        out_specs=(VMEM_SPEC, VMEM_SPEC),
        name="means",
    )(placed)
    return (means, mass[:, 0], log_evidence.reshape(ROWS))


def solution(mesh):
    fine = Mesh(
        np.asarray(mesh.devices).reshape([size for _, size in FINE]), [name for name, _ in FINE]
    )
    every = DOM + BLK
    return jax.shard_map(
        on_device,
        mesh=fine,
        in_specs=(P(every, None), P(BLK, None, None), P(), P(), P(every, None), P()),
        out_specs=(P(DOM, BLK), P(DOM), P(every)),
        check_vma=False,
    )
```

time: 1490 us -> 104 us (0.07); the launches traced: 1460 us -> 104 us
  waiting for transfers between devices: 1300 us -> 36 us
  blocking collectives: 77.8 us -> 21.6 us
  other arithmetic: 41.4 us -> 0.64 us
  starting transfers between devices: 0.08 us -> 25.9 us
    reduce_scatter x1 -> x0, waiting for transfers between devices: 1160 us -> none  [on_device(): lax.psum_scatter(outgoing, ('dom', 'blk'), scatter_dimension=0, tiled=True)]
    all_gather x1 -> x0, waiting for transfers between devices: 142 us -> none  [on_device(): piece = lax.all_gather(references, 'blk', axis=0, tiled=True)]
    unnamed x1 -> x0, blocking collectives: 77.8 us -> none
    all_to_all x0 -> x3, starting transfers between devices: none -> 21.4 us  [the longest x1 10.2 us: on_device(): gathered = lax.all_to_all(packed, BLK, 0, 0, tiled=True)]
    ppermute x0 -> x3, waiting for transfers between devices: none -> 21.2 us  [swap(): return lax.ppermute(x, axis, [(0, 1), (1, 0)])]
    all_to_all x0 -> x1, blocking collectives: none -> 16.6 us  [on_device(): placed = lax.all_to_all(placed, DOM, 0, 0, tiled=True)]
  transfers between devices with their start and end apart: 2 -> 6, of which waited for: 2 -> 3; matrix products, arithmetic and copies ran while one was open for 0% -> 1% of each run, Pallas kernels for 0% -> 0%
where the time goes in v1:
time: 104 us
  waiting for transfers between devices  36 us (35%)
  starting transfers between devices  25.9 us (25%)
  blocking collectives  21.6 us (21%)
  Pallas kernels  14.3 us (14%)
  local copies, waits for them, and re-layouts  4.64 us (4%)
    ppermute x3, waiting for transfers between devices, swap(): return lax.ppermute(x, axis, [(0, 1), (1, 0)])  21.2 us
    all_to_all x1, blocking collectives, on_device(): placed = lax.all_to_all(placed, DOM, 0, 0, tiled=True)  16.6 us
    all_to_all x1, starting transfers between devices, on_device(): gathered = lax.all_to_all(packed, BLK, 0, 0, tiled=True)  10.2 us
    all_to_all x1, waiting for transfers between devices, on_device(): sums = lax.all_to_all(sums, BLK, 0, 0, tiled=True)  7.87 us
    all_to_all x1, waiting for transfers between devices, on_device(): terms = lax.all_to_all(terms, POOL, 0, 0, tiled=True)  6.96 us
    all_to_all x1, starting transfers between devices, on_device(): sums = lax.all_to_all(sums, BLK, 0, 0, tiled=True)  6.82 us
    pallas_call x1, Pallas kernels, on_device(): pl.pallas_call(score_kernel, out_shape=jax.ShapeDtypeStruct((NPOOL, 56, N...  6.29 us
    all_gather x1, blocking collectives, on_device(): cand = lax.all_gather(candidates.T, POOL, axis=0, tiled=False)  5.01 us
  transfers between devices with their start and end apart: 6, of which 3 were waited for; matrix products, arithmetic and copies ran while one was open for 1% of the time, Pallas kernels for 0%

profile of v1, /device:TPU:1, one launch (start us, length us, event | category | flops | bytes accessed | tf_op | source)
XLA Modules:
  0.0 103.9 jit_solution(4926607868765165971)
XLA Ops:
  0.6 0.0 copy-start.2
  0.6 1.0 copy-done.2
  1.6 1.3 %pack.1 = bf16[16,288,128]{2,1,0:T(8,128)(2,1)} custom-call(s32[1]{0:T(128)} %bitcast.1.q_ref, bf16[3,12,4096]{2,1,0:T(8,128)(2,1)S(1)} %copy-done.2), custom_call_target="tpu_custom_call" | custom-call | tf_op jit(solution)/shard_map/pack/pallas_call | solution.py:228
  2.9 0.0 copy-start
  2.9 0.0 copy-start.6
  2.9 0.0 copy-start.3
  2.9 0.0 copy-start.5
  2.9 0.0 copy-start.7
  3.0 10.2 %all-to-all-start = ((bf16[16,288,128]{2,1,0:T(8,128)(2,1)}), bf16[16,288,128]{2,1,0:T(8,128)(2,1)S(1)}, u32[]{:S(2)}, u32[]{:S(2)}) async-start(bf16[16,288,128]{2,1,0:T(8,128)(2,1)} %pack.1), calls=%async_computation | async-start | bytes 2359296 | tf_op jit(solution)/shard_map/all_to_all | solution.py:237
  13.2 0.0 copy-done
  13.2 1.4 %collective-permute-start.1 = (bf16[128,4096]{1,0:T(8,128)(2,1)S(1)}, bf16[128,4096]{1,0:T(8,128)(2,1)S(1)}, u32[]{:S(2)}, u32[]{:S(2)}) collective-permute-start(bf16[128,4096]{1,0:T(8,128)(2,1)S(1)} %copy-done), channel_id=1, source_target_pairs={{0,32},{32,0},{1,33},{33,1},{2,34},{34,2},{3,35},{35,3},{4,36},{36... | collective-permute-start | bytes 3145736 | tf_op jit(solution)/shard_map/ppermute | solution.py:220
  14.5 1.2 %collective-permute-start = (bf16[128,4096]{1,0:T(8,128)(2,1)S(1)}, bf16[128,4096]{1,0:T(8,128)(2,1)}, u32[]{:S(2)}, u32[]{:S(2)}) collective-permute-start(bf16[128,4096]{1,0:T(8,128)(2,1)S(1)} %copy-done), channel_id=1, source_target_pairs={{0,16},{16,0},{1,17},{17,1},{2,18},{18,2},{3,19},{19,3},{4,20},{20... | collective-permute-start | bytes 3145736 | tf_op jit(solution)/shard_map/ppermute | solution.py:220
  15.8 21.2 %collective-permute-done.1.p2 = bf16[128,4096]{1,0:T(8,128)(2,1)S(1)} collective-permute-done((bf16[128,4096]{1,0:T(8,128)(2,1)S(1)}, bf16[128,4096]{1,0:T(8,128)(2,1)S(1)}, u32[]{:S(2)}, u32[]{:S(2)}) %collective-permute-start.1) | collective-permute-done | bytes 1048608 | tf_op jit(solution)/shard_map/ppermute | solution.py:220
  37.0 1.9 %collective-permute-start.2 = (bf16[128,4096]{1,0:T(8,128)(2,1)S(1)}, bf16[128,4096]{1,0:T(8,128)(2,1)}, u32[]{:S(2)}, u32[]{:S(2)}) collective-permute-start(bf16[128,4096]{1,0:T(8,128)(2,1)S(1)} %collective-permute-done.1.p2), channel_id=1, source_target_pairs={{0,16},{16,0},{1,17},{17,1},{2,18},{18,2},{3,19},{19,3},{4,20},{20... | collective-permute-start | bytes 3145736 | tf_op jit(solution)/shard_map/ppermute | solution.py:220
  38.8 0.0 copy-done.6
  38.8 0.1 mul.110
  38.9 0.1 mul.111
  39.0 0.1 mul.117
  39.1 0.1 mul.118
  39.2 0.0 copy-done.3
  39.2 0.2 bitcast_multiply_fusion
  39.4 0.0 copy-done.5
  39.4 5.0 %all-gather = s32[32,128]{1,0:T(8,128)S(1)} all-gather(s32[8,128]{1,0:T(8,128)S(1)} %bitcast.47), channel_id=2, replica_groups=mesh['xh'=2,'yh'=2,'yl'=2,'core'=2,'z'=8,'xl'=2] {'yl','core'}, dimensions={0}, use_global_device_ids=true | all-gather | bytes 20480 | tf_op jit(solution)/shard_map/all_gather | solution.py:242
  44.4 0.0 copy-done.7
  44.4 0.1 convert_reduce_fusion
  44.5 0.0 collective-permute-done.p1
  44.5 0.0 collective-permute-done.2.p3
  44.5 0.0 all-to-all-done
  44.5 6.3 %score.1 = f32[4,56,512]{2,1,0:T(8,128)S(1)} custom-call(s32[1]{0:T(128)} %bitcast.1.q_ref, bf16[4608,128]{1,0:T(8,128)(2,1)S(1)} %bitcast.43, bf16[128,4096]{1,0:T(8,128)(2,1)S(1)} %copy-done, bf16[128,4096]{1,0:T(8,128)(2,1)} %collective-permute-done.p1, bf16[128,4096]{1,0:T(8,128)(2,1)S(1)} %collective-permute-done.1.p2, ...), custom_call_target="tpu_custom_call" | custom-call | tf_op jit(solution)/shard_map/score/pallas_call | solution.py:250
  50.8 0.0 copy-start.1
  50.8 0.8 copy-done.1
  51.6 4.4 %all-to-all-start.1 = ((f32[4,56,512]{2,1,0:T(8,128)}), f32[4,56,512]{2,1,0:T(8,128)S(1)}, u32[]{:S(2)}, u32[]{:S(2)}) async-start(f32[4,56,512]{2,1,0:T(8,128)} %copy-done.1), calls=%async_computation.1 | async-start | bytes 917504 | tf_op jit(solution)/shard_map/all_to_all | solution.py:264
  56.0 0.3 fusion.5
  56.3 7.0 %all-to-all-done.1.x_ref = f32[4,56,512]{2,1,0:T(8,128)S(1)} async-done(((f32[4,56,512]{2,1,0:T(8,128)}), f32[4,56,512]{2,1,0:T(8,128)S(1)}, u32[]{:S(2)}, u32[]{:S(2)}) %all-to-all-start.1) | async-done | bytes 458784 | tf_op jit(solution)/shard_map/all_to_all | solution.py:264
  63.3 3.3 %classes.1 = (bf16[16,16,256]{2,1,0:T(8,128)(2,1)}, f32[1,128]{1,0:T(1,128)}) custom-call(s32[1]{0:T(128)} %bitcast.1.q_ref, f32[4,56,512]{2,1,0:T(8,128)S(1)} %all-to-all-done.1.x_ref, bf16[128,4096]{1,0:T(8,128)(2,1)S(1)} %copy-done, bf16[128,4096]{1,0:T(8,128)(2,1)} %collective-permute-done.p1, bf16[128,4096]{1,0:T(8,128)(2,1)S(1)} %collective-permute-done.1.p2, ...), custom_call_target="tpu_custom_call" | custom-call | tf_op jit(solution)/shard_map/classes/pallas_call | solution.py:266
  66.5 6.8 %all-to-all-start.2 = ((bf16[16,16,256]{2,1,0:T(8,128)(2,1)}), bf16[16,16,256]{2,1,0:T(8,128)(2,1)S(1)}, u32[]{:S(2)}, u32[]{:S(2)}) async-start(bf16[16,16,256]{2,1,0:T(8,128)(2,1)} %get-tuple-element.7), calls=%async_computation.2 | async-start | bytes 262144 | tf_op jit(solution)/shard_map/all_to_all | solution.py:283
  73.4 0.1 dynamic_slice.3
  73.4 0.5 pad_bitcast_fusion.target_ref
  74.0 7.9 %all-to-all-done.2.y_ref = bf16[16,16,256]{2,1,0:T(8,128)(2,1)S(1)} async-done(((bf16[16,16,256]{2,1,0:T(8,128)(2,1)}), bf16[16,16,256]{2,1,0:T(8,128)(2,1)S(1)}, u32[]{:S(2)}, u32[]{:S(2)}) %all-to-all-start.2) | async-done | bytes 131104 | tf_op jit(solution)/shard_map/all_to_all | solution.py:283
  81.8 0.0 copy-start.4
  81.8 0.7 copy-done.4
  82.5 1.8 %place.1 = bf16[16,16,256]{2,1,0:T(8,128)(2,1)} custom-call(s32[1,128]{1,0:T(1,128)} %pad_bitcast_fusion.target_ref, bf16[16,16,256]{2,1,0:T(8,128)(2,1)} %copy-done.4), custom_call_target="tpu_custom_call" | custom-call | tf_op jit(solution)/shard_map/place/pallas_call | solution.py:292
  84.3 16.6 %all_to_all.20.z_ref = bf16[16,16,256]{2,1,0:T(8,128)(2,1)} all-to-all(bf16[16,16,256]{2,1,0:T(8,128)(2,1)} %place.1), channel_id=1, replica_groups=mesh['xh'=2,'yh'=2,'yl'=2,'core'=2,'z'=8,'xl'=2] {'xh','yh','yl','core'}, dimensions={0} | all-to-all | bytes 262144 | tf_op jit(solution)/shard_map/all_to_all | solution.py:299
  100.9 1.7 %means.1 = (f32[8,256]{1,0:T(8,128)}, f32[8,128]{1,0:T(8,128)}) custom-call(bf16[16,16,256]{2,1,0:T(8,128)(2,1)} %all_to_all.20.z_ref), custom_call_target="tpu_custom_call" | custom-call | tf_op jit(solution)/shard_map/means/pallas_call | solution.py:300
  102.6 1.3 %slice_reduce_fusion = f32[8]{0:T(128)} fusion(f32[8,128]{1,0:T(8,128)} %get-tuple-element.9), kind=kLoop, calls=%fused_computation.36 | loop fusion | bytes 64 | tf_op jit(solution)/shard_map/slice | solution.py:310
  (4 shorter events, 0.0 us)
Async XLA Ops:
  0.6 1.0 copy-start.2
  2.9 10.2 %copy-start = (bf16[128,4096]{1,0:T(8,128)(2,1)S(1)}, bf16[128,4096]{1,0:T(8,128)(2,1)}, u32[]{:S(2)}) copy-start(bf16[128,4096]{1,0:T(8,128)(2,1)} %p0.3) | copy-start | bytes 3145732
  2.9 35.9 %copy-start.6 = (s32[4,2]{0,1:T(2,128)S(1)}, s32[4,2]{0,1:T(2,128)}, u32[]{:S(2)}) copy-start(s32[4,2]{0,1:T(2,128)} %param.9) | copy-start | bytes 100
  2.9 36.2 %copy-start.3 = (f32[2048]{0:T(1024)S(1)}, f32[2048]{0:T(1024)}, u32[]{:S(2)}) copy-start(f32[2048]{0:T(1024)} %param.8) | copy-start | bytes 24580
  2.9 36.5 %copy-start.5 = (s32[128,8]{0,1:T(8,128)S(1)}, s32[128,8]{0,1:T(8,128)}, u32[]{:S(2)}) copy-start(s32[128,8]{0,1:T(8,128)} %param.10) | copy-start | bytes 12292
  2.9 41.5 %copy-start.7 = (s32[48]{0:T(128)S(1)}, s32[48]{0:T(128)}, u32[]{:S(2)}) copy-start(s32[48]{0:T(128)} %param.11) | copy-start | bytes 580
  3.0 41.6 %all-to-all-start = ((bf16[16,288,128]{2,1,0:T(8,128)(2,1)}), bf16[16,288,128]{2,1,0:T(8,128)(2,1)S(1)}, u32[]{:S(2)}, u32[]{:S(2)}) async-start(bf16[16,288,128]{2,1,0:T(8,128)(2,1)} %pack.1), calls=%async_computation | async-start | bytes 2359296 | tf_op jit(solution)/shard_map/all_to_all | solution.py:237
  13.2 23.8 %collective-permute-start.1 = (bf16[128,4096]{1,0:T(8,128)(2,1)S(1)}, bf16[128,4096]{1,0:T(8,128)(2,1)S(1)}, u32[]{:S(2)}, u32[]{:S(2)}) collective-permute-start(bf16[128,4096]{1,0:T(8,128)(2,1)S(1)} %copy-done), channel_id=1, source_target_pairs={{0,32},{32,0},{1,33},{33,1},{2,34},{34,2},{3,35},{35,3},{4,36},{36... | collective-permute-start | bytes 3145736 | tf_op jit(solution)/shard_map/ppermute | solution.py:220
  14.5 30.0 %collective-permute-start = (bf16[128,4096]{1,0:T(8,128)(2,1)S(1)}, bf16[128,4096]{1,0:T(8,128)(2,1)}, u32[]{:S(2)}, u32[]{:S(2)}) collective-permute-start(bf16[128,4096]{1,0:T(8,128)(2,1)S(1)} %copy-done), channel_id=1, source_target_pairs={{0,16},{16,0},{1,17},{17,1},{2,18},{18,2},{3,19},{19,3},{4,20},{20... | collective-permute-start | bytes 3145736 | tf_op jit(solution)/shard_map/ppermute | solution.py:220
  37.0 7.6 %collective-permute-start.2 = (bf16[128,4096]{1,0:T(8,128)(2,1)S(1)}, bf16[128,4096]{1,0:T(8,128)(2,1)}, u32[]{:S(2)}, u32[]{:S(2)}) collective-permute-start(bf16[128,4096]{1,0:T(8,128)(2,1)S(1)} %collective-permute-done.1.p2), channel_id=1, source_target_pairs={{0,16},{16,0},{1,17},{17,1},{2,18},{18,2},{3,19},{19,3},{4,20},{20... | collective-permute-start | bytes 3145736 | tf_op jit(solution)/shard_map/ppermute | solution.py:220
  50.8 0.8 copy-start.1
  51.6 11.7 %all-to-all-start.1 = ((f32[4,56,512]{2,1,0:T(8,128)}), f32[4,56,512]{2,1,0:T(8,128)S(1)}, u32[]{:S(2)}, u32[]{:S(2)}) async-start(f32[4,56,512]{2,1,0:T(8,128)} %copy-done.1), calls=%async_computation.1 | async-start | bytes 917504 | tf_op jit(solution)/shard_map/all_to_all | solution.py:264
  66.5 15.3 %all-to-all-start.2 = ((bf16[16,16,256]{2,1,0:T(8,128)(2,1)}), bf16[16,16,256]{2,1,0:T(8,128)(2,1)S(1)}, u32[]{:S(2)}, u32[]{:S(2)}) async-start(bf16[16,16,256]{2,1,0:T(8,128)(2,1)} %get-tuple-element.7), calls=%async_computation.2 | async-start | bytes 262144 | tf_op jit(solution)/shard_map/all_to_all | solution.py:283
  81.8 0.7 copy-start.4

commit v2 on v1

--- a/solution.py
+++ b/solution.py
@@ -67,12 +67,15 @@
 
 
 def score_kernel(
-    q_ref, refs_ref, p0, p1, p2, p3, wc_ref, ws_ref, w_ref, cand_ref, out_ref, wide, table, pool, sem
+    q_ref, refs_ref, p0, p1, p2, p3, wc_ref, ws_ref, w_ref, c0_ref, c1_ref, c23_ref, out_hbm,
+    wide, table, pool, cands, out_ref, sem, out_sem
 ):
     q = q_ref[0]
     copies = pool_copies(q, (p0, p1, p2, p3), pool, sem)
     for copy in copies:
         copy.start()
+    for j, cand in enumerate((c0_ref[...], c23_ref[0], c1_ref[...], c23_ref[1])):
+        cands[:, pl.ds(pl.multiple_of((q ^ j) * ROWS, ROWS), ROWS)] = cand
     wide[...] = refs_ref[...].astype(F32)
     energy = [jnp.zeros((CLASSES, 128), F32) for _ in range(QROT)]
     stride = QROT * 32
@@ -92,12 +95,13 @@
     for copy in copies:
         copy.wait()
     class_id = lax.broadcasted_iota(jnp.int32, (CLASSES, 256), 0)
+    sends = []
     for n in range(2):
         lanes = slice(n * 256, (n + 1) * 256)
         scores = lax.dot_general(
             table[...], pool[lanes, :], (((1,), (1,)), ((), ())), preferred_element_type=F32
         )
-        cand = jnp.concatenate([cand_ref[2 * n], cand_ref[2 * n + 1]], axis=1)
+        cand = cands[:, lanes]
         allowed = class_id == cand[0:1, :]
         for k in range(1, 8):
             allowed = allowed | (class_id == cand[k : k + 1, :])
@@ -124,6 +128,11 @@
             out_ref[d, 48:49, lanes] = peak
             out_ref[d, 49:50, lanes] = evidence
             out_ref[d, 50:56, lanes] = jnp.zeros((6, 256), F32)
+        send = pltpu.make_async_copy(out_ref.at[:, :, lanes], out_hbm.at[:, :, lanes], out_sem.at[n])
+        send.start()
+        sends.append(send)
+    for send in sends:
+        send.wait()
 
 
 def class_kernel(
@@ -179,32 +188,35 @@
             out_ref[dest] = value.astype(BF16)
 
 
-def place_kernel(target_ref, y_ref, out_ref):
+def place_kernel(target_ref, y_ref, out_hbm, out_ref, sem):
     total = y_ref[0].astype(F32)
     for b in range(1, NBLK):
         total = total + y_ref[b].astype(F32)
     mass = total[QCLS : QCLS + 1, 0:128] + total[QCLS + 1 : QCLS + 2, 0:128]
-    row = lax.broadcasted_iota(jnp.int32, (NDOM * 16, 128), 0)
-    slot = row % 16
-    wanted = (row // 16) * SLOTS + slot % 8
-    hit = target_ref[...] == wanted
-    pick = jnp.where(hit & (slot < 8), 1.0, 0.0).astype(BF16)
+    row = lax.broadcasted_iota(jnp.int32, (NDOM * SLOTS, 128), 0)
+    hit = target_ref[...] == row
+    pick = jnp.where(hit, 1.0, 0.0).astype(BF16)
     placed = jnp.dot(pick[:, 0:16], total.astype(BF16), preferred_element_type=F32)
-    placed_mass = jnp.sum(jnp.where(hit & (slot >= 8), mass, 0.0), axis=1, keepdims=True)
+    placed_mass = jnp.sum(jnp.where(hit, mass, 0.0), axis=1, keepdims=True)
     high = placed_mass.astype(BF16).astype(F32)
-    lane = lax.broadcasted_iota(jnp.int32, (NDOM * 16, COLS), 1)
+    lane = lax.broadcasted_iota(jnp.int32, (NDOM * SLOTS, 128), 1)
     extra = jnp.where(lane == 0, high, jnp.where(lane == 1, placed_mass - high, 0.0))
-    out = (placed + extra).astype(BF16)
-    out_ref[...] = out.reshape(NDOM, 16, COLS)
+    out_ref[:, :, 0:COLS] = placed.reshape(NDOM, SLOTS, COLS).astype(BF16)
+    out_ref[:, :, COLS:] = extra.reshape(NDOM, SLOTS, 128).astype(BF16)
+    send = pltpu.make_async_copy(out_ref, out_hbm, sem)
+    send.start()
+    send.wait()
 
 
 def mean_kernel(z_ref, mean_ref, mass_ref):
     total = z_ref[0].astype(F32)
     for d in range(1, NDOM):
         total = total + z_ref[d].astype(F32)
-    mass = total[8:16, 0:1] + total[8:16, 1:2]
-    mean_ref[...] = total[0:8] / (mass + 1.0)
-    mass_ref[...] = jnp.broadcast_to(mass, (SLOTS, 128))
+    mass = total[:, COLS : COLS + 1] + total[:, COLS + 1 : COLS + 2]
+    mean_ref[...] = total[:, 0:COLS] / (mass + 1.0)
+    row = lax.broadcasted_iota(jnp.int32, (SLOTS, 128), 0)
+    lane = lax.broadcasted_iota(jnp.int32, (SLOTS, 128), 1)
+    mass_ref[...] = jnp.sum(jnp.where(row == lane, mass, 0.0), axis=0)[0:SLOTS]
 
 
 def phase_tables(offsets):
@@ -236,10 +248,13 @@
     )(q, references)
     gathered = lax.all_to_all(packed, BLK, 0, 0, tiled=True)
     near = swap(particles, "core")
+    cand = candidates.T
+    cand_far = swap(cand, "yl")
+    cand_near = swap(jnp.stack([cand, cand_far]), "core")
+    far, cand_near = lax.optimization_barrier((far, cand_near))
     far_near = swap(far, "core")
     pool = (particles, near, far, far_near)
 
-    cand = lax.all_gather(candidates.T, POOL, axis=0, tiled=False)
     cosine, sine = phase_tables(offsets)
     wc = (noise_weight * cosine).reshape(NSHIFT * 16, 128)
     ws = (noise_weight * sine).reshape(NSHIFT * 16, 128)
@@ -249,18 +264,21 @@
     pool_shape = VMEM((NPOOL * ROWS, 2 * K), BF16)
     terms = pl.pallas_call(
         score_kernel,
-        out_shape=jax.ShapeDtypeStruct((NPOOL, 56, NPOOL * ROWS), F32),
-        in_specs=[SMEM_SPEC, VMEM_SPEC] + [ANY_SPEC] * 4 + [VMEM_SPEC] * 4,
-        out_specs=VMEM_SPEC,
+        out_shape=pltpu.HBM((NPOOL, 56, NPOOL * ROWS), F32),
+        in_specs=[SMEM_SPEC, VMEM_SPEC] + [ANY_SPEC] * 4 + [VMEM_SPEC] * 6,
+        out_specs=pl.BlockSpec(memory_space=pltpu.HBM),
         scratch_shapes=[
             VMEM((NBLK * LOCAL * QROT * 32, 128), F32),
             VMEM((NSHIFT * QROT * CLASSES, 2 * K), BF16),
             pool_shape,
+            VMEM((8, NPOOL * ROWS), jnp.int32),
+            VMEM((NPOOL, 56, NPOOL * ROWS), F32),
             copies,
+            pltpu.SemaphoreType.DMA((2,)),
         ],
         compiler_params=params(40),
         name="score",
-    )(q, gathered.reshape(NBLK * LOCAL * QROT * 32, 128), *pool, wc, ws, weight, cand)
+    )(q, gathered.reshape(NBLK * LOCAL * QROT * 32, 128), *pool, wc, ws, weight, cand, cand_far, cand_near)
     terms = lax.all_to_all(terms, POOL, 0, 0, tiled=True)
 
     sums, log_evidence = pl.pallas_call(
@@ -291,9 +309,11 @@
     mine = jnp.pad(mine, (0, 128 - QCLS), constant_values=-1).reshape(1, 128)
     placed = pl.pallas_call(
         place_kernel,
-        out_shape=jax.ShapeDtypeStruct((NDOM, 16, COLS), BF16),
+        out_shape=pltpu.HBM((NDOM, SLOTS, COLS + 128), BF16),
         in_specs=[VMEM_SPEC, VMEM_SPEC],
-        out_specs=VMEM_SPEC,
+        out_specs=pl.BlockSpec(memory_space=pltpu.HBM),
+        scratch_shapes=[VMEM((NDOM, SLOTS, COLS + 128), BF16), pltpu.SemaphoreType.DMA],
+        compiler_params=params(4),
         name="place",
     )(mine, sums)
     placed = lax.all_to_all(placed, DOM, 0, 0, tiled=True)
@@ -301,13 +321,14 @@
         mean_kernel,
         out_shape=(
             jax.ShapeDtypeStruct((SLOTS, COLS), F32),
-            jax.ShapeDtypeStruct((SLOTS, 128), F32),
+            jax.ShapeDtypeStruct((SLOTS,), F32),
         ),
         in_specs=[VMEM_SPEC],
         out_specs=(VMEM_SPEC, VMEM_SPEC),
+        compiler_params=params(4),
         name="means",
     )(placed)
-    return (means, mass[:, 0], log_evidence.reshape(ROWS))
+    return (means, mass, log_evidence.reshape(ROWS))
 
 
 def solution(mesh):

time: 104 us -> 98.7 us (0.949)
  blocking collectives: 21.6 us -> 16.3 us
  waiting for transfers between devices: 36 us -> 40.9 us
  local copies, waits for them, and re-layouts: 4.64 us -> 1.41 us
  Pallas kernels: 14.3 us -> 13.1 us
    all_gather x1 -> x0, blocking collectives: 5.01 us -> none  [on_device(): cand = lax.all_gather(candidates.T, POOL, axis=0, tiled=False)]
    ppermute x3 -> x5, waiting for transfers between devices: 21.2 us -> 25.6 us  [swap(): return lax.ppermute(x, axis, [(0, 1), (1, 0)])]
    unnamed x16 -> x12, local copies, waits for them, and re-layouts: 2.43 us -> 1.01 us
    all_to_all x1, starting transfers between devices: 6.82 us -> 5.41 us  [on_device(): sums = lax.all_to_all(sums, BLK, 0, 0, tiled=True)]
    all_to_all x1, starting transfers between devices: 4.39 us -> 5.73 us  [on_device(): terms = lax.all_to_all(terms, POOL, 0, 0, tiled=True)]
    slice x1 -> x0, local copies, waits for them, and re-layouts: 1.3 us -> none  [on_device(): return (means, mass[:, 0], log_evidence.reshape(ROWS))]
    ppermute x3 -> x5, starting transfers between devices: 4.48 us -> 3.77 us  [swap(): return lax.ppermute(x, axis, [(0, 1), (1, 0)])]
  transfers between devices with their start and end apart: 6 -> 8, of which waited for: 3 -> 6; matrix products, arithmetic and copies ran while one was open for 1% -> 1% of each run, Pallas kernels for 0% -> 0%
where the time goes in v2:
time: 98.7 us; the launch traced here: 98.2 us
  waiting for transfers between devices  40.9 us (41%)
  starting transfers between devices  25.1 us (25%)
  blocking collectives  16.3 us (17%)
  Pallas kernels  13.1 us (13%)
  local copies, waits for them, and re-layouts  1.41 us (1%)
    ppermute x5, waiting for transfers between devices, swap(): return lax.ppermute(x, axis, [(0, 1), (1, 0)])  25.6 us
    all_to_all x1, blocking collectives, on_device(): placed = lax.all_to_all(placed, DOM, 0, 0, tiled=True)  16.3 us
    all_to_all x1, starting transfers between devices, on_device(): gathered = lax.all_to_all(packed, BLK, 0, 0, tiled=True)  10.2 us
    all_to_all x1, waiting for transfers between devices, on_device(): sums = lax.all_to_all(sums, BLK, 0, 0, tiled=True)  8.38 us
    pallas_call x1, Pallas kernels, on_device(): pl.pallas_call(score_kernel, out_shape=pltpu.HBM((NPOOL, 56, NPOOL * ROWS...  7.04 us
    all_to_all x1, waiting for transfers between devices, on_device(): terms = lax.all_to_all(terms, POOL, 0, 0, tiled=True)  6.96 us
    all_to_all x1, starting transfers between devices, on_device(): terms = lax.all_to_all(terms, POOL, 0, 0, tiled=True)  5.73 us
    all_to_all x1, starting transfers between devices, on_device(): sums = lax.all_to_all(sums, BLK, 0, 0, tiled=True)  5.41 us
  transfers between devices with their start and end apart: 8, of which 6 were waited for; matrix products, arithmetic and copies ran while one was open for 1% of the time, Pallas kernels for 0%

profile of v2, /device:TPU:1, one launch (start us, length us, event | category | flops | bytes accessed | tf_op | source)
XLA Modules:
  0.0 98.2 jit_solution(14507889051894859394)
XLA Ops:
  0.6 0.0 copy-start.1
  0.6 1.0 %copy-done.1 = bf16[3,12,4096]{2,1,0:T(8,128)(2,1)S(1)} copy-done((bf16[3,12,4096]{2,1,0:T(8,128)(2,1)S(1)}, bf16[3,12,4096]{2,1,0:T(8,128)(2,1)}, u32[]{:S(2)}) %copy-start.1) | copy-done | bytes 294936
  1.6 1.3 %pack.1 = bf16[16,288,128]{2,1,0:T(8,128)(2,1)} custom-call(s32[1]{0:T(128)} %bitcast.1.q_ref, bf16[3,12,4096]{2,1,0:T(8,128)(2,1)S(1)} %copy-done.1), custom_call_target="tpu_custom_call" | custom-call | tf_op jit(solution)/shard_map/pack/pallas_call | solution.py:240
  2.9 0.0 copy-start
  2.9 0.0 copy-start.3
  2.9 0.0 copy-start.4
  2.9 0.0 copy-start.2
  2.9 0.0 copy-start.5
  2.9 10.2 %all-to-all-start = ((bf16[16,288,128]{2,1,0:T(8,128)(2,1)}), bf16[16,288,128]{2,1,0:T(8,128)(2,1)S(1)}, u32[]{:S(2)}, u32[]{:S(2)}) async-start(bf16[16,288,128]{2,1,0:T(8,128)(2,1)} %pack.1), calls=%async_computation | async-start | bytes 2359296 | tf_op jit(solution)/shard_map/all_to_all | solution.py:249
  13.1 0.0 copy-done
  13.1 1.4 %collective-permute-start.1 = (bf16[128,4096]{1,0:T(8,128)(2,1)S(1)}, bf16[128,4096]{1,0:T(8,128)(2,1)S(1)}, u32[]{:S(2)}, u32[]{:S(2)}) collective-permute-start(bf16[128,4096]{1,0:T(8,128)(2,1)S(1)} %copy-done), channel_id=1, source_target_pairs={{0,32},{32,0},{1,33},{33,1},{2,34},{34,2},{3,35},{35,3},{4,36},{36... | collective-permute-start | bytes 3145736 | tf_op jit(solution)/shard_map/ppermute | solution.py:232
  14.5 0.0 copy-done.3
  14.5 0.2 collective-permute-start.2
  14.7 22.3 %collective-permute-done.2.c1_ref = s32[8,128]{1,0:T(8,128)S(1)} collective-permute-done((s32[8,128]{1,0:T(8,128)S(1)}, s32[8,128]{1,0:T(8,128)S(1)}, u32[]{:S(2)}, u32[]{:S(2)}) %collective-permute-start.2) | collective-permute-done | bytes 4128 | tf_op jit(solution)/shard_map/ppermute | solution.py:232
  37.0 1.9 %collective-permute-start.3 = (s32[2,8,128]{2,1,0:T(8,128)S(1)}, s32[2,8,128]{2,1,0:T(8,128)S(1)}, u32[]{:S(2)}, u32[]{:S(2)}) collective-permute-start(s32[2,8,128]{2,1,0:T(8,128)S(1)} %pad_add_fusion), channel_id=1, source_target_pairs={{0,16},{16,0},{1,17},{17,1},{2,18},{18,2},{3,19},{19,3},{4,20},{20... | collective-permute-start | bytes 24584 | tf_op jit(solution)/shard_map/ppermute | solution.py:232
  38.9 0.0 collective-permute-start
  38.9 0.8 collective-permute-done.3.c23_ref
  39.7 0.0 collective-permute-done.1.p2
  39.7 0.3 collective-permute-start.4
  40.1 0.0 copy-done.4
  40.1 0.1 mul.110
  40.2 0.1 mul.111
  40.2 0.1 mul.117
  40.3 0.1 mul.118
  40.4 0.0 copy-done.2
  40.4 0.2 bitcast_multiply_fusion
  40.7 0.0 copy-done.5
  40.7 0.1 convert_reduce_fusion
  40.8 0.9 collective-permute-done.p1
  41.7 1.5 %collective-permute-done.4.p3 = bf16[128,4096]{1,0:T(8,128)(2,1)} collective-permute-done((bf16[128,4096]{1,0:T(8,128)(2,1)S(1)}, bf16[128,4096]{1,0:T(8,128)(2,1)}, u32[]{:S(2)}, u32[]{:S(2)}) %collective-permute-start.4) | collective-permute-done | bytes 1048608 | tf_op jit(solution)/shard_map/ppermute | solution.py:232
  43.2 0.0 all-to-all-done
  43.2 7.0 %score.1 = f32[4,56,512]{2,1,0:T(8,128)} custom-call(s32[1]{0:T(128)} %bitcast.1.q_ref, bf16[4608,128]{1,0:T(8,128)(2,1)S(1)} %bitcast.45, bf16[128,4096]{1,0:T(8,128)(2,1)S(1)} %copy-done, bf16[128,4096]{1,0:T(8,128)(2,1)} %collective-permute-done.p1, bf16[128,4096]{1,0:T(8,128)(2,1)S(1)} %collective-permute-done.1.p2, ...), custom_call_target="tpu_custom_call" | custom-call | tf_op jit(solution)/shard_map/score/pallas_call | solution.py:265
  50.2 5.7 %all-to-all-start.1 = ((f32[4,56,512]{2,1,0:T(8,128)}), f32[4,56,512]{2,1,0:T(8,128)S(1)}, u32[]{:S(2)}, u32[]{:S(2)}) async-start(f32[4,56,512]{2,1,0:T(8,128)} %score.1), calls=%async_computation.1 | async-start | bytes 917504 | tf_op jit(solution)/shard_map/all_to_all | solution.py:282
  56.0 0.3 fusion.5
  56.3 7.0 %all-to-all-done.1.x_ref = f32[4,56,512]{2,1,0:T(8,128)S(1)} async-done(((f32[4,56,512]{2,1,0:T(8,128)}), f32[4,56,512]{2,1,0:T(8,128)S(1)}, u32[]{:S(2)}, u32[]{:S(2)}) %all-to-all-start.1) | async-done | bytes 458784 | tf_op jit(solution)/shard_map/all_to_all | solution.py:282
  63.3 3.2 %classes.1 = (bf16[16,16,256]{2,1,0:T(8,128)(2,1)}, f32[1,128]{1,0:T(1,128)}) custom-call(s32[1]{0:T(128)} %bitcast.1.q_ref, f32[4,56,512]{2,1,0:T(8,128)S(1)} %all-to-all-done.1.x_ref, bf16[128,4096]{1,0:T(8,128)(2,1)S(1)} %copy-done, bf16[128,4096]{1,0:T(8,128)(2,1)} %collective-permute-done.p1, bf16[128,4096]{1,0:T(8,128)(2,1)S(1)} %collective-permute-done.1.p2, ...), custom_call_target="tpu_custom_call" | custom-call | tf_op jit(solution)/shard_map/classes/pallas_call | solution.py:284
  66.5 5.4 %all-to-all-start.2 = ((bf16[16,16,256]{2,1,0:T(8,128)(2,1)}), bf16[16,16,256]{2,1,0:T(8,128)(2,1)S(1)}, u32[]{:S(2)}, u32[]{:S(2)}) async-start(bf16[16,16,256]{2,1,0:T(8,128)(2,1)} %get-tuple-element.11), calls=%async_computation.2 | async-start | bytes 262144 | tf_op jit(solution)/shard_map/all_to_all | solution.py:301
  71.9 0.1 dynamic_slice.3
  72.0 8.4 %all-to-all-done.2.y_ref = bf16[16,16,256]{2,1,0:T(8,128)(2,1)S(1)} async-done(((bf16[16,16,256]{2,1,0:T(8,128)(2,1)}), bf16[16,16,256]{2,1,0:T(8,128)(2,1)S(1)}, u32[]{:S(2)}, u32[]{:S(2)}) %all-to-all-start.2) | async-done | bytes 131104 | tf_op jit(solution)/shard_map/all_to_all | solution.py:301
  80.4 0.8 place.1
  81.2 16.3 %all_to_all.20.z_ref = bf16[16,8,384]{2,1,0:T(8,128)(2,1)S(1)} all-to-all(bf16[16,8,384]{2,1,0:T(8,128)(2,1)} %place.1), channel_id=1, replica_groups=mesh['xh'=2,'yh'=2,'yl'=2,'core'=2,'z'=8,'xl'=2] {'xh','yh','yl','core'}, dimensions={0} | all-to-all | bytes 196608 | tf_op jit(solution)/shard_map/all_to_all | solution.py:319
  97.5 0.8 means.1
  (6 shorter events, 0.0 us)
Async XLA Ops:
  0.6 1.0 %copy-start.1 = (bf16[3,12,4096]{2,1,0:T(8,128)(2,1)S(1)}, bf16[3,12,4096]{2,1,0:T(8,128)(2,1)}, u32[]{:S(2)}) copy-start(bf16[3,12,4096]{2,1,0:T(8,128)(2,1)} %refs_ref.1) | copy-start | bytes 884740
  2.9 10.2 %copy-start = (bf16[128,4096]{1,0:T(8,128)(2,1)S(1)}, bf16[128,4096]{1,0:T(8,128)(2,1)}, u32[]{:S(2)}) copy-start(bf16[128,4096]{1,0:T(8,128)(2,1)} %p0.3) | copy-start | bytes 3145732
  2.9 11.6 %copy-start.3 = (s32[128,8]{0,1:T(8,128)S(1)}, s32[128,8]{0,1:T(8,128)}, u32[]{:S(2)}) copy-start(s32[128,8]{0,1:T(8,128)} %param.10) | copy-start | bytes 12292
  2.9 37.2 %copy-start.4 = (s32[4,2]{0,1:T(2,128)S(1)}, s32[4,2]{0,1:T(2,128)}, u32[]{:S(2)}) copy-start(s32[4,2]{0,1:T(2,128)} %param.9) | copy-start | bytes 100
  2.9 37.5 %copy-start.2 = (f32[2048]{0:T(1024)S(1)}, f32[2048]{0:T(1024)}, u32[]{:S(2)}) copy-start(f32[2048]{0:T(1024)} %param.8) | copy-start | bytes 24580
  2.9 37.7 %copy-start.5 = (s32[48]{0:T(128)S(1)}, s32[48]{0:T(128)}, u32[]{:S(2)}) copy-start(s32[48]{0:T(128)} %param.11) | copy-start | bytes 580
  2.9 40.3 %all-to-all-start = ((bf16[16,288,128]{2,1,0:T(8,128)(2,1)}), bf16[16,288,128]{2,1,0:T(8,128)(2,1)S(1)}, u32[]{:S(2)}, u32[]{:S(2)}) async-start(bf16[16,288,128]{2,1,0:T(8,128)(2,1)} %pack.1), calls=%async_computation | async-start | bytes 2359296 | tf_op jit(solution)/shard_map/all_to_all | solution.py:249
  13.1 26.6 %collective-permute-start.1 = (bf16[128,4096]{1,0:T(8,128)(2,1)S(1)}, bf16[128,4096]{1,0:T(8,128)(2,1)S(1)}, u32[]{:S(2)}, u32[]{:S(2)}) collective-permute-start(bf16[128,4096]{1,0:T(8,128)(2,1)S(1)} %copy-done), channel_id=1, source_target_pairs={{0,32},{32,0},{1,33},{33,1},{2,34},{34,2},{3,35},{35,3},{4,36},{36... | collective-permute-start | bytes 3145736 | tf_op jit(solution)/shard_map/ppermute | solution.py:232
  14.5 22.5 %collective-permute-start.2 = (s32[8,128]{1,0:T(8,128)S(1)}, s32[8,128]{1,0:T(8,128)S(1)}, u32[]{:S(2)}, u32[]{:S(2)}) collective-permute-start(s32[8,128]{1,0:T(8,128)S(1)} %bitcast.48), channel_id=1, source_target_pairs={{0,32},{32,0},{1,33},{33,1},{2,34},{34,2},{3,35},{35,3},{4,36},{36... | collective-permute-start | bytes 12296 | tf_op jit(solution)/shard_map/ppermute | solution.py:232
  37.0 2.7 %collective-permute-start.3 = (s32[2,8,128]{2,1,0:T(8,128)S(1)}, s32[2,8,128]{2,1,0:T(8,128)S(1)}, u32[]{:S(2)}, u32[]{:S(2)}) collective-permute-start(s32[2,8,128]{2,1,0:T(8,128)S(1)} %pad_add_fusion), channel_id=1, source_target_pairs={{0,16},{16,0},{1,17},{17,1},{2,18},{18,2},{3,19},{19,3},{4,20},{20... | collective-permute-start | bytes 24584 | tf_op jit(solution)/shard_map/ppermute | solution.py:232
  38.9 2.8 %collective-permute-start = (bf16[128,4096]{1,0:T(8,128)(2,1)S(1)}, bf16[128,4096]{1,0:T(8,128)(2,1)}, u32[]{:S(2)}, u32[]{:S(2)}) collective-permute-start(bf16[128,4096]{1,0:T(8,128)(2,1)S(1)} %copy-done), channel_id=1, source_target_pairs={{0,16},{16,0},{1,17},{17,1},{2,18},{18,2},{3,19},{19,3},{4,20},{20... | collective-permute-start | bytes 3145736 | tf_op jit(solution)/shard_map/ppermute | solution.py:232
  39.7 3.5 %collective-permute-start.4 = (bf16[128,4096]{1,0:T(8,128)(2,1)S(1)}, bf16[128,4096]{1,0:T(8,128)(2,1)}, u32[]{:S(2)}, u32[]{:S(2)}) collective-permute-start(bf16[128,4096]{1,0:T(8,128)(2,1)S(1)} %collective-permute-done.1.p2), channel_id=1, source_target_pairs={{0,16},{16,0},{1,17},{17,1},{2,18},{18,2},{3,19},{19,3},{4,20},{20... | collective-permute-start | bytes 3145736 | tf_op jit(solution)/shard_map/ppermute | solution.py:232
  50.2 13.0 %all-to-all-start.1 = ((f32[4,56,512]{2,1,0:T(8,128)}), f32[4,56,512]{2,1,0:T(8,128)S(1)}, u32[]{:S(2)}, u32[]{:S(2)}) async-start(f32[4,56,512]{2,1,0:T(8,128)} %score.1), calls=%async_computation.1 | async-start | bytes 917504 | tf_op jit(solution)/shard_map/all_to_all | solution.py:282
  66.5 13.9 %all-to-all-start.2 = ((bf16[16,16,256]{2,1,0:T(8,128)(2,1)}), bf16[16,16,256]{2,1,0:T(8,128)(2,1)S(1)}, u32[]{:S(2)}, u32[]{:S(2)}) async-start(bf16[16,16,256]{2,1,0:T(8,128)(2,1)} %get-tuple-element.11), calls=%async_computation.2 | async-start | bytes 262144 | tf_op jit(solution)/shard_map/all_to_all | solution.py:301

commit v3 on v2

--- a/solution.py
+++ b/solution.py
@@ -25,6 +25,7 @@
 ROT = 12
 NSHIFT = 4
 ROWS = 128
+HALF = ROWS // 2
 NPOOL = 4
 QROT = ROT // NPOOL
 QCLS = CLASSES // NPOOL
@@ -32,6 +33,7 @@
 NDOM = 16
 LOCAL = 3
 COLS = 256
+STEP_TILES = 4
 F32 = jnp.float32
 BF16 = jnp.bfloat16
 VMEM = pltpu.VMEM
@@ -60,18 +62,26 @@
 
 def pool_copies(q, parts, pool, sem):
     copies = []
-    for j, part in enumerate(parts):
-        start = pl.multiple_of((q ^ j) * ROWS, ROWS)
-        copies.append(pltpu.make_async_copy(part, pool.at[pl.ds(start, ROWS), :], sem.at[j]))
+    for i, (part, j, offset) in enumerate(zip(parts, (0, 1, 2, 3, 3), (0, 0, 0, 0, HALF))):
+        start = pl.multiple_of((q ^ j) * ROWS + offset, HALF)
+        rows = pl.ds(start, part.shape[0])
+        copies.append(pltpu.make_async_copy(part, pool.at[rows, :], sem.at[i]))
     return copies
 
 
+def split(x):
+    high = x.astype(BF16).astype(F32)
+    middle = (x - high).astype(BF16).astype(F32)
+    return (high, middle, x - high - middle)
+
+
 def score_kernel(
-    q_ref, refs_ref, p0, p1, p2, p3, wc_ref, ws_ref, w_ref, c0_ref, c1_ref, c23_ref, out_hbm,
-    wide, table, pool, cands, out_ref, sem, out_sem
+    q_ref, refs_ref, p0, p1, p2, p3, p4, wc_ref, ws_ref, w_ref, c0_ref, c1_ref, c23_ref,
+    own_ref, near_ref, far_ref, cross_ref,
+    wide, table0, table1, pool, cands, scores, groups, sem
 ):
     q = q_ref[0]
-    copies = pool_copies(q, (p0, p1, p2, p3), pool, sem)
+    copies = pool_copies(q, (p0, p1, p2, p3, p4), pool, sem)
     for copy in copies:
         copy.start()
     for j, cand in enumerate((c0_ref[...], c23_ref[0], c1_ref[...], c23_ref[1])):
@@ -79,28 +89,55 @@
     wide[...] = refs_ref[...].astype(F32)
     energy = [jnp.zeros((CLASSES, 128), F32) for _ in range(QROT)]
     stride = QROT * 32
-    for a in range(16):
-        weight = w_ref[a : a + 1, :]
-        for r in range(QROT):
-            real = wide[pl.ds(r * 32 + a, CLASSES, stride=stride), :]
-            imag = wide[pl.ds(r * 32 + 16 + a, CLASSES, stride=stride), :]
-            energy[r] = energy[r] + weight * (real * real + imag * imag)
-            for s in range(NSHIFT):
-                wc = wc_ref[s * 16 + a : s * 16 + a + 1, :]
-                ws = ws_ref[s * 16 + a : s * 16 + a + 1, :]
-                row = (s * QROT + r) * CLASSES
-                table[row : row + CLASSES, a * 128 : (a + 1) * 128] = (wc * real - ws * imag).astype(BF16)
-                table[row : row + CLASSES, K + a * 128 : K + (a + 1) * 128] = (ws * real + wc * imag).astype(BF16)
-    half_energy = [0.5 * jnp.sum(e, axis=1, keepdims=True) for e in energy]
+    tables = (table0, table1)
+    wide_cols = 128 * STEP_TILES
+
+    def build(step):
+        table = tables[step % 2]
+        for t in range(STEP_TILES):
+            a = step * STEP_TILES + t
+            weight = w_ref[a : a + 1, :]
+            for r in range(QROT):
+                real = wide[pl.ds(r * 32 + a, CLASSES, stride=stride), :]
+                imag = wide[pl.ds(r * 32 + 16 + a, CLASSES, stride=stride), :]
+                energy[r] = energy[r] + weight * (real * real + imag * imag)
+                for s in range(NSHIFT):
+                    wc = wc_ref[s * 16 + a : s * 16 + a + 1, :]
+                    ws = ws_ref[s * 16 + a : s * 16 + a + 1, :]
+                    row = (s * QROT + r) * CLASSES
+                    at = slice(t * 128, (t + 1) * 128)
+                    at_im = slice(wide_cols + t * 128, wide_cols + (t + 1) * 128)
+                    table[row : row + CLASSES, at] = (wc * real - ws * imag).astype(BF16)
+                    table[row : row + CLASSES, at_im] = (ws * real + wc * imag).astype(BF16)
+
+    build(0)
     for copy in copies:
         copy.wait()
+    steps = 16 // STEP_TILES
+    for step in range(steps):
+        if step + 1 < steps:
+            build(step + 1)
+        table = tables[step % 2]
+        cols = slice(step * wide_cols, (step + 1) * wide_cols)
+        cols_im = slice(K + step * wide_cols, K + (step + 1) * wide_cols)
+        for n in range(2):
+            lanes = slice(n * 256, (n + 1) * 256)
+            part = lax.dot_general(
+                table[:, 0:wide_cols], pool[lanes, cols], (((1,), (1,)), ((), ())),
+                preferred_element_type=F32,
+            ) + lax.dot_general(
+                table[:, wide_cols:], pool[lanes, cols_im], (((1,), (1,)), ((), ())),
+                preferred_element_type=F32,
+            )
+            if step == 0:
+                scores[:, lanes] = part
+            else:
+                scores[:, lanes] += part
+
+    half_energy = [0.5 * jnp.sum(e, axis=1, keepdims=True) for e in energy]
     class_id = lax.broadcasted_iota(jnp.int32, (CLASSES, 256), 0)
-    sends = []
     for n in range(2):
         lanes = slice(n * 256, (n + 1) * 256)
-        scores = lax.dot_general(
-            table[...], pool[lanes, :], (((1,), (1,)), ((), ())), preferred_element_type=F32
-        )
         cand = cands[:, lanes]
         allowed = class_id == cand[0:1, :]
         for k in range(1, 8):
@@ -109,7 +146,7 @@
         for s in range(NSHIFT):
             for r in range(QROT):
                 row = (s * QROT + r) * CLASSES
-                value = INV_TEMP * (scores[row : row + CLASSES] - half_energy[r])
+                value = INV_TEMP * (scores[row : row + CLASSES, lanes] - half_energy[r])
                 loglik.append(jnp.where(allowed, value, FLOOR))
         top = loglik[0]
         for value in loglik[1:]:
@@ -123,34 +160,35 @@
                 terms = terms + jnp.where(allowed, jnp.exp(value - peak), 0.0)
             evidence = evidence + jnp.sum(terms, axis=0, keepdims=True)
             for d in range(NPOOL):
-                out_ref[d, s * QCLS : (s + 1) * QCLS, lanes] = terms[d * QCLS : (d + 1) * QCLS]
+                groups[d, s * QCLS : (s + 1) * QCLS, lanes] = terms[d * QCLS : (d + 1) * QCLS]
+        pieces = split(peak) + split(evidence)
         for d in range(NPOOL):
-            out_ref[d, 48:49, lanes] = peak
-            out_ref[d, 49:50, lanes] = evidence
-            out_ref[d, 50:56, lanes] = jnp.zeros((6, 256), F32)
-        send = pltpu.make_async_copy(out_ref.at[:, :, lanes], out_hbm.at[:, :, lanes], out_sem.at[n])
-        send.start()
-        sends.append(send)
-    for send in sends:
-        send.wait()
+            for i, piece in enumerate(pieces):
+                groups[d, 48 + i : 49 + i, lanes] = piece
+            groups[d, 54:56, lanes] = jnp.zeros((2, 256), F32)
+    own_ref[...] = groups[q]
+    for j, ref in enumerate((near_ref, far_ref, cross_ref)):
+        ref[...] = groups[q ^ (j + 1)].astype(BF16)
 
 
 def class_kernel(
-    q_ref, x_ref, p0, p1, p2, p3, cos_ref, sin_ref, out_ref, log_ref, pool, slots, line, sem
+    q_ref, x0, x1, x2, x3, p0, p1, p2, p3, p4, cos_ref, sin_ref, out_ref, log_ref, pool, slots, line, sem
 ):
     q = q_ref[0]
-    copies = pool_copies(q, (p0, p1, p2, p3), pool, sem)
+    copies = pool_copies(q, (p0, p1, p2, p3, p4), pool, sem)
     for copy in copies:
         copy.start()
-    peak = x_ref[0, 48:49, :]
-    for j in range(1, NPOOL):
-        peak = jnp.maximum(peak, x_ref[j, 48:49, :])
+    parts = [x[...].astype(F32) for x in (x0, x1, x2, x3)]
+    peaks = [x[48:49] + x[49:50] + x[50:51] for x in parts]
+    peak = peaks[0]
+    for value in peaks[1:]:
+        peak = jnp.maximum(peak, value)
     evidence = jnp.zeros_like(peak)
     terms = jnp.zeros((NSHIFT * QCLS, NPOOL * ROWS), F32)
-    for j in range(NPOOL):
-        scale = jnp.exp(x_ref[j, 48:49, :] - peak)
-        evidence = evidence + scale * x_ref[j, 49:50, :]
-        terms = terms + scale * x_ref[j, 0:48, :]
+    for x, value in zip(parts, peaks):
+        scale = jnp.exp(value - peak)
+        evidence = evidence + scale * (x[51:52] + x[52:53] + x[53:54])
+        terms = terms + scale * x[0:48]
     line[...] = peak + jnp.log(evidence)
     log_ref[...] = line[:, pl.ds(pl.multiple_of(q * ROWS, ROWS), ROWS)]
     probs = terms / evidence
@@ -232,10 +270,22 @@
     return lax.ppermute(x, axis, [(0, 1), (1, 0)])
 
 
+def trade(parts, axes):
+    own, near, far, cross = parts
+    return (
+        own,
+        swap(near, axes[1]),
+        swap(far, axes[0]),
+        lax.ppermute(cross, axes, [(i, 3 - i) for i in range(4)]),
+    )
+
+
 def on_device(particles, references, noise_weight, offsets, candidates, class_owner):
     pool_index = (lax.axis_index("yl") * 2 + lax.axis_index("core")).astype(jnp.int32)
     q = pool_index.reshape(1)
 
+    cand = candidates.T
+    cand_far = swap(cand, "yl")
     far = swap(particles, "yl")
     packed = pl.pallas_call(
         pack_kernel,
@@ -248,38 +298,45 @@
     )(q, references)
     gathered = lax.all_to_all(packed, BLK, 0, 0, tiled=True)
     near = swap(particles, "core")
-    cand = candidates.T
-    cand_far = swap(cand, "yl")
+    cand_far, far = lax.optimization_barrier((cand_far, far))
     cand_near = swap(jnp.stack([cand, cand_far]), "core")
-    far, cand_near = lax.optimization_barrier((far, cand_near))
-    far_near = swap(far, "core")
-    pool = (particles, near, far, far_near)
+    first = swap(far[:HALF], "core")
+    rest, first = lax.optimization_barrier((far[HALF:], first))
+    second = swap(rest, "core")
+    pool = (particles, near, far, first, second)
 
     cosine, sine = phase_tables(offsets)
     wc = (noise_weight * cosine).reshape(NSHIFT * 16, 128)
     ws = (noise_weight * sine).reshape(NSHIFT * 16, 128)
     weight = noise_weight.reshape(16, 128)
 
-    copies = pltpu.SemaphoreType.DMA((NPOOL,))
+    copies = pltpu.SemaphoreType.DMA((5,))
     pool_shape = VMEM((NPOOL * ROWS, 2 * K), BF16)
+    table_rows = NSHIFT * QROT * CLASSES
     terms = pl.pallas_call(
         score_kernel,
-        out_shape=pltpu.HBM((NPOOL, 56, NPOOL * ROWS), F32),
-        in_specs=[SMEM_SPEC, VMEM_SPEC] + [ANY_SPEC] * 4 + [VMEM_SPEC] * 6,
-        out_specs=pl.BlockSpec(memory_space=pltpu.HBM),
+        out_shape=[
+            jax.ShapeDtypeStruct((56, NPOOL * ROWS), F32 if j == 0 else BF16) for j in range(NPOOL)
+        ],
+        in_specs=[SMEM_SPEC, VMEM_SPEC] + [ANY_SPEC] * 5 + [VMEM_SPEC] * 6,
+        out_specs=[VMEM_SPEC] * NPOOL,
         scratch_shapes=[
             VMEM((NBLK * LOCAL * QROT * 32, 128), F32),
-            VMEM((NSHIFT * QROT * CLASSES, 2 * K), BF16),
+            VMEM((table_rows, 256 * STEP_TILES), BF16),
+            VMEM((table_rows, 256 * STEP_TILES), BF16),
             pool_shape,
             VMEM((8, NPOOL * ROWS), jnp.int32),
+            VMEM((table_rows, NPOOL * ROWS), F32),
             VMEM((NPOOL, 56, NPOOL * ROWS), F32),
             copies,
-            pltpu.SemaphoreType.DMA((2,)),
         ],
         compiler_params=params(40),
         name="score",
-    )(q, gathered.reshape(NBLK * LOCAL * QROT * 32, 128), *pool, wc, ws, weight, cand, cand_far, cand_near)
-    terms = lax.all_to_all(terms, POOL, 0, 0, tiled=True)
+    )(
+        q, gathered.reshape(NBLK * LOCAL * QROT * 32, 128), *pool,
+        wc, ws, weight, cand, cand_far, cand_near,
+    )
+    terms = trade(terms, POOL)
 
     sums, log_evidence = pl.pallas_call(
         class_kernel,
@@ -287,7 +344,7 @@
             jax.ShapeDtypeStruct((NBLK, 16, COLS), BF16),
             jax.ShapeDtypeStruct((1, ROWS), F32),
         ),
-        in_specs=[SMEM_SPEC, VMEM_SPEC] + [ANY_SPEC] * 4 + [VMEM_SPEC] * 2,
+        in_specs=[SMEM_SPEC] + [VMEM_SPEC] * 4 + [ANY_SPEC] * 5 + [VMEM_SPEC] * 2,
         out_specs=(VMEM_SPEC, VMEM_SPEC),
         scratch_shapes=[
             pool_shape,
@@ -297,7 +354,7 @@
         ],
         compiler_params=params(24),
         name="classes",
-    )(q, terms, *pool, cosine, sine)
+    )(q, *terms, *pool, cosine, sine)
     sums = lax.all_to_all(sums, BLK, 0, 0, tiled=True)
 
     class_ids = jnp.arange(CLASSES, dtype=jnp.int32)

time: 98.7 us -> 91.5 us (0.927)
  waiting for transfers between devices: 40.9 us -> 33.2 us
  local copies, waits for them, and re-layouts: 1.41 us -> 4.12 us
  Pallas kernels: 13.1 us -> 11.7 us
    ppermute x5 -> x8, waiting for transfers between devices: 25.6 us -> 14.6 us  [swap(): return lax.ppermute(x, axis, [(0, 1), (1, 0)])]
    all_to_all x1, waiting for transfers between devices: 0.01 us -> 8.33 us  [on_device(): gathered = lax.all_to_all(packed, BLK, 0, 0, tiled=True)]
    ppermute x5 -> x8, starting transfers between devices: 3.77 us -> 10.7 us  [swap(): return lax.ppermute(x, axis, [(0, 1), (1, 0)])]
    all_to_all x1 -> x0, waiting for transfers between devices: 6.96 us -> none  [on_device(): terms = lax.all_to_all(terms, POOL, 0, 0, tiled=True)]
    all_to_all x1 -> x0, starting transfers between devices: 5.73 us -> none  [on_device(): terms = lax.all_to_all(terms, POOL, 0, 0, tiled=True)]
    all_to_all x1, starting transfers between devices: 5.41 us -> 3.52 us  [on_device(): sums = lax.all_to_all(sums, BLK, 0, 0, tiled=True)]
    unnamed x12 -> x16, local copies, waits for them, and re-layouts: 1.01 us -> 2.85 us
    ppermute x0 -> x1, starting transfers between devices: none -> 1.55 us  [trade(): lax.ppermute(cross, axes, [(i, 3 - i) for i in range(4)])]
  transfers between devices with their start and end apart: 8 -> 11, of which waited for: 6 -> 8; matrix products, arithmetic and copies ran while one was open for 1% -> 2% of each run, Pallas kernels for 0% -> 1%
where the time goes in v3:
time: 91.5 us; the launch traced here: 91.1 us
  waiting for transfers between devices  33.2 us (36%)
  starting transfers between devices  25.2 us (28%)
  blocking collectives  15.5 us (17%)
  Pallas kernels  11.7 us (13%)
  local copies, waits for them, and re-layouts  4.12 us (5%)
    all_to_all x1, blocking collectives, on_device(): placed = lax.all_to_all(placed, DOM, 0, 0, tiled=True)  15.5 us
    ppermute x8, waiting for transfers between devices, swap(): return lax.ppermute(x, axis, [(0, 1), (1, 0)])  14.6 us
    ppermute x8, starting transfers between devices, swap(): return lax.ppermute(x, axis, [(0, 1), (1, 0)])  10.7 us
    all_to_all x1, starting transfers between devices, on_device(): gathered = lax.all_to_all(packed, BLK, 0, 0, tiled=True)  9.35 us
    all_to_all x1, waiting for transfers between devices, on_device(): sums = lax.all_to_all(sums, BLK, 0, 0, tiled=True)  8.81 us
    all_to_all x1, waiting for transfers between devices, on_device(): gathered = lax.all_to_all(packed, BLK, 0, 0, tiled=True)  8.33 us
    pallas_call x1, Pallas kernels, on_device(): pl.pallas_call(score_kernel, out_shape=[jax.ShapeDtypeStruct((56, NPOOL *...  5.82 us
    all_to_all x1, starting transfers between devices, on_device(): sums = lax.all_to_all(sums, BLK, 0, 0, tiled=True)  3.52 us
  transfers between devices with their start and end apart: 11, of which 8 were waited for; matrix products, arithmetic and copies ran while one was open for 2% of the time, Pallas kernels for 1%

profile of v3, /device:TPU:1, one launch (start us, length us, event | category | flops | bytes accessed | tf_op | source)
XLA Modules:
  0.0 91.1 jit_solution(8729309336816062653)
XLA Ops:
  0.6 2.2 %collective-permute-start.2 = (bf16[128,4096]{1,0:T(8,128)(2,1)}, bf16[128,4096]{1,0:T(8,128)(2,1)S(1)}, u32[]{:S(2)}, u32[]{:S(2)}) collective-permute-start(bf16[128,4096]{1,0:T(8,128)(2,1)} %p0.3), channel_id=1, source_target_pairs={{0,32},{32,0},{1,33},{33,1},{2,34},{34,2},{3,35},{35,3},{4,36},{36... | collective-permute-start | bytes 3145736 | tf_op jit(solution)/shard_map/ppermute | solution.py:270
  2.8 0.0 copy-start.3
  2.8 1.0 %copy-done.3 = bf16[3,12,4096]{2,1,0:T(8,128)(2,1)S(1)} copy-done((bf16[3,12,4096]{2,1,0:T(8,128)(2,1)S(1)}, bf16[3,12,4096]{2,1,0:T(8,128)(2,1)}, u32[]{:S(2)}) %copy-start.3) | copy-done | bytes 294936
  3.8 1.3 %pack.1 = bf16[16,288,128]{2,1,0:T(8,128)(2,1)} custom-call(s32[1]{0:T(128)} %bitcast.1.q_ref, bf16[3,12,4096]{2,1,0:T(8,128)(2,1)S(1)} %copy-done.3), custom_call_target="tpu_custom_call" | custom-call | tf_op jit(solution)/shard_map/pack/pallas_call | solution.py:290
  5.1 0.0 copy-start.5
  5.1 9.3 %all-to-all-start = ((bf16[16,288,128]{2,1,0:T(8,128)(2,1)}), bf16[16,288,128]{2,1,0:T(8,128)(2,1)S(1)}, u32[]{:S(2)}, u32[]{:S(2)}) async-start(bf16[16,288,128]{2,1,0:T(8,128)(2,1)} %pack.1), calls=%async_computation | async-start | bytes 2359296 | tf_op jit(solution)/shard_map/all_to_all | solution.py:299
  14.5 0.0 copy-start
  14.5 0.0 copy-start.6
  14.5 0.0 copy-start.4
  14.5 0.0 copy-done.5
  14.5 0.3 collective-permute-start.1
  14.8 10.0 %collective-permute-done.1.c1_ref = s32[8,128]{1,0:T(8,128)S(1)} collective-permute-done((s32[8,128]{1,0:T(8,128)S(1)}, s32[8,128]{1,0:T(8,128)S(1)}, u32[]{:S(2)}, u32[]{:S(2)}) %collective-permute-start.1) | collective-permute-done | bytes 4128 | tf_op jit(solution)/shard_map/ppermute | solution.py:270
  24.8 0.0 collective-permute-done.2.p2
  24.8 0.9 fusion.20
  25.7 2.5 %collective-permute-start.3 = (bf16[64,4096]{1,0:T(8,128)(2,1)S(1)}, bf16[64,4096]{1,0:T(8,128)(2,1)S(1)}, u32[]{:S(2)}, u32[]{:S(2)}) collective-permute-start(bf16[64,4096]{1,0:T(8,128)(2,1)S(1)} %get-tuple-element.27), channel_id=1, source_target_pairs={{0,16},{16,0},{1,17},{17,1},{2,18},{18,2},{3,19},{19,3},{4,20},{20... | collective-permute-start | bytes 1572872 | tf_op jit(solution)/shard_map/ppermute | solution.py:270
  28.1 0.0 copy-done
  28.1 0.0 collective-permute-start
  28.1 0.0 copy-done.6
  28.2 2.2 %collective-permute-done.3.p3 = bf16[64,4096]{1,0:T(8,128)(2,1)S(1)} collective-permute-done((bf16[64,4096]{1,0:T(8,128)(2,1)S(1)}, bf16[64,4096]{1,0:T(8,128)(2,1)S(1)}, u32[]{:S(2)}, u32[]{:S(2)}) %collective-permute-start.3) | collective-permute-done | bytes 524320 | tf_op jit(solution)/shard_map/ppermute | solution.py:270
  30.4 0.0 copy-start.1
  30.4 0.8 copy-done.1
  31.1 0.4 collective-permute-start.4
  31.5 0.3 fusion.5
  31.9 0.2 collective-permute-start.5
  32.1 0.1 mul.110
  32.2 0.1 mul.111
  32.2 0.1 mul.117
  32.3 0.1 mul.118
  32.4 0.0 copy-done.4
  32.4 0.2 bitcast_multiply_fusion
  32.6 0.0 collective-permute-done.p1
  32.6 0.5 collective-permute-done.5.c23_ref
  33.1 0.3 collective-permute-done.4.p4
  33.4 8.3 %all-to-all-done = bf16[16,288,128]{2,1,0:T(8,128)(2,1)S(1)} async-done(((bf16[16,288,128]{2,1,0:T(8,128)(2,1)}), bf16[16,288,128]{2,1,0:T(8,128)(2,1)S(1)}, u32[]{:S(2)}, u32[]{:S(2)}) %all-to-all-start) | async-done | bytes 1179680 | tf_op jit(solution)/shard_map/all_to_all | solution.py:299
  41.7 0.0 copy-start.2
  41.7 1.0 %copy-done.2 = bf16[64,4096]{1,0:T(8,128)(2,1)S(1)} copy-done((bf16[64,4096]{1,0:T(8,128)(2,1)S(1)}, bf16[64,4096]{1,0:T(8,128)(2,1)}, u32[]{:S(2)}) %copy-start.2) | copy-done | bytes 524312
  42.8 0.0 copy-start.7
  42.8 5.8 %score.1 = (f32[56,512]{1,0:T(8,128)S(1)}, bf16[56,512]{1,0:T(8,128)(2,1)S(1)}, bf16[56,512]{1,0:T(8,128)(2,1)S(1)}, bf16[56,512]{1,0:T(8,128)(2,1)S(1)}) custom-call(s32[1]{0:T(128)} %bitcast.1.q_ref, bf16[4608,128]{1,0:T(8,128)(2,1)S(1)} %bitcast.45, bf16[128,4096]{1,0:T(8,128)(2,1)S(1)} %copy-done, bf16[128,4096]{1,0:T(8,128)(2,1)} %collective-permute-done.p1, ...), custom_call_target="tpu_custom_call" | custom-call | tf_op jit(solution)/shard_map/score/pallas_call | solution.py:316
  48.6 5.0 %collective-permute-start.6 = (bf16[56,512]{1,0:T(8,128)(2,1)S(1)}, bf16[56,512]{1,0:T(8,128)(2,1)S(1)}, u32[]{:S(2)}, u32[]{:S(2)}) collective-permute-start(bf16[56,512]{1,0:T(8,128)(2,1)S(1)} %get-tuple-element.20), channel_id=1, source_target_pairs={{0,16},{16,0},{1,17},{17,1},{2,18},{18,2},{3,19},{19,3},{4,20},{20... | collective-permute-start | bytes 172040 | tf_op jit(solution)/shard_map/ppermute | solution.py:270
  53.6 0.2 collective-permute-start.7
  53.8 1.5 %collective-permute-start.8 = (bf16[56,512]{1,0:T(8,128)(2,1)S(1)}, bf16[56,512]{1,0:T(8,128)(2,1)S(1)}, u32[]{:S(2)}, u32[]{:S(2)}) collective-permute-start(bf16[56,512]{1,0:T(8,128)(2,1)S(1)} %get-tuple-element.22), channel_id=1, source_target_pairs={{0,48},{16,32},{32,16},{48,0},{1,49},{17,33},{33,17},{49,1},{2,50}... | collective-permute-start | bytes 172040 | tf_op jit(solution)/shard_map/ppermute | solution.py:279
  55.3 0.0 copy-done.7
  55.4 0.1 convert_reduce_fusion
  55.4 0.0 collective-permute-done.6.x1
  55.4 1.6 %collective-permute-done.7.x2 = bf16[56,512]{1,0:T(8,128)(2,1)S(1)} collective-permute-done((bf16[56,512]{1,0:T(8,128)(2,1)S(1)}, bf16[56,512]{1,0:T(8,128)(2,1)S(1)}, u32[]{:S(2)}, u32[]{:S(2)}) %collective-permute-start.7) | collective-permute-done | bytes 57376 | tf_op jit(solution)/shard_map/ppermute | solution.py:270
  57.1 1.4 %collective-permute-done.8.x3 = bf16[56,512]{1,0:T(8,128)(2,1)S(1)} collective-permute-done((bf16[56,512]{1,0:T(8,128)(2,1)S(1)}, bf16[56,512]{1,0:T(8,128)(2,1)S(1)}, u32[]{:S(2)}, u32[]{:S(2)}) %collective-permute-start.8) | collective-permute-done | bytes 57376 | tf_op jit(solution)/shard_map/ppermute | solution.py:279
  58.5 3.1 %classes.1 = (bf16[16,16,256]{2,1,0:T(8,128)(2,1)}, f32[1,128]{1,0:T(1,128)}) custom-call(s32[1]{0:T(128)} %bitcast.1.q_ref, f32[56,512]{1,0:T(8,128)S(1)} %get-tuple-element.19.x0, bf16[56,512]{1,0:T(8,128)(2,1)S(1)} %collective-permute-done.6.x1, bf16[56,512]{1,0:T(8,128)(2,1)S(1)} %collective-permute-done.7.x2, ...), custom_call_target="tpu_custom_call" | custom-call | tf_op jit(solution)/shard_map/classes/pallas_call | solution.py:341
  61.6 3.5 %all-to-all-start.1 = ((bf16[16,16,256]{2,1,0:T(8,128)(2,1)}), bf16[16,16,256]{2,1,0:T(8,128)(2,1)S(1)}, u32[]{:S(2)}, u32[]{:S(2)}) async-start(bf16[16,16,256]{2,1,0:T(8,128)(2,1)} %get-tuple-element.23), calls=%async_computation.1 | async-start | bytes 262144 | tf_op jit(solution)/shard_map/all_to_all | solution.py:358
  65.1 0.1 dynamic_slice.3
  65.2 8.8 %all-to-all-done.1.y_ref = bf16[16,16,256]{2,1,0:T(8,128)(2,1)S(1)} async-done(((bf16[16,16,256]{2,1,0:T(8,128)(2,1)}), bf16[16,16,256]{2,1,0:T(8,128)(2,1)S(1)}, u32[]{:S(2)}, u32[]{:S(2)}) %all-to-all-start.1) | async-done | bytes 131104 | tf_op jit(solution)/shard_map/all_to_all | solution.py:358
  74.0 0.8 place.1
  74.8 15.5 %all_to_all.15.z_ref = bf16[16,8,384]{2,1,0:T(8,128)(2,1)S(1)} all-to-all(bf16[16,8,384]{2,1,0:T(8,128)(2,1)} %place.1), channel_id=1, replica_groups=mesh['xh'=2,'yh'=2,'yl'=2,'core'=2,'z'=8,'xl'=2] {'xh','yh','yl','core'}, dimensions={0} | all-to-all | bytes 196608 | tf_op jit(solution)/shard_map/all_to_all | solution.py:376
  90.3 0.8 means.1
  (6 shorter events, 0.0 us)
Async XLA Ops:
  0.6 24.2 %collective-permute-start.2 = (bf16[128,4096]{1,0:T(8,128)(2,1)}, bf16[128,4096]{1,0:T(8,128)(2,1)S(1)}, u32[]{:S(2)}, u32[]{:S(2)}) collective-permute-start(bf16[128,4096]{1,0:T(8,128)(2,1)} %p0.3), channel_id=1, source_target_pairs={{0,32},{32,0},{1,33},{33,1},{2,34},{34,2},{3,35},{35,3},{4,36},{36... | collective-permute-start | bytes 3145736 | tf_op jit(solution)/shard_map/ppermute | solution.py:270
  2.8 1.0 %copy-start.3 = (bf16[3,12,4096]{2,1,0:T(8,128)(2,1)S(1)}, bf16[3,12,4096]{2,1,0:T(8,128)(2,1)}, u32[]{:S(2)}) copy-start(bf16[3,12,4096]{2,1,0:T(8,128)(2,1)} %refs_ref.1) | copy-start | bytes 884740
  5.1 9.4 %copy-start.5 = (s32[128,8]{0,1:T(8,128)S(1)}, s32[128,8]{0,1:T(8,128)}, u32[]{:S(2)}) copy-start(s32[128,8]{0,1:T(8,128)} %param.10) | copy-start | bytes 12292
  5.1 36.6 %all-to-all-start = ((bf16[16,288,128]{2,1,0:T(8,128)(2,1)}), bf16[16,288,128]{2,1,0:T(8,128)(2,1)S(1)}, u32[]{:S(2)}, u32[]{:S(2)}) async-start(bf16[16,288,128]{2,1,0:T(8,128)(2,1)} %pack.1), calls=%async_computation | async-start | bytes 2359296 | tf_op jit(solution)/shard_map/all_to_all | solution.py:299
  14.5 13.6 %copy-start = (bf16[128,4096]{1,0:T(8,128)(2,1)S(1)}, bf16[128,4096]{1,0:T(8,128)(2,1)}, u32[]{:S(2)}) copy-start(bf16[128,4096]{1,0:T(8,128)(2,1)} %p0.3) | copy-start | bytes 3145732
  14.5 13.6 %copy-start.6 = (s32[4,2]{0,1:T(2,128)S(1)}, s32[4,2]{0,1:T(2,128)}, u32[]{:S(2)}) copy-start(s32[4,2]{0,1:T(2,128)} %param.9) | copy-start | bytes 100
  14.5 17.9 %copy-start.4 = (f32[2048]{0:T(1024)S(1)}, f32[2048]{0:T(1024)}, u32[]{:S(2)}) copy-start(f32[2048]{0:T(1024)} %param.8) | copy-start | bytes 24580
  14.5 10.3 %collective-permute-start.1 = (s32[8,128]{1,0:T(8,128)S(1)}, s32[8,128]{1,0:T(8,128)S(1)}, u32[]{:S(2)}, u32[]{:S(2)}) collective-permute-start(s32[8,128]{1,0:T(8,128)S(1)} %bitcast.48), channel_id=1, source_target_pairs={{0,32},{32,0},{1,33},{33,1},{2,34},{34,2},{3,35},{35,3},{4,36},{36... | collective-permute-start | bytes 12296 | tf_op jit(solution)/shard_map/ppermute | solution.py:270
  25.7 4.7 %collective-permute-start.3 = (bf16[64,4096]{1,0:T(8,128)(2,1)S(1)}, bf16[64,4096]{1,0:T(8,128)(2,1)S(1)}, u32[]{:S(2)}, u32[]{:S(2)}) collective-permute-start(bf16[64,4096]{1,0:T(8,128)(2,1)S(1)} %get-tuple-element.27), channel_id=1, source_target_pairs={{0,16},{16,0},{1,17},{17,1},{2,18},{18,2},{3,19},{19,3},{4,20},{20... | collective-permute-start | bytes 1572872 | tf_op jit(solution)/shard_map/ppermute | solution.py:270
  28.1 4.5 %collective-permute-start = (bf16[128,4096]{1,0:T(8,128)(2,1)S(1)}, bf16[128,4096]{1,0:T(8,128)(2,1)}, u32[]{:S(2)}, u32[]{:S(2)}) collective-permute-start(bf16[128,4096]{1,0:T(8,128)(2,1)S(1)} %copy-done), channel_id=1, source_target_pairs={{0,16},{16,0},{1,17},{17,1},{2,18},{18,2},{3,19},{19,3},{4,20},{20... | collective-permute-start | bytes 3145736 | tf_op jit(solution)/shard_map/ppermute | solution.py:270
  30.4 0.8 copy-start.1
  31.1 2.3 %collective-permute-start.4 = (bf16[64,4096]{1,0:T(8,128)(2,1)}, bf16[64,4096]{1,0:T(8,128)(2,1)}, u32[]{:S(2)}, u32[]{:S(2)}) collective-permute-start(bf16[64,4096]{1,0:T(8,128)(2,1)} %get-tuple-element.17), channel_id=1, source_target_pairs={{0,16},{16,0},{1,17},{17,1},{2,18},{18,2},{3,19},{19,3},{4,20},{20... | collective-permute-start | bytes 1572872 | tf_op jit(solution)/shard_map/ppermute | solution.py:270
  31.9 1.3 %collective-permute-start.5 = (s32[2,8,128]{2,1,0:T(8,128)S(1)}, s32[2,8,128]{2,1,0:T(8,128)S(1)}, u32[]{:S(2)}, u32[]{:S(2)}) collective-permute-start(s32[2,8,128]{2,1,0:T(8,128)S(1)} %pad_add_fusion), channel_id=1, source_target_pairs={{0,16},{16,0},{1,17},{17,1},{2,18},{18,2},{3,19},{19,3},{4,20},{20... | collective-permute-start | bytes 24584 | tf_op jit(solution)/shard_map/ppermute | solution.py:270
  41.7 1.0 %copy-start.2 = (bf16[64,4096]{1,0:T(8,128)(2,1)S(1)}, bf16[64,4096]{1,0:T(8,128)(2,1)}, u32[]{:S(2)}) copy-start(bf16[64,4096]{1,0:T(8,128)(2,1)} %copy-done.1) | copy-start | bytes 1572868
  42.8 12.6 %copy-start.7 = (s32[48]{0:T(128)S(1)}, s32[48]{0:T(128)}, u32[]{:S(2)}) copy-start(s32[48]{0:T(128)} %param.11) | copy-start | bytes 580
  48.6 6.8 %collective-permute-start.6 = (bf16[56,512]{1,0:T(8,128)(2,1)S(1)}, bf16[56,512]{1,0:T(8,128)(2,1)S(1)}, u32[]{:S(2)}, u32[]{:S(2)}) collective-permute-start(bf16[56,512]{1,0:T(8,128)(2,1)S(1)} %get-tuple-element.20), channel_id=1, source_target_pairs={{0,16},{16,0},{1,17},{17,1},{2,18},{18,2},{3,19},{19,3},{4,20},{20... | collective-permute-start | bytes 172040 | tf_op jit(solution)/shard_map/ppermute | solution.py:270
  53.6 3.5 %collective-permute-start.7 = (bf16[56,512]{1,0:T(8,128)(2,1)S(1)}, bf16[56,512]{1,0:T(8,128)(2,1)S(1)}, u32[]{:S(2)}, u32[]{:S(2)}) collective-permute-start(bf16[56,512]{1,0:T(8,128)(2,1)S(1)} %get-tuple-element.21), channel_id=1, source_target_pairs={{0,32},{32,0},{1,33},{33,1},{2,34},{34,2},{3,35},{35,3},{4,36},{36... | collective-permute-start | bytes 172040 | tf_op jit(solution)/shard_map/ppermute | solution.py:270
  53.8 4.7 %collective-permute-start.8 = (bf16[56,512]{1,0:T(8,128)(2,1)S(1)}, bf16[56,512]{1,0:T(8,128)(2,1)S(1)}, u32[]{:S(2)}, u32[]{:S(2)}) collective-permute-start(bf16[56,512]{1,0:T(8,128)(2,1)S(1)} %get-tuple-element.22), channel_id=1, source_target_pairs={{0,48},{16,32},{32,16},{48,0},{1,49},{17,33},{33,17},{49,1},{2,50}... | collective-permute-start | bytes 172040 | tf_op jit(solution)/shard_map/ppermute | solution.py:279
  61.6 12.4 %all-to-all-start.1 = ((bf16[16,16,256]{2,1,0:T(8,128)(2,1)}), bf16[16,16,256]{2,1,0:T(8,128)(2,1)S(1)}, u32[]{:S(2)}, u32[]{:S(2)}) async-start(bf16[16,16,256]{2,1,0:T(8,128)(2,1)} %get-tuple-element.23), calls=%async_computation.1 | async-start | bytes 262144 | tf_op jit(solution)/shard_map/all_to_all | solution.py:358

commit v4 on v3

--- a/solution.py
+++ b/solution.py
@@ -40,6 +40,7 @@
 SMEM_SPEC = pl.BlockSpec(memory_space=pltpu.SMEM)
 VMEM_SPEC = pl.BlockSpec(memory_space=pltpu.VMEM)
 ANY_SPEC = pl.BlockSpec(memory_space=pl.ANY)
+HBM_SPEC = pl.BlockSpec(memory_space=pltpu.HBM)
 
 
 def params(mib):
@@ -60,13 +61,19 @@
         out_ref[d] = packed
 
 
-def pool_copies(q, parts, pool, sem):
+def pool_kernel(q_ref, p0, p1, p2, p3, p4, p5, c0_ref, c1_ref, c23_ref, pool, cands, sem):
+    q = q_ref[0]
     copies = []
-    for i, (part, j, offset) in enumerate(zip(parts, (0, 1, 2, 3, 3), (0, 0, 0, 0, HALF))):
-        start = pl.multiple_of((q ^ j) * ROWS + offset, HALF)
-        rows = pl.ds(start, part.shape[0])
+    places = ((0, 0), (1, 0), (2, 0), (2, HALF), (3, 0), (3, HALF))
+    for i, (part, (j, offset)) in enumerate(zip((p0, p1, p2, p3, p4, p5), places)):
+        rows = pl.ds(pl.multiple_of((q ^ j) * ROWS + offset, HALF), part.shape[0])
         copies.append(pltpu.make_async_copy(part, pool.at[rows, :], sem.at[i]))
-    return copies
+    for copy in copies:
+        copy.start()
+    for j, cand in enumerate((c0_ref[...], c23_ref[0], c1_ref[...], c23_ref[1])):
+        cands[:, pl.ds(pl.multiple_of((q ^ j) * ROWS, ROWS), ROWS)] = cand
+    for copy in copies:
+        copy.wait()
 
 
 def split(x):
@@ -76,21 +83,26 @@
 
 
 def score_kernel(
-    q_ref, refs_ref, p0, p1, p2, p3, p4, wc_ref, ws_ref, w_ref, c0_ref, c1_ref, c23_ref,
+    q_ref, refs_ref, pool_hbm, wc_ref, ws_ref, w_ref, cands,
     own_ref, near_ref, far_ref, cross_ref,
-    wide, table0, table1, pool, cands, scores, groups, sem
+    wide, table0, table1, scores, groups, pool, sem
 ):
     q = q_ref[0]
-    copies = pool_copies(q, (p0, p1, p2, p3, p4), pool, sem)
+    steps = 16 // STEP_TILES
+    wide_cols = 128 * STEP_TILES
+    copies = []
+    for step in range(steps):
+        for part in range(2):
+            cols = pl.ds(part * K + step * wide_cols, wide_cols)
+            copies.append(
+                pltpu.make_async_copy(pool_hbm.at[:, cols], pool.at[:, cols], sem.at[step, part])
+            )
     for copy in copies:
         copy.start()
-    for j, cand in enumerate((c0_ref[...], c23_ref[0], c1_ref[...], c23_ref[1])):
-        cands[:, pl.ds(pl.multiple_of((q ^ j) * ROWS, ROWS), ROWS)] = cand
     wide[...] = refs_ref[...].astype(F32)
     energy = [jnp.zeros((CLASSES, 128), F32) for _ in range(QROT)]
     stride = QROT * 32
     tables = (table0, table1)
-    wide_cols = 128 * STEP_TILES
 
     def build(step):
         table = tables[step % 2]
@@ -111,10 +123,9 @@
                     table[row : row + CLASSES, at_im] = (ws * real + wc * imag).astype(BF16)
 
     build(0)
-    for copy in copies:
-        copy.wait()
-    steps = 16 // STEP_TILES
     for step in range(steps):
+        copies[2 * step].wait()
+        copies[2 * step + 1].wait()
         if step + 1 < steps:
             build(step + 1)
         table = tables[step % 2]
@@ -172,12 +183,9 @@
 
 
 def class_kernel(
-    q_ref, x0, x1, x2, x3, p0, p1, p2, p3, p4, cos_ref, sin_ref, out_ref, log_ref, pool, slots, line, sem
+    q_ref, x0, x1, x2, x3, pool, cos_ref, sin_ref, out_ref, log_ref, slots, line
 ):
     q = q_ref[0]
-    copies = pool_copies(q, (p0, p1, p2, p3, p4), pool, sem)
-    for copy in copies:
-        copy.start()
     parts = [x[...].astype(F32) for x in (x0, x1, x2, x3)]
     peaks = [x[48:49] + x[49:50] + x[50:51] for x in parts]
     peak = peaks[0]
@@ -204,8 +212,6 @@
     mass_row = jnp.sum(jnp.where(row_id == lane_id, mass, 0.0), axis=0, keepdims=True)
     mass_high = mass_row.astype(BF16).astype(F32)
     mass_low = mass_row - mass_high
-    for copy in copies:
-        copy.wait()
     for b in range(NBLK // 2):
         cols = slice(b * COLS, (b + 1) * COLS)
         cols_im = slice(K + b * COLS, K + (b + 1) * COLS)
@@ -266,6 +272,10 @@
     return (jnp.cos(angle), jnp.sin(angle))
 
 
+def in_hbm(x):
+    return pltpu.with_memory_space_constraint(x, pltpu.HBM)
+
+
 def swap(x, axis):
     return lax.ppermute(x, axis, [(0, 1), (1, 0)])
 
@@ -285,8 +295,10 @@
     q = pool_index.reshape(1)
 
     cand = candidates.T
+    far0 = swap(particles[:HALF], "yl")
     cand_far = swap(cand, "yl")
-    far = swap(particles, "yl")
+    rest, far0, cand_far = lax.optimization_barrier((particles[HALF:], far0, cand_far))
+    far1 = swap(rest, "yl")
     packed = pl.pallas_call(
         pack_kernel,
         out_shape=jax.ShapeDtypeStruct((NBLK, LOCAL * QROT * 32, 128), BF16),
@@ -298,44 +310,51 @@
     )(q, references)
     gathered = lax.all_to_all(packed, BLK, 0, 0, tiled=True)
     near = swap(particles, "core")
-    cand_far, far = lax.optimization_barrier((cand_far, far))
+    near1 = swap(far1, "core")
+    far0, near1 = lax.optimization_barrier((far0, near1))
+    near0 = swap(far0, "core")
     cand_near = swap(jnp.stack([cand, cand_far]), "core")
-    first = swap(far[:HALF], "core")
-    rest, first = lax.optimization_barrier((far[HALF:], first))
-    second = swap(rest, "core")
-    pool = (particles, near, far, first, second)
+    pool, cands = pl.pallas_call(
+        pool_kernel,
+        out_shape=(
+            pltpu.HBM((NPOOL * ROWS, 2 * K), BF16),
+            jax.ShapeDtypeStruct((8, NPOOL * ROWS), jnp.int32),
+        ),
+        in_specs=[SMEM_SPEC] + [ANY_SPEC] * 6 + [VMEM_SPEC] * 3,
+        out_specs=(HBM_SPEC, VMEM_SPEC),
+        scratch_shapes=[pltpu.SemaphoreType.DMA((6,))],
+        compiler_params=params(4),
+        name="pool",
+    )(
+        q, *[in_hbm(x) for x in (particles, near, far0, far1, near0, near1)],
+        cand, cand_far, cand_near,
+    )
 
     cosine, sine = phase_tables(offsets)
     wc = (noise_weight * cosine).reshape(NSHIFT * 16, 128)
     ws = (noise_weight * sine).reshape(NSHIFT * 16, 128)
     weight = noise_weight.reshape(16, 128)
 
-    copies = pltpu.SemaphoreType.DMA((5,))
-    pool_shape = VMEM((NPOOL * ROWS, 2 * K), BF16)
     table_rows = NSHIFT * QROT * CLASSES
     terms = pl.pallas_call(
         score_kernel,
         out_shape=[
             jax.ShapeDtypeStruct((56, NPOOL * ROWS), F32 if j == 0 else BF16) for j in range(NPOOL)
         ],
-        in_specs=[SMEM_SPEC, VMEM_SPEC] + [ANY_SPEC] * 5 + [VMEM_SPEC] * 6,
+        in_specs=[SMEM_SPEC, VMEM_SPEC, HBM_SPEC] + [VMEM_SPEC] * 4,
         out_specs=[VMEM_SPEC] * NPOOL,
         scratch_shapes=[
             VMEM((NBLK * LOCAL * QROT * 32, 128), F32),
             VMEM((table_rows, 256 * STEP_TILES), BF16),
             VMEM((table_rows, 256 * STEP_TILES), BF16),
-            pool_shape,
-            VMEM((8, NPOOL * ROWS), jnp.int32),
             VMEM((table_rows, NPOOL * ROWS), F32),
             VMEM((NPOOL, 56, NPOOL * ROWS), F32),
-            copies,
+            VMEM((NPOOL * ROWS, 2 * K), BF16),
+            pltpu.SemaphoreType.DMA((16 // STEP_TILES, 2)),
         ],
-        compiler_params=params(40),
+        compiler_params=params(20),
         name="score",
-    )(
-        q, gathered.reshape(NBLK * LOCAL * QROT * 32, 128), *pool,
-        wc, ws, weight, cand, cand_far, cand_near,
-    )
+    )(q, gathered.reshape(NBLK * LOCAL * QROT * 32, 128), in_hbm(pool), wc, ws, weight, cands)
     terms = trade(terms, POOL)
 
     sums, log_evidence = pl.pallas_call(
@@ -344,17 +363,15 @@
             jax.ShapeDtypeStruct((NBLK, 16, COLS), BF16),
             jax.ShapeDtypeStruct((1, ROWS), F32),
         ),
-        in_specs=[SMEM_SPEC] + [VMEM_SPEC] * 4 + [ANY_SPEC] * 5 + [VMEM_SPEC] * 2,
+        in_specs=[SMEM_SPEC] + [VMEM_SPEC] * 7,
         out_specs=(VMEM_SPEC, VMEM_SPEC),
         scratch_shapes=[
-            pool_shape,
             VMEM((NSHIFT * 16, NPOOL * ROWS), F32),
             VMEM((1, NPOOL * ROWS), F32),
-            copies,
         ],
-        compiler_params=params(24),
+        compiler_params=params(16),
         name="classes",
-    )(q, *terms, *pool, cosine, sine)
+    )(q, *terms, pool, cosine, sine)
     sums = lax.all_to_all(sums, BLK, 0, 0, tiled=True)
 
     class_ids = jnp.arange(CLASSES, dtype=jnp.int32)

time: 91.5 us -> 214 us (2.34)
  Pallas kernels: 11.7 us -> 139 us
  waiting for transfers between devices: 33.2 us -> 26.4 us
    pallas_call x0 -> x1, Pallas kernels: none -> 128 us  [on_device(): pl.pallas_call(pool_kernel, out_shape=(pltpu.HBM((NPOOL * ROWS, 2 * K), B...]
    all_to_all x1, waiting for transfers between devices: 8.33 us -> 0.01 us  [on_device(): gathered = lax.all_to_all(packed, BLK, 0, 0, tiled=True)]
    all_to_all x1, starting transfers between devices: 3.52 us -> 8.2 us  [on_device(): sums = lax.all_to_all(sums, BLK, 0, 0, tiled=True)]
    ppermute x8 -> x9, starting transfers between devices: 10.7 us -> 8.14 us  [swap(): return lax.ppermute(x, axis, [(0, 1), (1, 0)])]
    ppermute x8 -> x9, waiting for transfers between devices: 14.6 us -> 16.2 us  [swap(): return lax.ppermute(x, axis, [(0, 1), (1, 0)])]
  transfers between devices with their start and end apart: 11 -> 12, of which waited for: 8 -> 8; matrix products, arithmetic and copies ran while one was open for 2% -> 0% of each run, Pallas kernels for 1% -> 61%
where the time goes in v4:
time: 214 us; the launch traced here: 213 us
  Pallas kernels  139 us (65%)
  starting transfers between devices  26.9 us (13%)
  waiting for transfers between devices  26.4 us (12%)
  blocking collectives  15.8 us (7%)
  local copies, waits for them, and re-layouts  3.36 us (2%)
    pallas_call x1, Pallas kernels, on_device(): pl.pallas_call(pool_kernel, out_shape=(pltpu.HBM((NPOOL * ROWS, 2 * K), B...  128 us
    ppermute x9, waiting for transfers between devices, swap(): return lax.ppermute(x, axis, [(0, 1), (1, 0)])  16.2 us
    all_to_all x1, blocking collectives, on_device(): placed = lax.all_to_all(placed, DOM, 0, 0, tiled=True)  15.8 us
    all_to_all x1, starting transfers between devices, on_device(): gathered = lax.all_to_all(packed, BLK, 0, 0, tiled=True)  9.36 us
    all_to_all x1, waiting for transfers between devices, on_device(): sums = lax.all_to_all(sums, BLK, 0, 0, tiled=True)  8.37 us
    all_to_all x1, starting transfers between devices, on_device(): sums = lax.all_to_all(sums, BLK, 0, 0, tiled=True)  8.2 us
    ppermute x9, starting transfers between devices, swap(): return lax.ppermute(x, axis, [(0, 1), (1, 0)])  8.14 us
    pallas_call x1, Pallas kernels, on_device(): pl.pallas_call(score_kernel, out_shape=[jax.ShapeDtypeStruct((56, NPOOL *...  6.71 us
  transfers between devices with their start and end apart: 12, of which 8 were waited for; matrix products, arithmetic and copies ran while one was open for 0% of the time, Pallas kernels for 61%

profile of v4, /device:TPU:1, one launch (start us, length us, event | category | flops | bytes accessed | tf_op | source)
XLA Modules:
  0.0 213.3 jit_solution(2154247667792399041)
XLA Ops:
  0.6 0.0 copy-start.1
  0.6 2.1 fusion.20
  2.8 2.1 collective-permute-start.1
  4.9 0.0 copy-done.1
  4.9 1.3 pack.1
  6.2 0.0 copy-start.3
  6.2 0.0 copy-start.4
  6.2 0.0 copy-start.9
  6.2 0.0 copy-start.2
  6.2 9.4 %all-to-all-start = ((bf16[16,288,128]{2,1,0:T(8,128)(2,1)}), bf16[16,288,128]{2,1,0:T(8,128)(2,1)S(1)}, u32[]{:S(2)}, u32[]{:S(2)}) async-start(bf16[16,288,128]{2,1,0:T(8,128)(2,1)} %pack.1), calls=%async_computation | async-start | bytes 2359296 | tf_op jit(solution)/shard_map/all_to_all | solution.py:311
  15.6 0.0 copy-done.3
  15.6 0.3 collective-permute-start.2
  15.8 2.3 %collective-permute-done.2.c1_ref = s32[8,128]{1,0:T(8,128)S(1)} collective-permute-done((s32[8,128]{1,0:T(8,128)S(1)}, s32[8,128]{1,0:T(8,128)S(1)}, u32[]{:S(2)}, u32[]{:S(2)}) %collective-permute-start.2) | collective-permute-done | bytes 4128 | tf_op jit(solution)/shard_map/ppermute | solution.py:280
  18.1 0.0 collective-permute-done.1.p2
  18.1 0.0 copy-start.6
  18.1 0.6 collective-permute-start.3
  18.7 10.5 %collective-permute-done.3.p3 = bf16[64,4096]{1,0:T(8,128)(2,1)S(1)} collective-permute-done((bf16[64,4096]{1,0:T(8,128)(2,1)S(1)}, bf16[64,4096]{1,0:T(8,128)(2,1)S(1)}, u32[]{:S(2)}, u32[]{:S(2)}) %collective-permute-start.3) | collective-permute-done | bytes 524320 | tf_op jit(solution)/shard_map/ppermute | solution.py:280
  29.2 0.0 copy-done.6
  29.2 0.0 copy-start.7
  29.2 3.3 %collective-permute-start.4 = (bf16[64,4096]{1,0:T(8,128)(2,1)S(1)}, bf16[64,4096]{1,0:T(8,128)(2,1)S(1)}, u32[]{:S(2)}, u32[]{:S(2)}) collective-permute-start(bf16[64,4096]{1,0:T(8,128)(2,1)S(1)} %collective-permute-done.3.p3), channel_id=1, source_target_pairs={{0,16},{16,0},{1,17},{17,1},{2,18},{18,2},{3,19},{19,3},{4,20},{20... | collective-permute-start | bytes 1572872 | tf_op jit(solution)/shard_map/ppermute | solution.py:280
  32.5 0.0 copy-done.4
  32.5 0.1 collective-permute-start
  32.6 0.0 copy-done.9
  32.6 1.4 collective-permute-done.4.p5
  34.0 0.0 copy-start.8
  34.0 0.4 collective-permute-start.5
  34.4 0.3 fusion.5
  34.7 0.0 copy-done.7
  34.7 0.1 copy-done.8
  34.8 0.4 collective-permute-start.6
  35.2 0.1 mul.110
  35.3 0.1 mul.111
  35.4 0.1 mul.117
  35.5 0.1 mul.118
  35.5 0.0 copy-done.2
  35.5 0.2 bitcast_multiply_fusion
  35.8 0.5 collective-permute-done.6.c23_ref
  36.3 0.0 collective-permute-done.p1
  36.3 0.0 copy-start.5
  36.3 0.3 collective-permute-done.5.p4
  36.6 0.7 copy-done.5
  37.3 128.2 %pool.1 = (bf16[512,4096]{1,0:T(8,128)(2,1)}, s32[8,512]{1,0:T(8,128)S(1)}) custom-call(s32[1]{0:T(128)} %bitcast.1.q_ref, bf16[128,4096]{1,0:T(8,128)(2,1)} %p0.1, bf16[128,4096]{1,0:T(8,128)(2,1)} %copy-done.5, bf16[64,4096]{1,0:T(8,128)(2,1)} %copy-done.6, bf16[64,4096]{1,0:T(8,128)(2,1)} %copy-done.7, bf16[64,4096]{1,0:T(8,128)(2,1)} %collective-permute-done.5.p4, ...), custom_call_target="tpu_custom_call" | custom-call | tf_op jit(solution)/shard_map/pool/pallas_call | solution.py:317
  165.5 0.0 all-to-all-done
  165.5 0.0 copy-start.10
  165.5 0.0 copy-start
  165.5 6.7 %score.1 = (f32[56,512]{1,0:T(8,128)S(1)}, bf16[56,512]{1,0:T(8,128)(2,1)S(1)}, bf16[56,512]{1,0:T(8,128)(2,1)S(1)}, bf16[56,512]{1,0:T(8,128)(2,1)S(1)}) custom-call(s32[1]{0:T(128)} %bitcast.1.q_ref, bf16[4608,128]{1,0:T(8,128)(2,1)S(1)} %bitcast.45, bf16[512,4096]{1,0:T(8,128)(2,1)} %get-tuple-element.23.pool_hbm.pool, ...), custom_call_target="tpu_custom_call" | custom-call | tf_op jit(solution)/shard_map/score/pallas_call | solution.py:339
  172.2 0.5 collective-permute-start.7
  172.7 0.6 collective-permute-start.8
  173.3 1.2 collective-permute-start.9
  174.5 0.0 copy-done.10
  174.5 0.1 convert_reduce_fusion
  174.6 0.0 collective-permute-done.7.x1
  174.6 1.1 collective-permute-done.8.x2
  175.7 1.8 collective-permute-done.9.x3
  177.6 0.0 copy-done
  177.6 1.7 classes.1
  179.3 8.2 %all-to-all-start.1 = ((bf16[16,16,256]{2,1,0:T(8,128)(2,1)}), bf16[16,16,256]{2,1,0:T(8,128)(2,1)S(1)}, u32[]{:S(2)}, u32[]{:S(2)}) async-start(bf16[16,16,256]{2,1,0:T(8,128)(2,1)} %get-tuple-element.29), calls=%async_computation.1 | async-start | bytes 262144 | tf_op jit(solution)/shard_map/all_to_all | solution.py:375
  187.5 0.1 dynamic_slice.3
  187.6 8.4 %all-to-all-done.1.y_ref = bf16[16,16,256]{2,1,0:T(8,128)(2,1)S(1)} async-done(((bf16[16,16,256]{2,1,0:T(8,128)(2,1)}), bf16[16,16,256]{2,1,0:T(8,128)(2,1)S(1)}, u32[]{:S(2)}, u32[]{:S(2)}) %all-to-all-start.1) | async-done | bytes 131104 | tf_op jit(solution)/shard_map/all_to_all | solution.py:375
  195.9 0.8 place.1
  196.8 15.8 %all_to_all.15.z_ref = bf16[16,8,384]{2,1,0:T(8,128)(2,1)S(1)} all-to-all(bf16[16,8,384]{2,1,0:T(8,128)(2,1)} %place.1), channel_id=1, replica_groups=mesh['xh'=2,'yh'=2,'yl'=2,'core'=2,'z'=8,'xl'=2] {'xh','yh','yl','core'}, dimensions={0} | all-to-all | bytes 196608 | tf_op jit(solution)/shard_map/all_to_all | solution.py:393
  212.6 0.8 means.1
  (6 shorter events, 0.0 us)
Async XLA Ops:
  0.6 4.3 %copy-start.1 = (bf16[3,12,4096]{2,1,0:T(8,128)(2,1)S(1)}, bf16[3,12,4096]{2,1,0:T(8,128)(2,1)}, u32[]{:S(2)}) copy-start(bf16[3,12,4096]{2,1,0:T(8,128)(2,1)} %refs_ref.1) | copy-start | bytes 884740
  2.8 15.4 %collective-permute-start.1 = (bf16[64,4096]{1,0:T(8,128)(2,1)}, bf16[64,4096]{1,0:T(8,128)(2,1)S(1)}, u32[]{:S(2)}, u32[]{:S(2)}) collective-permute-start(bf16[64,4096]{1,0:T(8,128)(2,1)} %get-tuple-element.33), channel_id=1, source_target_pairs={{0,32},{32,0},{1,33},{33,1},{2,34},{34,2},{3,35},{35,3},{4,36},{36... | collective-permute-start | bytes 1572872 | tf_op jit(solution)/shard_map/ppermute | solution.py:280
  6.2 9.4 %copy-start.3 = (s32[128,8]{0,1:T(8,128)S(1)}, s32[128,8]{0,1:T(8,128)}, u32[]{:S(2)}) copy-start(s32[128,8]{0,1:T(8,128)} %param.10) | copy-start | bytes 12292
  6.2 26.3 %copy-start.4 = (bf16[128,4096]{1,0:T(8,128)(2,1)S(1)}, bf16[128,4096]{1,0:T(8,128)(2,1)}, u32[]{:S(2)}) copy-start(bf16[128,4096]{1,0:T(8,128)(2,1)} %p0.1) | copy-start | bytes 3145732
  6.2 26.4 %copy-start.9 = (s32[4,2]{0,1:T(2,128)S(1)}, s32[4,2]{0,1:T(2,128)}, u32[]{:S(2)}) copy-start(s32[4,2]{0,1:T(2,128)} %param.9) | copy-start | bytes 100
  6.2 29.4 %copy-start.2 = (f32[2048]{0:T(1024)S(1)}, f32[2048]{0:T(1024)}, u32[]{:S(2)}) copy-start(f32[2048]{0:T(1024)} %param.8) | copy-start | bytes 24580
  6.2 159.3 %all-to-all-start = ((bf16[16,288,128]{2,1,0:T(8,128)(2,1)}), bf16[16,288,128]{2,1,0:T(8,128)(2,1)S(1)}, u32[]{:S(2)}, u32[]{:S(2)}) async-start(bf16[16,288,128]{2,1,0:T(8,128)(2,1)} %pack.1), calls=%async_computation | async-start | bytes 2359296 | tf_op jit(solution)/shard_map/all_to_all | solution.py:311
  15.6 2.5 %collective-permute-start.2 = (s32[8,128]{1,0:T(8,128)S(1)}, s32[8,128]{1,0:T(8,128)S(1)}, u32[]{:S(2)}, u32[]{:S(2)}) collective-permute-start(s32[8,128]{1,0:T(8,128)S(1)} %bitcast.48), channel_id=1, source_target_pairs={{0,32},{32,0},{1,33},{33,1},{2,34},{34,2},{3,35},{35,3},{4,36},{36... | collective-permute-start | bytes 12296 | tf_op jit(solution)/shard_map/ppermute | solution.py:280
  18.1 11.0 %copy-start.6 = (bf16[64,4096]{1,0:T(8,128)(2,1)}, bf16[64,4096]{1,0:T(8,128)(2,1)S(1)}, u32[]{:S(2)}) copy-start(bf16[64,4096]{1,0:T(8,128)(2,1)S(1)} %collective-permute-done.1.p2) | copy-start | bytes 1572868
  18.1 11.0 %collective-permute-start.3 = (bf16[64,4096]{1,0:T(8,128)(2,1)S(1)}, bf16[64,4096]{1,0:T(8,128)(2,1)S(1)}, u32[]{:S(2)}, u32[]{:S(2)}) collective-permute-start(bf16[64,4096]{1,0:T(8,128)(2,1)S(1)} %get-tuple-element.19), channel_id=1, source_target_pairs={{0,32},{32,0},{1,33},{33,1},{2,34},{34,2},{3,35},{35,3},{4,36},{36... | collective-permute-start | bytes 1572872 | tf_op jit(solution)/shard_map/ppermute | solution.py:280
  29.2 5.5 %copy-start.7 = (bf16[64,4096]{1,0:T(8,128)(2,1)}, bf16[64,4096]{1,0:T(8,128)(2,1)S(1)}, u32[]{:S(2)}) copy-start(bf16[64,4096]{1,0:T(8,128)(2,1)S(1)} %collective-permute-done.3.p3) | copy-start | bytes 1572868
  29.2 4.8 %collective-permute-start.4 = (bf16[64,4096]{1,0:T(8,128)(2,1)S(1)}, bf16[64,4096]{1,0:T(8,128)(2,1)S(1)}, u32[]{:S(2)}, u32[]{:S(2)}) collective-permute-start(bf16[64,4096]{1,0:T(8,128)(2,1)S(1)} %collective-permute-done.3.p3), channel_id=1, source_target_pairs={{0,16},{16,0},{1,17},{17,1},{2,18},{18,2},{3,19},{19,3},{4,20},{20... | collective-permute-start | bytes 1572872 | tf_op jit(solution)/shard_map/ppermute | solution.py:280
  32.5 3.8 %collective-permute-start = (bf16[128,4096]{1,0:T(8,128)(2,1)S(1)}, bf16[128,4096]{1,0:T(8,128)(2,1)S(1)}, u32[]{:S(2)}, u32[]{:S(2)}) collective-permute-start(bf16[128,4096]{1,0:T(8,128)(2,1)S(1)} %copy-done.4), channel_id=1, source_target_pairs={{0,16},{16,0},{1,17},{17,1},{2,18},{18,2},{3,19},{19,3},{4,20},{20... | collective-permute-start | bytes 3145736 | tf_op jit(solution)/shard_map/ppermute | solution.py:280
  34.0 0.8 copy-start.8
  34.0 2.6 %collective-permute-start.5 = (bf16[64,4096]{1,0:T(8,128)(2,1)}, bf16[64,4096]{1,0:T(8,128)(2,1)}, u32[]{:S(2)}, u32[]{:S(2)}) collective-permute-start(bf16[64,4096]{1,0:T(8,128)(2,1)} %copy-done.6), channel_id=1, source_target_pairs={{0,16},{16,0},{1,17},{17,1},{2,18},{18,2},{3,19},{19,3},{4,20},{20... | collective-permute-start | bytes 1572872 | tf_op jit(solution)/shard_map/ppermute | solution.py:280
  34.8 1.4 collective-permute-start.6
  36.3 1.0 copy-start.5
  165.5 9.0 %copy-start.10 = (s32[48]{0:T(128)S(1)}, s32[48]{0:T(128)}, u32[]{:S(2)}) copy-start(s32[48]{0:T(128)} %param.11) | copy-start | bytes 580
  165.5 12.1 %copy-start = (bf16[512,4096]{1,0:T(8,128)(2,1)S(1)}, bf16[512,4096]{1,0:T(8,128)(2,1)}, u32[]{:S(2)}) copy-start(bf16[512,4096]{1,0:T(8,128)(2,1)} %get-tuple-element.23.pool_hbm.pool) | copy-start | bytes 12582916
  172.2 2.3 %collective-permute-start.7 = (bf16[56,512]{1,0:T(8,128)(2,1)S(1)}, bf16[56,512]{1,0:T(8,128)(2,1)S(1)}, u32[]{:S(2)}, u32[]{:S(2)}) collective-permute-start(bf16[56,512]{1,0:T(8,128)(2,1)S(1)} %get-tuple-element.26), channel_id=1, source_target_pairs={{0,16},{16,0},{1,17},{17,1},{2,18},{18,2},{3,19},{19,3},{4,20},{20... | collective-permute-start | bytes 172040 | tf_op jit(solution)/shard_map/ppermute | solution.py:280
  172.7 3.0 %collective-permute-start.8 = (bf16[56,512]{1,0:T(8,128)(2,1)S(1)}, bf16[56,512]{1,0:T(8,128)(2,1)S(1)}, u32[]{:S(2)}, u32[]{:S(2)}) collective-permute-start(bf16[56,512]{1,0:T(8,128)(2,1)S(1)} %get-tuple-element.27), channel_id=1, source_target_pairs={{0,32},{32,0},{1,33},{33,1},{2,34},{34,2},{3,35},{35,3},{4,36},{36... | collective-permute-start | bytes 172040 | tf_op jit(solution)/shard_map/ppermute | solution.py:280
  173.3 4.3 %collective-permute-start.9 = (bf16[56,512]{1,0:T(8,128)(2,1)S(1)}, bf16[56,512]{1,0:T(8,128)(2,1)S(1)}, u32[]{:S(2)}, u32[]{:S(2)}) collective-permute-start(bf16[56,512]{1,0:T(8,128)(2,1)S(1)} %get-tuple-element.28), channel_id=1, source_target_pairs={{0,48},{16,32},{32,16},{48,0},{1,49},{17,33},{33,17},{49,1},{2,50}... | collective-permute-start | bytes 172040 | tf_op jit(solution)/shard_map/ppermute | solution.py:289
  179.3 16.7 %all-to-all-start.1 = ((bf16[16,16,256]{2,1,0:T(8,128)(2,1)}), bf16[16,16,256]{2,1,0:T(8,128)(2,1)S(1)}, u32[]{:S(2)}, u32[]{:S(2)}) async-start(bf16[16,16,256]{2,1,0:T(8,128)(2,1)} %get-tuple-element.29), calls=%async_computation.1 | async-start | bytes 262144 | tf_op jit(solution)/shard_map/all_to_all | solution.py:375

commit v5 on v3

--- a/solution.py
+++ b/solution.py
@@ -25,7 +25,7 @@
 ROT = 12
 NSHIFT = 4
 ROWS = 128
-HALF = ROWS // 2
+FIRST = 48
 NPOOL = 4
 QROT = ROT // NPOOL
 QCLS = CLASSES // NPOOL
@@ -40,6 +40,7 @@
 SMEM_SPEC = pl.BlockSpec(memory_space=pltpu.SMEM)
 VMEM_SPEC = pl.BlockSpec(memory_space=pltpu.VMEM)
 ANY_SPEC = pl.BlockSpec(memory_space=pl.ANY)
+HBM_SPEC = pl.BlockSpec(memory_space=pltpu.HBM)
 
 
 def params(mib):
@@ -62,9 +63,9 @@
 
 def pool_copies(q, parts, pool, sem):
     copies = []
-    for i, (part, j, offset) in enumerate(zip(parts, (0, 1, 2, 3, 3), (0, 0, 0, 0, HALF))):
-        start = pl.multiple_of((q ^ j) * ROWS + offset, HALF)
-        rows = pl.ds(start, part.shape[0])
+    places = ((0, 0), (1, 0), (2, 0), (2, FIRST), (3, 0), (3, FIRST))
+    for i, (part, (j, offset)) in enumerate(zip(parts, places)):
+        rows = pl.ds(pl.multiple_of((q ^ j) * ROWS + offset, 16), part.shape[0])
         copies.append(pltpu.make_async_copy(part, pool.at[rows, :], sem.at[i]))
     return copies
 
@@ -76,12 +77,14 @@
 
 
 def score_kernel(
-    q_ref, refs_ref, p0, p1, p2, p3, p4, wc_ref, ws_ref, w_ref, c0_ref, c1_ref, c23_ref,
-    own_ref, near_ref, far_ref, cross_ref,
-    wide, table0, table1, pool, cands, scores, groups, sem
+    q_ref, refs_ref, p0, p1, p2, p3, p4, p5, wc_ref, ws_ref, w_ref, c0_ref, c1_ref, c23_ref,
+    own_ref, near_ref, far_ref, cross_ref, pool,
+    wide, table0, table1, scores, groups, cands, sem
 ):
     q = q_ref[0]
-    copies = pool_copies(q, (p0, p1, p2, p3, p4), pool, sem)
+    steps = 16 // STEP_TILES
+    wide_cols = 128 * STEP_TILES
+    copies = pool_copies(q, (p0, p1, p2, p3, p4, p5), pool, sem)
     for copy in copies:
         copy.start()
     for j, cand in enumerate((c0_ref[...], c23_ref[0], c1_ref[...], c23_ref[1])):
@@ -90,7 +93,6 @@
     energy = [jnp.zeros((CLASSES, 128), F32) for _ in range(QROT)]
     stride = QROT * 32
     tables = (table0, table1)
-    wide_cols = 128 * STEP_TILES
 
     def build(step):
         table = tables[step % 2]
@@ -113,7 +115,6 @@
     build(0)
     for copy in copies:
         copy.wait()
-    steps = 16 // STEP_TILES
     for step in range(steps):
         if step + 1 < steps:
             build(step + 1)
@@ -172,12 +173,9 @@
 
 
 def class_kernel(
-    q_ref, x0, x1, x2, x3, p0, p1, p2, p3, p4, cos_ref, sin_ref, out_ref, log_ref, pool, slots, line, sem
+    q_ref, x0, x1, x2, x3, pool, cos_ref, sin_ref, out_ref, log_ref, slots, line
 ):
     q = q_ref[0]
-    copies = pool_copies(q, (p0, p1, p2, p3, p4), pool, sem)
-    for copy in copies:
-        copy.start()
     parts = [x[...].astype(F32) for x in (x0, x1, x2, x3)]
     peaks = [x[48:49] + x[49:50] + x[50:51] for x in parts]
     peak = peaks[0]
@@ -204,8 +202,6 @@
     mass_row = jnp.sum(jnp.where(row_id == lane_id, mass, 0.0), axis=0, keepdims=True)
     mass_high = mass_row.astype(BF16).astype(F32)
     mass_low = mass_row - mass_high
-    for copy in copies:
-        copy.wait()
     for b in range(NBLK // 2):
         cols = slice(b * COLS, (b + 1) * COLS)
         cols_im = slice(K + b * COLS, K + (b + 1) * COLS)
@@ -266,6 +262,10 @@
     return (jnp.cos(angle), jnp.sin(angle))
 
 
+def in_hbm(x):
+    return pltpu.with_memory_space_constraint(x, pltpu.HBM)
+
+
 def swap(x, axis):
     return lax.ppermute(x, axis, [(0, 1), (1, 0)])
 
@@ -285,8 +285,8 @@
     q = pool_index.reshape(1)
 
     cand = candidates.T
+    far0 = swap(particles[:FIRST], "yl")
     cand_far = swap(cand, "yl")
-    far = swap(particles, "yl")
     packed = pl.pallas_call(
         pack_kernel,
         out_shape=jax.ShapeDtypeStruct((NBLK, LOCAL * QROT * 32, 128), BF16),
@@ -296,44 +296,44 @@
         compiler_params=params(16),
         name="pack",
     )(q, references)
+    packed, whole = lax.optimization_barrier((packed, particles))
     gathered = lax.all_to_all(packed, BLK, 0, 0, tiled=True)
+    rest, far0, cand_far = lax.optimization_barrier((whole[FIRST:], far0, cand_far))
+    far1 = swap(rest, "yl")
     near = swap(particles, "core")
-    cand_far, far = lax.optimization_barrier((cand_far, far))
+    near1 = swap(far1, "core")
+    far0, near1 = lax.optimization_barrier((far0, near1))
+    near0 = swap(far0, "core")
     cand_near = swap(jnp.stack([cand, cand_far]), "core")
-    first = swap(far[:HALF], "core")
-    rest, first = lax.optimization_barrier((far[HALF:], first))
-    second = swap(rest, "core")
-    pool = (particles, near, far, first, second)
+    parts = (in_hbm(particles), near, far0, far1, near0, near1)
 
     cosine, sine = phase_tables(offsets)
     wc = (noise_weight * cosine).reshape(NSHIFT * 16, 128)
     ws = (noise_weight * sine).reshape(NSHIFT * 16, 128)
     weight = noise_weight.reshape(16, 128)
 
-    copies = pltpu.SemaphoreType.DMA((5,))
-    pool_shape = VMEM((NPOOL * ROWS, 2 * K), BF16)
     table_rows = NSHIFT * QROT * CLASSES
-    terms = pl.pallas_call(
+    *terms, pool = pl.pallas_call(
         score_kernel,
         out_shape=[
             jax.ShapeDtypeStruct((56, NPOOL * ROWS), F32 if j == 0 else BF16) for j in range(NPOOL)
-        ],
-        in_specs=[SMEM_SPEC, VMEM_SPEC] + [ANY_SPEC] * 5 + [VMEM_SPEC] * 6,
-        out_specs=[VMEM_SPEC] * NPOOL,
+        ]
+        + [jax.ShapeDtypeStruct((NPOOL * ROWS, 2 * K), BF16)],
+        in_specs=[SMEM_SPEC, VMEM_SPEC] + [HBM_SPEC] + [ANY_SPEC] * 5 + [VMEM_SPEC] * 6,
+        out_specs=[VMEM_SPEC] * (NPOOL + 1),
         scratch_shapes=[
             VMEM((NBLK * LOCAL * QROT * 32, 128), F32),
             VMEM((table_rows, 256 * STEP_TILES), BF16),
             VMEM((table_rows, 256 * STEP_TILES), BF16),
-            pool_shape,
-            VMEM((8, NPOOL * ROWS), jnp.int32),
             VMEM((table_rows, NPOOL * ROWS), F32),
             VMEM((NPOOL, 56, NPOOL * ROWS), F32),
-            copies,
+            VMEM((8, NPOOL * ROWS), jnp.int32),
+            pltpu.SemaphoreType.DMA((6,)),
         ],
-        compiler_params=params(40),
+        compiler_params=params(20),
         name="score",
     )(
-        q, gathered.reshape(NBLK * LOCAL * QROT * 32, 128), *pool,
+        q, gathered.reshape(NBLK * LOCAL * QROT * 32, 128), *parts,
         wc, ws, weight, cand, cand_far, cand_near,
     )
     terms = trade(terms, POOL)
@@ -344,17 +344,15 @@
             jax.ShapeDtypeStruct((NBLK, 16, COLS), BF16),
             jax.ShapeDtypeStruct((1, ROWS), F32),
         ),
-        in_specs=[SMEM_SPEC] + [VMEM_SPEC] * 4 + [ANY_SPEC] * 5 + [VMEM_SPEC] * 2,
+        in_specs=[SMEM_SPEC] + [VMEM_SPEC] * 7,
         out_specs=(VMEM_SPEC, VMEM_SPEC),
         scratch_shapes=[
-            pool_shape,
             VMEM((NSHIFT * 16, NPOOL * ROWS), F32),
             VMEM((1, NPOOL * ROWS), F32),
-            copies,
         ],
-        compiler_params=params(24),
+        compiler_params=params(16),
         name="classes",
-    )(q, *terms, *pool, cosine, sine)
+    )(q, *terms, pool, cosine, sine)
     sums = lax.all_to_all(sums, BLK, 0, 0, tiled=True)
 
     class_ids = jnp.arange(CLASSES, dtype=jnp.int32)

time: 91.5 us -> 95.7 us (1.046)
  local copies, waits for them, and re-layouts: 4.12 us -> 9.11 us
  waiting for transfers between devices: 33.2 us -> 29.2 us
  other arithmetic: 0.65 us -> 3.82 us
    all_to_all x1, waiting for transfers between devices: 8.33 us -> 0.01 us  [on_device(): gathered = lax.all_to_all(packed, BLK, 0, 0, tiled=True)]
    ppermute x8 -> x9, waiting for transfers between devices: 14.6 us -> 19 us  [swap(): return lax.ppermute(x, axis, [(0, 1), (1, 0)])]
    all_to_all x1, starting transfers between devices: 3.52 us -> 6.69 us  [on_device(): sums = lax.all_to_all(sums, BLK, 0, 0, tiled=True)]
    ppermute x8 -> x9, starting transfers between devices: 10.7 us -> 8.02 us  [swap(): return lax.ppermute(x, axis, [(0, 1), (1, 0)])]
    mul x2, local copies, waits for them, and re-layouts: 0.15 us -> 2.49 us  [phase_tables(): offsets[:, 1:2] * rowpos[None, :]]
    mul x3, local copies, waits for them, and re-layouts: 0.16 us -> 1.84 us  [phase_tables(): offsets[:, 0:1] * column[None, :] + offsets[:, 1:2] * rowpos[None, :]]
    pallas_call x1, Pallas kernels: 3.07 us -> 1.63 us  [on_device(): pl.pallas_call(class_kernel, out_shape=(jax.ShapeDtypeStruct((NBLK, 16, C...]
    mul x1, other arithmetic: 0.21 us -> 1.58 us  [on_device(): ws = (noise_weight * sine).reshape(NSHIFT * 16, 128)]
  transfers between devices with their start and end apart: 11 -> 12, of which waited for: 8 -> 6; matrix products, arithmetic and copies ran while one was open for 2% -> 10% of each run, Pallas kernels for 1% -> 1%
where the time goes in v5:
time: 95.7 us; the launch traced here: 95 us
  waiting for transfers between devices  29.2 us (31%)
  starting transfers between devices  25.6 us (27%)
  blocking collectives  15.4 us (16%)
  Pallas kernels  11.1 us (12%)
  local copies, waits for them, and re-layouts  9.11 us (10%)
  other arithmetic  3.82 us (4%)
    ppermute x9, waiting for transfers between devices, swap(): return lax.ppermute(x, axis, [(0, 1), (1, 0)])  19 us
    all_to_all x1, blocking collectives, on_device(): placed = lax.all_to_all(placed, DOM, 0, 0, tiled=True)  15.4 us
    all_to_all x1, starting transfers between devices, on_device(): gathered = lax.all_to_all(packed, BLK, 0, 0, tiled=True)  9.35 us
    all_to_all x1, waiting for transfers between devices, on_device(): sums = lax.all_to_all(sums, BLK, 0, 0, tiled=True)  8.74 us
    ppermute x9, starting transfers between devices, swap(): return lax.ppermute(x, axis, [(0, 1), (1, 0)])  8.02 us
    all_to_all x1, starting transfers between devices, on_device(): sums = lax.all_to_all(sums, BLK, 0, 0, tiled=True)  6.69 us
    pallas_call x1, Pallas kernels, on_device(): pl.pallas_call(score_kernel, out_shape=[jax.ShapeDtypeStruct((56, NPOOL *...  6.6 us
    unnamed x22, local copies, waits for them, and re-layouts  2.54 us
  transfers between devices with their start and end apart: 12, of which 6 were waited for; matrix products, arithmetic and copies ran while one was open for 10% of the time, Pallas kernels for 1%

profile of v5, /device:TPU:1, one launch (start us, length us, event | category | flops | bytes accessed | tf_op | source)
XLA Modules:
  0.0 95.0 jit_solution(194829445060054467)
XLA Ops:
  0.6 1.0 %slice.13 = bf16[48,4096]{1,0:T(8,128)(2,1)S(1)} slice(bf16[128,4096]{1,0:T(8,128)(2,1)} %p0.1), slice={[0:48], [0:4096]} | slice | bytes 786432 | tf_op jit(solution)/shard_map/slice | solution.py:288
  1.7 2.2 %collective-permute-start.1 = (bf16[48,4096]{1,0:T(8,128)(2,1)S(1)}, bf16[48,4096]{1,0:T(8,128)(2,1)}, u32[]{:S(2)}, u32[]{:S(2)}) collective-permute-start(bf16[48,4096]{1,0:T(8,128)(2,1)S(1)} %slice.13), channel_id=1, source_target_pairs={{0,32},{32,0},{1,33},{33,1},{2,34},{34,2},{3,35},{35,3},{4,36},{36... | collective-permute-start | bytes 1179656 | tf_op jit(solution)/shard_map/ppermute | solution.py:270
  3.9 0.0 copy-start
  3.9 1.0 %copy-done = bf16[3,12,4096]{2,1,0:T(8,128)(2,1)S(1)} copy-done((bf16[3,12,4096]{2,1,0:T(8,128)(2,1)S(1)}, bf16[3,12,4096]{2,1,0:T(8,128)(2,1)}, u32[]{:S(2)}) %copy-start) | copy-done | bytes 294936
  4.9 1.3 %pack.1 = bf16[16,288,128]{2,1,0:T(8,128)(2,1)} custom-call(s32[1]{0:T(128)} %bitcast.1.q_ref, bf16[3,12,4096]{2,1,0:T(8,128)(2,1)S(1)} %copy-done), custom_call_target="tpu_custom_call" | custom-call | tf_op jit(solution)/shard_map/pack/pallas_call | solution.py:290
  6.1 0.0 copy-start.6
  6.1 9.3 %all-to-all-start = ((bf16[16,288,128]{2,1,0:T(8,128)(2,1)}), bf16[16,288,128]{2,1,0:T(8,128)(2,1)S(1)}, u32[]{:S(2)}, u32[]{:S(2)}) async-start(bf16[16,288,128]{2,1,0:T(8,128)(2,1)} %pack.1), calls=%async_computation | async-start | bytes 2359296 | tf_op jit(solution)/shard_map/all_to_all | solution.py:300
  15.5 0.0 copy-start.8
  15.5 0.0 copy-start.5
  15.5 0.0 copy-done.6
  15.5 0.3 collective-permute-start.2
  15.8 1.1 %slice.12 = bf16[80,4096]{1,0:T(8,128)(2,1)S(1)} slice(bf16[128,4096]{1,0:T(8,128)(2,1)} %p0.1), slice={[48:128], [0:4096]} | slice | bytes 1310720 | tf_op jit(solution)/shard_map/slice | solution.py:301
  16.9 1.2 %collective-permute-done.2.c1_ref = s32[8,128]{1,0:T(8,128)S(1)} collective-permute-done((s32[8,128]{1,0:T(8,128)S(1)}, s32[8,128]{1,0:T(8,128)S(1)}, u32[]{:S(2)}, u32[]{:S(2)}) %collective-permute-start.2) | collective-permute-done | bytes 4128 | tf_op jit(solution)/shard_map/ppermute | solution.py:270
  18.1 0.0 collective-permute-done.1.p2
  18.1 0.2 collective-permute-start.3
  18.3 13.6 %collective-permute-done.3.p3 = bf16[80,4096]{1,0:T(8,128)(2,1)S(1)} collective-permute-done((bf16[80,4096]{1,0:T(8,128)(2,1)S(1)}, bf16[80,4096]{1,0:T(8,128)(2,1)S(1)}, u32[]{:S(2)}, u32[]{:S(2)}) %collective-permute-start.3) | collective-permute-done | bytes 655392 | tf_op jit(solution)/shard_map/ppermute | solution.py:270
  31.9 3.3 %collective-permute-start.4 = (bf16[80,4096]{1,0:T(8,128)(2,1)S(1)}, bf16[80,4096]{1,0:T(8,128)(2,1)S(1)}, u32[]{:S(2)}, u32[]{:S(2)}) collective-permute-start(bf16[80,4096]{1,0:T(8,128)(2,1)S(1)} %collective-permute-done.3.p3), channel_id=1, source_target_pairs={{0,16},{16,0},{1,17},{17,1},{2,18},{18,2},{3,19},{19,3},{4,20},{20... | collective-permute-start | bytes 1966088 | tf_op jit(solution)/shard_map/ppermute | solution.py:270
  35.2 0.0 collective-permute-start
  35.2 0.0 copy-done.8
  35.2 0.0 copy-start.7
  35.3 2.6 %collective-permute-done.4.p5 = bf16[80,4096]{1,0:T(8,128)(2,1)S(1)} collective-permute-done((bf16[80,4096]{1,0:T(8,128)(2,1)S(1)}, bf16[80,4096]{1,0:T(8,128)(2,1)S(1)}, u32[]{:S(2)}, u32[]{:S(2)}) %collective-permute-start.4) | collective-permute-done | bytes 655392 | tf_op jit(solution)/shard_map/ppermute | solution.py:270
  37.8 0.4 collective-permute-start.5
  38.2 0.9 fusion.5
  39.2 0.0 copy-done.7
  39.2 0.6 pad_add_fusion
  39.8 0.1 collective-permute-start.6
  39.9 0.6 add_select_fusion.3
  40.5 0.6 mul.110
  41.1 1.2 %mul.111 = s32[64]{0:T(128)} reshape(s32[4,16]{1,0:T(4,128)} %mul.110) | data formatting | bytes 512 | tf_op jit(solution)/shard_map/mul | solution.py:260
  42.3 1.3 %mul.117 = s32[4,16]{1,0:T(4,128)} broadcast(s32[4]{0:T(128)} %copy-done.7), dimensions={0} | broadcast | bytes 272 | tf_op jit(solution)/shard_map/mul | solution.py:260
  43.6 1.2 %mul.118 = s32[64]{0:T(128)} reshape(s32[4,16]{1,0:T(4,128)} %mul.117) | data formatting | bytes 512 | tf_op jit(solution)/shard_map/mul | solution.py:260
  44.8 0.0 copy-done.5
  44.8 1.6 %bitcast_multiply_fusion = (f32[64,128]{1,0:T(8,128)}, f32[64,128]{1,0:T(8,128)}) fusion(s32[16,128]{1,0:T(8,128)} %get-tuple-element.42, s32[64]{0:T(128)} %mul.118, s32[16,128]{1,0:T(8,128)} %get-tuple-element.41, s32[64]{0:T(128)} %mul.111, f32[16,128]{1,0:T(8,128)S(1)} %bitcast.46), kind=kLoop, calls=%fused_computation | loop fusion | flops 57344 | bytes 90624 | tf_op jit(solution)/shard_map/mul | solution.py:312
  46.4 0.0 collective-permute-done.6.c23_ref
  46.4 0.0 collective-permute-done.p1
  46.4 0.0 collective-permute-done.5.p4
  46.4 0.0 all-to-all-done
  46.4 0.0 copy-start.3
  46.4 0.7 copy-done.3
  47.2 0.0 copy-start.4
  47.2 0.8 copy-done.4
  48.0 0.0 copy-start.9
  48.0 0.0 copy-start.1
  48.0 0.0 copy-start.2
  48.0 6.6 %score.1 = (f32[56,512]{1,0:T(8,128)S(1)}, bf16[56,512]{1,0:T(8,128)(2,1)S(1)}, bf16[56,512]{1,0:T(8,128)(2,1)S(1)}, bf16[56,512]{1,0:T(8,128)(2,1)S(1)}, bf16[512,4096]{1,0:T(8,128)(2,1)S(1)}) custom-call(s32[1]{0:T(128)} %bitcast.1.q_ref, bf16[4608,128]{1,0:T(8,128)(2,1)S(1)} %bitcast.45, bf16[128,4096]{1,0:T(8,128)(2,1)} %p0.1, ...), custom_call_target="tpu_custom_call" | custom-call | tf_op jit(solution)/shard_map/score/pallas_call | solution.py:316
  54.6 1.3 %collective-permute-start.7 = (bf16[56,512]{1,0:T(8,128)(2,1)S(1)}, bf16[56,512]{1,0:T(8,128)(2,1)S(1)}, u32[]{:S(2)}, u32[]{:S(2)}) collective-permute-start(bf16[56,512]{1,0:T(8,128)(2,1)S(1)} %get-tuple-element.27), channel_id=1, source_target_pairs={{0,16},{16,0},{1,17},{17,1},{2,18},{18,2},{3,19},{19,3},{4,20},{20... | collective-permute-start | bytes 172040 | tf_op jit(solution)/shard_map/ppermute | solution.py:270
  55.9 0.2 collective-permute-start.8
  56.1 1.5 %collective-permute-start.9 = (bf16[56,512]{1,0:T(8,128)(2,1)S(1)}, bf16[56,512]{1,0:T(8,128)(2,1)S(1)}, u32[]{:S(2)}, u32[]{:S(2)}) collective-permute-start(bf16[56,512]{1,0:T(8,128)(2,1)S(1)} %get-tuple-element.29), channel_id=1, source_target_pairs={{0,48},{16,32},{32,16},{48,0},{1,49},{17,33},{33,17},{49,1},{2,50}... | collective-permute-start | bytes 172040 | tf_op jit(solution)/shard_map/ppermute | solution.py:279
  57.6 0.0 copy-done.9
  57.6 0.1 convert_reduce_fusion
  57.7 0.0 collective-permute-done.7.x1
  57.7 1.6 %collective-permute-done.8.x2 = bf16[56,512]{1,0:T(8,128)(2,1)S(1)} collective-permute-done((bf16[56,512]{1,0:T(8,128)(2,1)S(1)}, bf16[56,512]{1,0:T(8,128)(2,1)S(1)}, u32[]{:S(2)}, u32[]{:S(2)}) %collective-permute-start.8) | collective-permute-done | bytes 57376 | tf_op jit(solution)/shard_map/ppermute | solution.py:270
  59.4 1.4 %collective-permute-done.9.x3 = bf16[56,512]{1,0:T(8,128)(2,1)S(1)} collective-permute-done((bf16[56,512]{1,0:T(8,128)(2,1)S(1)}, bf16[56,512]{1,0:T(8,128)(2,1)S(1)}, u32[]{:S(2)}, u32[]{:S(2)}) %collective-permute-start.9) | collective-permute-done | bytes 57376 | tf_op jit(solution)/shard_map/ppermute | solution.py:279
  60.8 0.0 copy-done.1
  60.8 0.0 copy-done.2
  60.8 0.0 copy-start.10
  60.8 1.6 %classes.1 = (bf16[16,16,256]{2,1,0:T(8,128)(2,1)}, f32[1,128]{1,0:T(1,128)}) custom-call(s32[1]{0:T(128)} %bitcast.1.q_ref, f32[56,512]{1,0:T(8,128)S(1)} %get-tuple-element.26.x0, bf16[56,512]{1,0:T(8,128)(2,1)S(1)} %collective-permute-done.7.x1, bf16[56,512]{1,0:T(8,128)(2,1)S(1)} %collective-permute-done.8.x2, ...), custom_call_target="tpu_custom_call" | custom-call | tf_op jit(solution)/shard_map/classes/pallas_call | solution.py:341
  62.4 6.7 %all-to-all-start.1 = ((bf16[16,16,256]{2,1,0:T(8,128)(2,1)}), bf16[16,16,256]{2,1,0:T(8,128)(2,1)S(1)}, u32[]{:S(2)}, u32[]{:S(2)}) async-start(bf16[16,16,256]{2,1,0:T(8,128)(2,1)} %get-tuple-element.31), calls=%async_computation.1 | async-start | bytes 262144 | tf_op jit(solution)/shard_map/all_to_all | solution.py:356
  69.1 0.0 copy-done.10
  69.1 0.1 dynamic_slice.3
  69.2 8.7 %all-to-all-done.1.y_ref = bf16[16,16,256]{2,1,0:T(8,128)(2,1)S(1)} async-done(((bf16[16,16,256]{2,1,0:T(8,128)(2,1)}), bf16[16,16,256]{2,1,0:T(8,128)(2,1)S(1)}, u32[]{:S(2)}, u32[]{:S(2)}) %all-to-all-start.1) | async-done | bytes 131104 | tf_op jit(solution)/shard_map/all_to_all | solution.py:356
  77.9 0.8 place.1
  78.8 15.4 %all_to_all.15.z_ref = bf16[16,8,384]{2,1,0:T(8,128)(2,1)S(1)} all-to-all(bf16[16,8,384]{2,1,0:T(8,128)(2,1)} %place.1), channel_id=1, replica_groups=mesh['xh'=2,'yh'=2,'yl'=2,'core'=2,'z'=8,'xl'=2] {'xh','yh','yl','core'}, dimensions={0} | all-to-all | bytes 196608 | tf_op jit(solution)/shard_map/all_to_all | solution.py:374
  94.2 0.8 means.1
  (4 shorter events, 0.0 us)
Async XLA Ops:
  1.7 16.4 %collective-permute-start.1 = (bf16[48,4096]{1,0:T(8,128)(2,1)S(1)}, bf16[48,4096]{1,0:T(8,128)(2,1)}, u32[]{:S(2)}, u32[]{:S(2)}) collective-permute-start(bf16[48,4096]{1,0:T(8,128)(2,1)S(1)} %slice.13), channel_id=1, source_target_pairs={{0,32},{32,0},{1,33},{33,1},{2,34},{34,2},{3,35},{35,3},{4,36},{36... | collective-permute-start | bytes 1179656 | tf_op jit(solution)/shard_map/ppermute | solution.py:270
  3.9 1.0 %copy-start = (bf16[3,12,4096]{2,1,0:T(8,128)(2,1)S(1)}, bf16[3,12,4096]{2,1,0:T(8,128)(2,1)}, u32[]{:S(2)}) copy-start(bf16[3,12,4096]{2,1,0:T(8,128)(2,1)} %refs_ref.1) | copy-start | bytes 884740
  6.1 9.4 %copy-start.6 = (s32[128,8]{0,1:T(8,128)S(1)}, s32[128,8]{0,1:T(8,128)}, u32[]{:S(2)}) copy-start(s32[128,8]{0,1:T(8,128)} %param.10) | copy-start | bytes 12292
  6.1 40.3 %all-to-all-start = ((bf16[16,288,128]{2,1,0:T(8,128)(2,1)}), bf16[16,288,128]{2,1,0:T(8,128)(2,1)S(1)}, u32[]{:S(2)}, u32[]{:S(2)}) async-start(bf16[16,288,128]{2,1,0:T(8,128)(2,1)} %pack.1), calls=%async_computation | async-start | bytes 2359296 | tf_op jit(solution)/shard_map/all_to_all | solution.py:300
  15.5 19.7 %copy-start.8 = (s32[4,2]{0,1:T(2,128)S(1)}, s32[4,2]{0,1:T(2,128)}, u32[]{:S(2)}) copy-start(s32[4,2]{0,1:T(2,128)} %param.9) | copy-start | bytes 100
  15.5 29.3 %copy-start.5 = (f32[2048]{0:T(1024)S(1)}, f32[2048]{0:T(1024)}, u32[]{:S(2)}) copy-start(f32[2048]{0:T(1024)} %param.8) | copy-start | bytes 24580
  15.5 2.5 %collective-permute-start.2 = (s32[8,128]{1,0:T(8,128)S(1)}, s32[8,128]{1,0:T(8,128)S(1)}, u32[]{:S(2)}, u32[]{:S(2)}) collective-permute-start(s32[8,128]{1,0:T(8,128)S(1)} %bitcast.48), channel_id=1, source_target_pairs={{0,32},{32,0},{1,33},{33,1},{2,34},{34,2},{3,35},{35,3},{4,36},{36... | collective-permute-start | bytes 12296 | tf_op jit(solution)/shard_map/ppermute | solution.py:270
  18.1 13.8 %collective-permute-start.3 = (bf16[80,4096]{1,0:T(8,128)(2,1)S(1)}, bf16[80,4096]{1,0:T(8,128)(2,1)S(1)}, u32[]{:S(2)}, u32[]{:S(2)}) collective-permute-start(bf16[80,4096]{1,0:T(8,128)(2,1)S(1)} %slice.12), channel_id=1, source_target_pairs={{0,32},{32,0},{1,33},{33,1},{2,34},{34,2},{3,35},{35,3},{4,36},{36... | collective-permute-start | bytes 1966088 | tf_op jit(solution)/shard_map/ppermute | solution.py:270
  31.9 5.9 %collective-permute-start.4 = (bf16[80,4096]{1,0:T(8,128)(2,1)S(1)}, bf16[80,4096]{1,0:T(8,128)(2,1)S(1)}, u32[]{:S(2)}, u32[]{:S(2)}) collective-permute-start(bf16[80,4096]{1,0:T(8,128)(2,1)S(1)} %collective-permute-done.3.p3), channel_id=1, source_target_pairs={{0,16},{16,0},{1,17},{17,1},{2,18},{18,2},{3,19},{19,3},{4,20},{20... | collective-permute-start | bytes 1966088 | tf_op jit(solution)/shard_map/ppermute | solution.py:270
  35.2 11.2 %collective-permute-start = (bf16[128,4096]{1,0:T(8,128)(2,1)}, bf16[128,4096]{1,0:T(8,128)(2,1)S(1)}, u32[]{:S(2)}, u32[]{:S(2)}) collective-permute-start(bf16[128,4096]{1,0:T(8,128)(2,1)} %p0.1), channel_id=1, source_target_pairs={{0,16},{16,0},{1,17},{17,1},{2,18},{18,2},{3,19},{19,3},{4,20},{20... | collective-permute-start | bytes 3145736 | tf_op jit(solution)/shard_map/ppermute | solution.py:270
  35.2 3.9 %copy-start.7 = (s32[4]{0:T(128)}, s32[4]{0:T(128)S(1)}, u32[]{:S(2)}) copy-start(s32[4]{0:T(128)S(1)} %get-tuple-element.40) | copy-start | bytes 52
  37.8 8.6 %collective-permute-start.5 = (bf16[48,4096]{1,0:T(8,128)(2,1)}, bf16[48,4096]{1,0:T(8,128)(2,1)}, u32[]{:S(2)}, u32[]{:S(2)}) collective-permute-start(bf16[48,4096]{1,0:T(8,128)(2,1)} %collective-permute-done.1.p2), channel_id=1, source_target_pairs={{0,16},{16,0},{1,17},{17,1},{2,18},{18,2},{3,19},{19,3},{4,20},{20... | collective-permute-start | bytes 1179656 | tf_op jit(solution)/shard_map/ppermute | solution.py:270
  39.8 6.7 %collective-permute-start.6 = (s32[2,8,128]{2,1,0:T(8,128)}, s32[2,8,128]{2,1,0:T(8,128)}, u32[]{:S(2)}, u32[]{:S(2)}) collective-permute-start(s32[2,8,128]{2,1,0:T(8,128)} %pad_add_fusion), channel_id=1, source_target_pairs={{0,16},{16,0},{1,17},{17,1},{2,18},{18,2},{3,19},{19,3},{4,20},{20... | collective-permute-start | bytes 24584 | tf_op jit(solution)/shard_map/ppermute | solution.py:270
  46.4 0.8 copy-start.3
  47.2 0.8 copy-start.4
  48.0 9.7 %copy-start.9 = (s32[48]{0:T(128)S(1)}, s32[48]{0:T(128)}, u32[]{:S(2)}) copy-start(s32[48]{0:T(128)} %param.11) | copy-start | bytes 580
  48.0 12.8 %copy-start.1 = (f32[4,2048]{1,0:T(4,128)S(1)}, f32[4,2048]{1,0:T(4,128)}, u32[]{:S(2)}) copy-start(f32[4,2048]{1,0:T(4,128)} %get-tuple-element.37.sin_ref) | copy-start | bytes 98308
  48.0 12.8 %copy-start.2 = (f32[4,2048]{1,0:T(4,128)S(1)}, f32[4,2048]{1,0:T(4,128)}, u32[]{:S(2)}) copy-start(f32[4,2048]{1,0:T(4,128)} %get-tuple-element.38.cos_ref) | copy-start | bytes 98308
  54.6 3.1 %collective-permute-start.7 = (bf16[56,512]{1,0:T(8,128)(2,1)S(1)}, bf16[56,512]{1,0:T(8,128)(2,1)S(1)}, u32[]{:S(2)}, u32[]{:S(2)}) collective-permute-start(bf16[56,512]{1,0:T(8,128)(2,1)S(1)} %get-tuple-element.27), channel_id=1, source_target_pairs={{0,16},{16,0},{1,17},{17,1},{2,18},{18,2},{3,19},{19,3},{4,20},{20... | collective-permute-start | bytes 172040 | tf_op jit(solution)/shard_map/ppermute | solution.py:270
  55.9 3.5 %collective-permute-start.8 = (bf16[56,512]{1,0:T(8,128)(2,1)S(1)}, bf16[56,512]{1,0:T(8,128)(2,1)S(1)}, u32[]{:S(2)}, u32[]{:S(2)}) collective-permute-start(bf16[56,512]{1,0:T(8,128)(2,1)S(1)} %get-tuple-element.28), channel_id=1, source_target_pairs={{0,32},{32,0},{1,33},{33,1},{2,34},{34,2},{3,35},{35,3},{4,36},{36... | collective-permute-start | bytes 172040 | tf_op jit(solution)/shard_map/ppermute | solution.py:270
  56.1 4.7 %collective-permute-start.9 = (bf16[56,512]{1,0:T(8,128)(2,1)S(1)}, bf16[56,512]{1,0:T(8,128)(2,1)S(1)}, u32[]{:S(2)}, u32[]{:S(2)}) collective-permute-start(bf16[56,512]{1,0:T(8,128)(2,1)S(1)} %get-tuple-element.29), channel_id=1, source_target_pairs={{0,48},{16,32},{32,16},{48,0},{1,49},{17,33},{33,17},{49,1},{2,50}... | collective-permute-start | bytes 172040 | tf_op jit(solution)/shard_map/ppermute | solution.py:279
  60.8 8.3 %copy-start.10 = (s32[48]{0:T(128)S(1)}, s32[48]{0:T(128)}, u32[]{:S(2)}) copy-start(s32[48]{0:T(128)} %param.11) | copy-start | bytes 580
  62.4 15.5 %all-to-all-start.1 = ((bf16[16,16,256]{2,1,0:T(8,128)(2,1)}), bf16[16,16,256]{2,1,0:T(8,128)(2,1)S(1)}, u32[]{:S(2)}, u32[]{:S(2)}) async-start(bf16[16,16,256]{2,1,0:T(8,128)(2,1)} %get-tuple-element.31), calls=%async_computation.1 | async-start | bytes 262144 | tf_op jit(solution)/shard_map/all_to_all | solution.py:356

commit v6 on v5

--- a/solution.py
+++ b/solution.py
@@ -25,7 +25,7 @@
 ROT = 12
 NSHIFT = 4
 ROWS = 128
-FIRST = 48
+FIRST = 64
 NPOOL = 4
 QROT = ROT // NPOOL
 QCLS = CLASSES // NPOOL
@@ -59,6 +59,25 @@
     packed = rows[...].astype(BF16)
     for d in range(NBLK):
         out_ref[d] = packed
+
+
+def tables_kernel(off_ref, w_ref, c0_ref, c1_ref, cos_ref, sin_ref, wc_ref, ws_ref, both_ref):
+    row = lax.broadcasted_iota(jnp.int32, (16, 128), 0)
+    lane = lax.broadcasted_iota(jnp.int32, (16, 128), 1)
+    column = lane % KCOL
+    rowpos = row * (128 // KCOL) + lane // KCOL - KROW // 2
+    weight = w_ref[...]
+    for s in range(NSHIFT):
+        turns = (off_ref[s, 0] * column + off_ref[s, 1] * rowpos).astype(F32)
+        angle = turns * (2.0 * math.pi / BOX)
+        cosine, sine = jnp.cos(angle), jnp.sin(angle)
+        at = slice(s * 16, (s + 1) * 16)
+        cos_ref[at, :] = cosine
+        sin_ref[at, :] = sine
+        wc_ref[at, :] = weight * cosine
+        ws_ref[at, :] = weight * sine
+    both_ref[0] = c0_ref[...]
+    both_ref[1] = c1_ref[...]
 
 
 def pool_copies(q, parts, pool, sem):
@@ -210,8 +229,9 @@
         sum_re = jnp.zeros((16, COLS), F32)
         sum_im = jnp.zeros((16, COLS), F32)
         for s in range(NSHIFT):
-            c = cos_ref[s : s + 1, cols]
-            z = sin_ref[s : s + 1, cols]
+            at = s * 16 + 2 * b
+            c = jnp.concatenate([cos_ref[at : at + 1, :], cos_ref[at + 1 : at + 2, :]], axis=1)
+            z = jnp.concatenate([sin_ref[at : at + 1, :], sin_ref[at + 1 : at + 2, :]], axis=1)
             re = g_re[s * 16 : (s + 1) * 16]
             im = g_im[s * 16 : (s + 1) * 16]
             sum_re = sum_re + (c * re + z * im)
@@ -253,15 +273,6 @@
     mass_ref[...] = jnp.sum(jnp.where(row == lane, mass, 0.0), axis=0)[0:SLOTS]
 
 
-def phase_tables(offsets):
-    index = jnp.arange(KROW * KCOL, dtype=jnp.int32)
-    column = index % KCOL
-    rowpos = index // KCOL - KROW // 2
-    turns = (offsets[:, 0:1] * column[None, :] + offsets[:, 1:2] * rowpos[None, :]).astype(F32)
-    angle = turns * (2.0 * math.pi / BOX)
-    return (jnp.cos(angle), jnp.sin(angle))
-
-
 def in_hbm(x):
     return pltpu.with_memory_space_constraint(x, pltpu.HBM)
 
@@ -285,8 +296,8 @@
     q = pool_index.reshape(1)
 
     cand = candidates.T
+    weight = noise_weight.reshape(16, 128)
     far0 = swap(particles[:FIRST], "yl")
-    cand_far = swap(cand, "yl")
     packed = pl.pallas_call(
         pack_kernel,
         out_shape=jax.ShapeDtypeStruct((NBLK, LOCAL * QROT * 32, 128), BF16),
@@ -297,20 +308,29 @@
         name="pack",
     )(q, references)
     packed, whole = lax.optimization_barrier((packed, particles))
+    rest = whole[FIRST:]
     gathered = lax.all_to_all(packed, BLK, 0, 0, tiled=True)
-    rest, far0, cand_far = lax.optimization_barrier((whole[FIRST:], far0, cand_far))
+    rest, far0 = lax.optimization_barrier((rest, far0))
     far1 = swap(rest, "yl")
     near = swap(particles, "core")
+    cand, far0 = lax.optimization_barrier((cand, far0))
+    cand_far = swap(cand, "yl")
+    flat = jax.ShapeDtypeStruct((NSHIFT * 16, 128), F32)
+    cosine, sine, wc, ws, both = pl.pallas_call(
+        tables_kernel,
+        out_shape=(flat, flat, flat, flat, jax.ShapeDtypeStruct((2, 8, ROWS), jnp.int32)),
+        in_specs=[SMEM_SPEC] + [VMEM_SPEC] * 3,
+        out_specs=(VMEM_SPEC,) * 5,
+        compiler_params=params(4),
+        cost_estimate=pl.CostEstimate(flops=10 * 10**9, bytes_accessed=30 * 10**6, transcendentals=0),
+        name="tables",
+    )(offsets, weight, cand, cand_far)
+    far1, wc, both = lax.optimization_barrier((far1, wc, both))
     near1 = swap(far1, "core")
+    cand_near = swap(both, "core")
     far0, near1 = lax.optimization_barrier((far0, near1))
     near0 = swap(far0, "core")
-    cand_near = swap(jnp.stack([cand, cand_far]), "core")
-    parts = (in_hbm(particles), near, far0, far1, near0, near1)
-
-    cosine, sine = phase_tables(offsets)
-    wc = (noise_weight * cosine).reshape(NSHIFT * 16, 128)
-    ws = (noise_weight * sine).reshape(NSHIFT * 16, 128)
-    weight = noise_weight.reshape(16, 128)
+    parts = (in_hbm(particles), near, far0, far1, near0, in_hbm(near1))
 
     table_rows = NSHIFT * QROT * CLASSES
     *terms, pool = pl.pallas_call(

time: 95.7 us -> 89.3 us (0.933)
  local copies, waits for them, and re-layouts: 9.11 us -> 3.2 us
  other arithmetic: 3.82 us -> 0.1 us
  waiting for transfers between devices: 29.2 us -> 31.4 us
  starting transfers between devices: 25.6 us -> 26.8 us
    all_to_all x1, waiting for transfers between devices: 0.01 us -> 5.71 us  [on_device(): gathered = lax.all_to_all(packed, BLK, 0, 0, tiled=True)]
    ppermute x9, starting transfers between devices: 8.02 us -> 12.4 us  [swap(): return lax.ppermute(x, axis, [(0, 1), (1, 0)])]
    mul x5 -> x0, local copies, waits for them, and re-layouts: 4.32 us -> none  [the longest x2 2.49 us: phase_tables(): offsets[:, 1:2] * rowpos[None, :]]
    ppermute x9, waiting for transfers between devices: 19 us -> 15.5 us  [swap(): return lax.ppermute(x, axis, [(0, 1), (1, 0)])]
    all_to_all x1, starting transfers between devices: 6.69 us -> 3.51 us  [on_device(): sums = lax.all_to_all(sums, BLK, 0, 0, tiled=True)]
    unnamed x22 -> x13, local copies, waits for them, and re-layouts: 2.54 us -> 0.91 us
    mul x1 -> x0, other arithmetic: 1.58 us -> none  [on_device(): ws = (noise_weight * sine).reshape(NSHIFT * 16, 128)]
  transfers between devices with their start and end apart: 12 -> 12, of which waited for: 6 -> 9; matrix products, arithmetic and copies ran while one was open for 10% -> 2% of each run, Pallas kernels for 1% -> 2%
where the time goes in v6:
time: 89.3 us; the launch traced here: 88.8 us
  waiting for transfers between devices  31.4 us (35%)
  starting transfers between devices  26.8 us (30%)
  blocking collectives  15.5 us (17%)
  Pallas kernels  11.1 us (12%)
  local copies, waits for them, and re-layouts  3.2 us (4%)
    ppermute x9, waiting for transfers between devices, swap(): return lax.ppermute(x, axis, [(0, 1), (1, 0)])  15.5 us
    all_to_all x1, blocking collectives, on_device(): placed = lax.all_to_all(placed, DOM, 0, 0, tiled=True)  15.5 us
    ppermute x9, starting transfers between devices, swap(): return lax.ppermute(x, axis, [(0, 1), (1, 0)])  12.4 us
    all_to_all x1, starting transfers between devices, on_device(): gathered = lax.all_to_all(packed, BLK, 0, 0, tiled=True)  9.35 us
    all_to_all x1, waiting for transfers between devices, on_device(): sums = lax.all_to_all(sums, BLK, 0, 0, tiled=True)  8.81 us
    pallas_call x1, Pallas kernels, on_device(): pl.pallas_call(score_kernel, out_shape=[jax.ShapeDtypeStruct((56, NPOOL *...  5.91 us
    all_to_all x1, waiting for transfers between devices, on_device(): gathered = lax.all_to_all(packed, BLK, 0, 0, tiled=True)  5.71 us
    all_to_all x1, starting transfers between devices, on_device(): sums = lax.all_to_all(sums, BLK, 0, 0, tiled=True)  3.51 us
  transfers between devices with their start and end apart: 12, of which 9 were waited for; matrix products, arithmetic and copies ran while one was open for 2% of the time, Pallas kernels for 2%

profile of v6, /device:TPU:1, one launch (start us, length us, event | category | flops | bytes accessed | tf_op | source)
XLA Modules:
  0.0 88.8 jit_solution(7020341675976796642)
XLA Ops:
  0.6 0.0 copy-start
  0.6 1.1 %slice.7 = bf16[64,4096]{1,0:T(8,128)(2,1)S(1)} slice(bf16[128,4096]{1,0:T(8,128)(2,1)} %p0.1), slice={[0:64], [0:4096]} | slice | bytes 1048576 | tf_op jit(solution)/shard_map/slice | solution.py:300
  1.8 2.2 %collective-permute-start.1 = (bf16[64,4096]{1,0:T(8,128)(2,1)S(1)}, bf16[64,4096]{1,0:T(8,128)(2,1)S(1)}, u32[]{:S(2)}, u32[]{:S(2)}) collective-permute-start(bf16[64,4096]{1,0:T(8,128)(2,1)S(1)} %slice.7), channel_id=1, source_target_pairs={{0,32},{32,0},{1,33},{33,1},{2,34},{34,2},{3,35},{35,3},{4,36},{36... | collective-permute-start | bytes 1572872 | tf_op jit(solution)/shard_map/ppermute | solution.py:281
  4.0 0.0 copy-done
  4.0 1.3 %pack.1 = bf16[16,288,128]{2,1,0:T(8,128)(2,1)} custom-call(s32[1]{0:T(128)} %bitcast.1.q_ref, bf16[3,12,4096]{2,1,0:T(8,128)(2,1)S(1)} %copy-done), custom_call_target="tpu_custom_call" | custom-call | tf_op jit(solution)/shard_map/pack/pallas_call | solution.py:301
  5.3 0.0 copy-start.2
  5.3 0.0 copy-start.4
  5.3 0.0 copy-start.1
  5.3 9.3 %all-to-all-start = ((bf16[16,288,128]{2,1,0:T(8,128)(2,1)}), bf16[16,288,128]{2,1,0:T(8,128)(2,1)S(1)}, u32[]{:S(2)}, u32[]{:S(2)}) async-start(bf16[16,288,128]{2,1,0:T(8,128)(2,1)} %pack.1), calls=%async_computation | async-start | bytes 2359296 | tf_op jit(solution)/shard_map/all_to_all | solution.py:312
  14.6 1.1 %slice.6 = bf16[64,4096]{1,0:T(8,128)(2,1)S(1)} slice(bf16[128,4096]{1,0:T(8,128)(2,1)} %p0.1), slice={[64:128], [0:4096]} | slice | bytes 1048576 | tf_op jit(solution)/shard_map/slice | solution.py:311
  15.7 0.0 collective-permute-done.1.p2
  15.7 0.0 copy-done.2
  15.7 0.9 collective-permute-start.3
  16.6 0.0 copy-done.4
  16.6 0.1 copy.10.off_ref
  16.7 0.7 collective-permute-start.2
  17.4 0.9 %collective-permute-done.3.c1_ref = s32[8,128]{1,0:T(8,128)S(1)} collective-permute-done((s32[8,128]{1,0:T(8,128)S(1)}, s32[8,128]{1,0:T(8,128)S(1)}, u32[]{:S(2)}, u32[]{:S(2)}) %collective-permute-start.3) | collective-permute-done | bytes 4128 | tf_op jit(solution)/shard_map/ppermute | solution.py:281
  18.3 0.0 copy-done.1
  18.3 0.7 tables.1
  19.0 9.2 %collective-permute-done.2.p3 = bf16[64,4096]{1,0:T(8,128)(2,1)S(1)} collective-permute-done((bf16[64,4096]{1,0:T(8,128)(2,1)S(1)}, bf16[64,4096]{1,0:T(8,128)(2,1)S(1)}, u32[]{:S(2)}, u32[]{:S(2)}) %collective-permute-start.2) | collective-permute-done | bytes 524320 | tf_op jit(solution)/shard_map/ppermute | solution.py:281
  28.2 2.9 %collective-permute-start.4 = (bf16[64,4096]{1,0:T(8,128)(2,1)S(1)}, bf16[64,4096]{1,0:T(8,128)(2,1)S(1)}, u32[]{:S(2)}, u32[]{:S(2)}) collective-permute-start(bf16[64,4096]{1,0:T(8,128)(2,1)S(1)} %collective-permute-done.2.p3), channel_id=1, source_target_pairs={{0,16},{16,0},{1,17},{17,1},{2,18},{18,2},{3,19},{19,3},{4,20},{20... | collective-permute-start | bytes 1572872 | tf_op jit(solution)/shard_map/ppermute | solution.py:281
  31.1 0.0 collective-permute-start
  31.1 2.2 %collective-permute-done.4.p5 = bf16[64,4096]{1,0:T(8,128)(2,1)S(1)} collective-permute-done((bf16[64,4096]{1,0:T(8,128)(2,1)S(1)}, bf16[64,4096]{1,0:T(8,128)(2,1)S(1)}, u32[]{:S(2)}, u32[]{:S(2)}) %collective-permute-start.4) | collective-permute-done | bytes 524320 | tf_op jit(solution)/shard_map/ppermute | solution.py:281
  33.3 0.0 copy-start.3
  33.3 0.8 copy-done.3
  34.1 0.4 collective-permute-start.5
  34.5 0.1 collective-permute-start.6
  34.6 0.0 collective-permute-done.p1
  34.6 1.4 %collective-permute-done.6.c23_ref = s32[2,8,128]{2,1,0:T(8,128)S(1)} collective-permute-done((s32[2,8,128]{2,1,0:T(8,128)S(1)}, s32[2,8,128]{2,1,0:T(8,128)S(1)}, u32[]{:S(2)}, u32[]{:S(2)}) %collective-permute-start.6) | collective-permute-done | bytes 8224 | tf_op jit(solution)/shard_map/ppermute | solution.py:281
  36.0 0.1 collective-permute-done.5.p4
  36.2 5.7 %all-to-all-done = bf16[16,288,128]{2,1,0:T(8,128)(2,1)S(1)} async-done(((bf16[16,288,128]{2,1,0:T(8,128)(2,1)}), bf16[16,288,128]{2,1,0:T(8,128)(2,1)S(1)}, u32[]{:S(2)}, u32[]{:S(2)}) %all-to-all-start) | async-done | bytes 1179680 | tf_op jit(solution)/shard_map/all_to_all | solution.py:312
  41.9 0.0 copy-start.5
  41.9 5.9 %score.1 = (f32[56,512]{1,0:T(8,128)S(1)}, bf16[56,512]{1,0:T(8,128)(2,1)S(1)}, bf16[56,512]{1,0:T(8,128)(2,1)S(1)}, bf16[56,512]{1,0:T(8,128)(2,1)S(1)}, bf16[512,4096]{1,0:T(8,128)(2,1)S(1)}) custom-call(s32[1]{0:T(128)} %bitcast.1.q_ref, bf16[4608,128]{1,0:T(8,128)(2,1)S(1)} %bitcast.7, bf16[128,4096]{1,0:T(8,128)(2,1)} %p0.1, ...), custom_call_target="tpu_custom_call" | custom-call | tf_op jit(solution)/shard_map/score/pallas_call | solution.py:336
  47.8 5.0 %collective-permute-start.7 = (bf16[56,512]{1,0:T(8,128)(2,1)S(1)}, bf16[56,512]{1,0:T(8,128)(2,1)S(1)}, u32[]{:S(2)}, u32[]{:S(2)}) collective-permute-start(bf16[56,512]{1,0:T(8,128)(2,1)S(1)} %get-tuple-element.43), channel_id=1, source_target_pairs={{0,16},{16,0},{1,17},{17,1},{2,18},{18,2},{3,19},{19,3},{4,20},{20... | collective-permute-start | bytes 172040 | tf_op jit(solution)/shard_map/ppermute | solution.py:281
  52.8 0.2 collective-permute-start.8
  53.0 1.5 %collective-permute-start.9 = (bf16[56,512]{1,0:T(8,128)(2,1)S(1)}, bf16[56,512]{1,0:T(8,128)(2,1)S(1)}, u32[]{:S(2)}, u32[]{:S(2)}) collective-permute-start(bf16[56,512]{1,0:T(8,128)(2,1)S(1)} %get-tuple-element.45), channel_id=1, source_target_pairs={{0,48},{16,32},{32,16},{48,0},{1,49},{17,33},{33,17},{49,1},{2,50}... | collective-permute-start | bytes 172040 | tf_op jit(solution)/shard_map/ppermute | solution.py:290
  54.5 0.0 copy-done.5
  54.5 0.1 convert_reduce_fusion
  54.6 0.0 collective-permute-done.7.x1
  54.6 1.6 %collective-permute-done.8.x2 = bf16[56,512]{1,0:T(8,128)(2,1)S(1)} collective-permute-done((bf16[56,512]{1,0:T(8,128)(2,1)S(1)}, bf16[56,512]{1,0:T(8,128)(2,1)S(1)}, u32[]{:S(2)}, u32[]{:S(2)}) %collective-permute-start.8) | collective-permute-done | bytes 57376 | tf_op jit(solution)/shard_map/ppermute | solution.py:281
  56.3 1.4 %collective-permute-done.9.x3 = bf16[56,512]{1,0:T(8,128)(2,1)S(1)} collective-permute-done((bf16[56,512]{1,0:T(8,128)(2,1)S(1)}, bf16[56,512]{1,0:T(8,128)(2,1)S(1)}, u32[]{:S(2)}, u32[]{:S(2)}) %collective-permute-start.9) | collective-permute-done | bytes 57376 | tf_op jit(solution)/shard_map/ppermute | solution.py:290
  57.7 1.6 %classes.1 = (bf16[16,16,256]{2,1,0:T(8,128)(2,1)}, f32[1,128]{1,0:T(1,128)}) custom-call(s32[1]{0:T(128)} %bitcast.1.q_ref, f32[56,512]{1,0:T(8,128)S(1)} %get-tuple-element.42.x0, bf16[56,512]{1,0:T(8,128)(2,1)S(1)} %collective-permute-done.7.x1, bf16[56,512]{1,0:T(8,128)(2,1)S(1)} %collective-permute-done.8.x2, ...), custom_call_target="tpu_custom_call" | custom-call | tf_op jit(solution)/shard_map/classes/pallas_call | solution.py:361
  59.3 3.5 %all-to-all-start.1 = ((bf16[16,16,256]{2,1,0:T(8,128)(2,1)}), bf16[16,16,256]{2,1,0:T(8,128)(2,1)S(1)}, u32[]{:S(2)}, u32[]{:S(2)}) async-start(bf16[16,16,256]{2,1,0:T(8,128)(2,1)} %get-tuple-element.49), calls=%async_computation.1 | async-start | bytes 262144 | tf_op jit(solution)/shard_map/all_to_all | solution.py:376
  62.9 0.1 dynamic_slice.3
  62.9 8.8 %all-to-all-done.1.y_ref = bf16[16,16,256]{2,1,0:T(8,128)(2,1)S(1)} async-done(((bf16[16,16,256]{2,1,0:T(8,128)(2,1)}), bf16[16,16,256]{2,1,0:T(8,128)(2,1)S(1)}, u32[]{:S(2)}, u32[]{:S(2)}) %all-to-all-start.1) | async-done | bytes 131104 | tf_op jit(solution)/shard_map/all_to_all | solution.py:376
  71.8 0.8 place.1
  72.6 15.5 %all_to_all.15.z_ref = bf16[16,8,384]{2,1,0:T(8,128)(2,1)S(1)} all-to-all(bf16[16,8,384]{2,1,0:T(8,128)(2,1)} %place.1), channel_id=1, replica_groups=mesh['xh'=2,'yh'=2,'yl'=2,'core'=2,'z'=8,'xl'=2] {'xh','yh','yl','core'}, dimensions={0} | all-to-all | bytes 196608 | tf_op jit(solution)/shard_map/all_to_all | solution.py:394
  88.0 0.8 means.1
  (2 shorter events, 0.0 us)
Async XLA Ops:
  0.6 3.4 %copy-start = (bf16[3,12,4096]{2,1,0:T(8,128)(2,1)S(1)}, bf16[3,12,4096]{2,1,0:T(8,128)(2,1)}, u32[]{:S(2)}) copy-start(bf16[3,12,4096]{2,1,0:T(8,128)(2,1)} %refs_ref.1) | copy-start | bytes 884740
  1.8 13.9 %collective-permute-start.1 = (bf16[64,4096]{1,0:T(8,128)(2,1)S(1)}, bf16[64,4096]{1,0:T(8,128)(2,1)S(1)}, u32[]{:S(2)}, u32[]{:S(2)}) collective-permute-start(bf16[64,4096]{1,0:T(8,128)(2,1)S(1)} %slice.7), channel_id=1, source_target_pairs={{0,32},{32,0},{1,33},{33,1},{2,34},{34,2},{3,35},{35,3},{4,36},{36... | collective-permute-start | bytes 1572872 | tf_op jit(solution)/shard_map/ppermute | solution.py:281
  5.3 10.5 %copy-start.2 = (s32[128,8]{0,1:T(8,128)S(1)}, s32[128,8]{0,1:T(8,128)}, u32[]{:S(2)}) copy-start(s32[128,8]{0,1:T(8,128)} %param.10) | copy-start | bytes 12292
  5.3 11.3 %copy-start.4 = (s32[4,2]{0,1:T(2,128)S(1)}, s32[4,2]{0,1:T(2,128)}, u32[]{:S(2)}) copy-start(s32[4,2]{0,1:T(2,128)} %param.9) | copy-start | bytes 100
  5.3 13.0 %copy-start.1 = (f32[2048]{0:T(1024)S(1)}, f32[2048]{0:T(1024)}, u32[]{:S(2)}) copy-start(f32[2048]{0:T(1024)} %param.8) | copy-start | bytes 24580
  5.3 36.6 %all-to-all-start = ((bf16[16,288,128]{2,1,0:T(8,128)(2,1)}), bf16[16,288,128]{2,1,0:T(8,128)(2,1)S(1)}, u32[]{:S(2)}, u32[]{:S(2)}) async-start(bf16[16,288,128]{2,1,0:T(8,128)(2,1)} %pack.1), calls=%async_computation | async-start | bytes 2359296 | tf_op jit(solution)/shard_map/all_to_all | solution.py:312
  15.7 2.5 %collective-permute-start.3 = (s32[8,128]{1,0:T(8,128)S(1)}, s32[8,128]{1,0:T(8,128)S(1)}, u32[]{:S(2)}, u32[]{:S(2)}) collective-permute-start(s32[8,128]{1,0:T(8,128)S(1)} %bitcast.10), channel_id=1, source_target_pairs={{0,32},{32,0},{1,33},{33,1},{2,34},{34,2},{3,35},{35,3},{4,36},{36... | collective-permute-start | bytes 12296 | tf_op jit(solution)/shard_map/ppermute | solution.py:281
  16.7 11.5 %collective-permute-start.2 = (bf16[64,4096]{1,0:T(8,128)(2,1)S(1)}, bf16[64,4096]{1,0:T(8,128)(2,1)S(1)}, u32[]{:S(2)}, u32[]{:S(2)}) collective-permute-start(bf16[64,4096]{1,0:T(8,128)(2,1)S(1)} %slice.6), channel_id=1, source_target_pairs={{0,32},{32,0},{1,33},{33,1},{2,34},{34,2},{3,35},{35,3},{4,36},{36... | collective-permute-start | bytes 1572872 | tf_op jit(solution)/shard_map/ppermute | solution.py:281
  28.2 5.1 %collective-permute-start.4 = (bf16[64,4096]{1,0:T(8,128)(2,1)S(1)}, bf16[64,4096]{1,0:T(8,128)(2,1)S(1)}, u32[]{:S(2)}, u32[]{:S(2)}) collective-permute-start(bf16[64,4096]{1,0:T(8,128)(2,1)S(1)} %collective-permute-done.2.p3), channel_id=1, source_target_pairs={{0,16},{16,0},{1,17},{17,1},{2,18},{18,2},{3,19},{19,3},{4,20},{20... | collective-permute-start | bytes 1572872 | tf_op jit(solution)/shard_map/ppermute | solution.py:281
  31.1 3.6 %collective-permute-start = (bf16[128,4096]{1,0:T(8,128)(2,1)}, bf16[128,4096]{1,0:T(8,128)(2,1)S(1)}, u32[]{:S(2)}, u32[]{:S(2)}) collective-permute-start(bf16[128,4096]{1,0:T(8,128)(2,1)} %p0.1), channel_id=1, source_target_pairs={{0,16},{16,0},{1,17},{17,1},{2,18},{18,2},{3,19},{19,3},{4,20},{20... | collective-permute-start | bytes 3145736 | tf_op jit(solution)/shard_map/ppermute | solution.py:281
  33.3 0.8 copy-start.3
  34.1 2.0 %collective-permute-start.5 = (bf16[64,4096]{1,0:T(8,128)(2,1)S(1)}, bf16[64,4096]{1,0:T(8,128)(2,1)}, u32[]{:S(2)}, u32[]{:S(2)}) collective-permute-start(bf16[64,4096]{1,0:T(8,128)(2,1)S(1)} %collective-permute-done.1.p2), channel_id=1, source_target_pairs={{0,16},{16,0},{1,17},{17,1},{2,18},{18,2},{3,19},{19,3},{4,20},{20... | collective-permute-start | bytes 1572872 | tf_op jit(solution)/shard_map/ppermute | solution.py:281
  34.5 1.5 %collective-permute-start.6 = (s32[2,8,128]{2,1,0:T(8,128)S(1)}, s32[2,8,128]{2,1,0:T(8,128)S(1)}, u32[]{:S(2)}, u32[]{:S(2)}) collective-permute-start(s32[2,8,128]{2,1,0:T(8,128)S(1)} %get-tuple-element.41), channel_id=1, source_target_pairs={{0,16},{16,0},{1,17},{17,1},{2,18},{18,2},{3,19},{19,3},{4,20},{20... | collective-permute-start | bytes 24584 | tf_op jit(solution)/shard_map/ppermute | solution.py:281
  41.9 12.7 %copy-start.5 = (s32[48]{0:T(128)S(1)}, s32[48]{0:T(128)}, u32[]{:S(2)}) copy-start(s32[48]{0:T(128)} %param.11) | copy-start | bytes 580
  47.8 6.8 %collective-permute-start.7 = (bf16[56,512]{1,0:T(8,128)(2,1)S(1)}, bf16[56,512]{1,0:T(8,128)(2,1)S(1)}, u32[]{:S(2)}, u32[]{:S(2)}) collective-permute-start(bf16[56,512]{1,0:T(8,128)(2,1)S(1)} %get-tuple-element.43), channel_id=1, source_target_pairs={{0,16},{16,0},{1,17},{17,1},{2,18},{18,2},{3,19},{19,3},{4,20},{20... | collective-permute-start | bytes 172040 | tf_op jit(solution)/shard_map/ppermute | solution.py:281
  52.8 3.5 %collective-permute-start.8 = (bf16[56,512]{1,0:T(8,128)(2,1)S(1)}, bf16[56,512]{1,0:T(8,128)(2,1)S(1)}, u32[]{:S(2)}, u32[]{:S(2)}) collective-permute-start(bf16[56,512]{1,0:T(8,128)(2,1)S(1)} %get-tuple-element.44), channel_id=1, source_target_pairs={{0,32},{32,0},{1,33},{33,1},{2,34},{34,2},{3,35},{35,3},{4,36},{36... | collective-permute-start | bytes 172040 | tf_op jit(solution)/shard_map/ppermute | solution.py:281
  53.0 4.7 %collective-permute-start.9 = (bf16[56,512]{1,0:T(8,128)(2,1)S(1)}, bf16[56,512]{1,0:T(8,128)(2,1)S(1)}, u32[]{:S(2)}, u32[]{:S(2)}) collective-permute-start(bf16[56,512]{1,0:T(8,128)(2,1)S(1)} %get-tuple-element.45), channel_id=1, source_target_pairs={{0,48},{16,32},{32,16},{48,0},{1,49},{17,33},{33,17},{49,1},{2,50}... | collective-permute-start | bytes 172040 | tf_op jit(solution)/shard_map/ppermute | solution.py:290
  59.3 12.4 %all-to-all-start.1 = ((bf16[16,16,256]{2,1,0:T(8,128)(2,1)}), bf16[16,16,256]{2,1,0:T(8,128)(2,1)S(1)}, u32[]{:S(2)}, u32[]{:S(2)}) async-start(bf16[16,16,256]{2,1,0:T(8,128)(2,1)} %get-tuple-element.49), calls=%async_computation.1 | async-start | bytes 262144 | tf_op jit(solution)/shard_map/all_to_all | solution.py:376

commit v7 on v6

--- a/solution.py
+++ b/solution.py
@@ -25,13 +25,14 @@
 ROT = 12
 NSHIFT = 4
 ROWS = 128
-FIRST = 64
+EXTENDED = ROWS + 8
 NPOOL = 4
 QROT = ROT // NPOOL
 QCLS = CLASSES // NPOOL
 NBLK = 16
 NDOM = 16
 LOCAL = 3
+BLOCK = LOCAL * QROT * 32
 COLS = 256
 STEP_TILES = 4
 F32 = jnp.float32
@@ -56,12 +57,18 @@
             for a in range(32):
                 at = (c * QROT + r) * 32 + a
                 rows[at : at + 1, :] = row[:, a * 128 : (a + 1) * 128]
-    packed = rows[...].astype(BF16)
-    for d in range(NBLK):
-        out_ref[d] = packed
-
-
-def tables_kernel(off_ref, w_ref, c0_ref, c1_ref, cos_ref, sin_ref, wc_ref, ws_ref, both_ref):
+    out_ref[...] = rows[...].astype(BF16)
+
+
+def extend_kernel(cand_ref, particles_hbm, out_ref, sem):
+    copy = pltpu.make_async_copy(particles_hbm, out_ref.at[pl.ds(0, ROWS), :], sem)
+    copy.start()
+    out_ref[ROWS:EXTENDED, 0:128] = cand_ref[...].astype(F32).astype(BF16)
+    out_ref[ROWS:EXTENDED, 128:] = jnp.zeros((8, 2 * K - 128), BF16)
+    copy.wait()
+
+
+def tables_kernel(off_ref, w_ref, cos_ref, sin_ref, wc_ref, ws_ref):
     row = lax.broadcasted_iota(jnp.int32, (16, 128), 0)
     lane = lax.broadcasted_iota(jnp.int32, (16, 128), 1)
     column = lane % KCOL
@@ -76,16 +83,15 @@
         sin_ref[at, :] = sine
         wc_ref[at, :] = weight * cosine
         ws_ref[at, :] = weight * sine
-    both_ref[0] = c0_ref[...]
-    both_ref[1] = c1_ref[...]
-
-
-def pool_copies(q, parts, pool, sem):
+
+
+def pool_copies(q, parts, pool, listed, sem):
     copies = []
-    places = ((0, 0), (1, 0), (2, 0), (2, FIRST), (3, 0), (3, FIRST))
-    for i, (part, (j, offset)) in enumerate(zip(parts, places)):
-        rows = pl.ds(pl.multiple_of((q ^ j) * ROWS + offset, 16), part.shape[0])
-        copies.append(pltpu.make_async_copy(part, pool.at[rows, :], sem.at[i]))
+    for j, part in enumerate(parts):
+        rows = pl.ds(pl.multiple_of((q ^ j) * ROWS, ROWS), ROWS)
+        copies.append(pltpu.make_async_copy(part.at[pl.ds(0, ROWS), :], pool.at[rows, :], sem.at[0, j]))
+        few = part.at[pl.ds(ROWS, 8), pl.ds(0, ROWS)]
+        copies.append(pltpu.make_async_copy(few, listed.at[j], sem.at[1, j]))
     return copies
 
 
@@ -96,19 +102,21 @@
 
 
 def score_kernel(
-    q_ref, refs_ref, p0, p1, p2, p3, p4, p5, wc_ref, ws_ref, w_ref, c0_ref, c1_ref, c23_ref,
-    own_ref, near_ref, far_ref, cross_ref, pool,
-    wide, table0, table1, scores, groups, cands, sem
+    index_ref, *refs
 ):
-    q = q_ref[0]
+    blocks = refs[:NBLK]
+    p0, p1, p2, p3, wc_ref, ws_ref, w_ref = refs[NBLK : NBLK + 7]
+    own_ref, near_ref, far_ref, cross_ref, pool = refs[NBLK + 7 : NBLK + 12]
+    wide, table0, table1, scores, groups, cands, listed, sem = refs[NBLK + 12 :]
+    q, z, xl = index_ref[0], index_ref[1], index_ref[2]
     steps = 16 // STEP_TILES
     wide_cols = 128 * STEP_TILES
-    copies = pool_copies(q, (p0, p1, p2, p3, p4, p5), pool, sem)
+    copies = pool_copies(q, (p0, p1, p2, p3), pool, listed, sem)
     for copy in copies:
         copy.start()
-    for j, cand in enumerate((c0_ref[...], c23_ref[0], c1_ref[...], c23_ref[1])):
-        cands[:, pl.ds(pl.multiple_of((q ^ j) * ROWS, ROWS), ROWS)] = cand
-    wide[...] = refs_ref[...].astype(F32)
+    for i, block in enumerate(blocks):
+        source = ((z + NBLK // 2 - i // 2) % (NBLK // 2)) * 2 + (xl ^ (i % 2))
+        wide[pl.ds(pl.multiple_of(source * BLOCK, BLOCK), BLOCK), :] = block[...].astype(F32)
     energy = [jnp.zeros((CLASSES, 128), F32) for _ in range(QROT)]
     stride = QROT * 32
     tables = (table0, table1)
@@ -134,6 +142,9 @@
     build(0)
     for copy in copies:
         copy.wait()
+    for j in range(NPOOL):
+        cand = listed[j].astype(F32).astype(jnp.int32)
+        cands[:, pl.ds(pl.multiple_of((q ^ j) * ROWS, ROWS), ROWS)] = cand
     for step in range(steps):
         if step + 1 < steps:
             build(step + 1)
@@ -295,42 +306,48 @@
     pool_index = (lax.axis_index("yl") * 2 + lax.axis_index("core")).astype(jnp.int32)
     q = pool_index.reshape(1)
 
-    cand = candidates.T
+    zi, xi = lax.axis_index("z").astype(jnp.int32), lax.axis_index("xl").astype(jnp.int32)
+    place = jnp.stack([pool_index, zi, xi])
     weight = noise_weight.reshape(16, 128)
-    far0 = swap(particles[:FIRST], "yl")
+    particles = pl.pallas_call(
+        extend_kernel,
+        out_shape=jax.ShapeDtypeStruct((EXTENDED, 2 * K), BF16),
+        in_specs=[VMEM_SPEC, HBM_SPEC],
+        out_specs=VMEM_SPEC,
+        scratch_shapes=[pltpu.SemaphoreType.DMA],
+        compiler_params=params(4),
+        name="extend",
+    )(candidates.T, in_hbm(particles))
+    far = swap(particles, "yl")
     packed = pl.pallas_call(
         pack_kernel,
-        out_shape=jax.ShapeDtypeStruct((NBLK, LOCAL * QROT * 32, 128), BF16),
+        out_shape=jax.ShapeDtypeStruct((BLOCK, 128), BF16),
         in_specs=[SMEM_SPEC, VMEM_SPEC],
         out_specs=VMEM_SPEC,
-        scratch_shapes=[VMEM((LOCAL, ROT, 2 * K), F32), VMEM((LOCAL * QROT * 32, 128), F32)],
+        scratch_shapes=[VMEM((LOCAL, ROT, 2 * K), F32), VMEM((BLOCK, 128), F32)],
         compiler_params=params(16),
         name="pack",
     )(q, references)
-    packed, whole = lax.optimization_barrier((packed, particles))
-    rest = whole[FIRST:]
-    gathered = lax.all_to_all(packed, BLK, 0, 0, tiled=True)
-    rest, far0 = lax.optimization_barrier((rest, far0))
-    far1 = swap(rest, "yl")
+    depth = NBLK // 2
+    along = [packed] + [
+        lax.ppermute(packed, "z", [(i, (i + k) % depth) for i in range(depth)])
+        for k in range(1, depth)
+    ]
+    across = [swap(block, "xl") for block in along]
     near = swap(particles, "core")
-    cand, far0 = lax.optimization_barrier((cand, far0))
-    cand_far = swap(cand, "yl")
     flat = jax.ShapeDtypeStruct((NSHIFT * 16, 128), F32)
-    cosine, sine, wc, ws, both = pl.pallas_call(
+    cosine, sine, wc, ws = pl.pallas_call(
         tables_kernel,
-        out_shape=(flat, flat, flat, flat, jax.ShapeDtypeStruct((2, 8, ROWS), jnp.int32)),
-        in_specs=[SMEM_SPEC] + [VMEM_SPEC] * 3,
-        out_specs=(VMEM_SPEC,) * 5,
+        out_shape=(flat, flat, flat, flat),
+        in_specs=[SMEM_SPEC, VMEM_SPEC],
+        out_specs=(VMEM_SPEC,) * 4,
         compiler_params=params(4),
-        cost_estimate=pl.CostEstimate(flops=10 * 10**9, bytes_accessed=30 * 10**6, transcendentals=0),
+        cost_estimate=pl.CostEstimate(flops=4 * 10**9, bytes_accessed=12 * 10**6, transcendentals=0),
         name="tables",
-    )(offsets, weight, cand, cand_far)
-    far1, wc, both = lax.optimization_barrier((far1, wc, both))
-    near1 = swap(far1, "core")
-    cand_near = swap(both, "core")
-    far0, near1 = lax.optimization_barrier((far0, near1))
-    near0 = swap(far0, "core")
-    parts = (in_hbm(particles), near, far0, far1, near0, in_hbm(near1))
+    )(offsets, weight)
+    far, wc, along[1:], across = lax.optimization_barrier((far, wc, along[1:], across))
+    parts = (particles, near, far, swap(far, "core"))
+    blocks = [block for pair in zip(along, across) for block in pair]
 
     table_rows = NSHIFT * QROT * CLASSES
     *terms, pool = pl.pallas_call(
@@ -339,7 +356,7 @@
             jax.ShapeDtypeStruct((56, NPOOL * ROWS), F32 if j == 0 else BF16) for j in range(NPOOL)
         ]
         + [jax.ShapeDtypeStruct((NPOOL * ROWS, 2 * K), BF16)],
-        in_specs=[SMEM_SPEC, VMEM_SPEC] + [HBM_SPEC] + [ANY_SPEC] * 5 + [VMEM_SPEC] * 6,
+        in_specs=[SMEM_SPEC] + [VMEM_SPEC] * NBLK + [ANY_SPEC] * 4 + [VMEM_SPEC] * 3,
         out_specs=[VMEM_SPEC] * (NPOOL + 1),
         scratch_shapes=[
             VMEM((NBLK * LOCAL * QROT * 32, 128), F32),
@@ -348,13 +365,14 @@
             VMEM((table_rows, NPOOL * ROWS), F32),
             VMEM((NPOOL, 56, NPOOL * ROWS), F32),
             VMEM((8, NPOOL * ROWS), jnp.int32),
-            pltpu.SemaphoreType.DMA((6,)),
+            VMEM((NPOOL, 8, ROWS), BF16),
+            pltpu.SemaphoreType.DMA((2, NPOOL)),
         ],
         compiler_params=params(20),
         name="score",
     )(
-        q, gathered.reshape(NBLK * LOCAL * QROT * 32, 128), *parts,
-        wc, ws, weight, cand, cand_far, cand_near,
+        place, *blocks, *parts,
+        wc, ws, weight,
     )
     terms = trade(terms, POOL)
 

time: 89.3 us -> 105 us (1.18)
  local copies, waits for them, and re-layouts: 3.2 us -> 16.6 us
  waiting for transfers between devices: 31.4 us -> 22.5 us
  starting transfers between devices: 26.8 us -> 35.4 us
  Pallas kernels: 11.1 us -> 12.3 us
    ppermute x0 -> x7, starting transfers between devices: none -> 16.5 us  [on_device(): lax.ppermute(packed, 'z', [(i, (i + k) % depth) for i in range(depth)])]
    unnamed x13 -> x67, local copies, waits for them, and re-layouts: 0.91 us -> 16.5 us
    ppermute x9 -> x13, waiting for transfers between devices: 15.5 us -> 5.19 us  [swap(): return lax.ppermute(x, axis, [(0, 1), (1, 0)])]
    all_to_all x1 -> x0, starting transfers between devices: 9.35 us -> none  [on_device(): gathered = lax.all_to_all(packed, BLK, 0, 0, tiled=True)]
    ppermute x0 -> x7, waiting for transfers between devices: none -> 6.67 us  [on_device(): lax.ppermute(packed, 'z', [(i, (i + k) % depth) for i in range(depth)])]
    all_to_all x1 -> x0, waiting for transfers between devices: 5.71 us -> none  [on_device(): gathered = lax.all_to_all(packed, BLK, 0, 0, tiled=True)]
    slice x2 -> x0, local copies, waits for them, and re-layouts: 2.21 us -> none  [the longest x1 1.13 us: on_device(): far0 = swap(particles[:FIRST], 'yl')]
    ppermute x9 -> x13, starting transfers between devices: 12.4 us -> 12.8 us  [swap(): return lax.ppermute(x, axis, [(0, 1), (1, 0)])]
  transfers between devices with their start and end apart: 12 -> 22, of which waited for: 9 -> 11; matrix products, arithmetic and copies ran while one was open for 2% -> 0% of each run, Pallas kernels for 2% -> 1%
where the time goes in v7:
time: 105 us; the launch traced here: 104 us
  starting transfers between devices  35.4 us (34%)
  waiting for transfers between devices  22.5 us (21%)
  local copies, waits for them, and re-layouts  16.6 us (16%)
  blocking collectives  15.8 us (15%)
  Pallas kernels  12.3 us (12%)
    unnamed x67, local copies, waits for them, and re-layouts  16.5 us
    ppermute x7, starting transfers between devices, on_device(): lax.ppermute(packed, 'z', [(i, (i + k) % depth) for i in range(depth)])  16.5 us
    all_to_all x1, blocking collectives, on_device(): placed = lax.all_to_all(placed, DOM, 0, 0, tiled=True)  15.8 us
    ppermute x13, starting transfers between devices, swap(): return lax.ppermute(x, axis, [(0, 1), (1, 0)])  12.8 us
    all_to_all x1, waiting for transfers between devices, on_device(): sums = lax.all_to_all(sums, BLK, 0, 0, tiled=True)  8.74 us
    pallas_call x1, Pallas kernels, on_device(): pl.pallas_call(score_kernel, out_shape=[jax.ShapeDtypeStruct((56, NPOOL *...  6.93 us
    ppermute x7, waiting for transfers between devices, on_device(): lax.ppermute(packed, 'z', [(i, (i + k) % depth) for i in range(depth)])  6.67 us
    ppermute x13, waiting for transfers between devices, swap(): return lax.ppermute(x, axis, [(0, 1), (1, 0)])  5.19 us
  transfers between devices with their start and end apart: 22, of which 11 were waited for; matrix products, arithmetic and copies ran while one was open for 0% of the time, Pallas kernels for 1%

profile of v7, /device:TPU:1, one launch (start us, length us, event | category | flops | bytes accessed | tf_op | source)
XLA Modules:
  0.0 103.6 jit_solution(16206311116443267215)
XLA Ops:
  0.7 0.7 copy-done.29
  1.4 1.3 %extend.1.refs_16_ = bf16[136,4096]{1,0:T(8,128)(2,1)S(1)} custom-call(s32[8,128]{1,0:T(8,128)S(1)} %bitcast.10, bf16[128,4096]{1,0:T(8,128)(2,1)} %particles_hbm.1), custom_call_target="tpu_custom_call" | custom-call | tf_op jit(solution)/shard_map/extend/pallas_call | solution.py:312
  2.7 2.2 %collective-permute-start = (bf16[136,4096]{1,0:T(8,128)(2,1)S(1)}, bf16[136,4096]{1,0:T(8,128)(2,1)S(1)}, u32[]{:S(2)}, u32[]{:S(2)}) collective-permute-start(bf16[136,4096]{1,0:T(8,128)(2,1)S(1)} %extend.1.refs_16_), channel_id=1, source_target_pairs={{0,32},{32,0},{1,33},{33,1},{2,34},{34,2},{3,35},{35,3},{4,36},{36... | collective-permute-start | bytes 3342344 | tf_op jit(solution)/shard_map/ppermute | solution.py:292
  4.9 0.2 pack.1.refs_0_
  5.1 3.1 %collective-permute-start.2 = (bf16[288,128]{1,0:T(8,128)(2,1)S(1)}, bf16[288,128]{1,0:T(8,128)(2,1)S(1)}, u32[]{:S(2)}, u32[]{:S(2)}) collective-permute-start(bf16[288,128]{1,0:T(8,128)(2,1)S(1)} %pack.1.refs_0_), channel_id=1, source_target_pairs={{0,4},{2,6},{4,8},{6,10},{8,12},{10,14},{12,0},{14,2},{1,5},{3,7},... | collective-permute-start | bytes 221192 | tf_op jit(solution)/shard_map/ppermute | solution.py:333
  8.1 4.7 %collective-permute-start.3 = (bf16[288,128]{1,0:T(8,128)(2,1)S(1)}, bf16[288,128]{1,0:T(8,128)(2,1)S(1)}, u32[]{:S(2)}, u32[]{:S(2)}) collective-permute-start(bf16[288,128]{1,0:T(8,128)(2,1)S(1)} %pack.1.refs_0_), channel_id=1, source_target_pairs={{0,6},{2,8},{4,10},{6,12},{8,14},{10,0},{12,2},{14,4},{1,7},{3,9},... | collective-permute-start | bytes 221192 | tf_op jit(solution)/shard_map/ppermute | solution.py:333
  12.8 1.0 collective-permute-start.4
  13.8 3.9 %collective-permute-start.5 = (bf16[288,128]{1,0:T(8,128)(2,1)S(1)}, bf16[288,128]{1,0:T(8,128)(2,1)S(1)}, u32[]{:S(2)}, u32[]{:S(2)}) collective-permute-start(bf16[288,128]{1,0:T(8,128)(2,1)S(1)} %pack.1.refs_0_), channel_id=1, source_target_pairs={{0,10},{2,12},{4,14},{6,0},{8,2},{10,4},{12,6},{14,8},{1,11},{3,13... | collective-permute-start | bytes 221192 | tf_op jit(solution)/shard_map/ppermute | solution.py:333
  17.7 2.4 %collective-permute-start.6 = (bf16[288,128]{1,0:T(8,128)(2,1)S(1)}, bf16[288,128]{1,0:T(8,128)(2,1)}, u32[]{:S(2)}, u32[]{:S(2)}) collective-permute-start(bf16[288,128]{1,0:T(8,128)(2,1)S(1)} %pack.1.refs_0_), channel_id=1, source_target_pairs={{0,12},{2,14},{4,0},{6,2},{8,4},{10,6},{12,8},{14,10},{1,13},{3,15... | collective-permute-start | bytes 221192 | tf_op jit(solution)/shard_map/ppermute | solution.py:333
  20.1 1.1 %collective-permute-done.3.refs_6_ = bf16[288,128]{1,0:T(8,128)(2,1)S(1)} collective-permute-done((bf16[288,128]{1,0:T(8,128)(2,1)S(1)}, bf16[288,128]{1,0:T(8,128)(2,1)S(1)}, u32[]{:S(2)}, u32[]{:S(2)}) %collective-permute-start.3) | collective-permute-done | bytes 73760 | tf_op jit(solution)/shard_map/ppermute | solution.py:333
  21.2 1.5 %collective-permute-start.1 = (bf16[288,128]{1,0:T(8,128)(2,1)S(1)}, bf16[288,128]{1,0:T(8,128)(2,1)}, u32[]{:S(2)}, u32[]{:S(2)}) collective-permute-start(bf16[288,128]{1,0:T(8,128)(2,1)S(1)} %pack.1.refs_0_), channel_id=1, source_target_pairs={{0,2},{2,4},{4,6},{6,8},{8,10},{10,12},{12,14},{14,0},{1,3},{3,5},... | collective-permute-start | bytes 221192 | tf_op jit(solution)/shard_map/ppermute | solution.py:333
  22.7 1.6 %collective-permute-done.5.refs_10_ = bf16[288,128]{1,0:T(8,128)(2,1)S(1)} collective-permute-done((bf16[288,128]{1,0:T(8,128)(2,1)S(1)}, bf16[288,128]{1,0:T(8,128)(2,1)S(1)}, u32[]{:S(2)}, u32[]{:S(2)}) %collective-permute-start.5) | collective-permute-done | bytes 73760 | tf_op jit(solution)/shard_map/ppermute | solution.py:333
  24.3 1.2 %collective-permute-start.8 = (bf16[288,128]{1,0:T(8,128)(2,1)S(1)}, bf16[288,128]{1,0:T(8,128)(2,1)S(1)}, u32[]{:S(2)}, u32[]{:S(2)}) collective-permute-start(bf16[288,128]{1,0:T(8,128)(2,1)S(1)} %pack.1.refs_0_), channel_id=1, source_target_pairs={{0,1},{1,0},{2,3},{3,2},{4,5},{5,4},{6,7},{7,6},{8,9},{9,8},{10,11... | collective-permute-start | bytes 221192 | tf_op jit(solution)/shard_map/ppermute | solution.py:292
  25.5 3.9 %collective-permute-done.6.refs_12_ = bf16[288,128]{1,0:T(8,128)(2,1)} collective-permute-done((bf16[288,128]{1,0:T(8,128)(2,1)S(1)}, bf16[288,128]{1,0:T(8,128)(2,1)}, u32[]{:S(2)}, u32[]{:S(2)}) %collective-permute-start.6) | collective-permute-done | bytes 73760 | tf_op jit(solution)/shard_map/ppermute | solution.py:333
  29.4 1.2 %collective-permute-start.10 = (bf16[288,128]{1,0:T(8,128)(2,1)S(1)}, bf16[288,128]{1,0:T(8,128)(2,1)S(1)}, u32[]{:S(2)}, u32[]{:S(2)}) collective-permute-start(bf16[288,128]{1,0:T(8,128)(2,1)S(1)} %collective-permute-done.2.refs_4_), channel_id=1, source_target_pairs={{0,1},{1,0},{2,3},{3,2},{4,5},{5,4},{6,7},{7,6},{8,9},{9,8},{10,11... | collective-permute-start | bytes 221192 | tf_op jit(solution)/shard_map/ppermute | solution.py:292
  30.7 0.3 collective-permute-start.11
  30.9 1.2 %collective-permute-start.12 = (bf16[288,128]{1,0:T(8,128)(2,1)S(1)}, bf16[288,128]{1,0:T(8,128)(2,1)S(1)}, u32[]{:S(2)}, u32[]{:S(2)}) collective-permute-start(bf16[288,128]{1,0:T(8,128)(2,1)S(1)} %collective-permute-done.4.refs_8_), channel_id=1, source_target_pairs={{0,1},{1,0},{2,3},{3,2},{4,5},{5,4},{6,7},{7,6},{8,9},{9,8},{10,11... | collective-permute-start | bytes 221192 | tf_op jit(solution)/shard_map/ppermute | solution.py:292
  32.1 0.1 copy.10.off_ref
  32.2 0.3 collective-permute-start.13
  32.5 0.9 collective-permute-done.10.refs_5_
  33.4 1.2 %collective-permute-start.14 = (bf16[288,128]{1,0:T(8,128)(2,1)}, bf16[288,128]{1,0:T(8,128)(2,1)S(1)}, u32[]{:S(2)}, u32[]{:S(2)}) collective-permute-start(bf16[288,128]{1,0:T(8,128)(2,1)} %collective-permute-done.6.refs_12_), channel_id=1, source_target_pairs={{0,1},{1,0},{2,3},{3,2},{4,5},{5,4},{6,7},{7,6},{8,9},{9,8},{10,11... | collective-permute-start | bytes 221192 | tf_op jit(solution)/shard_map/ppermute | solution.py:292
  34.6 0.4 collective-permute-done.11.refs_7_
  35.0 1.2 %collective-permute-start.15 = (bf16[288,128]{1,0:T(8,128)(2,1)}, bf16[288,128]{1,0:T(8,128)(2,1)S(1)}, u32[]{:S(2)}, u32[]{:S(2)}) collective-permute-start(bf16[288,128]{1,0:T(8,128)(2,1)} %collective-permute-done.7.refs_14_), channel_id=1, source_target_pairs={{0,1},{1,0},{2,3},{3,2},{4,5},{5,4},{6,7},{7,6},{8,9},{9,8},{10,11... | collective-permute-start | bytes 221192 | tf_op jit(solution)/shard_map/ppermute | solution.py:292
  36.2 0.4 collective-permute-done.12.refs_9_
  36.6 1.2 %collective-permute-start.9 = (bf16[288,128]{1,0:T(8,128)(2,1)}, bf16[288,128]{1,0:T(8,128)(2,1)S(1)}, u32[]{:S(2)}, u32[]{:S(2)}) collective-permute-start(bf16[288,128]{1,0:T(8,128)(2,1)} %collective-permute-done.1.refs_2_), channel_id=1, source_target_pairs={{0,1},{1,0},{2,3},{3,2},{4,5},{5,4},{6,7},{7,6},{8,9},{9,8},{10,11... | collective-permute-start | bytes 221192 | tf_op jit(solution)/shard_map/ppermute | solution.py:292
  37.8 0.7 tables.1
  38.6 0.6 copy-done.23
  39.2 0.6 copy-done.25
  39.8 0.6 copy-done.15
  40.4 2.1 %collective-permute-start.16 = (bf16[136,4096]{1,0:T(8,128)(2,1)S(1)}, bf16[136,4096]{1,0:T(8,128)(2,1)S(1)}, u32[]{:S(2)}, u32[]{:S(2)}) collective-permute-start(bf16[136,4096]{1,0:T(8,128)(2,1)S(1)} %extend.1.refs_16_), channel_id=1, source_target_pairs={{0,16},{16,0},{1,17},{17,1},{2,18},{18,2},{3,19},{19,3},{4,20},{20... | collective-permute-start | bytes 3342344 | tf_op jit(solution)/shard_map/ppermute | solution.py:292
  42.5 0.6 copy-done.17
  43.2 0.6 copy-done.19
  43.8 0.6 copy-done.21
  44.4 0.2 collective-permute-start.17
  44.7 0.2 collective-permute-done.16.refs_17_
  44.9 2.4 %collective-permute-done.17.refs_19_ = bf16[136,4096]{1,0:T(8,128)(2,1)} collective-permute-done((bf16[136,4096]{1,0:T(8,128)(2,1)S(1)}, bf16[136,4096]{1,0:T(8,128)(2,1)}, u32[]{:S(2)}, u32[]{:S(2)}) %collective-permute-start.17) | collective-permute-done | bytes 1114144 | tf_op jit(solution)/shard_map/ppermute | solution.py:292
  47.3 0.9 copy-done.2
  48.2 0.9 copy-done.4
  49.1 0.9 copy-done.6
  50.0 0.9 copy-done.8
  50.9 0.9 copy-done.10
  51.7 0.9 copy-done.12
  52.6 0.9 copy-done.14
  53.5 0.9 copy-done.16
  54.4 0.9 copy-done.18
  55.3 0.9 copy-done.20
  56.2 0.9 copy-done.22
  57.0 0.8 copy-done.24
  57.8 0.8 copy-done.26
  58.6 0.7 copy-done.28
  59.3 6.9 %score.1 = (f32[56,512]{1,0:T(8,128)S(1)}, bf16[56,512]{1,0:T(8,128)(2,1)S(1)}, bf16[56,512]{1,0:T(8,128)(2,1)S(1)}, bf16[56,512]{1,0:T(8,128)(2,1)S(1)}, bf16[512,4096]{1,0:T(8,128)(2,1)S(1)}) custom-call(s32[3]{0:T(128)S(1)} %pad_add_fusion.index_ref, bf16[288,128]{1,0:T(8,128)(2,1)S(1)} %pack.1.refs_0_, bf16[288,128]{1,0:T(8,128)(2,1)S(1)} %copy-done.8, ...), custom_call_target="tpu_custom_call" | custom-call | tf_op jit(solution)/shard_map/score/pallas_call | solution.py:353
  66.2 0.3 collective-permute-start.18
  66.5 0.2 collective-permute-start.19
  66.6 1.8 %collective-permute-start.20 = (bf16[56,512]{1,0:T(8,128)(2,1)S(1)}, bf16[56,512]{1,0:T(8,128)(2,1)S(1)}, u32[]{:S(2)}, u32[]{:S(2)}) collective-permute-start(bf16[56,512]{1,0:T(8,128)(2,1)S(1)} %get-tuple-element.55), channel_id=1, source_target_pairs={{0,48},{16,32},{32,16},{48,0},{1,49},{17,33},{33,17},{49,1},{2,50}... | collective-permute-start | bytes 172040 | tf_op jit(solution)/shard_map/ppermute | solution.py:301
  68.4 0.1 convert_reduce_fusion
  68.5 1.0 collective-permute-done.19.x2
  69.5 1.9 %collective-permute-done.20.x3 = bf16[56,512]{1,0:T(8,128)(2,1)S(1)} collective-permute-done((bf16[56,512]{1,0:T(8,128)(2,1)S(1)}, bf16[56,512]{1,0:T(8,128)(2,1)S(1)}, u32[]{:S(2)}, u32[]{:S(2)}) %collective-permute-start.20) | collective-permute-done | bytes 57376 | tf_op jit(solution)/shard_map/ppermute | solution.py:301
  71.4 1.7 %classes.1 = (bf16[16,16,256]{2,1,0:T(8,128)(2,1)}, f32[1,128]{1,0:T(1,128)}) custom-call(s32[1]{0:T(128)} %bitcast.1.q_ref, f32[56,512]{1,0:T(8,128)S(1)} %get-tuple-element.52.x0, bf16[56,512]{1,0:T(8,128)(2,1)S(1)} %collective-permute-done.18.x1, bf16[56,512]{1,0:T(8,128)(2,1)S(1)} %collective-permute-done.19.x2, ...), custom_call_target="tpu_custom_call" | custom-call | tf_op jit(solution)/shard_map/classes/pallas_call | solution.py:379
  73.1 4.3 %all-to-all-start = ((bf16[16,16,256]{2,1,0:T(8,128)(2,1)}), bf16[16,16,256]{2,1,0:T(8,128)(2,1)S(1)}, u32[]{:S(2)}, u32[]{:S(2)}) async-start(bf16[16,16,256]{2,1,0:T(8,128)(2,1)} %get-tuple-element.59), calls=%async_computation | async-start | bytes 262144 | tf_op jit(solution)/shard_map/all_to_all | solution.py:394
  77.4 0.1 dynamic_slice.3
  77.5 8.7 %all-to-all-done.y_ref = bf16[16,16,256]{2,1,0:T(8,128)(2,1)S(1)} async-done(((bf16[16,16,256]{2,1,0:T(8,128)(2,1)}), bf16[16,16,256]{2,1,0:T(8,128)(2,1)S(1)}, u32[]{:S(2)}, u32[]{:S(2)}) %all-to-all-start) | async-done | bytes 131104 | tf_op jit(solution)/shard_map/all_to_all | solution.py:394
  86.3 0.8 place.1
  87.1 15.8 %all_to_all.10.z_ref = bf16[16,8,384]{2,1,0:T(8,128)(2,1)S(1)} all-to-all(bf16[16,8,384]{2,1,0:T(8,128)(2,1)} %place.1), channel_id=1, replica_groups=mesh['xh'=2,'yh'=2,'yl'=2,'core'=2,'z'=8,'xl'=2] {'xh','yh','yl','core'}, dimensions={0} | all-to-all | bytes 196608 | tf_op jit(solution)/shard_map/all_to_all | solution.py:412
  102.9 0.8 means.1
  (60 shorter events, 0.2 us)
Async XLA Ops:
  0.6 4.2 %copy-start = (bf16[3,12,4096]{2,1,0:T(8,128)(2,1)S(1)}, bf16[3,12,4096]{2,1,0:T(8,128)(2,1)}, u32[]{:S(2)}) copy-start(bf16[3,12,4096]{2,1,0:T(8,128)(2,1)} %refs_ref.1) | copy-start | bytes 884740
  0.6 0.7 copy-start.29
  1.4 30.8 %copy-start.30 = (s32[4,2]{0,1:T(2,128)S(1)}, s32[4,2]{0,1:T(2,128)}, u32[]{:S(2)}) copy-start(s32[4,2]{0,1:T(2,128)} %param.9) | copy-start | bytes 100
  1.4 36.4 %copy-start.27 = (f32[2048]{0:T(1024)S(1)}, f32[2048]{0:T(1024)}, u32[]{:S(2)}) copy-start(f32[2048]{0:T(1024)} %param.8) | copy-start | bytes 24580
  2.7 41.8 %collective-permute-start = (bf16[136,4096]{1,0:T(8,128)(2,1)S(1)}, bf16[136,4096]{1,0:T(8,128)(2,1)S(1)}, u32[]{:S(2)}, u32[]{:S(2)}) collective-permute-start(bf16[136,4096]{1,0:T(8,128)(2,1)S(1)} %extend.1.refs_16_), channel_id=1, source_target_pairs={{0,32},{32,0},{1,33},{33,1},{2,34},{34,2},{3,35},{35,3},{4,36},{36... | collective-permute-start | bytes 3342344 | tf_op jit(solution)/shard_map/ppermute | solution.py:292
  5.1 12.7 %collective-permute-start.2 = (bf16[288,128]{1,0:T(8,128)(2,1)S(1)}, bf16[288,128]{1,0:T(8,128)(2,1)S(1)}, u32[]{:S(2)}, u32[]{:S(2)}) collective-permute-start(bf16[288,128]{1,0:T(8,128)(2,1)S(1)} %pack.1.refs_0_), channel_id=1, source_target_pairs={{0,4},{2,6},{4,8},{6,10},{8,12},{10,14},{12,0},{14,2},{1,5},{3,7},... | collective-permute-start | bytes 221192 | tf_op jit(solution)/shard_map/ppermute | solution.py:333
  8.1 13.1 %collective-permute-start.3 = (bf16[288,128]{1,0:T(8,128)(2,1)S(1)}, bf16[288,128]{1,0:T(8,128)(2,1)S(1)}, u32[]{:S(2)}, u32[]{:S(2)}) collective-permute-start(bf16[288,128]{1,0:T(8,128)(2,1)S(1)} %pack.1.refs_0_), channel_id=1, source_target_pairs={{0,6},{2,8},{4,10},{6,12},{8,14},{10,0},{12,2},{14,4},{1,7},{3,9},... | collective-permute-start | bytes 221192 | tf_op jit(solution)/shard_map/ppermute | solution.py:333
  12.8 8.4 %collective-permute-start.4 = (bf16[288,128]{1,0:T(8,128)(2,1)S(1)}, bf16[288,128]{1,0:T(8,128)(2,1)S(1)}, u32[]{:S(2)}, u32[]{:S(2)}) collective-permute-start(bf16[288,128]{1,0:T(8,128)(2,1)S(1)} %pack.1.refs_0_), channel_id=1, source_target_pairs={{0,8},{2,10},{4,12},{6,14},{8,0},{10,2},{12,4},{14,6},{1,9},{3,11}... | collective-permute-start | bytes 221192 | tf_op jit(solution)/shard_map/ppermute | solution.py:333
  13.8 10.5 %collective-permute-start.5 = (bf16[288,128]{1,0:T(8,128)(2,1)S(1)}, bf16[288,128]{1,0:T(8,128)(2,1)S(1)}, u32[]{:S(2)}, u32[]{:S(2)}) collective-permute-start(bf16[288,128]{1,0:T(8,128)(2,1)S(1)} %pack.1.refs_0_), channel_id=1, source_target_pairs={{0,10},{2,12},{4,14},{6,0},{8,2},{10,4},{12,6},{14,8},{1,11},{3,13... | collective-permute-start | bytes 221192 | tf_op jit(solution)/shard_map/ppermute | solution.py:333
  17.7 11.7 %collective-permute-start.6 = (bf16[288,128]{1,0:T(8,128)(2,1)S(1)}, bf16[288,128]{1,0:T(8,128)(2,1)}, u32[]{:S(2)}, u32[]{:S(2)}) collective-permute-start(bf16[288,128]{1,0:T(8,128)(2,1)S(1)} %pack.1.refs_0_), channel_id=1, source_target_pairs={{0,12},{2,14},{4,0},{6,2},{8,4},{10,6},{12,8},{14,10},{1,13},{3,15... | collective-permute-start | bytes 221192 | tf_op jit(solution)/shard_map/ppermute | solution.py:333
  21.2 17.3 %copy-start.1 = (bf16[288,128]{1,0:T(8,128)(2,1)}, bf16[288,128]{1,0:T(8,128)(2,1)S(1)}, u32[]{:S(2)}) copy-start(bf16[288,128]{1,0:T(8,128)(2,1)S(1)} %collective-permute-done.3.refs_6_) | copy-start | bytes 221188
  21.2 9.4 %collective-permute-start.7 = (bf16[288,128]{1,0:T(8,128)(2,1)S(1)}, bf16[288,128]{1,0:T(8,128)(2,1)}, u32[]{:S(2)}, u32[]{:S(2)}) collective-permute-start(bf16[288,128]{1,0:T(8,128)(2,1)S(1)} %pack.1.refs_0_), channel_id=1, source_target_pairs={{0,14},{2,0},{4,2},{6,4},{8,6},{10,8},{12,10},{14,12},{1,15},{3,1}... | collective-permute-start | bytes 221192 | tf_op jit(solution)/shard_map/ppermute | solution.py:333
  21.2 17.3 %copy-start.3 = (bf16[288,128]{1,0:T(8,128)(2,1)}, bf16[288,128]{1,0:T(8,128)(2,1)S(1)}, u32[]{:S(2)}) copy-start(bf16[288,128]{1,0:T(8,128)(2,1)S(1)} %collective-permute-done.4.refs_8_) | copy-start | bytes 221188
  21.2 9.7 %collective-permute-start.1 = (bf16[288,128]{1,0:T(8,128)(2,1)S(1)}, bf16[288,128]{1,0:T(8,128)(2,1)}, u32[]{:S(2)}, u32[]{:S(2)}) collective-permute-start(bf16[288,128]{1,0:T(8,128)(2,1)S(1)} %pack.1.refs_0_), channel_id=1, source_target_pairs={{0,2},{2,4},{4,6},{6,8},{8,10},{10,12},{12,14},{14,0},{1,3},{3,5},... | collective-permute-start | bytes 221192 | tf_op jit(solution)/shard_map/ppermute | solution.py:333
  24.3 14.2 %copy-start.5 = (bf16[288,128]{1,0:T(8,128)(2,1)}, bf16[288,128]{1,0:T(8,128)(2,1)S(1)}, u32[]{:S(2)}) copy-start(bf16[288,128]{1,0:T(8,128)(2,1)S(1)} %collective-permute-done.5.refs_10_) | copy-start | bytes 221188
  24.3 7.9 %collective-permute-start.8 = (bf16[288,128]{1,0:T(8,128)(2,1)S(1)}, bf16[288,128]{1,0:T(8,128)(2,1)S(1)}, u32[]{:S(2)}, u32[]{:S(2)}) collective-permute-start(bf16[288,128]{1,0:T(8,128)(2,1)S(1)} %pack.1.refs_0_), channel_id=1, source_target_pairs={{0,1},{1,0},{2,3},{3,2},{4,5},{5,4},{6,7},{7,6},{8,9},{9,8},{10,11... | collective-permute-start | bytes 221192 | tf_op jit(solution)/shard_map/ppermute | solution.py:292
  29.4 4.0 %collective-permute-start.10 = (bf16[288,128]{1,0:T(8,128)(2,1)S(1)}, bf16[288,128]{1,0:T(8,128)(2,1)S(1)}, u32[]{:S(2)}, u32[]{:S(2)}) collective-permute-start(bf16[288,128]{1,0:T(8,128)(2,1)S(1)} %collective-permute-done.2.refs_4_), channel_id=1, source_target_pairs={{0,1},{1,0},{2,3},{3,2},{4,5},{5,4},{6,7},{7,6},{8,9},{9,8},{10,11... | collective-permute-start | bytes 221192 | tf_op jit(solution)/shard_map/ppermute | solution.py:292
  30.7 4.3 %collective-permute-start.11 = (bf16[288,128]{1,0:T(8,128)(2,1)S(1)}, bf16[288,128]{1,0:T(8,128)(2,1)S(1)}, u32[]{:S(2)}, u32[]{:S(2)}) collective-permute-start(bf16[288,128]{1,0:T(8,128)(2,1)S(1)} %collective-permute-done.3.refs_6_), channel_id=1, source_target_pairs={{0,1},{1,0},{2,3},{3,2},{4,5},{5,4},{6,7},{7,6},{8,9},{9,8},{10,11... | collective-permute-start | bytes 221192 | tf_op jit(solution)/shard_map/ppermute | solution.py:292
  30.9 5.6 %collective-permute-start.12 = (bf16[288,128]{1,0:T(8,128)(2,1)S(1)}, bf16[288,128]{1,0:T(8,128)(2,1)S(1)}, u32[]{:S(2)}, u32[]{:S(2)}) collective-permute-start(bf16[288,128]{1,0:T(8,128)(2,1)S(1)} %collective-permute-done.4.refs_8_), channel_id=1, source_target_pairs={{0,1},{1,0},{2,3},{3,2},{4,5},{5,4},{6,7},{7,6},{8,9},{9,8},{10,11... | collective-permute-start | bytes 221192 | tf_op jit(solution)/shard_map/ppermute | solution.py:292
  32.2 6.3 %copy-start.7 = (bf16[288,128]{1,0:T(8,128)(2,1)}, bf16[288,128]{1,0:T(8,128)(2,1)S(1)}, u32[]{:S(2)}) copy-start(bf16[288,128]{1,0:T(8,128)(2,1)S(1)} %collective-permute-done.8.refs_1_) | copy-start | bytes 221188
  32.2 7.5 %collective-permute-start.13 = (bf16[288,128]{1,0:T(8,128)(2,1)S(1)}, bf16[288,128]{1,0:T(8,128)(2,1)S(1)}, u32[]{:S(2)}, u32[]{:S(2)}) collective-permute-start(bf16[288,128]{1,0:T(8,128)(2,1)S(1)} %collective-permute-done.5.refs_10_), channel_id=1, source_target_pairs={{0,1},{1,0},{2,3},{3,2},{4,5},{5,4},{6,7},{7,6},{8,9},{9,8},{10,11... | collective-permute-start | bytes 221192 | tf_op jit(solution)/shard_map/ppermute | solution.py:292
  33.4 5.1 %copy-start.9 = (bf16[288,128]{1,0:T(8,128)(2,1)}, bf16[288,128]{1,0:T(8,128)(2,1)S(1)}, u32[]{:S(2)}) copy-start(bf16[288,128]{1,0:T(8,128)(2,1)S(1)} %collective-permute-done.10.refs_5_) | copy-start | bytes 221188
  33.4 9.1 %collective-permute-start.14 = (bf16[288,128]{1,0:T(8,128)(2,1)}, bf16[288,128]{1,0:T(8,128)(2,1)S(1)}, u32[]{:S(2)}, u32[]{:S(2)}) collective-permute-start(bf16[288,128]{1,0:T(8,128)(2,1)} %collective-permute-done.6.refs_12_), channel_id=1, source_target_pairs={{0,1},{1,0},{2,3},{3,2},{4,5},{5,4},{6,7},{7,6},{8,9},{9,8},{10,11... | collective-permute-start | bytes 221192 | tf_op jit(solution)/shard_map/ppermute | solution.py:292
  35.0 3.6 %copy-start.11 = (bf16[288,128]{1,0:T(8,128)(2,1)}, bf16[288,128]{1,0:T(8,128)(2,1)S(1)}, u32[]{:S(2)}) copy-start(bf16[288,128]{1,0:T(8,128)(2,1)S(1)} %collective-permute-done.11.refs_7_) | copy-start | bytes 221188
  35.0 8.2 %collective-permute-start.15 = (bf16[288,128]{1,0:T(8,128)(2,1)}, bf16[288,128]{1,0:T(8,128)(2,1)S(1)}, u32[]{:S(2)}, u32[]{:S(2)}) collective-permute-start(bf16[288,128]{1,0:T(8,128)(2,1)} %collective-permute-done.7.refs_14_), channel_id=1, source_target_pairs={{0,1},{1,0},{2,3},{3,2},{4,5},{5,4},{6,7},{7,6},{8,9},{9,8},{10,11... | collective-permute-start | bytes 221192 | tf_op jit(solution)/shard_map/ppermute | solution.py:292
  36.6 2.0 %copy-start.13 = (bf16[288,128]{1,0:T(8,128)(2,1)}, bf16[288,128]{1,0:T(8,128)(2,1)S(1)}, u32[]{:S(2)}) copy-start(bf16[288,128]{1,0:T(8,128)(2,1)S(1)} %collective-permute-done.12.refs_9_) | copy-start | bytes 221188
  36.6 7.2 %collective-permute-start.9 = (bf16[288,128]{1,0:T(8,128)(2,1)}, bf16[288,128]{1,0:T(8,128)(2,1)S(1)}, u32[]{:S(2)}, u32[]{:S(2)}) collective-permute-start(bf16[288,128]{1,0:T(8,128)(2,1)} %collective-permute-done.1.refs_2_), channel_id=1, source_target_pairs={{0,1},{1,0},{2,3},{3,2},{4,5},{5,4},{6,7},{7,6},{8,9},{9,8},{10,11... | collective-permute-start | bytes 221192 | tf_op jit(solution)/shard_map/ppermute | solution.py:292
  38.6 0.6 copy-start.23
  39.2 0.6 copy-start.25
  39.8 0.6 copy-start.15
  40.4 4.5 %collective-permute-start.16 = (bf16[136,4096]{1,0:T(8,128)(2,1)S(1)}, bf16[136,4096]{1,0:T(8,128)(2,1)S(1)}, u32[]{:S(2)}, u32[]{:S(2)}) collective-permute-start(bf16[136,4096]{1,0:T(8,128)(2,1)S(1)} %extend.1.refs_16_), channel_id=1, source_target_pairs={{0,16},{16,0},{1,17},{17,1},{2,18},{18,2},{3,19},{19,3},{4,20},{20... | collective-permute-start | bytes 3342344 | tf_op jit(solution)/shard_map/ppermute | solution.py:292
  42.5 0.6 copy-start.17
  43.2 0.6 copy-start.19
  43.8 0.6 copy-start.21
  44.4 2.9 %collective-permute-start.17 = (bf16[136,4096]{1,0:T(8,128)(2,1)S(1)}, bf16[136,4096]{1,0:T(8,128)(2,1)}, u32[]{:S(2)}, u32[]{:S(2)}) collective-permute-start(bf16[136,4096]{1,0:T(8,128)(2,1)S(1)} %collective-permute-done.refs_18_), channel_id=1, source_target_pairs={{0,16},{16,0},{1,17},{17,1},{2,18},{18,2},{3,19},{19,3},{4,20},{20... | collective-permute-start | bytes 3342344 | tf_op jit(solution)/shard_map/ppermute | solution.py:292
  47.3 0.9 copy-start.2
  48.2 0.9 copy-start.4
  49.1 0.9 copy-start.6
  50.0 0.9 copy-start.8
  50.8 0.9 copy-start.10
  51.7 0.9 copy-start.12
  52.6 0.9 copy-start.14
  53.5 0.9 copy-start.16
  54.4 0.9 copy-start.18
  55.3 0.9 copy-start.20
  56.2 0.9 copy-start.22
  57.0 0.8 copy-start.24
  57.8 0.8 copy-start.26
  58.6 0.7 copy-start.28
  59.3 9.2 %copy-start.31 = (s32[48]{0:T(128)S(1)}, s32[48]{0:T(128)}, u32[]{:S(2)}) copy-start(s32[48]{0:T(128)} %param.11) | copy-start | bytes 580
  66.2 2.3 %collective-permute-start.18 = (bf16[56,512]{1,0:T(8,128)(2,1)S(1)}, bf16[56,512]{1,0:T(8,128)(2,1)S(1)}, u32[]{:S(2)}, u32[]{:S(2)}) collective-permute-start(bf16[56,512]{1,0:T(8,128)(2,1)S(1)} %get-tuple-element.53), channel_id=1, source_target_pairs={{0,16},{16,0},{1,17},{17,1},{2,18},{18,2},{3,19},{19,3},{4,20},{20... | collective-permute-start | bytes 172040 | tf_op jit(solution)/shard_map/ppermute | solution.py:292
  66.5 3.0 %collective-permute-start.19 = (bf16[56,512]{1,0:T(8,128)(2,1)S(1)}, bf16[56,512]{1,0:T(8,128)(2,1)S(1)}, u32[]{:S(2)}, u32[]{:S(2)}) collective-permute-start(bf16[56,512]{1,0:T(8,128)(2,1)S(1)} %get-tuple-element.54), channel_id=1, source_target_pairs={{0,32},{32,0},{1,33},{33,1},{2,34},{34,2},{3,35},{35,3},{4,36},{36... | collective-permute-start | bytes 172040 | tf_op jit(solution)/shard_map/ppermute | solution.py:292
  66.6 4.7 %collective-permute-start.20 = (bf16[56,512]{1,0:T(8,128)(2,1)S(1)}, bf16[56,512]{1,0:T(8,128)(2,1)S(1)}, u32[]{:S(2)}, u32[]{:S(2)}) collective-permute-start(bf16[56,512]{1,0:T(8,128)(2,1)S(1)} %get-tuple-element.55), channel_id=1, source_target_pairs={{0,48},{16,32},{32,16},{48,0},{1,49},{17,33},{33,17},{49,1},{2,50}... | collective-permute-start | bytes 172040 | tf_op jit(solution)/shard_map/ppermute | solution.py:301
  71.4 6.0 %copy-start.32 = (s32[48]{0:T(128)S(1)}, s32[48]{0:T(128)}, u32[]{:S(2)}) copy-start(s32[48]{0:T(128)} %param.11) | copy-start | bytes 580
  73.1 13.2 %all-to-all-start = ((bf16[16,16,256]{2,1,0:T(8,128)(2,1)}), bf16[16,16,256]{2,1,0:T(8,128)(2,1)S(1)}, u32[]{:S(2)}, u32[]{:S(2)}) async-start(bf16[16,16,256]{2,1,0:T(8,128)(2,1)} %get-tuple-element.59), calls=%async_computation | async-start | bytes 262144 | tf_op jit(solution)/shard_map/all_to_all | solution.py:394

commit v8 on v7

--- a/solution.py
+++ b/solution.py
@@ -32,9 +32,10 @@
 NBLK = 16
 NDOM = 16
 LOCAL = 3
+DEPTH = 8
 BLOCK = LOCAL * QROT * 32
 COLS = 256
-STEP_TILES = 4
+STEP_TILES = 2
 F32 = jnp.float32
 BF16 = jnp.bfloat16
 VMEM = pltpu.VMEM
@@ -48,7 +49,11 @@
     return pltpu.CompilerParams(vmem_limit_bytes=mib << 20)
 
 
-def pack_kernel(q_ref, refs_ref, out_ref, wide, rows):
+def pack_kernel(q_ref, cand_ref, refs_ref, particles_hbm, out_ref, extended_ref, wide, rows, sem):
+    copy = pltpu.make_async_copy(particles_hbm, extended_ref.at[pl.ds(0, ROWS), :], sem)
+    copy.start()
+    extended_ref[ROWS:EXTENDED, 0:128] = cand_ref[...].astype(F32).astype(BF16)
+    extended_ref[ROWS:EXTENDED, 128:] = jnp.zeros((8, 2 * K - 128), BF16)
     q = q_ref[0]
     wide[...] = refs_ref[...].astype(F32)
     for c in range(LOCAL):
@@ -58,13 +63,6 @@
                 at = (c * QROT + r) * 32 + a
                 rows[at : at + 1, :] = row[:, a * 128 : (a + 1) * 128]
     out_ref[...] = rows[...].astype(BF16)
-
-
-def extend_kernel(cand_ref, particles_hbm, out_ref, sem):
-    copy = pltpu.make_async_copy(particles_hbm, out_ref.at[pl.ds(0, ROWS), :], sem)
-    copy.start()
-    out_ref[ROWS:EXTENDED, 0:128] = cand_ref[...].astype(F32).astype(BF16)
-    out_ref[ROWS:EXTENDED, 128:] = jnp.zeros((8, 2 * K - 128), BF16)
     copy.wait()
 
 
@@ -104,19 +102,29 @@
 def score_kernel(
     index_ref, *refs
 ):
-    blocks = refs[:NBLK]
-    p0, p1, p2, p3, wc_ref, ws_ref, w_ref = refs[NBLK : NBLK + 7]
-    own_ref, near_ref, far_ref, cross_ref, pool = refs[NBLK + 7 : NBLK + 12]
-    wide, table0, table1, scores, groups, cands, listed, sem = refs[NBLK + 12 :]
+    blocks = refs[:DEPTH]
+    p0, p1, p2, p3, wc_ref, ws_ref, w_ref = refs[DEPTH : DEPTH + 7]
+    own_ref, near_ref, far_ref, cross_ref, pool = refs[DEPTH + 7 : DEPTH + 12]
+    stage, wide, table0, table1, scores, groups, cands, listed, sem, block_sem = refs[DEPTH + 12 :]
     q, z, xl = index_ref[0], index_ref[1], index_ref[2]
+    block_copies = []
+    for k, block in enumerate(blocks):
+        for side in range(2):
+            source = ((z + DEPTH - k) % DEPTH) * 2 + (xl ^ side)
+            rows = pl.ds(pl.multiple_of(source * BLOCK, BLOCK), BLOCK)
+            block_copies.append(
+                pltpu.make_async_copy(block.at[side], stage.at[rows, :], block_sem.at[k, side])
+            )
+    for copy in block_copies:
+        copy.start()
     steps = 16 // STEP_TILES
     wide_cols = 128 * STEP_TILES
     copies = pool_copies(q, (p0, p1, p2, p3), pool, listed, sem)
     for copy in copies:
         copy.start()
-    for i, block in enumerate(blocks):
-        source = ((z + NBLK // 2 - i // 2) % (NBLK // 2)) * 2 + (xl ^ (i % 2))
-        wide[pl.ds(pl.multiple_of(source * BLOCK, BLOCK), BLOCK), :] = block[...].astype(F32)
+    for copy in block_copies:
+        copy.wait()
+    wide[...] = stage[...].astype(F32)
     energy = [jnp.zeros((CLASSES, 128), F32) for _ in range(QROT)]
     stride = QROT * 32
     tables = (table0, table1)
@@ -292,6 +300,10 @@
     return lax.ppermute(x, axis, [(0, 1), (1, 0)])
 
 
+def turn(x, step):
+    return lax.ppermute(x, "z", [(i, (i + step) % DEPTH) for i in range(DEPTH)])
+
+
 def trade(parts, axes):
     own, near, far, cross = parts
     return (
@@ -309,31 +321,29 @@
     zi, xi = lax.axis_index("z").astype(jnp.int32), lax.axis_index("xl").astype(jnp.int32)
     place = jnp.stack([pool_index, zi, xi])
     weight = noise_weight.reshape(16, 128)
-    particles = pl.pallas_call(
-        extend_kernel,
-        out_shape=jax.ShapeDtypeStruct((EXTENDED, 2 * K), BF16),
-        in_specs=[VMEM_SPEC, HBM_SPEC],
-        out_specs=VMEM_SPEC,
-        scratch_shapes=[pltpu.SemaphoreType.DMA],
-        compiler_params=params(4),
-        name="extend",
-    )(candidates.T, in_hbm(particles))
+    packed, particles = pl.pallas_call(
+        pack_kernel,
+        out_shape=(
+            jax.ShapeDtypeStruct((BLOCK, 128), BF16),
+            jax.ShapeDtypeStruct((EXTENDED, 2 * K), BF16),
+        ),
+        in_specs=[SMEM_SPEC, VMEM_SPEC, VMEM_SPEC, HBM_SPEC],
+        out_specs=(VMEM_SPEC, VMEM_SPEC),
+        scratch_shapes=[
+            VMEM((LOCAL, ROT, 2 * K), F32),
+            VMEM((BLOCK, 128), F32),
+            pltpu.SemaphoreType.DMA,
+        ],
+        compiler_params=params(8),
+        name="pack",
+    )(q, candidates.T, references, in_hbm(particles))
     far = swap(particles, "yl")
-    packed = pl.pallas_call(
-        pack_kernel,
-        out_shape=jax.ShapeDtypeStruct((BLOCK, 128), BF16),
-        in_specs=[SMEM_SPEC, VMEM_SPEC],
-        out_specs=VMEM_SPEC,
-        scratch_shapes=[VMEM((LOCAL, ROT, 2 * K), F32), VMEM((BLOCK, 128), F32)],
-        compiler_params=params(16),
-        name="pack",
-    )(q, references)
-    depth = NBLK // 2
-    along = [packed] + [
-        lax.ppermute(packed, "z", [(i, (i + k) % depth) for i in range(depth)])
-        for k in range(1, depth)
-    ]
-    across = [swap(block, "xl") for block in along]
+    ring = [None] * DEPTH
+    ring[0] = up = down = jnp.stack([packed, swap(packed, "xl")])
+    for k in range(1, DEPTH // 2):
+        ring[k] = up = turn(up, 1)
+        ring[DEPTH - k] = down = turn(down, -1)
+    ring[DEPTH // 2] = turn(up, 1)
     near = swap(particles, "core")
     flat = jax.ShapeDtypeStruct((NSHIFT * 16, 128), F32)
     cosine, sine, wc, ws = pl.pallas_call(
@@ -342,13 +352,11 @@
         in_specs=[SMEM_SPEC, VMEM_SPEC],
         out_specs=(VMEM_SPEC,) * 4,
         compiler_params=params(4),
-        cost_estimate=pl.CostEstimate(flops=4 * 10**9, bytes_accessed=12 * 10**6, transcendentals=0),
+        cost_estimate=pl.CostEstimate(flops=1 * 10**9, bytes_accessed=3 * 10**6, transcendentals=0),
         name="tables",
     )(offsets, weight)
-    far, wc, along[1:], across = lax.optimization_barrier((far, wc, along[1:], across))
+    far, wc, ring = lax.optimization_barrier((far, wc, ring))
     parts = (particles, near, far, swap(far, "core"))
-    blocks = [block for pair in zip(along, across) for block in pair]
-
     table_rows = NSHIFT * QROT * CLASSES
     *terms, pool = pl.pallas_call(
         score_kernel,
@@ -356,10 +364,11 @@
             jax.ShapeDtypeStruct((56, NPOOL * ROWS), F32 if j == 0 else BF16) for j in range(NPOOL)
         ]
         + [jax.ShapeDtypeStruct((NPOOL * ROWS, 2 * K), BF16)],
-        in_specs=[SMEM_SPEC] + [VMEM_SPEC] * NBLK + [ANY_SPEC] * 4 + [VMEM_SPEC] * 3,
+        in_specs=[SMEM_SPEC] + [HBM_SPEC] * DEPTH + [ANY_SPEC] * 4 + [VMEM_SPEC] * 3,
         out_specs=[VMEM_SPEC] * (NPOOL + 1),
         scratch_shapes=[
-            VMEM((NBLK * LOCAL * QROT * 32, 128), F32),
+            VMEM((NBLK * BLOCK, 128), BF16),
+            VMEM((NBLK * BLOCK, 128), F32),
             VMEM((table_rows, 256 * STEP_TILES), BF16),
             VMEM((table_rows, 256 * STEP_TILES), BF16),
             VMEM((table_rows, NPOOL * ROWS), F32),
@@ -367,11 +376,12 @@
             VMEM((8, NPOOL * ROWS), jnp.int32),
             VMEM((NPOOL, 8, ROWS), BF16),
             pltpu.SemaphoreType.DMA((2, NPOOL)),
+            pltpu.SemaphoreType.DMA((DEPTH, 2)),
         ],
         compiler_params=params(20),
         name="score",
     )(
-        place, *blocks, *parts,
+        place, *[in_hbm(x) for x in ring], *parts,
         wc, ws, weight,
     )
     terms = trade(terms, POOL)

time: 105 us -> 89.6 us (0.85)
  local copies, waits for them, and re-layouts: 16.6 us -> 1.89 us
    unnamed x67 -> x19, local copies, waits for them, and re-layouts: 16.5 us -> 1.8 us
    ppermute x7, starting transfers between devices: 16.5 us -> 11.6 us  [turn(): return lax.ppermute(x, 'z', [(i, (i + step) % DEPTH) for i in range(DEPTH)])]
    ppermute x13 -> x6, starting transfers between devices: 12.8 us -> 15.5 us  [swap(): return lax.ppermute(x, axis, [(0, 1), (1, 0)])]
    all_to_all x1, starting transfers between devices: 4.34 us -> 6.91 us  [on_device(): sums = lax.all_to_all(sums, BLK, 0, 0, tiled=True)]
    ppermute x13 -> x6, waiting for transfers between devices: 5.19 us -> 5.94 us  [swap(): return lax.ppermute(x, axis, [(0, 1), (1, 0)])]
  transfers between devices with their start and end apart: 22 -> 15, of which waited for: 11 -> 8; matrix products, arithmetic and copies ran while one was open for 0% -> 0% of each run, Pallas kernels for 1% -> 1%
where the time goes in v8:
time: 89.6 us; the launch traced here: 89.2 us
  starting transfers between devices  35.3 us (39%)
  waiting for transfers between devices  23.4 us (26%)
  blocking collectives  15.6 us (17%)
  Pallas kernels  12.1 us (14%)
  local copies, waits for them, and re-layouts  1.89 us (2%)
    all_to_all x1, blocking collectives, on_device(): placed = lax.all_to_all(placed, DOM, 0, 0, tiled=True)  15.6 us
    ppermute x6, starting transfers between devices, swap(): return lax.ppermute(x, axis, [(0, 1), (1, 0)])  15.5 us
    ppermute x7, starting transfers between devices, turn(): return lax.ppermute(x, 'z', [(i, (i + step) % DEPTH) for i in range(DEPTH)])  11.6 us
    all_to_all x1, waiting for transfers between devices, on_device(): sums = lax.all_to_all(sums, BLK, 0, 0, tiled=True)  8.63 us
    ppermute x7, waiting for transfers between devices, turn(): return lax.ppermute(x, 'z', [(i, (i + step) % DEPTH) for i in range(DEPTH)])  7.34 us
    all_to_all x1, starting transfers between devices, on_device(): sums = lax.all_to_all(sums, BLK, 0, 0, tiled=True)  6.91 us
    pallas_call x1, Pallas kernels, on_device(): pl.pallas_call(score_kernel, out_shape=[jax.ShapeDtypeStruct((56, NPOOL *...  6.87 us
    ppermute x6, waiting for transfers between devices, swap(): return lax.ppermute(x, axis, [(0, 1), (1, 0)])  5.94 us
  transfers between devices with their start and end apart: 15, of which 8 were waited for; matrix products, arithmetic and copies ran while one was open for 0% of the time, Pallas kernels for 1%

profile of v8, /device:TPU:1, one launch (start us, length us, event | category | flops | bytes accessed | tf_op | source)
XLA Modules:
  0.0 89.2 jit_solution(17938034741317301195)
XLA Ops:
  0.6 0.0 copy-start.7
  0.6 0.0 copy-start.1
  0.7 0.0 copy-start
  0.7 1.0 %copy-done = bf16[3,12,4096]{2,1,0:T(8,128)(2,1)S(1)} copy-done((bf16[3,12,4096]{2,1,0:T(8,128)(2,1)S(1)}, bf16[3,12,4096]{2,1,0:T(8,128)(2,1)}, u32[]{:S(2)}) %copy-start) | copy-done | bytes 294936
  1.7 0.0 copy-start.2
  1.7 0.7 copy-done.2
  2.3 1.2 %pack.1 = (bf16[288,128]{1,0:T(8,128)(2,1)S(1)}, bf16[136,4096]{1,0:T(8,128)(2,1)S(1)}) custom-call(s32[1]{0:T(128)} %bitcast.1.q_ref, s32[8,128]{1,0:T(8,128)S(1)} %bitcast.13, bf16[3,12,4096]{2,1,0:T(8,128)(2,1)S(1)} %copy-done, bf16[128,4096]{1,0:T(8,128)(2,1)} %particles_hbm.1), custom_call_target="tpu_custom_call" | custom-call | tf_op jit(solution)/shard_map/pack/pallas_call | solution.py:324
  3.6 2.2 %collective-permute-start = (bf16[136,4096]{1,0:T(8,128)(2,1)S(1)}, bf16[136,4096]{1,0:T(8,128)(2,1)S(1)}, u32[]{:S(2)}, u32[]{:S(2)}) collective-permute-start(bf16[136,4096]{1,0:T(8,128)(2,1)S(1)} %get-tuple-element.28.refs_8_), channel_id=1, source_target_pairs={{0,32},{32,0},{1,33},{33,1},{2,34},{34,2},{3,35},{35,3},{4,36},{36... | collective-permute-start | bytes 3342344 | tf_op jit(solution)/shard_map/ppermute | solution.py:300
  5.8 1.2 %collective-permute-start.1 = (bf16[288,128]{1,0:T(8,128)(2,1)S(1)}, bf16[288,128]{1,0:T(8,128)(2,1)S(1)}, u32[]{:S(2)}, u32[]{:S(2)}) collective-permute-start(bf16[288,128]{1,0:T(8,128)(2,1)S(1)} %get-tuple-element.30), channel_id=1, source_target_pairs={{0,1},{1,0},{2,3},{3,2},{4,5},{5,4},{6,7},{7,6},{8,9},{9,8},{10,11... | collective-permute-start | bytes 221192 | tf_op jit(solution)/shard_map/ppermute | solution.py:300
  7.0 2.0 %collective-permute-done.1 = bf16[288,128]{1,0:T(8,128)(2,1)S(1)} collective-permute-done((bf16[288,128]{1,0:T(8,128)(2,1)S(1)}, bf16[288,128]{1,0:T(8,128)(2,1)S(1)}, u32[]{:S(2)}, u32[]{:S(2)}) %collective-permute-start.1) | collective-permute-done | bytes 73760 | tf_op jit(solution)/shard_map/ppermute | solution.py:300
  9.0 0.0 copy-start.3
  9.0 2.0 %collective-permute-start.2 = (bf16[2,288,128]{2,1,0:T(8,128)(2,1)S(1)}, bf16[2,288,128]{2,1,0:T(8,128)(2,1)S(1)}, u32[]{:S(2)}, u32[]{:S(2)}) collective-permute-start(bf16[2,288,128]{2,1,0:T(8,128)(2,1)S(1)} %pad_maximum_fusion.refs_0_), channel_id=1, source_target_pairs={{0,2},{2,4},{4,6},{6,8},{8,10},{10,12},{12,14},{14,0},{1,3},{3,5},... | collective-permute-start | bytes 442376 | tf_op jit(solution)/shard_map/ppermute | solution.py:304
  11.0 4.0 %collective-permute-start.6 = (bf16[2,288,128]{2,1,0:T(8,128)(2,1)S(1)}, bf16[2,288,128]{2,1,0:T(8,128)(2,1)S(1)}, u32[]{:S(2)}, u32[]{:S(2)}) collective-permute-start(bf16[2,288,128]{2,1,0:T(8,128)(2,1)S(1)} %pad_maximum_fusion.refs_0_), channel_id=1, source_target_pairs={{0,14},{2,0},{4,2},{6,4},{8,6},{10,8},{12,10},{14,12},{1,15},{3,1}... | collective-permute-start | bytes 442376 | tf_op jit(solution)/shard_map/ppermute | solution.py:304
  15.1 2.4 %collective-permute-done.2.refs_1_ = bf16[2,288,128]{2,1,0:T(8,128)(2,1)S(1)} collective-permute-done((bf16[2,288,128]{2,1,0:T(8,128)(2,1)S(1)}, bf16[2,288,128]{2,1,0:T(8,128)(2,1)S(1)}, u32[]{:S(2)}, u32[]{:S(2)}) %collective-permute-start.2) | collective-permute-done | bytes 147488 | tf_op jit(solution)/shard_map/ppermute | solution.py:304
  17.5 0.0 copy-start.4
  17.5 0.0 collective-permute-start.3
  17.5 0.0 collective-permute-done.6.refs_7_
  17.5 0.0 copy-start.5
  17.5 2.7 %collective-permute-start.7 = (bf16[2,288,128]{2,1,0:T(8,128)(2,1)S(1)}, bf16[2,288,128]{2,1,0:T(8,128)(2,1)}, u32[]{:S(2)}, u32[]{:S(2)}) collective-permute-start(bf16[2,288,128]{2,1,0:T(8,128)(2,1)S(1)} %collective-permute-done.6.refs_7_), channel_id=1, source_target_pairs={{0,14},{2,0},{4,2},{6,4},{8,6},{10,8},{12,10},{14,12},{1,15},{3,1}... | collective-permute-start | bytes 442376 | tf_op jit(solution)/shard_map/ppermute | solution.py:304
  20.3 2.4 %collective-permute-done.3.refs_2_ = bf16[2,288,128]{2,1,0:T(8,128)(2,1)S(1)} collective-permute-done((bf16[2,288,128]{2,1,0:T(8,128)(2,1)S(1)}, bf16[2,288,128]{2,1,0:T(8,128)(2,1)S(1)}, u32[]{:S(2)}, u32[]{:S(2)}) %collective-permute-start.3) | collective-permute-done | bytes 147488 | tf_op jit(solution)/shard_map/ppermute | solution.py:304
  22.7 0.0 copy-start.6
  22.7 0.0 collective-permute-start.4
  22.7 0.0 collective-permute-done.7.refs_6_
  22.7 2.9 %collective-permute-start.8 = (bf16[2,288,128]{2,1,0:T(8,128)(2,1)}, bf16[2,288,128]{2,1,0:T(8,128)(2,1)}, u32[]{:S(2)}, u32[]{:S(2)}) collective-permute-start(bf16[2,288,128]{2,1,0:T(8,128)(2,1)} %collective-permute-done.7.refs_6_), channel_id=1, source_target_pairs={{0,14},{2,0},{4,2},{6,4},{8,6},{10,8},{12,10},{14,12},{1,15},{3,1}... | collective-permute-start | bytes 442376 | tf_op jit(solution)/shard_map/ppermute | solution.py:304
  25.6 2.4 %collective-permute-done.4.refs_3_ = bf16[2,288,128]{2,1,0:T(8,128)(2,1)} collective-permute-done((bf16[2,288,128]{2,1,0:T(8,128)(2,1)S(1)}, bf16[2,288,128]{2,1,0:T(8,128)(2,1)}, u32[]{:S(2)}, u32[]{:S(2)}) %collective-permute-start.4) | collective-permute-done | bytes 147488 | tf_op jit(solution)/shard_map/ppermute | solution.py:304
  28.0 0.0 copy-done.3
  28.0 0.0 collective-permute-start.5
  28.0 0.0 copy-done.4
  28.0 0.0 copy-done.5
  28.1 0.0 copy-done.6
  28.1 5.4 %collective-permute-start.9 = (bf16[136,4096]{1,0:T(8,128)(2,1)S(1)}, bf16[136,4096]{1,0:T(8,128)(2,1)S(1)}, u32[]{:S(2)}, u32[]{:S(2)}) collective-permute-start(bf16[136,4096]{1,0:T(8,128)(2,1)S(1)} %get-tuple-element.28.refs_8_), channel_id=1, source_target_pairs={{0,16},{16,0},{1,17},{17,1},{2,18},{18,2},{3,19},{19,3},{4,20},{20... | collective-permute-start | bytes 3342344 | tf_op jit(solution)/shard_map/ppermute | solution.py:300
  33.4 0.0 copy-done.7
  33.4 0.1 copy.10.off_ref
  33.5 0.0 copy-done.1
  33.5 0.7 tables.1
  34.2 0.0 collective-permute-done.8.refs_5_
  34.3 0.0 collective-permute-done.5.refs_4_
  34.3 0.0 collective-permute-done.refs_10_
  34.3 5.7 %collective-permute-start.10 = (bf16[136,4096]{1,0:T(8,128)(2,1)S(1)}, bf16[136,4096]{1,0:T(8,128)(2,1)}, u32[]{:S(2)}, u32[]{:S(2)}) collective-permute-start(bf16[136,4096]{1,0:T(8,128)(2,1)S(1)} %collective-permute-done.refs_10_), channel_id=1, source_target_pairs={{0,16},{16,0},{1,17},{17,1},{2,18},{18,2},{3,19},{19,3},{4,20},{20... | collective-permute-start | bytes 3342344 | tf_op jit(solution)/shard_map/ppermute | solution.py:300
  40.0 0.1 pad_add_fusion.index_ref
  40.1 0.0 collective-permute-done.9.refs_9_
  40.1 2.4 %collective-permute-done.10.refs_11_ = bf16[136,4096]{1,0:T(8,128)(2,1)} collective-permute-done((bf16[136,4096]{1,0:T(8,128)(2,1)S(1)}, bf16[136,4096]{1,0:T(8,128)(2,1)}, u32[]{:S(2)}, u32[]{:S(2)}) %collective-permute-start.10) | collective-permute-done | bytes 1114144 | tf_op jit(solution)/shard_map/ppermute | solution.py:300
  42.5 0.0 copy-start.8
  42.5 6.9 %score.1 = (f32[56,512]{1,0:T(8,128)S(1)}, bf16[56,512]{1,0:T(8,128)(2,1)S(1)}, bf16[56,512]{1,0:T(8,128)(2,1)S(1)}, bf16[56,512]{1,0:T(8,128)(2,1)S(1)}, bf16[512,4096]{1,0:T(8,128)(2,1)S(1)}) custom-call(s32[3]{0:T(128)S(1)} %pad_add_fusion.index_ref, bf16[2,288,128]{2,1,0:T(8,128)(2,1)} %copy-done.3, bf16[2,288,128]{2,1,0:T(8,128)(2,1)} %copy-done.4, ...), custom_call_target="tpu_custom_call" | custom-call | tf_op jit(solution)/shard_map/score/pallas_call | solution.py:361
  49.4 0.5 collective-permute-start.11
  49.9 0.5 collective-permute-start.12
  50.4 1.3 %collective-permute-start.13 = (bf16[56,512]{1,0:T(8,128)(2,1)S(1)}, bf16[56,512]{1,0:T(8,128)(2,1)S(1)}, u32[]{:S(2)}, u32[]{:S(2)}) collective-permute-start(bf16[56,512]{1,0:T(8,128)(2,1)S(1)} %get-tuple-element.45), channel_id=1, source_target_pairs={{0,48},{16,32},{32,16},{48,0},{1,49},{17,33},{33,17},{49,1},{2,50}... | collective-permute-start | bytes 172040 | tf_op jit(solution)/shard_map/ppermute | solution.py:313
  51.6 0.0 copy-done.8
  51.6 0.1 convert_reduce_fusion
  51.7 0.0 collective-permute-done.11.x1
  51.7 1.5 %collective-permute-done.12.x2 = bf16[56,512]{1,0:T(8,128)(2,1)S(1)} collective-permute-done((bf16[56,512]{1,0:T(8,128)(2,1)S(1)}, bf16[56,512]{1,0:T(8,128)(2,1)S(1)}, u32[]{:S(2)}, u32[]{:S(2)}) %collective-permute-start.12) | collective-permute-done | bytes 57376 | tf_op jit(solution)/shard_map/ppermute | solution.py:300
  53.2 1.5 %collective-permute-done.13.x3 = bf16[56,512]{1,0:T(8,128)(2,1)S(1)} collective-permute-done((bf16[56,512]{1,0:T(8,128)(2,1)S(1)}, bf16[56,512]{1,0:T(8,128)(2,1)S(1)}, u32[]{:S(2)}, u32[]{:S(2)}) %collective-permute-start.13) | collective-permute-done | bytes 57376 | tf_op jit(solution)/shard_map/ppermute | solution.py:313
  54.7 1.7 %classes.1 = (bf16[16,16,256]{2,1,0:T(8,128)(2,1)}, f32[1,128]{1,0:T(1,128)}) custom-call(s32[1]{0:T(128)} %bitcast.1.q_ref, f32[56,512]{1,0:T(8,128)S(1)} %get-tuple-element.42.x0, bf16[56,512]{1,0:T(8,128)(2,1)S(1)} %collective-permute-done.11.x1, bf16[56,512]{1,0:T(8,128)(2,1)S(1)} %collective-permute-done.12.x2, ...), custom_call_target="tpu_custom_call" | custom-call | tf_op jit(solution)/shard_map/classes/pallas_call | solution.py:389
  56.4 6.9 %all-to-all-start = ((bf16[16,16,256]{2,1,0:T(8,128)(2,1)}), bf16[16,16,256]{2,1,0:T(8,128)(2,1)S(1)}, u32[]{:S(2)}, u32[]{:S(2)}) async-start(bf16[16,16,256]{2,1,0:T(8,128)(2,1)} %get-tuple-element.49), calls=%async_computation | async-start | bytes 262144 | tf_op jit(solution)/shard_map/all_to_all | solution.py:404
  63.4 0.1 dynamic_slice.3
  63.4 8.6 %all-to-all-done.y_ref = bf16[16,16,256]{2,1,0:T(8,128)(2,1)S(1)} async-done(((bf16[16,16,256]{2,1,0:T(8,128)(2,1)}), bf16[16,16,256]{2,1,0:T(8,128)(2,1)S(1)}, u32[]{:S(2)}, u32[]{:S(2)}) %all-to-all-start) | async-done | bytes 131104 | tf_op jit(solution)/shard_map/all_to_all | solution.py:404
  72.1 0.8 place.1
  72.9 15.6 %all_to_all.10.z_ref = bf16[16,8,384]{2,1,0:T(8,128)(2,1)S(1)} all-to-all(bf16[16,8,384]{2,1,0:T(8,128)(2,1)} %place.1), channel_id=1, replica_groups=mesh['xh'=2,'yh'=2,'yl'=2,'core'=2,'z'=8,'xl'=2] {'xh','yh','yl','core'}, dimensions={0} | all-to-all | bytes 196608 | tf_op jit(solution)/shard_map/all_to_all | solution.py:422
  88.4 0.8 means.1
  (3 shorter events, 0.0 us)
Async XLA Ops:
  0.6 32.8 %copy-start.7 = (s32[4,2]{0,1:T(2,128)S(1)}, s32[4,2]{0,1:T(2,128)}, u32[]{:S(2)}) copy-start(s32[4,2]{0,1:T(2,128)} %param.9) | copy-start | bytes 100
  0.6 32.9 %copy-start.1 = (f32[2048]{0:T(1024)S(1)}, f32[2048]{0:T(1024)}, u32[]{:S(2)}) copy-start(f32[2048]{0:T(1024)} %param.8) | copy-start | bytes 24580
  0.7 1.0 %copy-start = (bf16[3,12,4096]{2,1,0:T(8,128)(2,1)S(1)}, bf16[3,12,4096]{2,1,0:T(8,128)(2,1)}, u32[]{:S(2)}) copy-start(bf16[3,12,4096]{2,1,0:T(8,128)(2,1)} %refs_ref.1) | copy-start | bytes 884740
  1.7 0.7 copy-start.2
  3.6 30.7 %collective-permute-start = (bf16[136,4096]{1,0:T(8,128)(2,1)S(1)}, bf16[136,4096]{1,0:T(8,128)(2,1)S(1)}, u32[]{:S(2)}, u32[]{:S(2)}) collective-permute-start(bf16[136,4096]{1,0:T(8,128)(2,1)S(1)} %get-tuple-element.28.refs_8_), channel_id=1, source_target_pairs={{0,32},{32,0},{1,33},{33,1},{2,34},{34,2},{3,35},{35,3},{4,36},{36... | collective-permute-start | bytes 3342344 | tf_op jit(solution)/shard_map/ppermute | solution.py:300
  5.8 3.2 %collective-permute-start.1 = (bf16[288,128]{1,0:T(8,128)(2,1)S(1)}, bf16[288,128]{1,0:T(8,128)(2,1)S(1)}, u32[]{:S(2)}, u32[]{:S(2)}) collective-permute-start(bf16[288,128]{1,0:T(8,128)(2,1)S(1)} %get-tuple-element.30), channel_id=1, source_target_pairs={{0,1},{1,0},{2,3},{3,2},{4,5},{5,4},{6,7},{7,6},{8,9},{9,8},{10,11... | collective-permute-start | bytes 221192 | tf_op jit(solution)/shard_map/ppermute | solution.py:300
  9.0 19.0 %copy-start.3 = (bf16[2,288,128]{2,1,0:T(8,128)(2,1)}, bf16[2,288,128]{2,1,0:T(8,128)(2,1)S(1)}, u32[]{:S(2)}) copy-start(bf16[2,288,128]{2,1,0:T(8,128)(2,1)S(1)} %pad_maximum_fusion.refs_0_) | copy-start | bytes 442372
  9.0 8.5 %collective-permute-start.2 = (bf16[2,288,128]{2,1,0:T(8,128)(2,1)S(1)}, bf16[2,288,128]{2,1,0:T(8,128)(2,1)S(1)}, u32[]{:S(2)}, u32[]{:S(2)}) collective-permute-start(bf16[2,288,128]{2,1,0:T(8,128)(2,1)S(1)} %pad_maximum_fusion.refs_0_), channel_id=1, source_target_pairs={{0,2},{2,4},{4,6},{6,8},{8,10},{10,12},{12,14},{14,0},{1,3},{3,5},... | collective-permute-start | bytes 442376 | tf_op jit(solution)/shard_map/ppermute | solution.py:304
  11.0 6.5 %collective-permute-start.6 = (bf16[2,288,128]{2,1,0:T(8,128)(2,1)S(1)}, bf16[2,288,128]{2,1,0:T(8,128)(2,1)S(1)}, u32[]{:S(2)}, u32[]{:S(2)}) collective-permute-start(bf16[2,288,128]{2,1,0:T(8,128)(2,1)S(1)} %pad_maximum_fusion.refs_0_), channel_id=1, source_target_pairs={{0,14},{2,0},{4,2},{6,4},{8,6},{10,8},{12,10},{14,12},{1,15},{3,1}... | collective-permute-start | bytes 442376 | tf_op jit(solution)/shard_map/ppermute | solution.py:304
  17.5 10.5 %copy-start.4 = (bf16[2,288,128]{2,1,0:T(8,128)(2,1)}, bf16[2,288,128]{2,1,0:T(8,128)(2,1)S(1)}, u32[]{:S(2)}) copy-start(bf16[2,288,128]{2,1,0:T(8,128)(2,1)S(1)} %collective-permute-done.2.refs_1_) | copy-start | bytes 442372
  17.5 5.2 %collective-permute-start.3 = (bf16[2,288,128]{2,1,0:T(8,128)(2,1)S(1)}, bf16[2,288,128]{2,1,0:T(8,128)(2,1)S(1)}, u32[]{:S(2)}, u32[]{:S(2)}) collective-permute-start(bf16[2,288,128]{2,1,0:T(8,128)(2,1)S(1)} %collective-permute-done.2.refs_1_), channel_id=1, source_target_pairs={{0,2},{2,4},{4,6},{6,8},{8,10},{10,12},{12,14},{14,0},{1,3},{3,5},... | collective-permute-start | bytes 442376 | tf_op jit(solution)/shard_map/ppermute | solution.py:304
  17.5 10.5 %copy-start.5 = (bf16[2,288,128]{2,1,0:T(8,128)(2,1)}, bf16[2,288,128]{2,1,0:T(8,128)(2,1)S(1)}, u32[]{:S(2)}) copy-start(bf16[2,288,128]{2,1,0:T(8,128)(2,1)S(1)} %collective-permute-done.6.refs_7_) | copy-start | bytes 442372
  17.5 5.2 %collective-permute-start.7 = (bf16[2,288,128]{2,1,0:T(8,128)(2,1)S(1)}, bf16[2,288,128]{2,1,0:T(8,128)(2,1)}, u32[]{:S(2)}, u32[]{:S(2)}) collective-permute-start(bf16[2,288,128]{2,1,0:T(8,128)(2,1)S(1)} %collective-permute-done.6.refs_7_), channel_id=1, source_target_pairs={{0,14},{2,0},{4,2},{6,4},{8,6},{10,8},{12,10},{14,12},{1,15},{3,1}... | collective-permute-start | bytes 442376 | tf_op jit(solution)/shard_map/ppermute | solution.py:304
  22.7 5.3 %copy-start.6 = (bf16[2,288,128]{2,1,0:T(8,128)(2,1)}, bf16[2,288,128]{2,1,0:T(8,128)(2,1)S(1)}, u32[]{:S(2)}) copy-start(bf16[2,288,128]{2,1,0:T(8,128)(2,1)S(1)} %collective-permute-done.3.refs_2_) | copy-start | bytes 442372
  22.7 5.3 %collective-permute-start.4 = (bf16[2,288,128]{2,1,0:T(8,128)(2,1)S(1)}, bf16[2,288,128]{2,1,0:T(8,128)(2,1)}, u32[]{:S(2)}, u32[]{:S(2)}) collective-permute-start(bf16[2,288,128]{2,1,0:T(8,128)(2,1)S(1)} %collective-permute-done.3.refs_2_), channel_id=1, source_target_pairs={{0,2},{2,4},{4,6},{6,8},{8,10},{10,12},{12,14},{14,0},{1,3},{3,5},... | collective-permute-start | bytes 442376 | tf_op jit(solution)/shard_map/ppermute | solution.py:304
  22.7 11.5 %collective-permute-start.8 = (bf16[2,288,128]{2,1,0:T(8,128)(2,1)}, bf16[2,288,128]{2,1,0:T(8,128)(2,1)}, u32[]{:S(2)}, u32[]{:S(2)}) collective-permute-start(bf16[2,288,128]{2,1,0:T(8,128)(2,1)} %collective-permute-done.7.refs_6_), channel_id=1, source_target_pairs={{0,14},{2,0},{4,2},{6,4},{8,6},{10,8},{12,10},{14,12},{1,15},{3,1}... | collective-permute-start | bytes 442376 | tf_op jit(solution)/shard_map/ppermute | solution.py:304
  28.0 6.2 %collective-permute-start.5 = (bf16[2,288,128]{2,1,0:T(8,128)(2,1)}, bf16[2,288,128]{2,1,0:T(8,128)(2,1)}, u32[]{:S(2)}, u32[]{:S(2)}) collective-permute-start(bf16[2,288,128]{2,1,0:T(8,128)(2,1)} %collective-permute-done.4.refs_3_), channel_id=1, source_target_pairs={{0,2},{2,4},{4,6},{6,8},{8,10},{10,12},{12,14},{14,0},{1,3},{3,5},... | collective-permute-start | bytes 442376 | tf_op jit(solution)/shard_map/ppermute | solution.py:304
  28.1 12.0 %collective-permute-start.9 = (bf16[136,4096]{1,0:T(8,128)(2,1)S(1)}, bf16[136,4096]{1,0:T(8,128)(2,1)S(1)}, u32[]{:S(2)}, u32[]{:S(2)}) collective-permute-start(bf16[136,4096]{1,0:T(8,128)(2,1)S(1)} %get-tuple-element.28.refs_8_), channel_id=1, source_target_pairs={{0,16},{16,0},{1,17},{17,1},{2,18},{18,2},{3,19},{19,3},{4,20},{20... | collective-permute-start | bytes 3342344 | tf_op jit(solution)/shard_map/ppermute | solution.py:300
  34.3 8.2 %collective-permute-start.10 = (bf16[136,4096]{1,0:T(8,128)(2,1)S(1)}, bf16[136,4096]{1,0:T(8,128)(2,1)}, u32[]{:S(2)}, u32[]{:S(2)}) collective-permute-start(bf16[136,4096]{1,0:T(8,128)(2,1)S(1)} %collective-permute-done.refs_10_), channel_id=1, source_target_pairs={{0,16},{16,0},{1,17},{17,1},{2,18},{18,2},{3,19},{19,3},{4,20},{20... | collective-permute-start | bytes 3342344 | tf_op jit(solution)/shard_map/ppermute | solution.py:300
  42.5 9.1 %copy-start.8 = (s32[48]{0:T(128)S(1)}, s32[48]{0:T(128)}, u32[]{:S(2)}) copy-start(s32[48]{0:T(128)} %param.11) | copy-start | bytes 580
  49.4 2.3 %collective-permute-start.11 = (bf16[56,512]{1,0:T(8,128)(2,1)S(1)}, bf16[56,512]{1,0:T(8,128)(2,1)S(1)}, u32[]{:S(2)}, u32[]{:S(2)}) collective-permute-start(bf16[56,512]{1,0:T(8,128)(2,1)S(1)} %get-tuple-element.43), channel_id=1, source_target_pairs={{0,16},{16,0},{1,17},{17,1},{2,18},{18,2},{3,19},{19,3},{4,20},{20... | collective-permute-start | bytes 172040 | tf_op jit(solution)/shard_map/ppermute | solution.py:300
  49.9 3.4 %collective-permute-start.12 = (bf16[56,512]{1,0:T(8,128)(2,1)S(1)}, bf16[56,512]{1,0:T(8,128)(2,1)S(1)}, u32[]{:S(2)}, u32[]{:S(2)}) collective-permute-start(bf16[56,512]{1,0:T(8,128)(2,1)S(1)} %get-tuple-element.44), channel_id=1, source_target_pairs={{0,32},{32,0},{1,33},{33,1},{2,34},{34,2},{3,35},{35,3},{4,36},{36... | collective-permute-start | bytes 172040 | tf_op jit(solution)/shard_map/ppermute | solution.py:300
  50.4 4.4 %collective-permute-start.13 = (bf16[56,512]{1,0:T(8,128)(2,1)S(1)}, bf16[56,512]{1,0:T(8,128)(2,1)S(1)}, u32[]{:S(2)}, u32[]{:S(2)}) collective-permute-start(bf16[56,512]{1,0:T(8,128)(2,1)S(1)} %get-tuple-element.45), channel_id=1, source_target_pairs={{0,48},{16,32},{32,16},{48,0},{1,49},{17,33},{33,17},{49,1},{2,50}... | collective-permute-start | bytes 172040 | tf_op jit(solution)/shard_map/ppermute | solution.py:313
  56.4 15.6 %all-to-all-start = ((bf16[16,16,256]{2,1,0:T(8,128)(2,1)}), bf16[16,16,256]{2,1,0:T(8,128)(2,1)S(1)}, u32[]{:S(2)}, u32[]{:S(2)}) async-start(bf16[16,16,256]{2,1,0:T(8,128)(2,1)} %get-tuple-element.49), calls=%async_computation | async-start | bytes 262144 | tf_op jit(solution)/shard_map/all_to_all | solution.py:404

commit v9 on v8

--- a/solution.py
+++ b/solution.py
@@ -336,15 +336,15 @@
         ],
         compiler_params=params(8),
         name="pack",
-    )(q, candidates.T, references, in_hbm(particles))
+    )(q, in_hbm(candidates.T), in_hbm(references), in_hbm(particles))
     far = swap(particles, "yl")
     ring = [None] * DEPTH
-    ring[0] = up = down = jnp.stack([packed, swap(packed, "xl")])
+    near, beside = lax.optimization_barrier((swap(particles, "core"), swap(packed, "xl")))
+    ring[0] = up = down = jnp.stack([packed, beside])
     for k in range(1, DEPTH // 2):
         ring[k] = up = turn(up, 1)
         ring[DEPTH - k] = down = turn(down, -1)
     ring[DEPTH // 2] = turn(up, 1)
-    near = swap(particles, "core")
     flat = jax.ShapeDtypeStruct((NSHIFT * 16, 128), F32)
     cosine, sine, wc, ws = pl.pallas_call(
         tables_kernel,
@@ -355,7 +355,10 @@
         cost_estimate=pl.CostEstimate(flops=1 * 10**9, bytes_accessed=3 * 10**6, transcendentals=0),
         name="tables",
     )(offsets, weight)
-    far, wc, ring = lax.optimization_barrier((far, wc, ring))
+    last = DEPTH // 2
+    far, wc, ring[last - 1], ring[last + 1] = lax.optimization_barrier(
+        (far, wc, ring[last - 1], ring[last + 1])
+    )
     parts = (particles, near, far, swap(far, "core"))
     table_rows = NSHIFT * QROT * CLASSES
     *terms, pool = pl.pallas_call(

time: 89.6 us -> 88.6 us (0.989)
  starting transfers between devices: 35.3 us -> 24.4 us
  waiting for transfers between devices: 23.4 us -> 33.9 us
  local copies, waits for them, and re-layouts: 1.89 us -> 0.2 us
  Pallas kernels: 12.1 us -> 13.1 us
    ppermute x6, starting transfers between devices: 15.5 us -> 7.06 us  [swap(): return lax.ppermute(x, axis, [(0, 1), (1, 0)])]
    ppermute x7, waiting for transfers between devices: 7.34 us -> 13.6 us  [turn(): return lax.ppermute(x, 'z', [(i, (i + step) % DEPTH) for i in range(DEPTH)])]
    ppermute x6, waiting for transfers between devices: 5.94 us -> 10.2 us  [swap(): return lax.ppermute(x, axis, [(0, 1), (1, 0)])]
    unnamed x19 -> x13, local copies, waits for them, and re-layouts: 1.8 us -> 0.12 us
    ppermute x7, starting transfers between devices: 11.6 us -> 10.6 us  [turn(): return lax.ppermute(x, 'z', [(i, (i + step) % DEPTH) for i in range(DEPTH)])]
    pallas_call x1, Pallas kernels: 1.23 us -> 2.25 us  [on_device(): pl.pallas_call(pack_kernel, out_shape=(jax.ShapeDtypeStruct((BLOCK, 128),...]
where the time goes in v9:
time: 88.6 us; the launch traced here: 88.3 us
  waiting for transfers between devices  33.9 us (38%)
  starting transfers between devices  24.4 us (28%)
  blocking collectives  15.8 us (18%)
  Pallas kernels  13.1 us (15%)
    all_to_all x1, blocking collectives, on_device(): placed = lax.all_to_all(placed, DOM, 0, 0, tiled=True)  15.8 us
    ppermute x7, waiting for transfers between devices, turn(): return lax.ppermute(x, 'z', [(i, (i + step) % DEPTH) for i in range(DEPTH)])  13.6 us
    ppermute x7, starting transfers between devices, turn(): return lax.ppermute(x, 'z', [(i, (i + step) % DEPTH) for i in range(DEPTH)])  10.6 us
    ppermute x6, waiting for transfers between devices, swap(): return lax.ppermute(x, axis, [(0, 1), (1, 0)])  10.2 us
    all_to_all x1, waiting for transfers between devices, on_device(): sums = lax.all_to_all(sums, BLK, 0, 0, tiled=True)  8.4 us
    ppermute x6, starting transfers between devices, swap(): return lax.ppermute(x, axis, [(0, 1), (1, 0)])  7.06 us
    pallas_call x1, Pallas kernels, on_device(): pl.pallas_call(score_kernel, out_shape=[jax.ShapeDtypeStruct((56, NPOOL *...  6.88 us
    all_to_all x1, starting transfers between devices, on_device(): sums = lax.all_to_all(sums, BLK, 0, 0, tiled=True)  6.33 us
  transfers between devices with their start and end apart: 15, of which 8 were waited for; matrix products, arithmetic and copies ran while one was open for 0% of the time, Pallas kernels for 1%

profile of v9, /device:TPU:1, one launch (start us, length us, event | category | flops | bytes accessed | tf_op | source)
XLA Modules:
  0.0 88.3 jit_solution(975699596416660310)
XLA Ops:
  0.6 0.0 copy-start.4
  0.6 0.0 copy-start
  0.7 2.2 %pack.1 = (bf16[288,128]{1,0:T(8,128)(2,1)S(1)}, bf16[136,4096]{1,0:T(8,128)(2,1)S(1)}) custom-call(s32[1]{0:T(128)} %bitcast.1.q_ref, s32[8,128]{1,0:T(8,128)} %bitcast.14, bf16[3,12,4096]{2,1,0:T(8,128)(2,1)} %refs_ref.1, bf16[128,4096]{1,0:T(8,128)(2,1)} %particles_hbm.1), custom_call_target="tpu_custom_call" | custom-call | tf_op jit(solution)/shard_map/pack/pallas_call | solution.py:324
  2.9 3.3 %collective-permute-start = (bf16[136,4096]{1,0:T(8,128)(2,1)S(1)}, bf16[136,4096]{1,0:T(8,128)(2,1)S(1)}, u32[]{:S(2)}, u32[]{:S(2)}) collective-permute-start(bf16[136,4096]{1,0:T(8,128)(2,1)S(1)} %get-tuple-element.25.refs_8_), channel_id=1, source_target_pairs={{0,16},{16,0},{1,17},{17,1},{2,18},{18,2},{3,19},{19,3},{4,20},{20... | collective-permute-start | bytes 3342344 | tf_op jit(solution)/shard_map/ppermute | solution.py:300
  6.2 0.0 collective-permute-start.4
  6.2 0.8 collective-permute-start.1
  7.0 2.9 %collective-permute-done.1 = bf16[288,128]{1,0:T(8,128)(2,1)S(1)} collective-permute-done((bf16[288,128]{1,0:T(8,128)(2,1)S(1)}, bf16[288,128]{1,0:T(8,128)(2,1)S(1)}, u32[]{:S(2)}, u32[]{:S(2)}) %collective-permute-start.1) | collective-permute-done | bytes 73760 | tf_op jit(solution)/shard_map/ppermute | solution.py:300
  9.9 0.0 collective-permute-done.refs_9_
  9.9 0.0 copy-start.1
  10.0 1.1 %collective-permute-start.2 = (bf16[2,288,128]{2,1,0:T(8,128)(2,1)S(1)}, bf16[2,288,128]{2,1,0:T(8,128)(2,1)S(1)}, u32[]{:S(2)}, u32[]{:S(2)}) collective-permute-start(bf16[2,288,128]{2,1,0:T(8,128)(2,1)S(1)} %pad_maximum_fusion.refs_0_), channel_id=1, source_target_pairs={{0,2},{2,4},{4,6},{6,8},{8,10},{10,12},{12,14},{14,0},{1,3},{3,5},... | collective-permute-start | bytes 442376 | tf_op jit(solution)/shard_map/ppermute | solution.py:304
  11.1 4.0 %collective-permute-start.6 = (bf16[2,288,128]{2,1,0:T(8,128)(2,1)S(1)}, bf16[2,288,128]{2,1,0:T(8,128)(2,1)S(1)}, u32[]{:S(2)}, u32[]{:S(2)}) collective-permute-start(bf16[2,288,128]{2,1,0:T(8,128)(2,1)S(1)} %pad_maximum_fusion.refs_0_), channel_id=1, source_target_pairs={{0,14},{2,0},{4,2},{6,4},{8,6},{10,8},{12,10},{14,12},{1,15},{3,1}... | collective-permute-start | bytes 442376 | tf_op jit(solution)/shard_map/ppermute | solution.py:304
  15.1 2.9 %collective-permute-done.2.refs_1_ = bf16[2,288,128]{2,1,0:T(8,128)(2,1)S(1)} collective-permute-done((bf16[2,288,128]{2,1,0:T(8,128)(2,1)S(1)}, bf16[2,288,128]{2,1,0:T(8,128)(2,1)S(1)}, u32[]{:S(2)}, u32[]{:S(2)}) %collective-permute-start.2) | collective-permute-done | bytes 147488 | tf_op jit(solution)/shard_map/ppermute | solution.py:304
  18.0 0.0 copy-start.2
  18.0 0.0 collective-permute-start.3
  18.0 0.0 collective-permute-done.6.refs_7_
  18.0 0.0 copy-start.3
  18.0 2.7 %collective-permute-start.7 = (bf16[2,288,128]{2,1,0:T(8,128)(2,1)S(1)}, bf16[2,288,128]{2,1,0:T(8,128)(2,1)}, u32[]{:S(2)}, u32[]{:S(2)}) collective-permute-start(bf16[2,288,128]{2,1,0:T(8,128)(2,1)S(1)} %collective-permute-done.6.refs_7_), channel_id=1, source_target_pairs={{0,14},{2,0},{4,2},{6,4},{8,6},{10,8},{12,10},{14,12},{1,15},{3,1}... | collective-permute-start | bytes 442376 | tf_op jit(solution)/shard_map/ppermute | solution.py:304
  20.6 2.6 %collective-permute-done.3.refs_2_ = bf16[2,288,128]{2,1,0:T(8,128)(2,1)} collective-permute-done((bf16[2,288,128]{2,1,0:T(8,128)(2,1)S(1)}, bf16[2,288,128]{2,1,0:T(8,128)(2,1)}, u32[]{:S(2)}, u32[]{:S(2)}) %collective-permute-start.3) | collective-permute-done | bytes 147488 | tf_op jit(solution)/shard_map/ppermute | solution.py:304
  23.3 0.0 collective-permute-start.5
  23.3 0.0 collective-permute-done.7.refs_6_
  23.3 0.0 copy-done.1
  23.3 0.0 copy-done.2
  23.3 0.0 copy-done.3
  23.3 2.7 %collective-permute-start.8 = (bf16[2,288,128]{2,1,0:T(8,128)(2,1)}, bf16[2,288,128]{2,1,0:T(8,128)(2,1)}, u32[]{:S(2)}, u32[]{:S(2)}) collective-permute-start(bf16[2,288,128]{2,1,0:T(8,128)(2,1)} %collective-permute-done.7.refs_6_), channel_id=1, source_target_pairs={{0,14},{2,0},{4,2},{6,4},{8,6},{10,8},{12,10},{14,12},{1,15},{3,1}... | collective-permute-start | bytes 442376 | tf_op jit(solution)/shard_map/ppermute | solution.py:304
  26.0 0.0 copy-done.4
  26.1 0.1 copy.10.off_ref
  26.1 0.0 copy-done
  26.1 0.7 tables.1
  26.9 5.6 %collective-permute-done.4.refs_10_ = bf16[136,4096]{1,0:T(8,128)(2,1)S(1)} collective-permute-done((bf16[136,4096]{1,0:T(8,128)(2,1)S(1)}, bf16[136,4096]{1,0:T(8,128)(2,1)S(1)}, u32[]{:S(2)}, u32[]{:S(2)}) %collective-permute-start.4) | collective-permute-done | bytes 1114144 | tf_op jit(solution)/shard_map/ppermute | solution.py:300
  32.5 0.0 collective-permute-done.5.refs_3_
  32.5 0.0 collective-permute-done.8.refs_5_
  32.5 0.8 collective-permute-start.10
  33.2 0.0 collective-permute-start.9
  33.3 0.1 pad_add_fusion.index_ref
  33.3 8.1 %collective-permute-done.9.refs_4_ = bf16[2,288,128]{2,1,0:T(8,128)(2,1)} collective-permute-done((bf16[2,288,128]{2,1,0:T(8,128)(2,1)}, bf16[2,288,128]{2,1,0:T(8,128)(2,1)}, u32[]{:S(2)}, u32[]{:S(2)}) %collective-permute-start.9) | collective-permute-done | bytes 147488 | tf_op jit(solution)/shard_map/ppermute | solution.py:304
  41.4 0.0 collective-permute-done.10.refs_11_
  41.4 0.0 copy-start.5
  41.4 6.9 %score.1 = (f32[56,512]{1,0:T(8,128)S(1)}, bf16[56,512]{1,0:T(8,128)(2,1)S(1)}, bf16[56,512]{1,0:T(8,128)(2,1)S(1)}, bf16[56,512]{1,0:T(8,128)(2,1)S(1)}, bf16[512,4096]{1,0:T(8,128)(2,1)S(1)}) custom-call(s32[3]{0:T(128)S(1)} %pad_add_fusion.index_ref, bf16[2,288,128]{2,1,0:T(8,128)(2,1)} %copy-done.1, bf16[2,288,128]{2,1,0:T(8,128)(2,1)} %copy-done.2, ...), custom_call_target="tpu_custom_call" | custom-call | tf_op jit(solution)/shard_map/score/pallas_call | solution.py:364
  48.3 0.9 collective-permute-start.11
  49.2 1.3 %collective-permute-start.12 = (bf16[56,512]{1,0:T(8,128)(2,1)S(1)}, bf16[56,512]{1,0:T(8,128)(2,1)S(1)}, u32[]{:S(2)}, u32[]{:S(2)}) collective-permute-start(bf16[56,512]{1,0:T(8,128)(2,1)S(1)} %get-tuple-element.36), channel_id=1, source_target_pairs={{0,32},{32,0},{1,33},{33,1},{2,34},{34,2},{3,35},{35,3},{4,36},{36... | collective-permute-start | bytes 172040 | tf_op jit(solution)/shard_map/ppermute | solution.py:300
  50.5 0.4 collective-permute-start.13
  50.9 0.0 copy-done.5
  50.9 0.1 convert_reduce_fusion
  51.0 0.0 collective-permute-done.11.x1
  51.0 1.6 %collective-permute-done.12.x2 = bf16[56,512]{1,0:T(8,128)(2,1)S(1)} collective-permute-done((bf16[56,512]{1,0:T(8,128)(2,1)S(1)}, bf16[56,512]{1,0:T(8,128)(2,1)S(1)}, u32[]{:S(2)}, u32[]{:S(2)}) %collective-permute-start.12) | collective-permute-done | bytes 57376 | tf_op jit(solution)/shard_map/ppermute | solution.py:300
  52.7 1.7 %collective-permute-done.13.x3 = bf16[56,512]{1,0:T(8,128)(2,1)S(1)} collective-permute-done((bf16[56,512]{1,0:T(8,128)(2,1)S(1)}, bf16[56,512]{1,0:T(8,128)(2,1)S(1)}, u32[]{:S(2)}, u32[]{:S(2)}) %collective-permute-start.13) | collective-permute-done | bytes 57376 | tf_op jit(solution)/shard_map/ppermute | solution.py:313
  54.4 1.7 %classes.1 = (bf16[16,16,256]{2,1,0:T(8,128)(2,1)}, f32[1,128]{1,0:T(1,128)}) custom-call(s32[1]{0:T(128)} %bitcast.1.q_ref, f32[56,512]{1,0:T(8,128)S(1)} %get-tuple-element.34.x0, bf16[56,512]{1,0:T(8,128)(2,1)S(1)} %collective-permute-done.11.x1, bf16[56,512]{1,0:T(8,128)(2,1)S(1)} %collective-permute-done.12.x2, ...), custom_call_target="tpu_custom_call" | custom-call | tf_op jit(solution)/shard_map/classes/pallas_call | solution.py:392
  56.1 6.3 %all-to-all-start = ((bf16[16,16,256]{2,1,0:T(8,128)(2,1)}), bf16[16,16,256]{2,1,0:T(8,128)(2,1)S(1)}, u32[]{:S(2)}, u32[]{:S(2)}) async-start(bf16[16,16,256]{2,1,0:T(8,128)(2,1)} %get-tuple-element.41), calls=%async_computation | async-start | bytes 262144 | tf_op jit(solution)/shard_map/all_to_all | solution.py:407
  62.4 0.1 dynamic_slice.3
  62.5 8.4 %all-to-all-done.y_ref = bf16[16,16,256]{2,1,0:T(8,128)(2,1)S(1)} async-done(((bf16[16,16,256]{2,1,0:T(8,128)(2,1)}), bf16[16,16,256]{2,1,0:T(8,128)(2,1)S(1)}, u32[]{:S(2)}, u32[]{:S(2)}) %all-to-all-start) | async-done | bytes 131104 | tf_op jit(solution)/shard_map/all_to_all | solution.py:407
  70.9 0.8 place.1
  71.7 15.8 %all_to_all.10.z_ref = bf16[16,8,384]{2,1,0:T(8,128)(2,1)S(1)} all-to-all(bf16[16,8,384]{2,1,0:T(8,128)(2,1)} %place.1), channel_id=1, replica_groups=mesh['xh'=2,'yh'=2,'yl'=2,'core'=2,'z'=8,'xl'=2] {'xh','yh','yl','core'}, dimensions={0} | all-to-all | bytes 196608 | tf_op jit(solution)/shard_map/all_to_all | solution.py:425
  87.5 0.8 means.1
  (3 shorter events, 0.0 us)
Async XLA Ops:
  0.6 25.4 %copy-start.4 = (s32[4,2]{0,1:T(2,128)S(1)}, s32[4,2]{0,1:T(2,128)}, u32[]{:S(2)}) copy-start(s32[4,2]{0,1:T(2,128)} %param.9) | copy-start | bytes 100
  0.6 25.5 %copy-start = (f32[2048]{0:T(1024)S(1)}, f32[2048]{0:T(1024)}, u32[]{:S(2)}) copy-start(f32[2048]{0:T(1024)} %param.8) | copy-start | bytes 24580
  2.9 7.0 %collective-permute-start = (bf16[136,4096]{1,0:T(8,128)(2,1)S(1)}, bf16[136,4096]{1,0:T(8,128)(2,1)S(1)}, u32[]{:S(2)}, u32[]{:S(2)}) collective-permute-start(bf16[136,4096]{1,0:T(8,128)(2,1)S(1)} %get-tuple-element.25.refs_8_), channel_id=1, source_target_pairs={{0,16},{16,0},{1,17},{17,1},{2,18},{18,2},{3,19},{19,3},{4,20},{20... | collective-permute-start | bytes 3342344 | tf_op jit(solution)/shard_map/ppermute | solution.py:300
  6.2 26.2 %collective-permute-start.4 = (bf16[136,4096]{1,0:T(8,128)(2,1)S(1)}, bf16[136,4096]{1,0:T(8,128)(2,1)S(1)}, u32[]{:S(2)}, u32[]{:S(2)}) collective-permute-start(bf16[136,4096]{1,0:T(8,128)(2,1)S(1)} %get-tuple-element.25.refs_8_), channel_id=1, source_target_pairs={{0,32},{32,0},{1,33},{33,1},{2,34},{34,2},{3,35},{35,3},{4,36},{36... | collective-permute-start | bytes 3342344 | tf_op jit(solution)/shard_map/ppermute | solution.py:300
  6.2 3.7 %collective-permute-start.1 = (bf16[288,128]{1,0:T(8,128)(2,1)S(1)}, bf16[288,128]{1,0:T(8,128)(2,1)S(1)}, u32[]{:S(2)}, u32[]{:S(2)}) collective-permute-start(bf16[288,128]{1,0:T(8,128)(2,1)S(1)} %get-tuple-element.24), channel_id=1, source_target_pairs={{0,1},{1,0},{2,3},{3,2},{4,5},{5,4},{6,7},{7,6},{8,9},{9,8},{10,11... | collective-permute-start | bytes 221192 | tf_op jit(solution)/shard_map/ppermute | solution.py:300
  9.9 13.3 %copy-start.1 = (bf16[2,288,128]{2,1,0:T(8,128)(2,1)}, bf16[2,288,128]{2,1,0:T(8,128)(2,1)S(1)}, u32[]{:S(2)}) copy-start(bf16[2,288,128]{2,1,0:T(8,128)(2,1)S(1)} %pad_maximum_fusion.refs_0_) | copy-start | bytes 442372
  10.0 8.0 %collective-permute-start.2 = (bf16[2,288,128]{2,1,0:T(8,128)(2,1)S(1)}, bf16[2,288,128]{2,1,0:T(8,128)(2,1)S(1)}, u32[]{:S(2)}, u32[]{:S(2)}) collective-permute-start(bf16[2,288,128]{2,1,0:T(8,128)(2,1)S(1)} %pad_maximum_fusion.refs_0_), channel_id=1, source_target_pairs={{0,2},{2,4},{4,6},{6,8},{8,10},{10,12},{12,14},{14,0},{1,3},{3,5},... | collective-permute-start | bytes 442376 | tf_op jit(solution)/shard_map/ppermute | solution.py:304
  11.1 6.9 %collective-permute-start.6 = (bf16[2,288,128]{2,1,0:T(8,128)(2,1)S(1)}, bf16[2,288,128]{2,1,0:T(8,128)(2,1)S(1)}, u32[]{:S(2)}, u32[]{:S(2)}) collective-permute-start(bf16[2,288,128]{2,1,0:T(8,128)(2,1)S(1)} %pad_maximum_fusion.refs_0_), channel_id=1, source_target_pairs={{0,14},{2,0},{4,2},{6,4},{8,6},{10,8},{12,10},{14,12},{1,15},{3,1}... | collective-permute-start | bytes 442376 | tf_op jit(solution)/shard_map/ppermute | solution.py:304
  18.0 5.3 %copy-start.2 = (bf16[2,288,128]{2,1,0:T(8,128)(2,1)}, bf16[2,288,128]{2,1,0:T(8,128)(2,1)S(1)}, u32[]{:S(2)}) copy-start(bf16[2,288,128]{2,1,0:T(8,128)(2,1)S(1)} %collective-permute-done.2.refs_1_) | copy-start | bytes 442372
  18.0 5.3 %collective-permute-start.3 = (bf16[2,288,128]{2,1,0:T(8,128)(2,1)S(1)}, bf16[2,288,128]{2,1,0:T(8,128)(2,1)}, u32[]{:S(2)}, u32[]{:S(2)}) collective-permute-start(bf16[2,288,128]{2,1,0:T(8,128)(2,1)S(1)} %collective-permute-done.2.refs_1_), channel_id=1, source_target_pairs={{0,2},{2,4},{4,6},{6,8},{8,10},{10,12},{12,14},{14,0},{1,3},{3,5},... | collective-permute-start | bytes 442376 | tf_op jit(solution)/shard_map/ppermute | solution.py:304
  18.0 5.3 %copy-start.3 = (bf16[2,288,128]{2,1,0:T(8,128)(2,1)}, bf16[2,288,128]{2,1,0:T(8,128)(2,1)S(1)}, u32[]{:S(2)}) copy-start(bf16[2,288,128]{2,1,0:T(8,128)(2,1)S(1)} %collective-permute-done.6.refs_7_) | copy-start | bytes 442372
  18.0 5.3 %collective-permute-start.7 = (bf16[2,288,128]{2,1,0:T(8,128)(2,1)S(1)}, bf16[2,288,128]{2,1,0:T(8,128)(2,1)}, u32[]{:S(2)}, u32[]{:S(2)}) collective-permute-start(bf16[2,288,128]{2,1,0:T(8,128)(2,1)S(1)} %collective-permute-done.6.refs_7_), channel_id=1, source_target_pairs={{0,14},{2,0},{4,2},{6,4},{8,6},{10,8},{12,10},{14,12},{1,15},{3,1}... | collective-permute-start | bytes 442376 | tf_op jit(solution)/shard_map/ppermute | solution.py:304
  23.3 9.2 %collective-permute-start.5 = (bf16[2,288,128]{2,1,0:T(8,128)(2,1)}, bf16[2,288,128]{2,1,0:T(8,128)(2,1)}, u32[]{:S(2)}, u32[]{:S(2)}) collective-permute-start(bf16[2,288,128]{2,1,0:T(8,128)(2,1)} %collective-permute-done.3.refs_2_), channel_id=1, source_target_pairs={{0,2},{2,4},{4,6},{6,8},{8,10},{10,12},{12,14},{14,0},{1,3},{3,5},... | collective-permute-start | bytes 442376 | tf_op jit(solution)/shard_map/ppermute | solution.py:304
  23.3 9.2 %collective-permute-start.8 = (bf16[2,288,128]{2,1,0:T(8,128)(2,1)}, bf16[2,288,128]{2,1,0:T(8,128)(2,1)}, u32[]{:S(2)}, u32[]{:S(2)}) collective-permute-start(bf16[2,288,128]{2,1,0:T(8,128)(2,1)} %collective-permute-done.7.refs_6_), channel_id=1, source_target_pairs={{0,14},{2,0},{4,2},{6,4},{8,6},{10,8},{12,10},{14,12},{1,15},{3,1}... | collective-permute-start | bytes 442376 | tf_op jit(solution)/shard_map/ppermute | solution.py:304
  32.5 9.0 %collective-permute-start.10 = (bf16[136,4096]{1,0:T(8,128)(2,1)S(1)}, bf16[136,4096]{1,0:T(8,128)(2,1)}, u32[]{:S(2)}, u32[]{:S(2)}) collective-permute-start(bf16[136,4096]{1,0:T(8,128)(2,1)S(1)} %collective-permute-done.4.refs_10_), channel_id=1, source_target_pairs={{0,16},{16,0},{1,17},{17,1},{2,18},{18,2},{3,19},{19,3},{4,20},{20... | collective-permute-start | bytes 3342344 | tf_op jit(solution)/shard_map/ppermute | solution.py:300
  33.2 8.2 %collective-permute-start.9 = (bf16[2,288,128]{2,1,0:T(8,128)(2,1)}, bf16[2,288,128]{2,1,0:T(8,128)(2,1)}, u32[]{:S(2)}, u32[]{:S(2)}) collective-permute-start(bf16[2,288,128]{2,1,0:T(8,128)(2,1)} %collective-permute-done.5.refs_3_), channel_id=1, source_target_pairs={{0,2},{2,4},{4,6},{6,8},{8,10},{10,12},{12,14},{14,0},{1,3},{3,5},... | collective-permute-start | bytes 442376 | tf_op jit(solution)/shard_map/ppermute | solution.py:304
  41.4 9.5 %copy-start.5 = (s32[48]{0:T(128)S(1)}, s32[48]{0:T(128)}, u32[]{:S(2)}) copy-start(s32[48]{0:T(128)} %param.11) | copy-start | bytes 580
  48.3 2.7 %collective-permute-start.11 = (bf16[56,512]{1,0:T(8,128)(2,1)S(1)}, bf16[56,512]{1,0:T(8,128)(2,1)S(1)}, u32[]{:S(2)}, u32[]{:S(2)}) collective-permute-start(bf16[56,512]{1,0:T(8,128)(2,1)S(1)} %get-tuple-element.35), channel_id=1, source_target_pairs={{0,16},{16,0},{1,17},{17,1},{2,18},{18,2},{3,19},{19,3},{4,20},{20... | collective-permute-start | bytes 172040 | tf_op jit(solution)/shard_map/ppermute | solution.py:300
  49.2 3.5 %collective-permute-start.12 = (bf16[56,512]{1,0:T(8,128)(2,1)S(1)}, bf16[56,512]{1,0:T(8,128)(2,1)S(1)}, u32[]{:S(2)}, u32[]{:S(2)}) collective-permute-start(bf16[56,512]{1,0:T(8,128)(2,1)S(1)} %get-tuple-element.36), channel_id=1, source_target_pairs={{0,32},{32,0},{1,33},{33,1},{2,34},{34,2},{3,35},{35,3},{4,36},{36... | collective-permute-start | bytes 172040 | tf_op jit(solution)/shard_map/ppermute | solution.py:300
  50.5 3.9 %collective-permute-start.13 = (bf16[56,512]{1,0:T(8,128)(2,1)S(1)}, bf16[56,512]{1,0:T(8,128)(2,1)S(1)}, u32[]{:S(2)}, u32[]{:S(2)}) collective-permute-start(bf16[56,512]{1,0:T(8,128)(2,1)S(1)} %get-tuple-element.37), channel_id=1, source_target_pairs={{0,48},{16,32},{32,16},{48,0},{1,49},{17,33},{33,17},{49,1},{2,50}... | collective-permute-start | bytes 172040 | tf_op jit(solution)/shard_map/ppermute | solution.py:313
  56.1 14.8 %all-to-all-start = ((bf16[16,16,256]{2,1,0:T(8,128)(2,1)}), bf16[16,16,256]{2,1,0:T(8,128)(2,1)S(1)}, u32[]{:S(2)}, u32[]{:S(2)}) async-start(bf16[16,16,256]{2,1,0:T(8,128)(2,1)} %get-tuple-element.41), calls=%async_computation | async-start | bytes 262144 | tf_op jit(solution)/shard_map/all_to_all | solution.py:407

commit v10 on v9

--- a/solution.py
+++ b/solution.py
@@ -109,12 +109,7 @@
     q, z, xl = index_ref[0], index_ref[1], index_ref[2]
     block_copies = []
     for k, block in enumerate(blocks):
-        for side in range(2):
-            source = ((z + DEPTH - k) % DEPTH) * 2 + (xl ^ side)
-            rows = pl.ds(pl.multiple_of(source * BLOCK, BLOCK), BLOCK)
-            block_copies.append(
-                pltpu.make_async_copy(block.at[side], stage.at[rows, :], block_sem.at[k, side])
-            )
+        block_copies.append(pltpu.make_async_copy(block, stage.at[k], block_sem.at[k]))
     for copy in block_copies:
         copy.start()
     steps = 16 // STEP_TILES
@@ -122,9 +117,12 @@
     copies = pool_copies(q, (p0, p1, p2, p3), pool, listed, sem)
     for copy in copies:
         copy.start()
-    for copy in block_copies:
+    for k, copy in enumerate(block_copies):
         copy.wait()
-    wide[...] = stage[...].astype(F32)
+        for side in range(2):
+            source = ((z + DEPTH - k) % DEPTH) * 2 + (xl ^ side)
+            rows = pl.ds(pl.multiple_of(source * BLOCK, BLOCK), BLOCK)
+            wide[rows, :] = stage[k, side].astype(F32)
     energy = [jnp.zeros((CLASSES, 128), F32) for _ in range(QROT)]
     stride = QROT * 32
     tables = (table0, table1)
@@ -355,10 +353,7 @@
         cost_estimate=pl.CostEstimate(flops=1 * 10**9, bytes_accessed=3 * 10**6, transcendentals=0),
         name="tables",
     )(offsets, weight)
-    last = DEPTH // 2
-    far, wc, ring[last - 1], ring[last + 1] = lax.optimization_barrier(
-        (far, wc, ring[last - 1], ring[last + 1])
-    )
+    far, wc, ring = lax.optimization_barrier((far, wc, ring))
     parts = (particles, near, far, swap(far, "core"))
     table_rows = NSHIFT * QROT * CLASSES
     *terms, pool = pl.pallas_call(
@@ -370,7 +365,7 @@
         in_specs=[SMEM_SPEC] + [HBM_SPEC] * DEPTH + [ANY_SPEC] * 4 + [VMEM_SPEC] * 3,
         out_specs=[VMEM_SPEC] * (NPOOL + 1),
         scratch_shapes=[
-            VMEM((NBLK * BLOCK, 128), BF16),
+            VMEM((DEPTH, 2, BLOCK, 128), BF16),
             VMEM((NBLK * BLOCK, 128), F32),
             VMEM((table_rows, 256 * STEP_TILES), BF16),
             VMEM((table_rows, 256 * STEP_TILES), BF16),
@@ -379,7 +374,7 @@
             VMEM((8, NPOOL * ROWS), jnp.int32),
             VMEM((NPOOL, 8, ROWS), BF16),
             pltpu.SemaphoreType.DMA((2, NPOOL)),
-            pltpu.SemaphoreType.DMA((DEPTH, 2)),
+            pltpu.SemaphoreType.DMA((DEPTH,)),
         ],
         compiler_params=params(20),
         name="score",

time: 88.6 us -> 88.3 us (level)
  starting transfers between devices: 24.4 us -> 28.8 us
  waiting for transfers between devices: 33.9 us -> 29.7 us
    ppermute x7, waiting for transfers between devices: 13.6 us -> 9.64 us  [turn(): return lax.ppermute(x, 'z', [(i, (i + step) % DEPTH) for i in range(DEPTH)])]
    ppermute x6, starting transfers between devices: 7.06 us -> 10.1 us  [swap(): return lax.ppermute(x, axis, [(0, 1), (1, 0)])]
    ppermute x1, starting transfers between devices: 0.42 us -> 1.6 us  [trade(): lax.ppermute(cross, axes, [(i, 3 - i) for i in range(4)])]
  transfers between devices with their start and end apart: 15 -> 15, of which waited for: 8 -> 10; matrix products, arithmetic and copies ran while one was open for 0% -> 0% of each run, Pallas kernels for 1% -> 1%
where the time goes in v10:
time: 88.3 us; the launch traced here: 87.9 us
  waiting for transfers between devices  29.7 us (34%)
  starting transfers between devices  28.8 us (33%)
  blocking collectives  15.4 us (17%)
  Pallas kernels  12.9 us (15%)
    all_to_all x1, blocking collectives, on_device(): placed = lax.all_to_all(placed, DOM, 0, 0, tiled=True)  15.4 us
    ppermute x7, starting transfers between devices, turn(): return lax.ppermute(x, 'z', [(i, (i + step) % DEPTH) for i in range(DEPTH)])  10.7 us
    ppermute x6, starting transfers between devices, swap(): return lax.ppermute(x, axis, [(0, 1), (1, 0)])  10.1 us
    ppermute x7, waiting for transfers between devices, turn(): return lax.ppermute(x, 'z', [(i, (i + step) % DEPTH) for i in range(DEPTH)])  9.64 us
    ppermute x6, waiting for transfers between devices, swap(): return lax.ppermute(x, axis, [(0, 1), (1, 0)])  9.43 us
    all_to_all x1, waiting for transfers between devices, on_device(): sums = lax.all_to_all(sums, BLK, 0, 0, tiled=True)  8.75 us
    pallas_call x1, Pallas kernels, on_device(): pl.pallas_call(score_kernel, out_shape=[jax.ShapeDtypeStruct((56, NPOOL *...  6.72 us
    all_to_all x1, starting transfers between devices, on_device(): sums = lax.all_to_all(sums, BLK, 0, 0, tiled=True)  6.43 us
  transfers between devices with their start and end apart: 15, of which 10 were waited for; matrix products, arithmetic and copies ran while one was open for 0% of the time, Pallas kernels for 1%

profile of v10, /device:TPU:1, one launch (start us, length us, event | category | flops | bytes accessed | tf_op | source)
XLA Modules:
  0.0 87.9 jit_solution(18420392958525944102)
XLA Ops:
  0.6 0.0 copy-start.5
  0.6 0.0 copy-start
  0.7 2.2 %pack.1 = (bf16[288,128]{1,0:T(8,128)(2,1)S(1)}, bf16[136,4096]{1,0:T(8,128)(2,1)S(1)}) custom-call(s32[1]{0:T(128)} %bitcast.1.q_ref, s32[8,128]{1,0:T(8,128)} %bitcast.14, bf16[3,12,4096]{2,1,0:T(8,128)(2,1)} %refs_ref.1, bf16[128,4096]{1,0:T(8,128)(2,1)} %particles_hbm.1), custom_call_target="tpu_custom_call" | custom-call | tf_op jit(solution)/shard_map/pack/pallas_call | solution.py:322
  2.9 3.3 %collective-permute-start.1 = (bf16[136,4096]{1,0:T(8,128)(2,1)S(1)}, bf16[136,4096]{1,0:T(8,128)(2,1)S(1)}, u32[]{:S(2)}, u32[]{:S(2)}) collective-permute-start(bf16[136,4096]{1,0:T(8,128)(2,1)S(1)} %get-tuple-element.30.refs_8_), channel_id=1, source_target_pairs={{0,16},{16,0},{1,17},{17,1},{2,18},{18,2},{3,19},{19,3},{4,20},{20... | collective-permute-start | bytes 3342344 | tf_op jit(solution)/shard_map/ppermute | solution.py:298
  6.2 0.0 collective-permute-start
  6.2 0.8 collective-permute-start.2
  7.0 2.9 %collective-permute-done.2 = bf16[288,128]{1,0:T(8,128)(2,1)S(1)} collective-permute-done((bf16[288,128]{1,0:T(8,128)(2,1)S(1)}, bf16[288,128]{1,0:T(8,128)(2,1)S(1)}, u32[]{:S(2)}, u32[]{:S(2)}) %collective-permute-start.2) | collective-permute-done | bytes 73760 | tf_op jit(solution)/shard_map/ppermute | solution.py:298
  9.9 0.0 collective-permute-done.1.refs_9_
  9.9 0.0 copy-start.1
  10.0 1.1 %collective-permute-start.3 = (bf16[2,288,128]{2,1,0:T(8,128)(2,1)S(1)}, bf16[2,288,128]{2,1,0:T(8,128)(2,1)S(1)}, u32[]{:S(2)}, u32[]{:S(2)}) collective-permute-start(bf16[2,288,128]{2,1,0:T(8,128)(2,1)S(1)} %pad_maximum_fusion.refs_0_), channel_id=1, source_target_pairs={{0,2},{2,4},{4,6},{6,8},{8,10},{10,12},{12,14},{14,0},{1,3},{3,5},... | collective-permute-start | bytes 442376 | tf_op jit(solution)/shard_map/ppermute | solution.py:302
  11.1 4.0 %collective-permute-start.7 = (bf16[2,288,128]{2,1,0:T(8,128)(2,1)S(1)}, bf16[2,288,128]{2,1,0:T(8,128)(2,1)S(1)}, u32[]{:S(2)}, u32[]{:S(2)}) collective-permute-start(bf16[2,288,128]{2,1,0:T(8,128)(2,1)S(1)} %pad_maximum_fusion.refs_0_), channel_id=1, source_target_pairs={{0,14},{2,0},{4,2},{6,4},{8,6},{10,8},{12,10},{14,12},{1,15},{3,1}... | collective-permute-start | bytes 442376 | tf_op jit(solution)/shard_map/ppermute | solution.py:302
  15.1 2.9 %collective-permute-done.3.refs_1_ = bf16[2,288,128]{2,1,0:T(8,128)(2,1)S(1)} collective-permute-done((bf16[2,288,128]{2,1,0:T(8,128)(2,1)S(1)}, bf16[2,288,128]{2,1,0:T(8,128)(2,1)S(1)}, u32[]{:S(2)}, u32[]{:S(2)}) %collective-permute-start.3) | collective-permute-done | bytes 147488 | tf_op jit(solution)/shard_map/ppermute | solution.py:302
  18.0 0.0 copy-start.2
  18.0 0.0 collective-permute-start.4
  18.0 0.0 collective-permute-done.7.refs_7_
  18.0 0.0 copy-start.3
  18.0 2.7 %collective-permute-start.8 = (bf16[2,288,128]{2,1,0:T(8,128)(2,1)S(1)}, bf16[2,288,128]{2,1,0:T(8,128)(2,1)}, u32[]{:S(2)}, u32[]{:S(2)}) collective-permute-start(bf16[2,288,128]{2,1,0:T(8,128)(2,1)S(1)} %collective-permute-done.7.refs_7_), channel_id=1, source_target_pairs={{0,14},{2,0},{4,2},{6,4},{8,6},{10,8},{12,10},{14,12},{1,15},{3,1}... | collective-permute-start | bytes 442376 | tf_op jit(solution)/shard_map/ppermute | solution.py:302
  20.6 2.5 %collective-permute-done.4.refs_2_ = bf16[2,288,128]{2,1,0:T(8,128)(2,1)S(1)} collective-permute-done((bf16[2,288,128]{2,1,0:T(8,128)(2,1)S(1)}, bf16[2,288,128]{2,1,0:T(8,128)(2,1)S(1)}, u32[]{:S(2)}, u32[]{:S(2)}) %collective-permute-start.4) | collective-permute-done | bytes 147488 | tf_op jit(solution)/shard_map/ppermute | solution.py:302
  23.2 0.0 copy-start.4
  23.2 0.0 collective-permute-start.5
  23.2 0.0 collective-permute-done.8.refs_6_
  23.2 2.8 %collective-permute-start.9 = (bf16[2,288,128]{2,1,0:T(8,128)(2,1)}, bf16[2,288,128]{2,1,0:T(8,128)(2,1)}, u32[]{:S(2)}, u32[]{:S(2)}) collective-permute-start(bf16[2,288,128]{2,1,0:T(8,128)(2,1)} %collective-permute-done.8.refs_6_), channel_id=1, source_target_pairs={{0,14},{2,0},{4,2},{6,4},{8,6},{10,8},{12,10},{14,12},{1,15},{3,1}... | collective-permute-start | bytes 442376 | tf_op jit(solution)/shard_map/ppermute | solution.py:302
  26.0 2.5 %collective-permute-done.5.refs_3_ = bf16[2,288,128]{2,1,0:T(8,128)(2,1)} collective-permute-done((bf16[2,288,128]{2,1,0:T(8,128)(2,1)S(1)}, bf16[2,288,128]{2,1,0:T(8,128)(2,1)}, u32[]{:S(2)}, u32[]{:S(2)}) %collective-permute-start.5) | collective-permute-done | bytes 147488 | tf_op jit(solution)/shard_map/ppermute | solution.py:302
  28.5 0.0 copy-done.1
  28.5 0.0 copy-done.2
  28.5 0.0 copy-done.3
  28.5 0.0 copy-done.4
  28.5 0.1 collective-permute-start.6
  28.6 0.0 copy-done.5
  28.6 0.1 copy.10.off_ref
  28.7 0.0 copy-done
  28.7 0.7 tables.1
  29.4 3.0 %collective-permute-done.refs_10_ = bf16[136,4096]{1,0:T(8,128)(2,1)S(1)} collective-permute-done((bf16[136,4096]{1,0:T(8,128)(2,1)S(1)}, bf16[136,4096]{1,0:T(8,128)(2,1)S(1)}, u32[]{:S(2)}, u32[]{:S(2)}) %collective-permute-start) | collective-permute-done | bytes 1114144 | tf_op jit(solution)/shard_map/ppermute | solution.py:298
  32.4 0.0 collective-permute-done.9.refs_5_
  32.4 1.7 %collective-permute-done.6.refs_4_ = bf16[2,288,128]{2,1,0:T(8,128)(2,1)} collective-permute-done((bf16[2,288,128]{2,1,0:T(8,128)(2,1)}, bf16[2,288,128]{2,1,0:T(8,128)(2,1)}, u32[]{:S(2)}, u32[]{:S(2)}) %collective-permute-start.6) | collective-permute-done | bytes 147488 | tf_op jit(solution)/shard_map/ppermute | solution.py:302
  34.1 5.3 %collective-permute-start.10 = (bf16[136,4096]{1,0:T(8,128)(2,1)S(1)}, bf16[136,4096]{1,0:T(8,128)(2,1)}, u32[]{:S(2)}, u32[]{:S(2)}) collective-permute-start(bf16[136,4096]{1,0:T(8,128)(2,1)S(1)} %collective-permute-done.refs_10_), channel_id=1, source_target_pairs={{0,16},{16,0},{1,17},{17,1},{2,18},{18,2},{3,19},{19,3},{4,20},{20... | collective-permute-start | bytes 3342344 | tf_op jit(solution)/shard_map/ppermute | solution.py:298
  39.4 0.1 pad_add_fusion.index_ref
  39.5 2.4 %collective-permute-done.10.refs_11_ = bf16[136,4096]{1,0:T(8,128)(2,1)} collective-permute-done((bf16[136,4096]{1,0:T(8,128)(2,1)S(1)}, bf16[136,4096]{1,0:T(8,128)(2,1)}, u32[]{:S(2)}, u32[]{:S(2)}) %collective-permute-start.10) | collective-permute-done | bytes 1114144 | tf_op jit(solution)/shard_map/ppermute | solution.py:298
  41.9 0.0 copy-start.6
  41.9 6.7 %score.1 = (f32[56,512]{1,0:T(8,128)S(1)}, bf16[56,512]{1,0:T(8,128)(2,1)S(1)}, bf16[56,512]{1,0:T(8,128)(2,1)S(1)}, bf16[56,512]{1,0:T(8,128)(2,1)S(1)}, bf16[512,4096]{1,0:T(8,128)(2,1)S(1)}) custom-call(s32[3]{0:T(128)S(1)} %pad_add_fusion.index_ref, bf16[2,288,128]{2,1,0:T(8,128)(2,1)} %copy-done.1, bf16[2,288,128]{2,1,0:T(8,128)(2,1)} %copy-done.2, ...), custom_call_target="tpu_custom_call" | custom-call | tf_op jit(solution)/shard_map/score/pallas_call | solution.py:359
  48.6 0.5 collective-permute-start.11
  49.1 0.2 collective-permute-start.12
  49.3 1.6 %collective-permute-start.13 = (bf16[56,512]{1,0:T(8,128)(2,1)S(1)}, bf16[56,512]{1,0:T(8,128)(2,1)S(1)}, u32[]{:S(2)}, u32[]{:S(2)}) collective-permute-start(bf16[56,512]{1,0:T(8,128)(2,1)S(1)} %get-tuple-element.49), channel_id=1, source_target_pairs={{0,48},{16,32},{32,16},{48,0},{1,49},{17,33},{33,17},{49,1},{2,50}... | collective-permute-start | bytes 172040 | tf_op jit(solution)/shard_map/ppermute | solution.py:311
  50.9 0.0 copy-done.6
  50.9 0.1 convert_reduce_fusion
  51.0 0.0 collective-permute-done.11.x1
  51.0 1.1 %collective-permute-done.12.x2 = bf16[56,512]{1,0:T(8,128)(2,1)S(1)} collective-permute-done((bf16[56,512]{1,0:T(8,128)(2,1)S(1)}, bf16[56,512]{1,0:T(8,128)(2,1)S(1)}, u32[]{:S(2)}, u32[]{:S(2)}) %collective-permute-start.12) | collective-permute-done | bytes 57376 | tf_op jit(solution)/shard_map/ppermute | solution.py:298
  52.1 1.8 %collective-permute-done.13.x3 = bf16[56,512]{1,0:T(8,128)(2,1)S(1)} collective-permute-done((bf16[56,512]{1,0:T(8,128)(2,1)S(1)}, bf16[56,512]{1,0:T(8,128)(2,1)S(1)}, u32[]{:S(2)}, u32[]{:S(2)}) %collective-permute-start.13) | collective-permute-done | bytes 57376 | tf_op jit(solution)/shard_map/ppermute | solution.py:311
  54.0 1.7 %classes.1 = (bf16[16,16,256]{2,1,0:T(8,128)(2,1)}, f32[1,128]{1,0:T(1,128)}) custom-call(s32[1]{0:T(128)} %bitcast.1.q_ref, f32[56,512]{1,0:T(8,128)S(1)} %get-tuple-element.46.x0, bf16[56,512]{1,0:T(8,128)(2,1)S(1)} %collective-permute-done.11.x1, bf16[56,512]{1,0:T(8,128)(2,1)S(1)} %collective-permute-done.12.x2, ...), custom_call_target="tpu_custom_call" | custom-call | tf_op jit(solution)/shard_map/classes/pallas_call | solution.py:387
  55.6 6.4 %all-to-all-start = ((bf16[16,16,256]{2,1,0:T(8,128)(2,1)}), bf16[16,16,256]{2,1,0:T(8,128)(2,1)S(1)}, u32[]{:S(2)}, u32[]{:S(2)}) async-start(bf16[16,16,256]{2,1,0:T(8,128)(2,1)} %get-tuple-element.53), calls=%async_computation | async-start | bytes 262144 | tf_op jit(solution)/shard_map/all_to_all | solution.py:402
  62.1 0.1 dynamic_slice.3
  62.2 8.7 %all-to-all-done.y_ref = bf16[16,16,256]{2,1,0:T(8,128)(2,1)S(1)} async-done(((bf16[16,16,256]{2,1,0:T(8,128)(2,1)}), bf16[16,16,256]{2,1,0:T(8,128)(2,1)S(1)}, u32[]{:S(2)}, u32[]{:S(2)}) %all-to-all-start) | async-done | bytes 131104 | tf_op jit(solution)/shard_map/all_to_all | solution.py:402
  70.9 0.8 place.1
  71.8 15.4 %all_to_all.10.z_ref = bf16[16,8,384]{2,1,0:T(8,128)(2,1)S(1)} all-to-all(bf16[16,8,384]{2,1,0:T(8,128)(2,1)} %place.1), channel_id=1, replica_groups=mesh['xh'=2,'yh'=2,'yl'=2,'core'=2,'z'=8,'xl'=2] {'xh','yh','yl','core'}, dimensions={0} | all-to-all | bytes 196608 | tf_op jit(solution)/shard_map/all_to_all | solution.py:420
  87.2 0.8 means.1
  (3 shorter events, 0.0 us)
Async XLA Ops:
  0.6 28.0 %copy-start.5 = (s32[4,2]{0,1:T(2,128)S(1)}, s32[4,2]{0,1:T(2,128)}, u32[]{:S(2)}) copy-start(s32[4,2]{0,1:T(2,128)} %param.9) | copy-start | bytes 100
  0.6 28.1 %copy-start = (f32[2048]{0:T(1024)S(1)}, f32[2048]{0:T(1024)}, u32[]{:S(2)}) copy-start(f32[2048]{0:T(1024)} %param.8) | copy-start | bytes 24580
  2.9 7.0 %collective-permute-start.1 = (bf16[136,4096]{1,0:T(8,128)(2,1)S(1)}, bf16[136,4096]{1,0:T(8,128)(2,1)S(1)}, u32[]{:S(2)}, u32[]{:S(2)}) collective-permute-start(bf16[136,4096]{1,0:T(8,128)(2,1)S(1)} %get-tuple-element.30.refs_8_), channel_id=1, source_target_pairs={{0,16},{16,0},{1,17},{17,1},{2,18},{18,2},{3,19},{19,3},{4,20},{20... | collective-permute-start | bytes 3342344 | tf_op jit(solution)/shard_map/ppermute | solution.py:298
  6.2 26.1 %collective-permute-start = (bf16[136,4096]{1,0:T(8,128)(2,1)S(1)}, bf16[136,4096]{1,0:T(8,128)(2,1)S(1)}, u32[]{:S(2)}, u32[]{:S(2)}) collective-permute-start(bf16[136,4096]{1,0:T(8,128)(2,1)S(1)} %get-tuple-element.30.refs_8_), channel_id=1, source_target_pairs={{0,32},{32,0},{1,33},{33,1},{2,34},{34,2},{3,35},{35,3},{4,36},{36... | collective-permute-start | bytes 3342344 | tf_op jit(solution)/shard_map/ppermute | solution.py:298
  6.2 3.7 %collective-permute-start.2 = (bf16[288,128]{1,0:T(8,128)(2,1)S(1)}, bf16[288,128]{1,0:T(8,128)(2,1)S(1)}, u32[]{:S(2)}, u32[]{:S(2)}) collective-permute-start(bf16[288,128]{1,0:T(8,128)(2,1)S(1)} %get-tuple-element.32), channel_id=1, source_target_pairs={{0,1},{1,0},{2,3},{3,2},{4,5},{5,4},{6,7},{7,6},{8,9},{9,8},{10,11... | collective-permute-start | bytes 221192 | tf_op jit(solution)/shard_map/ppermute | solution.py:298
  9.9 18.5 %copy-start.1 = (bf16[2,288,128]{2,1,0:T(8,128)(2,1)}, bf16[2,288,128]{2,1,0:T(8,128)(2,1)S(1)}, u32[]{:S(2)}) copy-start(bf16[2,288,128]{2,1,0:T(8,128)(2,1)S(1)} %pad_maximum_fusion.refs_0_) | copy-start | bytes 442372
  10.0 8.0 %collective-permute-start.3 = (bf16[2,288,128]{2,1,0:T(8,128)(2,1)S(1)}, bf16[2,288,128]{2,1,0:T(8,128)(2,1)S(1)}, u32[]{:S(2)}, u32[]{:S(2)}) collective-permute-start(bf16[2,288,128]{2,1,0:T(8,128)(2,1)S(1)} %pad_maximum_fusion.refs_0_), channel_id=1, source_target_pairs={{0,2},{2,4},{4,6},{6,8},{8,10},{10,12},{12,14},{14,0},{1,3},{3,5},... | collective-permute-start | bytes 442376 | tf_op jit(solution)/shard_map/ppermute | solution.py:302
  11.1 6.9 %collective-permute-start.7 = (bf16[2,288,128]{2,1,0:T(8,128)(2,1)S(1)}, bf16[2,288,128]{2,1,0:T(8,128)(2,1)S(1)}, u32[]{:S(2)}, u32[]{:S(2)}) collective-permute-start(bf16[2,288,128]{2,1,0:T(8,128)(2,1)S(1)} %pad_maximum_fusion.refs_0_), channel_id=1, source_target_pairs={{0,14},{2,0},{4,2},{6,4},{8,6},{10,8},{12,10},{14,12},{1,15},{3,1}... | collective-permute-start | bytes 442376 | tf_op jit(solution)/shard_map/ppermute | solution.py:302
  18.0 10.5 %copy-start.2 = (bf16[2,288,128]{2,1,0:T(8,128)(2,1)}, bf16[2,288,128]{2,1,0:T(8,128)(2,1)S(1)}, u32[]{:S(2)}) copy-start(bf16[2,288,128]{2,1,0:T(8,128)(2,1)S(1)} %collective-permute-done.3.refs_1_) | copy-start | bytes 442372
  18.0 5.2 %collective-permute-start.4 = (bf16[2,288,128]{2,1,0:T(8,128)(2,1)S(1)}, bf16[2,288,128]{2,1,0:T(8,128)(2,1)S(1)}, u32[]{:S(2)}, u32[]{:S(2)}) collective-permute-start(bf16[2,288,128]{2,1,0:T(8,128)(2,1)S(1)} %collective-permute-done.3.refs_1_), channel_id=1, source_target_pairs={{0,2},{2,4},{4,6},{6,8},{8,10},{10,12},{12,14},{14,0},{1,3},{3,5},... | collective-permute-start | bytes 442376 | tf_op jit(solution)/shard_map/ppermute | solution.py:302
  18.0 10.5 %copy-start.3 = (bf16[2,288,128]{2,1,0:T(8,128)(2,1)}, bf16[2,288,128]{2,1,0:T(8,128)(2,1)S(1)}, u32[]{:S(2)}) copy-start(bf16[2,288,128]{2,1,0:T(8,128)(2,1)S(1)} %collective-permute-done.7.refs_7_) | copy-start | bytes 442372
  18.0 5.2 %collective-permute-start.8 = (bf16[2,288,128]{2,1,0:T(8,128)(2,1)S(1)}, bf16[2,288,128]{2,1,0:T(8,128)(2,1)}, u32[]{:S(2)}, u32[]{:S(2)}) collective-permute-start(bf16[2,288,128]{2,1,0:T(8,128)(2,1)S(1)} %collective-permute-done.7.refs_7_), channel_id=1, source_target_pairs={{0,14},{2,0},{4,2},{6,4},{8,6},{10,8},{12,10},{14,12},{1,15},{3,1}... | collective-permute-start | bytes 442376 | tf_op jit(solution)/shard_map/ppermute | solution.py:302
  23.2 5.3 %copy-start.4 = (bf16[2,288,128]{2,1,0:T(8,128)(2,1)}, bf16[2,288,128]{2,1,0:T(8,128)(2,1)S(1)}, u32[]{:S(2)}) copy-start(bf16[2,288,128]{2,1,0:T(8,128)(2,1)S(1)} %collective-permute-done.4.refs_2_) | copy-start | bytes 442372
  23.2 5.3 %collective-permute-start.5 = (bf16[2,288,128]{2,1,0:T(8,128)(2,1)S(1)}, bf16[2,288,128]{2,1,0:T(8,128)(2,1)}, u32[]{:S(2)}, u32[]{:S(2)}) collective-permute-start(bf16[2,288,128]{2,1,0:T(8,128)(2,1)S(1)} %collective-permute-done.4.refs_2_), channel_id=1, source_target_pairs={{0,2},{2,4},{4,6},{6,8},{8,10},{10,12},{12,14},{14,0},{1,3},{3,5},... | collective-permute-start | bytes 442376 | tf_op jit(solution)/shard_map/ppermute | solution.py:302
  23.2 9.2 %collective-permute-start.9 = (bf16[2,288,128]{2,1,0:T(8,128)(2,1)}, bf16[2,288,128]{2,1,0:T(8,128)(2,1)}, u32[]{:S(2)}, u32[]{:S(2)}) collective-permute-start(bf16[2,288,128]{2,1,0:T(8,128)(2,1)} %collective-permute-done.8.refs_6_), channel_id=1, source_target_pairs={{0,14},{2,0},{4,2},{6,4},{8,6},{10,8},{12,10},{14,12},{1,15},{3,1}... | collective-permute-start | bytes 442376 | tf_op jit(solution)/shard_map/ppermute | solution.py:302
  28.5 5.6 %collective-permute-start.6 = (bf16[2,288,128]{2,1,0:T(8,128)(2,1)}, bf16[2,288,128]{2,1,0:T(8,128)(2,1)}, u32[]{:S(2)}, u32[]{:S(2)}) collective-permute-start(bf16[2,288,128]{2,1,0:T(8,128)(2,1)} %collective-permute-done.5.refs_3_), channel_id=1, source_target_pairs={{0,2},{2,4},{4,6},{6,8},{8,10},{10,12},{12,14},{14,0},{1,3},{3,5},... | collective-permute-start | bytes 442376 | tf_op jit(solution)/shard_map/ppermute | solution.py:302
  34.1 7.8 %collective-permute-start.10 = (bf16[136,4096]{1,0:T(8,128)(2,1)S(1)}, bf16[136,4096]{1,0:T(8,128)(2,1)}, u32[]{:S(2)}, u32[]{:S(2)}) collective-permute-start(bf16[136,4096]{1,0:T(8,128)(2,1)S(1)} %collective-permute-done.refs_10_), channel_id=1, source_target_pairs={{0,16},{16,0},{1,17},{17,1},{2,18},{18,2},{3,19},{19,3},{4,20},{20... | collective-permute-start | bytes 3342344 | tf_op jit(solution)/shard_map/ppermute | solution.py:298
  41.9 9.0 %copy-start.6 = (s32[48]{0:T(128)S(1)}, s32[48]{0:T(128)}, u32[]{:S(2)}) copy-start(s32[48]{0:T(128)} %param.11) | copy-start | bytes 580
  48.6 2.3 %collective-permute-start.11 = (bf16[56,512]{1,0:T(8,128)(2,1)S(1)}, bf16[56,512]{1,0:T(8,128)(2,1)S(1)}, u32[]{:S(2)}, u32[]{:S(2)}) collective-permute-start(bf16[56,512]{1,0:T(8,128)(2,1)S(1)} %get-tuple-element.47), channel_id=1, source_target_pairs={{0,16},{16,0},{1,17},{17,1},{2,18},{18,2},{3,19},{19,3},{4,20},{20... | collective-permute-start | bytes 172040 | tf_op jit(solution)/shard_map/ppermute | solution.py:298
  49.1 3.0 %collective-permute-start.12 = (bf16[56,512]{1,0:T(8,128)(2,1)S(1)}, bf16[56,512]{1,0:T(8,128)(2,1)S(1)}, u32[]{:S(2)}, u32[]{:S(2)}) collective-permute-start(bf16[56,512]{1,0:T(8,128)(2,1)S(1)} %get-tuple-element.48), channel_id=1, source_target_pairs={{0,32},{32,0},{1,33},{33,1},{2,34},{34,2},{3,35},{35,3},{4,36},{36... | collective-permute-start | bytes 172040 | tf_op jit(solution)/shard_map/ppermute | solution.py:298
  49.3 4.7 %collective-permute-start.13 = (bf16[56,512]{1,0:T(8,128)(2,1)S(1)}, bf16[56,512]{1,0:T(8,128)(2,1)S(1)}, u32[]{:S(2)}, u32[]{:S(2)}) collective-permute-start(bf16[56,512]{1,0:T(8,128)(2,1)S(1)} %get-tuple-element.49), channel_id=1, source_target_pairs={{0,48},{16,32},{32,16},{48,0},{1,49},{17,33},{33,17},{49,1},{2,50}... | collective-permute-start | bytes 172040 | tf_op jit(solution)/shard_map/ppermute | solution.py:311
  55.6 15.3 %all-to-all-start = ((bf16[16,16,256]{2,1,0:T(8,128)(2,1)}), bf16[16,16,256]{2,1,0:T(8,128)(2,1)S(1)}, u32[]{:S(2)}, u32[]{:S(2)}) async-start(bf16[16,16,256]{2,1,0:T(8,128)(2,1)} %get-tuple-element.53), calls=%async_computation | async-start | bytes 262144 | tf_op jit(solution)/shard_map/all_to_all | solution.py:402

commit v11 on v10

--- a/solution.py
+++ b/solution.py
@@ -25,7 +25,7 @@
 ROT = 12
 NSHIFT = 4
 ROWS = 128
-EXTENDED = ROWS + 8
+EXTENDED = 2 * K + 128
 NPOOL = 4
 QROT = ROT // NPOOL
 QCLS = CLASSES // NPOOL
@@ -50,10 +50,10 @@
 
 
 def pack_kernel(q_ref, cand_ref, refs_ref, particles_hbm, out_ref, extended_ref, wide, rows, sem):
-    copy = pltpu.make_async_copy(particles_hbm, extended_ref.at[pl.ds(0, ROWS), :], sem)
+    copy = pltpu.make_async_copy(particles_hbm, extended_ref.at[:, pl.ds(0, 2 * K)], sem)
     copy.start()
-    extended_ref[ROWS:EXTENDED, 0:128] = cand_ref[...].astype(F32).astype(BF16)
-    extended_ref[ROWS:EXTENDED, 128:] = jnp.zeros((8, 2 * K - 128), BF16)
+    cand = jnp.concatenate([cand_ref[...].astype(F32), jnp.zeros((ROWS - 8, 128), F32)], axis=0)
+    extended_ref[:, 2 * K :] = cand.astype(BF16)
     q = q_ref[0]
     wide[...] = refs_ref[...].astype(F32)
     for c in range(LOCAL):
@@ -87,8 +87,9 @@
     copies = []
     for j, part in enumerate(parts):
         rows = pl.ds(pl.multiple_of((q ^ j) * ROWS, ROWS), ROWS)
-        copies.append(pltpu.make_async_copy(part.at[pl.ds(0, ROWS), :], pool.at[rows, :], sem.at[0, j]))
-        few = part.at[pl.ds(ROWS, 8), pl.ds(0, ROWS)]
+        whole = part.at[:, pl.ds(0, 2 * K)]
+        copies.append(pltpu.make_async_copy(whole, pool.at[rows, :], sem.at[0, j]))
+        few = part.at[pl.ds(0, 8), pl.ds(2 * K, ROWS)]
         copies.append(pltpu.make_async_copy(few, listed.at[j], sem.at[1, j]))
     return copies
 
@@ -323,7 +324,7 @@
         pack_kernel,
         out_shape=(
             jax.ShapeDtypeStruct((BLOCK, 128), BF16),
-            jax.ShapeDtypeStruct((EXTENDED, 2 * K), BF16),
+            jax.ShapeDtypeStruct((ROWS, EXTENDED), BF16),
         ),
         in_specs=[SMEM_SPEC, VMEM_SPEC, VMEM_SPEC, HBM_SPEC],
         out_specs=(VMEM_SPEC, VMEM_SPEC),

time: 88.3 us -> 88.2 us (level)
  no operation moved by 1% of the time
where the time goes in v11:
time: 88.2 us; the launch traced here: 87.9 us
  waiting for transfers between devices  29.6 us (34%)
  starting transfers between devices  28.7 us (33%)
  blocking collectives  15.4 us (17%)
  Pallas kernels  12.9 us (15%)
    all_to_all x1, blocking collectives, on_device(): placed = lax.all_to_all(placed, DOM, 0, 0, tiled=True)  15.4 us
    ppermute x7, starting transfers between devices, turn(): return lax.ppermute(x, 'z', [(i, (i + step) % DEPTH) for i in range(DEPTH)])  10.7 us
    ppermute x7, waiting for transfers between devices, turn(): return lax.ppermute(x, 'z', [(i, (i + step) % DEPTH) for i in range(DEPTH)])  10.2 us
    ppermute x6, starting transfers between devices, swap(): return lax.ppermute(x, axis, [(0, 1), (1, 0)])  10.1 us
    ppermute x6, waiting for transfers between devices, swap(): return lax.ppermute(x, axis, [(0, 1), (1, 0)])  9.15 us
    all_to_all x1, waiting for transfers between devices, on_device(): sums = lax.all_to_all(sums, BLK, 0, 0, tiled=True)  8.75 us
    pallas_call x1, Pallas kernels, on_device(): pl.pallas_call(score_kernel, out_shape=[jax.ShapeDtypeStruct((56, NPOOL *...  6.72 us
    all_to_all x1, starting transfers between devices, on_device(): sums = lax.all_to_all(sums, BLK, 0, 0, tiled=True)  6.39 us
  transfers between devices with their start and end apart: 15, of which 10 were waited for; matrix products, arithmetic and copies ran while one was open for 0% of the time, Pallas kernels for 1%

profile of v11, /device:TPU:1, one launch (start us, length us, event | category | flops | bytes accessed | tf_op | source)
XLA Modules:
  0.0 87.9 jit_solution(8133425709175077285)
XLA Ops:
  0.6 0.0 copy-start.5
  0.6 0.0 copy-start
  0.7 2.2 %pack.1 = (bf16[288,128]{1,0:T(8,128)(2,1)S(1)}, bf16[128,4224]{1,0:T(8,128)(2,1)S(1)}) custom-call(s32[1]{0:T(128)} %bitcast.1.q_ref, s32[8,128]{1,0:T(8,128)} %bitcast.14, bf16[3,12,4096]{2,1,0:T(8,128)(2,1)} %refs_ref.1, bf16[128,4096]{1,0:T(8,128)(2,1)} %particles_hbm.1), custom_call_target="tpu_custom_call" | custom-call | tf_op jit(solution)/shard_map/pack/pallas_call | solution.py:323
  2.9 3.3 %collective-permute-start.1 = (bf16[128,4224]{1,0:T(8,128)(2,1)S(1)}, bf16[128,4224]{1,0:T(8,128)(2,1)S(1)}, u32[]{:S(2)}, u32[]{:S(2)}) collective-permute-start(bf16[128,4224]{1,0:T(8,128)(2,1)S(1)} %get-tuple-element.30.refs_8_), channel_id=1, source_target_pairs={{0,16},{16,0},{1,17},{17,1},{2,18},{18,2},{3,19},{19,3},{4,20},{20... | collective-permute-start | bytes 3244040 | tf_op jit(solution)/shard_map/ppermute | solution.py:299
  6.2 0.0 collective-permute-start
  6.2 0.8 collective-permute-start.2
  7.0 2.9 %collective-permute-done.2 = bf16[288,128]{1,0:T(8,128)(2,1)S(1)} collective-permute-done((bf16[288,128]{1,0:T(8,128)(2,1)S(1)}, bf16[288,128]{1,0:T(8,128)(2,1)S(1)}, u32[]{:S(2)}, u32[]{:S(2)}) %collective-permute-start.2) | collective-permute-done | bytes 73760 | tf_op jit(solution)/shard_map/ppermute | solution.py:299
  9.9 0.0 collective-permute-done.1.refs_9_
  9.9 0.0 copy-start.1
  10.0 1.1 %collective-permute-start.3 = (bf16[2,288,128]{2,1,0:T(8,128)(2,1)S(1)}, bf16[2,288,128]{2,1,0:T(8,128)(2,1)S(1)}, u32[]{:S(2)}, u32[]{:S(2)}) collective-permute-start(bf16[2,288,128]{2,1,0:T(8,128)(2,1)S(1)} %pad_maximum_fusion.refs_0_), channel_id=1, source_target_pairs={{0,2},{2,4},{4,6},{6,8},{8,10},{10,12},{12,14},{14,0},{1,3},{3,5},... | collective-permute-start | bytes 442376 | tf_op jit(solution)/shard_map/ppermute | solution.py:303
  11.1 4.0 %collective-permute-start.7 = (bf16[2,288,128]{2,1,0:T(8,128)(2,1)S(1)}, bf16[2,288,128]{2,1,0:T(8,128)(2,1)S(1)}, u32[]{:S(2)}, u32[]{:S(2)}) collective-permute-start(bf16[2,288,128]{2,1,0:T(8,128)(2,1)S(1)} %pad_maximum_fusion.refs_0_), channel_id=1, source_target_pairs={{0,14},{2,0},{4,2},{6,4},{8,6},{10,8},{12,10},{14,12},{1,15},{3,1}... | collective-permute-start | bytes 442376 | tf_op jit(solution)/shard_map/ppermute | solution.py:303
  15.1 2.9 %collective-permute-done.3.refs_1_ = bf16[2,288,128]{2,1,0:T(8,128)(2,1)S(1)} collective-permute-done((bf16[2,288,128]{2,1,0:T(8,128)(2,1)S(1)}, bf16[2,288,128]{2,1,0:T(8,128)(2,1)S(1)}, u32[]{:S(2)}, u32[]{:S(2)}) %collective-permute-start.3) | collective-permute-done | bytes 147488 | tf_op jit(solution)/shard_map/ppermute | solution.py:303
  18.0 0.0 copy-start.2
  18.0 0.0 collective-permute-start.4
  18.0 0.0 collective-permute-done.7.refs_7_
  18.0 0.0 copy-start.3
  18.0 2.7 %collective-permute-start.8 = (bf16[2,288,128]{2,1,0:T(8,128)(2,1)S(1)}, bf16[2,288,128]{2,1,0:T(8,128)(2,1)}, u32[]{:S(2)}, u32[]{:S(2)}) collective-permute-start(bf16[2,288,128]{2,1,0:T(8,128)(2,1)S(1)} %collective-permute-done.7.refs_7_), channel_id=1, source_target_pairs={{0,14},{2,0},{4,2},{6,4},{8,6},{10,8},{12,10},{14,12},{1,15},{3,1}... | collective-permute-start | bytes 442376 | tf_op jit(solution)/shard_map/ppermute | solution.py:303
  20.6 2.5 %collective-permute-done.4.refs_2_ = bf16[2,288,128]{2,1,0:T(8,128)(2,1)S(1)} collective-permute-done((bf16[2,288,128]{2,1,0:T(8,128)(2,1)S(1)}, bf16[2,288,128]{2,1,0:T(8,128)(2,1)S(1)}, u32[]{:S(2)}, u32[]{:S(2)}) %collective-permute-start.4) | collective-permute-done | bytes 147488 | tf_op jit(solution)/shard_map/ppermute | solution.py:303
  23.2 0.0 copy-start.4
  23.2 0.0 collective-permute-start.5
  23.2 0.0 collective-permute-done.8.refs_6_
  23.2 2.8 %collective-permute-start.9 = (bf16[2,288,128]{2,1,0:T(8,128)(2,1)}, bf16[2,288,128]{2,1,0:T(8,128)(2,1)}, u32[]{:S(2)}, u32[]{:S(2)}) collective-permute-start(bf16[2,288,128]{2,1,0:T(8,128)(2,1)} %collective-permute-done.8.refs_6_), channel_id=1, source_target_pairs={{0,14},{2,0},{4,2},{6,4},{8,6},{10,8},{12,10},{14,12},{1,15},{3,1}... | collective-permute-start | bytes 442376 | tf_op jit(solution)/shard_map/ppermute | solution.py:303
  26.0 2.5 %collective-permute-done.5.refs_3_ = bf16[2,288,128]{2,1,0:T(8,128)(2,1)} collective-permute-done((bf16[2,288,128]{2,1,0:T(8,128)(2,1)S(1)}, bf16[2,288,128]{2,1,0:T(8,128)(2,1)}, u32[]{:S(2)}, u32[]{:S(2)}) %collective-permute-start.5) | collective-permute-done | bytes 147488 | tf_op jit(solution)/shard_map/ppermute | solution.py:303
  28.5 0.0 copy-done.2
  28.5 0.0 copy-done.3
  28.5 0.0 copy-done.4
  28.5 0.1 collective-permute-start.6
  28.6 0.0 copy-done.5
  28.6 0.1 copy.10.off_ref
  28.7 0.0 copy-done
  28.7 0.7 tables.1
  29.4 0.0 copy-done.1
  29.4 2.4 %collective-permute-done.refs_10_ = bf16[128,4224]{1,0:T(8,128)(2,1)S(1)} collective-permute-done((bf16[128,4224]{1,0:T(8,128)(2,1)S(1)}, bf16[128,4224]{1,0:T(8,128)(2,1)S(1)}, u32[]{:S(2)}, u32[]{:S(2)}) %collective-permute-start) | collective-permute-done | bytes 1081376 | tf_op jit(solution)/shard_map/ppermute | solution.py:299
  31.8 0.0 collective-permute-done.9.refs_5_
  31.8 2.3 %collective-permute-done.6.refs_4_ = bf16[2,288,128]{2,1,0:T(8,128)(2,1)} collective-permute-done((bf16[2,288,128]{2,1,0:T(8,128)(2,1)}, bf16[2,288,128]{2,1,0:T(8,128)(2,1)}, u32[]{:S(2)}, u32[]{:S(2)}) %collective-permute-start.6) | collective-permute-done | bytes 147488 | tf_op jit(solution)/shard_map/ppermute | solution.py:303
  34.1 5.3 %collective-permute-start.10 = (bf16[128,4224]{1,0:T(8,128)(2,1)S(1)}, bf16[128,4224]{1,0:T(8,128)(2,1)}, u32[]{:S(2)}, u32[]{:S(2)}) collective-permute-start(bf16[128,4224]{1,0:T(8,128)(2,1)S(1)} %collective-permute-done.refs_10_), channel_id=1, source_target_pairs={{0,16},{16,0},{1,17},{17,1},{2,18},{18,2},{3,19},{19,3},{4,20},{20... | collective-permute-start | bytes 3244040 | tf_op jit(solution)/shard_map/ppermute | solution.py:299
  39.4 0.1 pad_add_fusion.index_ref
  39.5 2.4 %collective-permute-done.10.refs_11_ = bf16[128,4224]{1,0:T(8,128)(2,1)} collective-permute-done((bf16[128,4224]{1,0:T(8,128)(2,1)S(1)}, bf16[128,4224]{1,0:T(8,128)(2,1)}, u32[]{:S(2)}, u32[]{:S(2)}) %collective-permute-start.10) | collective-permute-done | bytes 1081376 | tf_op jit(solution)/shard_map/ppermute | solution.py:299
  41.9 0.0 copy-start.6
  41.9 6.7 %score.1 = (f32[56,512]{1,0:T(8,128)S(1)}, bf16[56,512]{1,0:T(8,128)(2,1)S(1)}, bf16[56,512]{1,0:T(8,128)(2,1)S(1)}, bf16[56,512]{1,0:T(8,128)(2,1)S(1)}, bf16[512,4096]{1,0:T(8,128)(2,1)S(1)}) custom-call(s32[3]{0:T(128)S(1)} %pad_add_fusion.index_ref, bf16[2,288,128]{2,1,0:T(8,128)(2,1)} %copy-done.1, bf16[2,288,128]{2,1,0:T(8,128)(2,1)} %copy-done.2, ...), custom_call_target="tpu_custom_call" | custom-call | tf_op jit(solution)/shard_map/score/pallas_call | solution.py:360
  48.6 0.5 collective-permute-start.11
  49.1 0.2 collective-permute-start.12
  49.2 1.6 %collective-permute-start.13 = (bf16[56,512]{1,0:T(8,128)(2,1)S(1)}, bf16[56,512]{1,0:T(8,128)(2,1)S(1)}, u32[]{:S(2)}, u32[]{:S(2)}) collective-permute-start(bf16[56,512]{1,0:T(8,128)(2,1)S(1)} %get-tuple-element.49), channel_id=1, source_target_pairs={{0,48},{16,32},{32,16},{48,0},{1,49},{17,33},{33,17},{49,1},{2,50}... | collective-permute-start | bytes 172040 | tf_op jit(solution)/shard_map/ppermute | solution.py:312
  50.8 0.0 copy-done.6
  50.8 0.1 convert_reduce_fusion
  50.9 0.0 collective-permute-done.11.x1
  50.9 1.5 %collective-permute-done.12.x2 = bf16[56,512]{1,0:T(8,128)(2,1)S(1)} collective-permute-done((bf16[56,512]{1,0:T(8,128)(2,1)S(1)}, bf16[56,512]{1,0:T(8,128)(2,1)S(1)}, u32[]{:S(2)}, u32[]{:S(2)}) %collective-permute-start.12) | collective-permute-done | bytes 57376 | tf_op jit(solution)/shard_map/ppermute | solution.py:299
  52.4 1.5 %collective-permute-done.13.x3 = bf16[56,512]{1,0:T(8,128)(2,1)S(1)} collective-permute-done((bf16[56,512]{1,0:T(8,128)(2,1)S(1)}, bf16[56,512]{1,0:T(8,128)(2,1)S(1)}, u32[]{:S(2)}, u32[]{:S(2)}) %collective-permute-start.13) | collective-permute-done | bytes 57376 | tf_op jit(solution)/shard_map/ppermute | solution.py:312
  53.9 1.7 %classes.1 = (bf16[16,16,256]{2,1,0:T(8,128)(2,1)}, f32[1,128]{1,0:T(1,128)}) custom-call(s32[1]{0:T(128)} %bitcast.1.q_ref, f32[56,512]{1,0:T(8,128)S(1)} %get-tuple-element.46.x0, bf16[56,512]{1,0:T(8,128)(2,1)S(1)} %collective-permute-done.11.x1, bf16[56,512]{1,0:T(8,128)(2,1)S(1)} %collective-permute-done.12.x2, ...), custom_call_target="tpu_custom_call" | custom-call | tf_op jit(solution)/shard_map/classes/pallas_call | solution.py:388
  55.6 6.4 %all-to-all-start = ((bf16[16,16,256]{2,1,0:T(8,128)(2,1)}), bf16[16,16,256]{2,1,0:T(8,128)(2,1)S(1)}, u32[]{:S(2)}, u32[]{:S(2)}) async-start(bf16[16,16,256]{2,1,0:T(8,128)(2,1)} %get-tuple-element.53), calls=%async_computation | async-start | bytes 262144 | tf_op jit(solution)/shard_map/all_to_all | solution.py:403
  62.0 0.1 dynamic_slice.3
  62.1 8.8 %all-to-all-done.y_ref = bf16[16,16,256]{2,1,0:T(8,128)(2,1)S(1)} async-done(((bf16[16,16,256]{2,1,0:T(8,128)(2,1)}), bf16[16,16,256]{2,1,0:T(8,128)(2,1)S(1)}, u32[]{:S(2)}, u32[]{:S(2)}) %all-to-all-start) | async-done | bytes 131104 | tf_op jit(solution)/shard_map/all_to_all | solution.py:403
  70.9 0.8 place.1
  71.7 15.4 %all_to_all.10.z_ref = bf16[16,8,384]{2,1,0:T(8,128)(2,1)S(1)} all-to-all(bf16[16,8,384]{2,1,0:T(8,128)(2,1)} %place.1), channel_id=1, replica_groups=mesh['xh'=2,'yh'=2,'yl'=2,'core'=2,'z'=8,'xl'=2] {'xh','yh','yl','core'}, dimensions={0} | all-to-all | bytes 196608 | tf_op jit(solution)/shard_map/all_to_all | solution.py:421
  87.1 0.8 means.1
  (3 shorter events, 0.0 us)
Async XLA Ops:
  0.6 28.0 %copy-start.5 = (s32[4,2]{0,1:T(2,128)S(1)}, s32[4,2]{0,1:T(2,128)}, u32[]{:S(2)}) copy-start(s32[4,2]{0,1:T(2,128)} %param.9) | copy-start | bytes 100
  0.6 28.0 %copy-start = (f32[2048]{0:T(1024)S(1)}, f32[2048]{0:T(1024)}, u32[]{:S(2)}) copy-start(f32[2048]{0:T(1024)} %param.8) | copy-start | bytes 24580
  2.9 7.0 %collective-permute-start.1 = (bf16[128,4224]{1,0:T(8,128)(2,1)S(1)}, bf16[128,4224]{1,0:T(8,128)(2,1)S(1)}, u32[]{:S(2)}, u32[]{:S(2)}) collective-permute-start(bf16[128,4224]{1,0:T(8,128)(2,1)S(1)} %get-tuple-element.30.refs_8_), channel_id=1, source_target_pairs={{0,16},{16,0},{1,17},{17,1},{2,18},{18,2},{3,19},{19,3},{4,20},{20... | collective-permute-start | bytes 3244040 | tf_op jit(solution)/shard_map/ppermute | solution.py:299
  6.2 25.5 %collective-permute-start = (bf16[128,4224]{1,0:T(8,128)(2,1)S(1)}, bf16[128,4224]{1,0:T(8,128)(2,1)S(1)}, u32[]{:S(2)}, u32[]{:S(2)}) collective-permute-start(bf16[128,4224]{1,0:T(8,128)(2,1)S(1)} %get-tuple-element.30.refs_8_), channel_id=1, source_target_pairs={{0,32},{32,0},{1,33},{33,1},{2,34},{34,2},{3,35},{35,3},{4,36},{36... | collective-permute-start | bytes 3244040 | tf_op jit(solution)/shard_map/ppermute | solution.py:299
  6.2 3.7 %collective-permute-start.2 = (bf16[288,128]{1,0:T(8,128)(2,1)S(1)}, bf16[288,128]{1,0:T(8,128)(2,1)S(1)}, u32[]{:S(2)}, u32[]{:S(2)}) collective-permute-start(bf16[288,128]{1,0:T(8,128)(2,1)S(1)} %get-tuple-element.32), channel_id=1, source_target_pairs={{0,1},{1,0},{2,3},{3,2},{4,5},{5,4},{6,7},{7,6},{8,9},{9,8},{10,11... | collective-permute-start | bytes 221192 | tf_op jit(solution)/shard_map/ppermute | solution.py:299
  9.9 19.5 %copy-start.1 = (bf16[2,288,128]{2,1,0:T(8,128)(2,1)}, bf16[2,288,128]{2,1,0:T(8,128)(2,1)S(1)}, u32[]{:S(2)}) copy-start(bf16[2,288,128]{2,1,0:T(8,128)(2,1)S(1)} %pad_maximum_fusion.refs_0_) | copy-start | bytes 442372
  10.0 8.0 %collective-permute-start.3 = (bf16[2,288,128]{2,1,0:T(8,128)(2,1)S(1)}, bf16[2,288,128]{2,1,0:T(8,128)(2,1)S(1)}, u32[]{:S(2)}, u32[]{:S(2)}) collective-permute-start(bf16[2,288,128]{2,1,0:T(8,128)(2,1)S(1)} %pad_maximum_fusion.refs_0_), channel_id=1, source_target_pairs={{0,2},{2,4},{4,6},{6,8},{8,10},{10,12},{12,14},{14,0},{1,3},{3,5},... | collective-permute-start | bytes 442376 | tf_op jit(solution)/shard_map/ppermute | solution.py:303
  11.1 6.9 %collective-permute-start.7 = (bf16[2,288,128]{2,1,0:T(8,128)(2,1)S(1)}, bf16[2,288,128]{2,1,0:T(8,128)(2,1)S(1)}, u32[]{:S(2)}, u32[]{:S(2)}) collective-permute-start(bf16[2,288,128]{2,1,0:T(8,128)(2,1)S(1)} %pad_maximum_fusion.refs_0_), channel_id=1, source_target_pairs={{0,14},{2,0},{4,2},{6,4},{8,6},{10,8},{12,10},{14,12},{1,15},{3,1}... | collective-permute-start | bytes 442376 | tf_op jit(solution)/shard_map/ppermute | solution.py:303
  18.0 10.5 %copy-start.2 = (bf16[2,288,128]{2,1,0:T(8,128)(2,1)}, bf16[2,288,128]{2,1,0:T(8,128)(2,1)S(1)}, u32[]{:S(2)}) copy-start(bf16[2,288,128]{2,1,0:T(8,128)(2,1)S(1)} %collective-permute-done.3.refs_1_) | copy-start | bytes 442372
  18.0 5.2 %collective-permute-start.4 = (bf16[2,288,128]{2,1,0:T(8,128)(2,1)S(1)}, bf16[2,288,128]{2,1,0:T(8,128)(2,1)S(1)}, u32[]{:S(2)}, u32[]{:S(2)}) collective-permute-start(bf16[2,288,128]{2,1,0:T(8,128)(2,1)S(1)} %collective-permute-done.3.refs_1_), channel_id=1, source_target_pairs={{0,2},{2,4},{4,6},{6,8},{8,10},{10,12},{12,14},{14,0},{1,3},{3,5},... | collective-permute-start | bytes 442376 | tf_op jit(solution)/shard_map/ppermute | solution.py:303
  18.0 10.5 %copy-start.3 = (bf16[2,288,128]{2,1,0:T(8,128)(2,1)}, bf16[2,288,128]{2,1,0:T(8,128)(2,1)S(1)}, u32[]{:S(2)}) copy-start(bf16[2,288,128]{2,1,0:T(8,128)(2,1)S(1)} %collective-permute-done.7.refs_7_) | copy-start | bytes 442372
  18.0 5.2 %collective-permute-start.8 = (bf16[2,288,128]{2,1,0:T(8,128)(2,1)S(1)}, bf16[2,288,128]{2,1,0:T(8,128)(2,1)}, u32[]{:S(2)}, u32[]{:S(2)}) collective-permute-start(bf16[2,288,128]{2,1,0:T(8,128)(2,1)S(1)} %collective-permute-done.7.refs_7_), channel_id=1, source_target_pairs={{0,14},{2,0},{4,2},{6,4},{8,6},{10,8},{12,10},{14,12},{1,15},{3,1}... | collective-permute-start | bytes 442376 | tf_op jit(solution)/shard_map/ppermute | solution.py:303
  23.2 5.3 %copy-start.4 = (bf16[2,288,128]{2,1,0:T(8,128)(2,1)}, bf16[2,288,128]{2,1,0:T(8,128)(2,1)S(1)}, u32[]{:S(2)}) copy-start(bf16[2,288,128]{2,1,0:T(8,128)(2,1)S(1)} %collective-permute-done.4.refs_2_) | copy-start | bytes 442372
  23.2 5.3 %collective-permute-start.5 = (bf16[2,288,128]{2,1,0:T(8,128)(2,1)S(1)}, bf16[2,288,128]{2,1,0:T(8,128)(2,1)}, u32[]{:S(2)}, u32[]{:S(2)}) collective-permute-start(bf16[2,288,128]{2,1,0:T(8,128)(2,1)S(1)} %collective-permute-done.4.refs_2_), channel_id=1, source_target_pairs={{0,2},{2,4},{4,6},{6,8},{8,10},{10,12},{12,14},{14,0},{1,3},{3,5},... | collective-permute-start | bytes 442376 | tf_op jit(solution)/shard_map/ppermute | solution.py:303
  23.2 8.6 %collective-permute-start.9 = (bf16[2,288,128]{2,1,0:T(8,128)(2,1)}, bf16[2,288,128]{2,1,0:T(8,128)(2,1)}, u32[]{:S(2)}, u32[]{:S(2)}) collective-permute-start(bf16[2,288,128]{2,1,0:T(8,128)(2,1)} %collective-permute-done.8.refs_6_), channel_id=1, source_target_pairs={{0,14},{2,0},{4,2},{6,4},{8,6},{10,8},{12,10},{14,12},{1,15},{3,1}... | collective-permute-start | bytes 442376 | tf_op jit(solution)/shard_map/ppermute | solution.py:303
  28.5 5.6 %collective-permute-start.6 = (bf16[2,288,128]{2,1,0:T(8,128)(2,1)}, bf16[2,288,128]{2,1,0:T(8,128)(2,1)}, u32[]{:S(2)}, u32[]{:S(2)}) collective-permute-start(bf16[2,288,128]{2,1,0:T(8,128)(2,1)} %collective-permute-done.5.refs_3_), channel_id=1, source_target_pairs={{0,2},{2,4},{4,6},{6,8},{8,10},{10,12},{12,14},{14,0},{1,3},{3,5},... | collective-permute-start | bytes 442376 | tf_op jit(solution)/shard_map/ppermute | solution.py:303
  34.1 7.8 %collective-permute-start.10 = (bf16[128,4224]{1,0:T(8,128)(2,1)S(1)}, bf16[128,4224]{1,0:T(8,128)(2,1)}, u32[]{:S(2)}, u32[]{:S(2)}) collective-permute-start(bf16[128,4224]{1,0:T(8,128)(2,1)S(1)} %collective-permute-done.refs_10_), channel_id=1, source_target_pairs={{0,16},{16,0},{1,17},{17,1},{2,18},{18,2},{3,19},{19,3},{4,20},{20... | collective-permute-start | bytes 3244040 | tf_op jit(solution)/shard_map/ppermute | solution.py:299
  41.9 9.0 %copy-start.6 = (s32[48]{0:T(128)S(1)}, s32[48]{0:T(128)}, u32[]{:S(2)}) copy-start(s32[48]{0:T(128)} %param.11) | copy-start | bytes 580
  48.6 2.4 %collective-permute-start.11 = (bf16[56,512]{1,0:T(8,128)(2,1)S(1)}, bf16[56,512]{1,0:T(8,128)(2,1)S(1)}, u32[]{:S(2)}, u32[]{:S(2)}) collective-permute-start(bf16[56,512]{1,0:T(8,128)(2,1)S(1)} %get-tuple-element.47), channel_id=1, source_target_pairs={{0,16},{16,0},{1,17},{17,1},{2,18},{18,2},{3,19},{19,3},{4,20},{20... | collective-permute-start | bytes 172040 | tf_op jit(solution)/shard_map/ppermute | solution.py:299
  49.1 3.4 %collective-permute-start.12 = (bf16[56,512]{1,0:T(8,128)(2,1)S(1)}, bf16[56,512]{1,0:T(8,128)(2,1)S(1)}, u32[]{:S(2)}, u32[]{:S(2)}) collective-permute-start(bf16[56,512]{1,0:T(8,128)(2,1)S(1)} %get-tuple-element.48), channel_id=1, source_target_pairs={{0,32},{32,0},{1,33},{33,1},{2,34},{34,2},{3,35},{35,3},{4,36},{36... | collective-permute-start | bytes 172040 | tf_op jit(solution)/shard_map/ppermute | solution.py:299
  49.2 4.7 %collective-permute-start.13 = (bf16[56,512]{1,0:T(8,128)(2,1)S(1)}, bf16[56,512]{1,0:T(8,128)(2,1)S(1)}, u32[]{:S(2)}, u32[]{:S(2)}) collective-permute-start(bf16[56,512]{1,0:T(8,128)(2,1)S(1)} %get-tuple-element.49), channel_id=1, source_target_pairs={{0,48},{16,32},{32,16},{48,0},{1,49},{17,33},{33,17},{49,1},{2,50}... | collective-permute-start | bytes 172040 | tf_op jit(solution)/shard_map/ppermute | solution.py:312
  55.6 15.3 %all-to-all-start = ((bf16[16,16,256]{2,1,0:T(8,128)(2,1)}), bf16[16,16,256]{2,1,0:T(8,128)(2,1)S(1)}, u32[]{:S(2)}, u32[]{:S(2)}) async-start(bf16[16,16,256]{2,1,0:T(8,128)(2,1)} %get-tuple-element.53), calls=%async_computation | async-start | bytes 262144 | tf_op jit(solution)/shard_map/all_to_all | solution.py:403

commit v12 on v11

--- a/solution.py
+++ b/solution.py
@@ -103,14 +103,17 @@
 def score_kernel(
     index_ref, *refs
 ):
-    blocks = refs[:DEPTH]
+    blocks, refs = refs[: DEPTH + 1], refs[1:]
     p0, p1, p2, p3, wc_ref, ws_ref, w_ref = refs[DEPTH : DEPTH + 7]
     own_ref, near_ref, far_ref, cross_ref, pool = refs[DEPTH + 7 : DEPTH + 12]
     stage, wide, table0, table1, scores, groups, cands, listed, sem, block_sem = refs[DEPTH + 12 :]
     q, z, xl = index_ref[0], index_ref[1], index_ref[2]
     block_copies = []
     for k, block in enumerate(blocks):
-        block_copies.append(pltpu.make_async_copy(block, stage.at[k], block_sem.at[k]))
+        slot = stage.at[k % DEPTH]
+        if k in (DEPTH // 2, DEPTH):
+            slot = stage.at[DEPTH // 2, k // DEPTH]
+        block_copies.append(pltpu.make_async_copy(block, slot, block_sem.at[k]))
     for copy in block_copies:
         copy.start()
     steps = 16 // STEP_TILES
@@ -118,8 +121,10 @@
     copies = pool_copies(q, (p0, p1, p2, p3), pool, listed, sem)
     for copy in copies:
         copy.start()
-    for k, copy in enumerate(block_copies):
-        copy.wait()
+    for k in range(DEPTH):
+        block_copies[k].wait()
+        if k == DEPTH // 2:
+            block_copies[DEPTH].wait()
         for side in range(2):
             source = ((z + DEPTH - k) % DEPTH) * 2 + (xl ^ side)
             rows = pl.ds(pl.multiple_of(source * BLOCK, BLOCK), BLOCK)
@@ -343,7 +348,8 @@
     for k in range(1, DEPTH // 2):
         ring[k] = up = turn(up, 1)
         ring[DEPTH - k] = down = turn(down, -1)
-    ring[DEPTH // 2] = turn(up, 1)
+    ring[DEPTH // 2] = turn(up[0], 1)
+    ring.append(turn(down[1], -1))
     flat = jax.ShapeDtypeStruct((NSHIFT * 16, 128), F32)
     cosine, sine, wc, ws = pl.pallas_call(
         tables_kernel,
@@ -363,7 +369,7 @@
             jax.ShapeDtypeStruct((56, NPOOL * ROWS), F32 if j == 0 else BF16) for j in range(NPOOL)
         ]
         + [jax.ShapeDtypeStruct((NPOOL * ROWS, 2 * K), BF16)],
-        in_specs=[SMEM_SPEC] + [HBM_SPEC] * DEPTH + [ANY_SPEC] * 4 + [VMEM_SPEC] * 3,
+        in_specs=[SMEM_SPEC] + [HBM_SPEC] * (DEPTH + 1) + [ANY_SPEC] * 4 + [VMEM_SPEC] * 3,
         out_specs=[VMEM_SPEC] * (NPOOL + 1),
         scratch_shapes=[
             VMEM((DEPTH, 2, BLOCK, 128), BF16),
@@ -375,7 +381,7 @@
             VMEM((8, NPOOL * ROWS), jnp.int32),
             VMEM((NPOOL, 8, ROWS), BF16),
             pltpu.SemaphoreType.DMA((2, NPOOL)),
-            pltpu.SemaphoreType.DMA((DEPTH,)),
+            pltpu.SemaphoreType.DMA((DEPTH + 1,)),
         ],
         compiler_params=params(20),
         name="score",

time: 88.2 us -> 88.8 us (level)
  waiting for transfers between devices: 29.6 us -> 27.4 us
  local copies, waits for them, and re-layouts: 0.21 us -> 1.73 us
    ppermute x7 -> x8, starting transfers between devices: 10.7 us -> 13.9 us  [turn(): return lax.ppermute(x, 'z', [(i, (i + step) % DEPTH) for i in range(DEPTH)])]
    all_to_all x1, starting transfers between devices: 6.39 us -> 3.63 us  [on_device(): sums = lax.all_to_all(sums, BLK, 0, 0, tiled=True)]
    ppermute x6, waiting for transfers between devices: 9.15 us -> 6.57 us  [swap(): return lax.ppermute(x, axis, [(0, 1), (1, 0)])]
    ppermute x6, starting transfers between devices: 10.1 us -> 11.4 us  [swap(): return lax.ppermute(x, axis, [(0, 1), (1, 0)])]
    ppermute x1, starting transfers between devices: 1.61 us -> 0.49 us  [trade(): lax.ppermute(cross, axes, [(i, 3 - i) for i in range(4)])]
    squeeze x0 -> x2, local copies, waits for them, and re-layouts: none -> 0.89 us  [the longest x1 0.89 us: on_device(): ring.append(turn(down[1], -1))]
    ppermute x7 -> x8, waiting for transfers between devices: 10.2 us -> 10.2 us  [turn(): return lax.ppermute(x, 'z', [(i, (i + step) % DEPTH) for i in range(DEPTH)])]
  transfers between devices with their start and end apart: 15 -> 16, of which waited for: 10 -> 11; matrix products, arithmetic and copies ran while one was open for 0% -> 1% of each run, Pallas kernels for 1% -> 1%
where the time goes in v12:
time: 88.8 us; the launch traced here: 88.5 us
  starting transfers between devices  29.4 us (33%)
  waiting for transfers between devices  27.4 us (31%)
  blocking collectives  16 us (18%)
  Pallas kernels  13 us (15%)
  local copies, waits for them, and re-layouts  1.73 us (2%)
    all_to_all x1, blocking collectives, on_device(): placed = lax.all_to_all(placed, DOM, 0, 0, tiled=True)  16 us
    ppermute x8, starting transfers between devices, turn(): return lax.ppermute(x, 'z', [(i, (i + step) % DEPTH) for i in range(DEPTH)])  13.9 us
    ppermute x6, starting transfers between devices, swap(): return lax.ppermute(x, axis, [(0, 1), (1, 0)])  11.4 us
    ppermute x8, waiting for transfers between devices, turn(): return lax.ppermute(x, 'z', [(i, (i + step) % DEPTH) for i in range(DEPTH)])  10.2 us
    all_to_all x1, waiting for transfers between devices, on_device(): sums = lax.all_to_all(sums, BLK, 0, 0, tiled=True)  8.37 us
    pallas_call x1, Pallas kernels, on_device(): pl.pallas_call(score_kernel, out_shape=[jax.ShapeDtypeStruct((56, NPOOL *...  6.77 us
    ppermute x6, waiting for transfers between devices, swap(): return lax.ppermute(x, axis, [(0, 1), (1, 0)])  6.57 us
    all_to_all x1, starting transfers between devices, on_device(): sums = lax.all_to_all(sums, BLK, 0, 0, tiled=True)  3.63 us
  transfers between devices with their start and end apart: 16, of which 11 were waited for; matrix products, arithmetic and copies ran while one was open for 1% of the time, Pallas kernels for 1%

profile of v12, /device:TPU:1, one launch (start us, length us, event | category | flops | bytes accessed | tf_op | source)
XLA Modules:
  0.0 88.5 jit_solution(1673480399206483126)
XLA Ops:
  0.6 0.0 copy-start.6
  0.6 0.0 copy-start
  0.7 2.2 %pack.1 = (bf16[288,128]{1,0:T(8,128)(2,1)S(1)}, bf16[128,4224]{1,0:T(8,128)(2,1)S(1)}) custom-call(s32[1]{0:T(128)} %bitcast.1.q_ref, s32[8,128]{1,0:T(8,128)} %bitcast.18, bf16[3,12,4096]{2,1,0:T(8,128)(2,1)} %refs_ref.1, bf16[128,4096]{1,0:T(8,128)(2,1)} %particles_hbm.1), custom_call_target="tpu_custom_call" | custom-call | tf_op jit(solution)/shard_map/pack/pallas_call | solution.py:328
  2.9 3.3 %collective-permute-start.1 = (bf16[128,4224]{1,0:T(8,128)(2,1)S(1)}, bf16[128,4224]{1,0:T(8,128)(2,1)S(1)}, u32[]{:S(2)}, u32[]{:S(2)}) collective-permute-start(bf16[128,4224]{1,0:T(8,128)(2,1)S(1)} %get-tuple-element.31.refs_9_), channel_id=1, source_target_pairs={{0,16},{16,0},{1,17},{17,1},{2,18},{18,2},{3,19},{19,3},{4,20},{20... | collective-permute-start | bytes 3244040 | tf_op jit(solution)/shard_map/ppermute | solution.py:304
  6.2 0.0 collective-permute-start.2
  6.2 0.8 collective-permute-start
  7.0 3.0 %collective-permute-done.2 = bf16[288,128]{1,0:T(8,128)(2,1)S(1)} collective-permute-done((bf16[288,128]{1,0:T(8,128)(2,1)S(1)}, bf16[288,128]{1,0:T(8,128)(2,1)S(1)}, u32[]{:S(2)}, u32[]{:S(2)}) %collective-permute-start.2) | collective-permute-done | bytes 73760 | tf_op jit(solution)/shard_map/ppermute | solution.py:304
  10.1 0.0 collective-permute-done.1.refs_10_
  10.1 0.0 copy-start.1
  10.1 3.9 %collective-permute-start.7 = (bf16[2,288,128]{2,1,0:T(8,128)(2,1)S(1)}, bf16[2,288,128]{2,1,0:T(8,128)(2,1)S(1)}, u32[]{:S(2)}, u32[]{:S(2)}) collective-permute-start(bf16[2,288,128]{2,1,0:T(8,128)(2,1)S(1)} %pad_maximum_fusion.refs_0_), channel_id=1, source_target_pairs={{0,14},{2,0},{4,2},{6,4},{8,6},{10,8},{12,10},{14,12},{1,15},{3,1}... | collective-permute-start | bytes 442376 | tf_op jit(solution)/shard_map/ppermute | solution.py:308
  14.0 0.0 collective-permute-start.3
  14.0 2.1 %collective-permute-done.7.refs_7_ = bf16[2,288,128]{2,1,0:T(8,128)(2,1)S(1)} collective-permute-done((bf16[2,288,128]{2,1,0:T(8,128)(2,1)S(1)}, bf16[2,288,128]{2,1,0:T(8,128)(2,1)S(1)}, u32[]{:S(2)}, u32[]{:S(2)}) %collective-permute-start.7) | collective-permute-done | bytes 147488 | tf_op jit(solution)/shard_map/ppermute | solution.py:308
  16.1 0.0 copy-start.3
  16.1 3.6 %collective-permute-start.8 = (bf16[2,288,128]{2,1,0:T(8,128)(2,1)S(1)}, bf16[2,288,128]{2,1,0:T(8,128)(2,1)}, u32[]{:S(2)}, u32[]{:S(2)}) collective-permute-start(bf16[2,288,128]{2,1,0:T(8,128)(2,1)S(1)} %collective-permute-done.7.refs_7_), channel_id=1, source_target_pairs={{0,14},{2,0},{4,2},{6,4},{8,6},{10,8},{12,10},{14,12},{1,15},{3,1}... | collective-permute-start | bytes 442376 | tf_op jit(solution)/shard_map/ppermute | solution.py:308
  19.7 0.0 collective-permute-done.3.refs_1_
  19.7 0.0 collective-permute-start.4
  19.7 2.1 %collective-permute-done.8.refs_6_ = bf16[2,288,128]{2,1,0:T(8,128)(2,1)} collective-permute-done((bf16[2,288,128]{2,1,0:T(8,128)(2,1)S(1)}, bf16[2,288,128]{2,1,0:T(8,128)(2,1)}, u32[]{:S(2)}, u32[]{:S(2)}) %collective-permute-start.8) | collective-permute-done | bytes 147488 | tf_op jit(solution)/shard_map/ppermute | solution.py:308
  21.8 0.0 copy-done.3
  21.8 3.2 %collective-permute-start.9 = (bf16[2,288,128]{2,1,0:T(8,128)(2,1)}, bf16[2,288,128]{2,1,0:T(8,128)(2,1)}, u32[]{:S(2)}, u32[]{:S(2)}) collective-permute-start(bf16[2,288,128]{2,1,0:T(8,128)(2,1)} %collective-permute-done.8.refs_6_), channel_id=1, source_target_pairs={{0,14},{2,0},{4,2},{6,4},{8,6},{10,8},{12,10},{14,12},{1,15},{3,1}... | collective-permute-start | bytes 442376 | tf_op jit(solution)/shard_map/ppermute | solution.py:308
  25.0 0.0 copy-done.6
  25.0 0.1 copy.10.off_ref
  25.1 0.1 collective-permute-done.4.refs_2_
  25.3 0.0 collective-permute-start.5
  25.3 2.2 %collective-permute-done.9.refs_5_ = bf16[2,288,128]{2,1,0:T(8,128)(2,1)} collective-permute-done((bf16[2,288,128]{2,1,0:T(8,128)(2,1)}, bf16[2,288,128]{2,1,0:T(8,128)(2,1)}, u32[]{:S(2)}, u32[]{:S(2)}) %collective-permute-start.9) | collective-permute-done | bytes 147488 | tf_op jit(solution)/shard_map/ppermute | solution.py:308
  27.5 0.9 %slice_bitcast_fusion = bf16[288,128]{1,0:T(8,128)(2,1)S(1)} fusion(bf16[2,288,128]{2,1,0:T(8,128)(2,1)} %collective-permute-done.9.refs_5_), kind=kLoop, calls=%fused_computation.1 | loop fusion | bytes 147456 | tf_op jit(solution)/shard_map/squeeze | solution.py:352
  28.3 3.1 %collective-permute-start.10 = (bf16[288,128]{1,0:T(8,128)(2,1)S(1)}, bf16[288,128]{1,0:T(8,128)(2,1)S(1)}, u32[]{:S(2)}, u32[]{:S(2)}) collective-permute-start(bf16[288,128]{1,0:T(8,128)(2,1)S(1)} %slice_bitcast_fusion), channel_id=1, source_target_pairs={{0,14},{2,0},{4,2},{6,4},{8,6},{10,8},{12,10},{14,12},{1,15},{3,1}... | collective-permute-start | bytes 221192 | tf_op jit(solution)/shard_map/ppermute | solution.py:308
  31.5 0.0 collective-permute-done.5.refs_3_
  31.5 0.0 copy-start.2
  31.5 0.1 collective-permute-start.6
  31.6 0.0 copy-done
  31.6 0.7 tables.1
  32.3 0.0 copy-done.1
  32.3 0.0 copy-done.2
  32.3 0.0 collective-permute-done.refs_11_
  32.3 0.5 collective-permute-done.10.refs_8_
  32.9 0.0 copy-start.4
  32.9 3.1 %collective-permute-done.6.refs_4_ = bf16[288,128]{1,0:T(8,128)(2,1)S(1)} collective-permute-done((bf16[288,128]{1,0:T(8,128)(2,1)S(1)}, bf16[288,128]{1,0:T(8,128)(2,1)S(1)}, u32[]{:S(2)}, u32[]{:S(2)}) %collective-permute-start.6) | collective-permute-done | bytes 73760 | tf_op jit(solution)/shard_map/ppermute | solution.py:308
  36.0 0.0 copy-done.4
  36.0 0.0 copy-start.5
  36.0 0.6 copy-done.5
  36.6 5.5 %collective-permute-start.11 = (bf16[128,4224]{1,0:T(8,128)(2,1)S(1)}, bf16[128,4224]{1,0:T(8,128)(2,1)}, u32[]{:S(2)}, u32[]{:S(2)}) collective-permute-start(bf16[128,4224]{1,0:T(8,128)(2,1)S(1)} %collective-permute-done.refs_11_), channel_id=1, source_target_pairs={{0,16},{16,0},{1,17},{17,1},{2,18},{18,2},{3,19},{19,3},{4,20},{20... | collective-permute-start | bytes 3244040 | tf_op jit(solution)/shard_map/ppermute | solution.py:304
  42.1 0.1 pad_add_fusion.index_ref
  42.2 2.4 %collective-permute-done.11.refs_12_ = bf16[128,4224]{1,0:T(8,128)(2,1)} collective-permute-done((bf16[128,4224]{1,0:T(8,128)(2,1)S(1)}, bf16[128,4224]{1,0:T(8,128)(2,1)}, u32[]{:S(2)}, u32[]{:S(2)}) %collective-permute-start.11) | collective-permute-done | bytes 1081376 | tf_op jit(solution)/shard_map/ppermute | solution.py:304
  44.6 0.0 copy-start.7
  44.6 6.8 %score.1 = (f32[56,512]{1,0:T(8,128)S(1)}, bf16[56,512]{1,0:T(8,128)(2,1)S(1)}, bf16[56,512]{1,0:T(8,128)(2,1)S(1)}, bf16[56,512]{1,0:T(8,128)(2,1)S(1)}, bf16[512,4096]{1,0:T(8,128)(2,1)S(1)}) custom-call(s32[3]{0:T(128)S(1)} %pad_add_fusion.index_ref, bf16[2,288,128]{2,1,0:T(8,128)(2,1)} %copy-done.1, bf16[2,288,128]{2,1,0:T(8,128)(2,1)} %collective-permute-done.3.refs_1_, ...), custom_call_target="tpu_custom_call" | custom-call | tf_op jit(solution)/shard_map/score/pallas_call | solution.py:366
  51.3 0.5 collective-permute-start.12
  51.8 1.3 %collective-permute-start.13 = (bf16[56,512]{1,0:T(8,128)(2,1)S(1)}, bf16[56,512]{1,0:T(8,128)(2,1)S(1)}, u32[]{:S(2)}, u32[]{:S(2)}) collective-permute-start(bf16[56,512]{1,0:T(8,128)(2,1)S(1)} %get-tuple-element.50), channel_id=1, source_target_pairs={{0,32},{32,0},{1,33},{33,1},{2,34},{34,2},{3,35},{35,3},{4,36},{36... | collective-permute-start | bytes 172040 | tf_op jit(solution)/shard_map/ppermute | solution.py:304
  53.1 0.5 collective-permute-start.14
  53.6 0.0 copy-done.7
  53.6 0.1 convert_reduce_fusion
  53.7 0.0 collective-permute-done.12.x1
  53.7 1.1 %collective-permute-done.13.x2 = bf16[56,512]{1,0:T(8,128)(2,1)S(1)} collective-permute-done((bf16[56,512]{1,0:T(8,128)(2,1)S(1)}, bf16[56,512]{1,0:T(8,128)(2,1)S(1)}, u32[]{:S(2)}, u32[]{:S(2)}) %collective-permute-start.13) | collective-permute-done | bytes 57376 | tf_op jit(solution)/shard_map/ppermute | solution.py:304
  54.8 2.3 %collective-permute-done.14.x3 = bf16[56,512]{1,0:T(8,128)(2,1)S(1)} collective-permute-done((bf16[56,512]{1,0:T(8,128)(2,1)S(1)}, bf16[56,512]{1,0:T(8,128)(2,1)S(1)}, u32[]{:S(2)}, u32[]{:S(2)}) %collective-permute-start.14) | collective-permute-done | bytes 57376 | tf_op jit(solution)/shard_map/ppermute | solution.py:317
  57.1 1.7 %classes.1 = (bf16[16,16,256]{2,1,0:T(8,128)(2,1)}, f32[1,128]{1,0:T(1,128)}) custom-call(s32[1]{0:T(128)} %bitcast.1.q_ref, f32[56,512]{1,0:T(8,128)S(1)} %get-tuple-element.48.x0, bf16[56,512]{1,0:T(8,128)(2,1)S(1)} %collective-permute-done.12.x1, bf16[56,512]{1,0:T(8,128)(2,1)S(1)} %collective-permute-done.13.x2, ...), custom_call_target="tpu_custom_call" | custom-call | tf_op jit(solution)/shard_map/classes/pallas_call | solution.py:394
  58.8 3.6 %all-to-all-start = ((bf16[16,16,256]{2,1,0:T(8,128)(2,1)}), bf16[16,16,256]{2,1,0:T(8,128)(2,1)S(1)}, u32[]{:S(2)}, u32[]{:S(2)}) async-start(bf16[16,16,256]{2,1,0:T(8,128)(2,1)} %get-tuple-element.55), calls=%async_computation | async-start | bytes 262144 | tf_op jit(solution)/shard_map/all_to_all | solution.py:409
  62.4 0.1 dynamic_slice.3
  62.5 8.4 %all-to-all-done.y_ref = bf16[16,16,256]{2,1,0:T(8,128)(2,1)S(1)} async-done(((bf16[16,16,256]{2,1,0:T(8,128)(2,1)}), bf16[16,16,256]{2,1,0:T(8,128)(2,1)S(1)}, u32[]{:S(2)}, u32[]{:S(2)}) %all-to-all-start) | async-done | bytes 131104 | tf_op jit(solution)/shard_map/all_to_all | solution.py:409
  70.9 0.8 place.1
  71.7 16.0 %all_to_all.10.z_ref = bf16[16,8,384]{2,1,0:T(8,128)(2,1)S(1)} all-to-all(bf16[16,8,384]{2,1,0:T(8,128)(2,1)} %place.1), channel_id=1, replica_groups=mesh['xh'=2,'yh'=2,'yl'=2,'core'=2,'z'=8,'xl'=2] {'xh','yh','yl','core'}, dimensions={0} | all-to-all | bytes 196608 | tf_op jit(solution)/shard_map/all_to_all | solution.py:427
  87.7 0.8 means.1
  (4 shorter events, 0.0 us)
Async XLA Ops:
  0.6 24.4 %copy-start.6 = (s32[4,2]{0,1:T(2,128)S(1)}, s32[4,2]{0,1:T(2,128)}, u32[]{:S(2)}) copy-start(s32[4,2]{0,1:T(2,128)} %param.9) | copy-start | bytes 100
  0.6 30.9 %copy-start = (f32[2048]{0:T(1024)S(1)}, f32[2048]{0:T(1024)}, u32[]{:S(2)}) copy-start(f32[2048]{0:T(1024)} %param.8) | copy-start | bytes 24580
  2.9 7.2 %collective-permute-start.1 = (bf16[128,4224]{1,0:T(8,128)(2,1)S(1)}, bf16[128,4224]{1,0:T(8,128)(2,1)S(1)}, u32[]{:S(2)}, u32[]{:S(2)}) collective-permute-start(bf16[128,4224]{1,0:T(8,128)(2,1)S(1)} %get-tuple-element.31.refs_9_), channel_id=1, source_target_pairs={{0,16},{16,0},{1,17},{17,1},{2,18},{18,2},{3,19},{19,3},{4,20},{20... | collective-permute-start | bytes 3244040 | tf_op jit(solution)/shard_map/ppermute | solution.py:304
  6.2 3.8 %collective-permute-start.2 = (bf16[288,128]{1,0:T(8,128)(2,1)S(1)}, bf16[288,128]{1,0:T(8,128)(2,1)S(1)}, u32[]{:S(2)}, u32[]{:S(2)}) collective-permute-start(bf16[288,128]{1,0:T(8,128)(2,1)S(1)} %get-tuple-element.33), channel_id=1, source_target_pairs={{0,1},{1,0},{2,3},{3,2},{4,5},{5,4},{6,7},{7,6},{8,9},{9,8},{10,11... | collective-permute-start | bytes 221192 | tf_op jit(solution)/shard_map/ppermute | solution.py:304
  6.2 26.1 %collective-permute-start = (bf16[128,4224]{1,0:T(8,128)(2,1)S(1)}, bf16[128,4224]{1,0:T(8,128)(2,1)S(1)}, u32[]{:S(2)}, u32[]{:S(2)}) collective-permute-start(bf16[128,4224]{1,0:T(8,128)(2,1)S(1)} %get-tuple-element.31.refs_9_), channel_id=1, source_target_pairs={{0,32},{32,0},{1,33},{33,1},{2,34},{34,2},{3,35},{35,3},{4,36},{36... | collective-permute-start | bytes 3244040 | tf_op jit(solution)/shard_map/ppermute | solution.py:304
  10.1 22.2 %copy-start.1 = (bf16[2,288,128]{2,1,0:T(8,128)(2,1)}, bf16[2,288,128]{2,1,0:T(8,128)(2,1)S(1)}, u32[]{:S(2)}) copy-start(bf16[2,288,128]{2,1,0:T(8,128)(2,1)S(1)} %pad_maximum_fusion.refs_0_) | copy-start | bytes 442372
  10.1 6.0 %collective-permute-start.7 = (bf16[2,288,128]{2,1,0:T(8,128)(2,1)S(1)}, bf16[2,288,128]{2,1,0:T(8,128)(2,1)S(1)}, u32[]{:S(2)}, u32[]{:S(2)}) collective-permute-start(bf16[2,288,128]{2,1,0:T(8,128)(2,1)S(1)} %pad_maximum_fusion.refs_0_), channel_id=1, source_target_pairs={{0,14},{2,0},{4,2},{6,4},{8,6},{10,8},{12,10},{14,12},{1,15},{3,1}... | collective-permute-start | bytes 442376 | tf_op jit(solution)/shard_map/ppermute | solution.py:308
  14.0 5.7 %collective-permute-start.3 = (bf16[2,288,128]{2,1,0:T(8,128)(2,1)S(1)}, bf16[2,288,128]{2,1,0:T(8,128)(2,1)}, u32[]{:S(2)}, u32[]{:S(2)}) collective-permute-start(bf16[2,288,128]{2,1,0:T(8,128)(2,1)S(1)} %pad_maximum_fusion.refs_0_), channel_id=1, source_target_pairs={{0,2},{2,4},{4,6},{6,8},{8,10},{10,12},{12,14},{14,0},{1,3},{3,5},... | collective-permute-start | bytes 442376 | tf_op jit(solution)/shard_map/ppermute | solution.py:308
  16.1 5.7 %copy-start.3 = (bf16[2,288,128]{2,1,0:T(8,128)(2,1)}, bf16[2,288,128]{2,1,0:T(8,128)(2,1)S(1)}, u32[]{:S(2)}) copy-start(bf16[2,288,128]{2,1,0:T(8,128)(2,1)S(1)} %collective-permute-done.7.refs_7_) | copy-start | bytes 442372
  16.1 5.7 %collective-permute-start.8 = (bf16[2,288,128]{2,1,0:T(8,128)(2,1)S(1)}, bf16[2,288,128]{2,1,0:T(8,128)(2,1)}, u32[]{:S(2)}, u32[]{:S(2)}) collective-permute-start(bf16[2,288,128]{2,1,0:T(8,128)(2,1)S(1)} %collective-permute-done.7.refs_7_), channel_id=1, source_target_pairs={{0,14},{2,0},{4,2},{6,4},{8,6},{10,8},{12,10},{14,12},{1,15},{3,1}... | collective-permute-start | bytes 442376 | tf_op jit(solution)/shard_map/ppermute | solution.py:308
  19.7 5.5 %collective-permute-start.4 = (bf16[2,288,128]{2,1,0:T(8,128)(2,1)}, bf16[2,288,128]{2,1,0:T(8,128)(2,1)}, u32[]{:S(2)}, u32[]{:S(2)}) collective-permute-start(bf16[2,288,128]{2,1,0:T(8,128)(2,1)} %collective-permute-done.3.refs_1_), channel_id=1, source_target_pairs={{0,2},{2,4},{4,6},{6,8},{8,10},{10,12},{12,14},{14,0},{1,3},{3,5},... | collective-permute-start | bytes 442376 | tf_op jit(solution)/shard_map/ppermute | solution.py:308
  21.8 5.6 %collective-permute-start.9 = (bf16[2,288,128]{2,1,0:T(8,128)(2,1)}, bf16[2,288,128]{2,1,0:T(8,128)(2,1)}, u32[]{:S(2)}, u32[]{:S(2)}) collective-permute-start(bf16[2,288,128]{2,1,0:T(8,128)(2,1)} %collective-permute-done.8.refs_6_), channel_id=1, source_target_pairs={{0,14},{2,0},{4,2},{6,4},{8,6},{10,8},{12,10},{14,12},{1,15},{3,1}... | collective-permute-start | bytes 442376 | tf_op jit(solution)/shard_map/ppermute | solution.py:308
  25.3 6.2 %collective-permute-start.5 = (bf16[2,288,128]{2,1,0:T(8,128)(2,1)}, bf16[2,288,128]{2,1,0:T(8,128)(2,1)S(1)}, u32[]{:S(2)}, u32[]{:S(2)}) collective-permute-start(bf16[2,288,128]{2,1,0:T(8,128)(2,1)} %collective-permute-done.4.refs_2_), channel_id=1, source_target_pairs={{0,2},{2,4},{4,6},{6,8},{8,10},{10,12},{12,14},{14,0},{1,3},{3,5},... | collective-permute-start | bytes 442376 | tf_op jit(solution)/shard_map/ppermute | solution.py:308
  28.3 4.5 %collective-permute-start.10 = (bf16[288,128]{1,0:T(8,128)(2,1)S(1)}, bf16[288,128]{1,0:T(8,128)(2,1)S(1)}, u32[]{:S(2)}, u32[]{:S(2)}) collective-permute-start(bf16[288,128]{1,0:T(8,128)(2,1)S(1)} %slice_bitcast_fusion), channel_id=1, source_target_pairs={{0,14},{2,0},{4,2},{6,4},{8,6},{10,8},{12,10},{14,12},{1,15},{3,1}... | collective-permute-start | bytes 221192 | tf_op jit(solution)/shard_map/ppermute | solution.py:308
  31.5 0.8 copy-start.2
  31.5 4.5 %collective-permute-start.6 = (bf16[288,128]{1,0:T(8,128)(2,1)S(1)}, bf16[288,128]{1,0:T(8,128)(2,1)S(1)}, u32[]{:S(2)}, u32[]{:S(2)}) collective-permute-start(bf16[288,128]{1,0:T(8,128)(2,1)S(1)} %slice_bitcast_fusion.1), channel_id=1, source_target_pairs={{0,2},{2,4},{4,6},{6,8},{8,10},{10,12},{12,14},{14,0},{1,3},{3,5},... | collective-permute-start | bytes 221192 | tf_op jit(solution)/shard_map/ppermute | solution.py:308
  32.9 3.1 %copy-start.4 = (bf16[288,128]{1,0:T(8,128)(2,1)}, bf16[288,128]{1,0:T(8,128)(2,1)S(1)}, u32[]{:S(2)}) copy-start(bf16[288,128]{1,0:T(8,128)(2,1)S(1)} %collective-permute-done.10.refs_8_) | copy-start | bytes 221188
  36.0 0.6 copy-start.5
  36.6 8.0 %collective-permute-start.11 = (bf16[128,4224]{1,0:T(8,128)(2,1)S(1)}, bf16[128,4224]{1,0:T(8,128)(2,1)}, u32[]{:S(2)}, u32[]{:S(2)}) collective-permute-start(bf16[128,4224]{1,0:T(8,128)(2,1)S(1)} %collective-permute-done.refs_11_), channel_id=1, source_target_pairs={{0,16},{16,0},{1,17},{17,1},{2,18},{18,2},{3,19},{19,3},{4,20},{20... | collective-permute-start | bytes 3244040 | tf_op jit(solution)/shard_map/ppermute | solution.py:304
  44.6 9.0 %copy-start.7 = (s32[48]{0:T(128)S(1)}, s32[48]{0:T(128)}, u32[]{:S(2)}) copy-start(s32[48]{0:T(128)} %param.11) | copy-start | bytes 580
  51.3 2.3 %collective-permute-start.12 = (bf16[56,512]{1,0:T(8,128)(2,1)S(1)}, bf16[56,512]{1,0:T(8,128)(2,1)S(1)}, u32[]{:S(2)}, u32[]{:S(2)}) collective-permute-start(bf16[56,512]{1,0:T(8,128)(2,1)S(1)} %get-tuple-element.49), channel_id=1, source_target_pairs={{0,16},{16,0},{1,17},{17,1},{2,18},{18,2},{3,19},{19,3},{4,20},{20... | collective-permute-start | bytes 172040 | tf_op jit(solution)/shard_map/ppermute | solution.py:304
  51.8 3.0 %collective-permute-start.13 = (bf16[56,512]{1,0:T(8,128)(2,1)S(1)}, bf16[56,512]{1,0:T(8,128)(2,1)S(1)}, u32[]{:S(2)}, u32[]{:S(2)}) collective-permute-start(bf16[56,512]{1,0:T(8,128)(2,1)S(1)} %get-tuple-element.50), channel_id=1, source_target_pairs={{0,32},{32,0},{1,33},{33,1},{2,34},{34,2},{3,35},{35,3},{4,36},{36... | collective-permute-start | bytes 172040 | tf_op jit(solution)/shard_map/ppermute | solution.py:304
  53.1 4.0 %collective-permute-start.14 = (bf16[56,512]{1,0:T(8,128)(2,1)S(1)}, bf16[56,512]{1,0:T(8,128)(2,1)S(1)}, u32[]{:S(2)}, u32[]{:S(2)}) collective-permute-start(bf16[56,512]{1,0:T(8,128)(2,1)S(1)} %get-tuple-element.51), channel_id=1, source_target_pairs={{0,48},{16,32},{32,16},{48,0},{1,49},{17,33},{33,17},{49,1},{2,50}... | collective-permute-start | bytes 172040 | tf_op jit(solution)/shard_map/ppermute | solution.py:317
  58.8 12.1 %all-to-all-start = ((bf16[16,16,256]{2,1,0:T(8,128)(2,1)}), bf16[16,16,256]{2,1,0:T(8,128)(2,1)S(1)}, u32[]{:S(2)}, u32[]{:S(2)}) async-start(bf16[16,16,256]{2,1,0:T(8,128)(2,1)} %get-tuple-element.55), calls=%async_computation | async-start | bytes 262144 | tf_op jit(solution)/shard_map/all_to_all | solution.py:409

commit v13 on v11

--- a/solution.py
+++ b/solution.py
@@ -35,7 +35,7 @@
 DEPTH = 8
 BLOCK = LOCAL * QROT * 32
 COLS = 256
-STEP_TILES = 2
+STEP_TILES = 4
 F32 = jnp.float32
 BF16 = jnp.bfloat16
 VMEM = pltpu.VMEM

time: 88.2 us -> 88.5 us (level)
  no operation moved by 1% of the time
where the time goes in v13:
time: 88.5 us; the launch traced here: 88.2 us
  waiting for transfers between devices  29.6 us (33%)
  starting transfers between devices  28.7 us (32%)
  blocking collectives  15.4 us (17%)
  Pallas kernels  13.3 us (15%)
    all_to_all x1, blocking collectives, on_device(): placed = lax.all_to_all(placed, DOM, 0, 0, tiled=True)  15.4 us
    ppermute x7, starting transfers between devices, turn(): return lax.ppermute(x, 'z', [(i, (i + step) % DEPTH) for i in range(DEPTH)])  10.7 us
    ppermute x7, waiting for transfers between devices, turn(): return lax.ppermute(x, 'z', [(i, (i + step) % DEPTH) for i in range(DEPTH)])  10.2 us
    ppermute x6, starting transfers between devices, swap(): return lax.ppermute(x, axis, [(0, 1), (1, 0)])  10 us
    ppermute x6, waiting for transfers between devices, swap(): return lax.ppermute(x, axis, [(0, 1), (1, 0)])  8.79 us
    all_to_all x1, waiting for transfers between devices, on_device(): sums = lax.all_to_all(sums, BLK, 0, 0, tiled=True)  8.75 us
    pallas_call x1, Pallas kernels, on_device(): pl.pallas_call(score_kernel, out_shape=[jax.ShapeDtypeStruct((56, NPOOL *...  7.09 us
    all_to_all x1, starting transfers between devices, on_device(): sums = lax.all_to_all(sums, BLK, 0, 0, tiled=True)  6.42 us
  transfers between devices with their start and end apart: 15, of which 10 were waited for; matrix products, arithmetic and copies ran while one was open for 0% of the time, Pallas kernels for 1%

profile of v13, /device:TPU:1, one launch (start us, length us, event | category | flops | bytes accessed | tf_op | source)
XLA Modules:
  0.0 88.2 jit_solution(10416496095845581152)
XLA Ops:
  0.6 0.0 copy-start.5
  0.6 0.0 copy-start
  0.7 2.2 %pack.1 = (bf16[288,128]{1,0:T(8,128)(2,1)S(1)}, bf16[128,4224]{1,0:T(8,128)(2,1)S(1)}) custom-call(s32[1]{0:T(128)} %bitcast.1.q_ref, s32[8,128]{1,0:T(8,128)} %bitcast.14, bf16[3,12,4096]{2,1,0:T(8,128)(2,1)} %refs_ref.1, bf16[128,4096]{1,0:T(8,128)(2,1)} %particles_hbm.1), custom_call_target="tpu_custom_call" | custom-call | tf_op jit(solution)/shard_map/pack/pallas_call | solution.py:323
  2.9 3.3 %collective-permute-start.1 = (bf16[128,4224]{1,0:T(8,128)(2,1)S(1)}, bf16[128,4224]{1,0:T(8,128)(2,1)S(1)}, u32[]{:S(2)}, u32[]{:S(2)}) collective-permute-start(bf16[128,4224]{1,0:T(8,128)(2,1)S(1)} %get-tuple-element.30.refs_8_), channel_id=1, source_target_pairs={{0,16},{16,0},{1,17},{17,1},{2,18},{18,2},{3,19},{19,3},{4,20},{20... | collective-permute-start | bytes 3244040 | tf_op jit(solution)/shard_map/ppermute | solution.py:299
  6.2 0.0 collective-permute-start
  6.2 0.8 collective-permute-start.2
  7.0 2.9 %collective-permute-done.2 = bf16[288,128]{1,0:T(8,128)(2,1)S(1)} collective-permute-done((bf16[288,128]{1,0:T(8,128)(2,1)S(1)}, bf16[288,128]{1,0:T(8,128)(2,1)S(1)}, u32[]{:S(2)}, u32[]{:S(2)}) %collective-permute-start.2) | collective-permute-done | bytes 73760 | tf_op jit(solution)/shard_map/ppermute | solution.py:299
  9.9 0.0 collective-permute-done.1.refs_9_
  9.9 0.0 copy-start.1
  10.0 1.1 %collective-permute-start.3 = (bf16[2,288,128]{2,1,0:T(8,128)(2,1)S(1)}, bf16[2,288,128]{2,1,0:T(8,128)(2,1)S(1)}, u32[]{:S(2)}, u32[]{:S(2)}) collective-permute-start(bf16[2,288,128]{2,1,0:T(8,128)(2,1)S(1)} %pad_maximum_fusion.refs_0_), channel_id=1, source_target_pairs={{0,2},{2,4},{4,6},{6,8},{8,10},{10,12},{12,14},{14,0},{1,3},{3,5},... | collective-permute-start | bytes 442376 | tf_op jit(solution)/shard_map/ppermute | solution.py:303
  11.1 4.0 %collective-permute-start.7 = (bf16[2,288,128]{2,1,0:T(8,128)(2,1)S(1)}, bf16[2,288,128]{2,1,0:T(8,128)(2,1)S(1)}, u32[]{:S(2)}, u32[]{:S(2)}) collective-permute-start(bf16[2,288,128]{2,1,0:T(8,128)(2,1)S(1)} %pad_maximum_fusion.refs_0_), channel_id=1, source_target_pairs={{0,14},{2,0},{4,2},{6,4},{8,6},{10,8},{12,10},{14,12},{1,15},{3,1}... | collective-permute-start | bytes 442376 | tf_op jit(solution)/shard_map/ppermute | solution.py:303
  15.1 2.9 %collective-permute-done.3.refs_1_ = bf16[2,288,128]{2,1,0:T(8,128)(2,1)S(1)} collective-permute-done((bf16[2,288,128]{2,1,0:T(8,128)(2,1)S(1)}, bf16[2,288,128]{2,1,0:T(8,128)(2,1)S(1)}, u32[]{:S(2)}, u32[]{:S(2)}) %collective-permute-start.3) | collective-permute-done | bytes 147488 | tf_op jit(solution)/shard_map/ppermute | solution.py:303
  18.0 0.0 copy-start.2
  18.0 0.0 collective-permute-start.4
  18.0 0.0 collective-permute-done.7.refs_7_
  18.0 0.0 copy-start.3
  18.0 2.7 %collective-permute-start.8 = (bf16[2,288,128]{2,1,0:T(8,128)(2,1)S(1)}, bf16[2,288,128]{2,1,0:T(8,128)(2,1)}, u32[]{:S(2)}, u32[]{:S(2)}) collective-permute-start(bf16[2,288,128]{2,1,0:T(8,128)(2,1)S(1)} %collective-permute-done.7.refs_7_), channel_id=1, source_target_pairs={{0,14},{2,0},{4,2},{6,4},{8,6},{10,8},{12,10},{14,12},{1,15},{3,1}... | collective-permute-start | bytes 442376 | tf_op jit(solution)/shard_map/ppermute | solution.py:303
  20.6 2.5 %collective-permute-done.4.refs_2_ = bf16[2,288,128]{2,1,0:T(8,128)(2,1)S(1)} collective-permute-done((bf16[2,288,128]{2,1,0:T(8,128)(2,1)S(1)}, bf16[2,288,128]{2,1,0:T(8,128)(2,1)S(1)}, u32[]{:S(2)}, u32[]{:S(2)}) %collective-permute-start.4) | collective-permute-done | bytes 147488 | tf_op jit(solution)/shard_map/ppermute | solution.py:303
  23.2 0.0 copy-start.4
  23.2 0.0 collective-permute-start.5
  23.2 0.0 collective-permute-done.8.refs_6_
  23.2 2.8 %collective-permute-start.9 = (bf16[2,288,128]{2,1,0:T(8,128)(2,1)}, bf16[2,288,128]{2,1,0:T(8,128)(2,1)}, u32[]{:S(2)}, u32[]{:S(2)}) collective-permute-start(bf16[2,288,128]{2,1,0:T(8,128)(2,1)} %collective-permute-done.8.refs_6_), channel_id=1, source_target_pairs={{0,14},{2,0},{4,2},{6,4},{8,6},{10,8},{12,10},{14,12},{1,15},{3,1}... | collective-permute-start | bytes 442376 | tf_op jit(solution)/shard_map/ppermute | solution.py:303
  26.0 2.5 %collective-permute-done.5.refs_3_ = bf16[2,288,128]{2,1,0:T(8,128)(2,1)} collective-permute-done((bf16[2,288,128]{2,1,0:T(8,128)(2,1)S(1)}, bf16[2,288,128]{2,1,0:T(8,128)(2,1)}, u32[]{:S(2)}, u32[]{:S(2)}) %collective-permute-start.5) | collective-permute-done | bytes 147488 | tf_op jit(solution)/shard_map/ppermute | solution.py:303
  28.5 0.0 copy-done.2
  28.5 0.0 copy-done.3
  28.5 0.0 copy-done.4
  28.5 0.1 collective-permute-start.6
  28.6 0.0 copy-done.5
  28.6 0.1 copy.10.off_ref
  28.7 0.0 copy-done
  28.7 0.7 tables.1
  29.4 0.0 copy-done.1
  29.4 2.4 %collective-permute-done.refs_10_ = bf16[128,4224]{1,0:T(8,128)(2,1)S(1)} collective-permute-done((bf16[128,4224]{1,0:T(8,128)(2,1)S(1)}, bf16[128,4224]{1,0:T(8,128)(2,1)S(1)}, u32[]{:S(2)}, u32[]{:S(2)}) %collective-permute-start) | collective-permute-done | bytes 1081376 | tf_op jit(solution)/shard_map/ppermute | solution.py:299
  31.8 0.0 collective-permute-done.9.refs_5_
  31.8 2.3 %collective-permute-done.6.refs_4_ = bf16[2,288,128]{2,1,0:T(8,128)(2,1)} collective-permute-done((bf16[2,288,128]{2,1,0:T(8,128)(2,1)}, bf16[2,288,128]{2,1,0:T(8,128)(2,1)}, u32[]{:S(2)}, u32[]{:S(2)}) %collective-permute-start.6) | collective-permute-done | bytes 147488 | tf_op jit(solution)/shard_map/ppermute | solution.py:303
  34.1 5.3 %collective-permute-start.10 = (bf16[128,4224]{1,0:T(8,128)(2,1)S(1)}, bf16[128,4224]{1,0:T(8,128)(2,1)}, u32[]{:S(2)}, u32[]{:S(2)}) collective-permute-start(bf16[128,4224]{1,0:T(8,128)(2,1)S(1)} %collective-permute-done.refs_10_), channel_id=1, source_target_pairs={{0,16},{16,0},{1,17},{17,1},{2,18},{18,2},{3,19},{19,3},{4,20},{20... | collective-permute-start | bytes 3244040 | tf_op jit(solution)/shard_map/ppermute | solution.py:299
  39.4 0.1 pad_add_fusion.index_ref
  39.5 2.4 %collective-permute-done.10.refs_11_ = bf16[128,4224]{1,0:T(8,128)(2,1)} collective-permute-done((bf16[128,4224]{1,0:T(8,128)(2,1)S(1)}, bf16[128,4224]{1,0:T(8,128)(2,1)}, u32[]{:S(2)}, u32[]{:S(2)}) %collective-permute-start.10) | collective-permute-done | bytes 1081376 | tf_op jit(solution)/shard_map/ppermute | solution.py:299
  41.9 0.0 copy-start.6
  41.9 7.1 %score.1 = (f32[56,512]{1,0:T(8,128)S(1)}, bf16[56,512]{1,0:T(8,128)(2,1)S(1)}, bf16[56,512]{1,0:T(8,128)(2,1)S(1)}, bf16[56,512]{1,0:T(8,128)(2,1)S(1)}, bf16[512,4096]{1,0:T(8,128)(2,1)S(1)}) custom-call(s32[3]{0:T(128)S(1)} %pad_add_fusion.index_ref, bf16[2,288,128]{2,1,0:T(8,128)(2,1)} %copy-done.1, bf16[2,288,128]{2,1,0:T(8,128)(2,1)} %copy-done.2, ...), custom_call_target="tpu_custom_call" | custom-call | tf_op jit(solution)/shard_map/score/pallas_call | solution.py:360
  48.9 0.5 collective-permute-start.11
  49.4 0.2 collective-permute-start.12
  49.6 1.6 %collective-permute-start.13 = (bf16[56,512]{1,0:T(8,128)(2,1)S(1)}, bf16[56,512]{1,0:T(8,128)(2,1)S(1)}, u32[]{:S(2)}, u32[]{:S(2)}) collective-permute-start(bf16[56,512]{1,0:T(8,128)(2,1)S(1)} %get-tuple-element.49), channel_id=1, source_target_pairs={{0,48},{16,32},{32,16},{48,0},{1,49},{17,33},{33,17},{49,1},{2,50}... | collective-permute-start | bytes 172040 | tf_op jit(solution)/shard_map/ppermute | solution.py:312
  51.2 0.0 copy-done.6
  51.2 0.1 convert_reduce_fusion
  51.3 0.0 collective-permute-done.11.x1
  51.3 1.1 %collective-permute-done.12.x2 = bf16[56,512]{1,0:T(8,128)(2,1)S(1)} collective-permute-done((bf16[56,512]{1,0:T(8,128)(2,1)S(1)}, bf16[56,512]{1,0:T(8,128)(2,1)S(1)}, u32[]{:S(2)}, u32[]{:S(2)}) %collective-permute-start.12) | collective-permute-done | bytes 57376 | tf_op jit(solution)/shard_map/ppermute | solution.py:299
  52.4 1.8 %collective-permute-done.13.x3 = bf16[56,512]{1,0:T(8,128)(2,1)S(1)} collective-permute-done((bf16[56,512]{1,0:T(8,128)(2,1)S(1)}, bf16[56,512]{1,0:T(8,128)(2,1)S(1)}, u32[]{:S(2)}, u32[]{:S(2)}) %collective-permute-start.13) | collective-permute-done | bytes 57376 | tf_op jit(solution)/shard_map/ppermute | solution.py:312
  54.3 1.7 %classes.1 = (bf16[16,16,256]{2,1,0:T(8,128)(2,1)}, f32[1,128]{1,0:T(1,128)}) custom-call(s32[1]{0:T(128)} %bitcast.1.q_ref, f32[56,512]{1,0:T(8,128)S(1)} %get-tuple-element.46.x0, bf16[56,512]{1,0:T(8,128)(2,1)S(1)} %collective-permute-done.11.x1, bf16[56,512]{1,0:T(8,128)(2,1)S(1)} %collective-permute-done.12.x2, ...), custom_call_target="tpu_custom_call" | custom-call | tf_op jit(solution)/shard_map/classes/pallas_call | solution.py:388
  56.0 6.4 %all-to-all-start = ((bf16[16,16,256]{2,1,0:T(8,128)(2,1)}), bf16[16,16,256]{2,1,0:T(8,128)(2,1)S(1)}, u32[]{:S(2)}, u32[]{:S(2)}) async-start(bf16[16,16,256]{2,1,0:T(8,128)(2,1)} %get-tuple-element.53), calls=%async_computation | async-start | bytes 262144 | tf_op jit(solution)/shard_map/all_to_all | solution.py:403
  62.4 0.1 dynamic_slice.3
  62.5 8.7 %all-to-all-done.y_ref = bf16[16,16,256]{2,1,0:T(8,128)(2,1)S(1)} async-done(((bf16[16,16,256]{2,1,0:T(8,128)(2,1)}), bf16[16,16,256]{2,1,0:T(8,128)(2,1)S(1)}, u32[]{:S(2)}, u32[]{:S(2)}) %all-to-all-start) | async-done | bytes 131104 | tf_op jit(solution)/shard_map/all_to_all | solution.py:403
  71.2 0.8 place.1
  72.0 15.4 %all_to_all.10.z_ref = bf16[16,8,384]{2,1,0:T(8,128)(2,1)S(1)} all-to-all(bf16[16,8,384]{2,1,0:T(8,128)(2,1)} %place.1), channel_id=1, replica_groups=mesh['xh'=2,'yh'=2,'yl'=2,'core'=2,'z'=8,'xl'=2] {'xh','yh','yl','core'}, dimensions={0} | all-to-all | bytes 196608 | tf_op jit(solution)/shard_map/all_to_all | solution.py:421
  87.5 0.8 means.1
  (3 shorter events, 0.0 us)
Async XLA Ops:
  0.6 28.0 %copy-start.5 = (s32[4,2]{0,1:T(2,128)S(1)}, s32[4,2]{0,1:T(2,128)}, u32[]{:S(2)}) copy-start(s32[4,2]{0,1:T(2,128)} %param.9) | copy-start | bytes 100
  0.6 28.0 %copy-start = (f32[2048]{0:T(1024)S(1)}, f32[2048]{0:T(1024)}, u32[]{:S(2)}) copy-start(f32[2048]{0:T(1024)} %param.8) | copy-start | bytes 24580
  2.9 7.0 %collective-permute-start.1 = (bf16[128,4224]{1,0:T(8,128)(2,1)S(1)}, bf16[128,4224]{1,0:T(8,128)(2,1)S(1)}, u32[]{:S(2)}, u32[]{:S(2)}) collective-permute-start(bf16[128,4224]{1,0:T(8,128)(2,1)S(1)} %get-tuple-element.30.refs_8_), channel_id=1, source_target_pairs={{0,16},{16,0},{1,17},{17,1},{2,18},{18,2},{3,19},{19,3},{4,20},{20... | collective-permute-start | bytes 3244040 | tf_op jit(solution)/shard_map/ppermute | solution.py:299
  6.2 25.5 %collective-permute-start = (bf16[128,4224]{1,0:T(8,128)(2,1)S(1)}, bf16[128,4224]{1,0:T(8,128)(2,1)S(1)}, u32[]{:S(2)}, u32[]{:S(2)}) collective-permute-start(bf16[128,4224]{1,0:T(8,128)(2,1)S(1)} %get-tuple-element.30.refs_8_), channel_id=1, source_target_pairs={{0,32},{32,0},{1,33},{33,1},{2,34},{34,2},{3,35},{35,3},{4,36},{36... | collective-permute-start | bytes 3244040 | tf_op jit(solution)/shard_map/ppermute | solution.py:299
  6.2 3.7 %collective-permute-start.2 = (bf16[288,128]{1,0:T(8,128)(2,1)S(1)}, bf16[288,128]{1,0:T(8,128)(2,1)S(1)}, u32[]{:S(2)}, u32[]{:S(2)}) collective-permute-start(bf16[288,128]{1,0:T(8,128)(2,1)S(1)} %get-tuple-element.32), channel_id=1, source_target_pairs={{0,1},{1,0},{2,3},{3,2},{4,5},{5,4},{6,7},{7,6},{8,9},{9,8},{10,11... | collective-permute-start | bytes 221192 | tf_op jit(solution)/shard_map/ppermute | solution.py:299
  9.9 19.5 %copy-start.1 = (bf16[2,288,128]{2,1,0:T(8,128)(2,1)}, bf16[2,288,128]{2,1,0:T(8,128)(2,1)S(1)}, u32[]{:S(2)}) copy-start(bf16[2,288,128]{2,1,0:T(8,128)(2,1)S(1)} %pad_maximum_fusion.refs_0_) | copy-start | bytes 442372
  10.0 8.0 %collective-permute-start.3 = (bf16[2,288,128]{2,1,0:T(8,128)(2,1)S(1)}, bf16[2,288,128]{2,1,0:T(8,128)(2,1)S(1)}, u32[]{:S(2)}, u32[]{:S(2)}) collective-permute-start(bf16[2,288,128]{2,1,0:T(8,128)(2,1)S(1)} %pad_maximum_fusion.refs_0_), channel_id=1, source_target_pairs={{0,2},{2,4},{4,6},{6,8},{8,10},{10,12},{12,14},{14,0},{1,3},{3,5},... | collective-permute-start | bytes 442376 | tf_op jit(solution)/shard_map/ppermute | solution.py:303
  11.1 6.9 %collective-permute-start.7 = (bf16[2,288,128]{2,1,0:T(8,128)(2,1)S(1)}, bf16[2,288,128]{2,1,0:T(8,128)(2,1)S(1)}, u32[]{:S(2)}, u32[]{:S(2)}) collective-permute-start(bf16[2,288,128]{2,1,0:T(8,128)(2,1)S(1)} %pad_maximum_fusion.refs_0_), channel_id=1, source_target_pairs={{0,14},{2,0},{4,2},{6,4},{8,6},{10,8},{12,10},{14,12},{1,15},{3,1}... | collective-permute-start | bytes 442376 | tf_op jit(solution)/shard_map/ppermute | solution.py:303
  18.0 10.5 %copy-start.2 = (bf16[2,288,128]{2,1,0:T(8,128)(2,1)}, bf16[2,288,128]{2,1,0:T(8,128)(2,1)S(1)}, u32[]{:S(2)}) copy-start(bf16[2,288,128]{2,1,0:T(8,128)(2,1)S(1)} %collective-permute-done.3.refs_1_) | copy-start | bytes 442372
  18.0 5.2 %collective-permute-start.4 = (bf16[2,288,128]{2,1,0:T(8,128)(2,1)S(1)}, bf16[2,288,128]{2,1,0:T(8,128)(2,1)S(1)}, u32[]{:S(2)}, u32[]{:S(2)}) collective-permute-start(bf16[2,288,128]{2,1,0:T(8,128)(2,1)S(1)} %collective-permute-done.3.refs_1_), channel_id=1, source_target_pairs={{0,2},{2,4},{4,6},{6,8},{8,10},{10,12},{12,14},{14,0},{1,3},{3,5},... | collective-permute-start | bytes 442376 | tf_op jit(solution)/shard_map/ppermute | solution.py:303
  18.0 10.5 %copy-start.3 = (bf16[2,288,128]{2,1,0:T(8,128)(2,1)}, bf16[2,288,128]{2,1,0:T(8,128)(2,1)S(1)}, u32[]{:S(2)}) copy-start(bf16[2,288,128]{2,1,0:T(8,128)(2,1)S(1)} %collective-permute-done.7.refs_7_) | copy-start | bytes 442372
  18.0 5.2 %collective-permute-start.8 = (bf16[2,288,128]{2,1,0:T(8,128)(2,1)S(1)}, bf16[2,288,128]{2,1,0:T(8,128)(2,1)}, u32[]{:S(2)}, u32[]{:S(2)}) collective-permute-start(bf16[2,288,128]{2,1,0:T(8,128)(2,1)S(1)} %collective-permute-done.7.refs_7_), channel_id=1, source_target_pairs={{0,14},{2,0},{4,2},{6,4},{8,6},{10,8},{12,10},{14,12},{1,15},{3,1}... | collective-permute-start | bytes 442376 | tf_op jit(solution)/shard_map/ppermute | solution.py:303
  23.2 5.3 %copy-start.4 = (bf16[2,288,128]{2,1,0:T(8,128)(2,1)}, bf16[2,288,128]{2,1,0:T(8,128)(2,1)S(1)}, u32[]{:S(2)}) copy-start(bf16[2,288,128]{2,1,0:T(8,128)(2,1)S(1)} %collective-permute-done.4.refs_2_) | copy-start | bytes 442372
  23.2 5.3 %collective-permute-start.5 = (bf16[2,288,128]{2,1,0:T(8,128)(2,1)S(1)}, bf16[2,288,128]{2,1,0:T(8,128)(2,1)}, u32[]{:S(2)}, u32[]{:S(2)}) collective-permute-start(bf16[2,288,128]{2,1,0:T(8,128)(2,1)S(1)} %collective-permute-done.4.refs_2_), channel_id=1, source_target_pairs={{0,2},{2,4},{4,6},{6,8},{8,10},{10,12},{12,14},{14,0},{1,3},{3,5},... | collective-permute-start | bytes 442376 | tf_op jit(solution)/shard_map/ppermute | solution.py:303
  23.2 8.6 %collective-permute-start.9 = (bf16[2,288,128]{2,1,0:T(8,128)(2,1)}, bf16[2,288,128]{2,1,0:T(8,128)(2,1)}, u32[]{:S(2)}, u32[]{:S(2)}) collective-permute-start(bf16[2,288,128]{2,1,0:T(8,128)(2,1)} %collective-permute-done.8.refs_6_), channel_id=1, source_target_pairs={{0,14},{2,0},{4,2},{6,4},{8,6},{10,8},{12,10},{14,12},{1,15},{3,1}... | collective-permute-start | bytes 442376 | tf_op jit(solution)/shard_map/ppermute | solution.py:303
  28.5 5.6 %collective-permute-start.6 = (bf16[2,288,128]{2,1,0:T(8,128)(2,1)}, bf16[2,288,128]{2,1,0:T(8,128)(2,1)}, u32[]{:S(2)}, u32[]{:S(2)}) collective-permute-start(bf16[2,288,128]{2,1,0:T(8,128)(2,1)} %collective-permute-done.5.refs_3_), channel_id=1, source_target_pairs={{0,2},{2,4},{4,6},{6,8},{8,10},{10,12},{12,14},{14,0},{1,3},{3,5},... | collective-permute-start | bytes 442376 | tf_op jit(solution)/shard_map/ppermute | solution.py:303
  34.1 7.8 %collective-permute-start.10 = (bf16[128,4224]{1,0:T(8,128)(2,1)S(1)}, bf16[128,4224]{1,0:T(8,128)(2,1)}, u32[]{:S(2)}, u32[]{:S(2)}) collective-permute-start(bf16[128,4224]{1,0:T(8,128)(2,1)S(1)} %collective-permute-done.refs_10_), channel_id=1, source_target_pairs={{0,16},{16,0},{1,17},{17,1},{2,18},{18,2},{3,19},{19,3},{4,20},{20... | collective-permute-start | bytes 3244040 | tf_op jit(solution)/shard_map/ppermute | solution.py:299
  41.9 9.3 %copy-start.6 = (s32[48]{0:T(128)S(1)}, s32[48]{0:T(128)}, u32[]{:S(2)}) copy-start(s32[48]{0:T(128)} %param.11) | copy-start | bytes 580
  48.9 2.3 %collective-permute-start.11 = (bf16[56,512]{1,0:T(8,128)(2,1)S(1)}, bf16[56,512]{1,0:T(8,128)(2,1)S(1)}, u32[]{:S(2)}, u32[]{:S(2)}) collective-permute-start(bf16[56,512]{1,0:T(8,128)(2,1)S(1)} %get-tuple-element.47), channel_id=1, source_target_pairs={{0,16},{16,0},{1,17},{17,1},{2,18},{18,2},{3,19},{19,3},{4,20},{20... | collective-permute-start | bytes 172040 | tf_op jit(solution)/shard_map/ppermute | solution.py:299
  49.4 3.0 %collective-permute-start.12 = (bf16[56,512]{1,0:T(8,128)(2,1)S(1)}, bf16[56,512]{1,0:T(8,128)(2,1)S(1)}, u32[]{:S(2)}, u32[]{:S(2)}) collective-permute-start(bf16[56,512]{1,0:T(8,128)(2,1)S(1)} %get-tuple-element.48), channel_id=1, source_target_pairs={{0,32},{32,0},{1,33},{33,1},{2,34},{34,2},{3,35},{35,3},{4,36},{36... | collective-permute-start | bytes 172040 | tf_op jit(solution)/shard_map/ppermute | solution.py:299
  49.6 4.7 %collective-permute-start.13 = (bf16[56,512]{1,0:T(8,128)(2,1)S(1)}, bf16[56,512]{1,0:T(8,128)(2,1)S(1)}, u32[]{:S(2)}, u32[]{:S(2)}) collective-permute-start(bf16[56,512]{1,0:T(8,128)(2,1)S(1)} %get-tuple-element.49), channel_id=1, source_target_pairs={{0,48},{16,32},{32,16},{48,0},{1,49},{17,33},{33,17},{49,1},{2,50}... | collective-permute-start | bytes 172040 | tf_op jit(solution)/shard_map/ppermute | solution.py:312
  56.0 15.3 %all-to-all-start = ((bf16[16,16,256]{2,1,0:T(8,128)(2,1)}), bf16[16,16,256]{2,1,0:T(8,128)(2,1)S(1)}, u32[]{:S(2)}, u32[]{:S(2)}) async-start(bf16[16,16,256]{2,1,0:T(8,128)(2,1)} %get-tuple-element.53), calls=%async_computation | async-start | bytes 262144 | tf_op jit(solution)/shard_map/all_to_all | solution.py:403
